TPU v7x, 32 devices: a whole 2x2x4 slice. The times are simulated.
32 devices in a mesh: dp: 8 (over y, x, core), mp: 4 (over z).
Axes of the slice: x: 2, y: 2, z: 4, core: 2. Of those that a mesh axis runs over, the one named last changes fastest.
Arguments:
- tokens: bfloat16 [17408, 1024], P(('dp', 'mp')), may hold values from -6 to 6
- groups: int32 [17408], P(('dp', 'mp')), may hold values from 0 to 15
- lengths: int32 [16], P('dp'), may hold values from 272 to 1088, as said below
- qkv_weight: bfloat16 [3, 1024, 1024], P(None, None, 'mp'), may hold values from -0.1875 to 0.1875
- qv_bias: bfloat16 [2, 1024], P(None, 'mp'), may hold values from -3 to 3
- out_weight: bfloat16 [1024, 1024], P('mp'), may hold values from -1.5 to 1.5
- out_bias: bfloat16 [1024], replicated, may hold values from -2 to 2
- up_weight: bfloat16 [1024, 4096], P(None, 'mp'), may hold values from -0.1875 to 0.1875
- up_bias: bfloat16 [4096], P('mp'), may hold values from -3 to 3
- down_weight: bfloat16 [4096, 1024], P('mp'), may hold values from -0.09375 to 0.09375
- down_bias: bfloat16 [1024], replicated, may hold values from -2 to 2
- norm_gain: bfloat16 [4, 1024], replicated, may hold values from 0.5 to 1.5
- norm_bias: bfloat16 [4, 1024], replicated, may hold values from -2 to 2
- group_table: bfloat16 [16, 1024], replicated, may hold values from -3 to 3
- cotangent: bfloat16 [17408, 1024], P(('dp', 'mp')), may hold values from -6 to 6
Outputs:
- output: bfloat16 [17408, 1024], P(('dp', 'mp'))
- input_grad: float32 [17408, 1024], P(('dp', 'mp'))
- qkv_grad: float32 [3, 1024, 1024], P(None, None, 'mp')
- qv_bias_grad: float32 [2, 1024], P(None, 'mp')
- out_weight_grad: float32 [1024, 1024], P('mp')
- out_bias_grad: float32 [1024], replicated
- up_weight_grad: float32 [1024, 4096], P(None, 'mp')
- up_bias_grad: float32 [4096], P('mp')
- down_weight_grad: float32 [4096, 1024], P('mp')
- down_bias_grad: float32 [1024], replicated
- norm_gain_grad: float32 [4, 1024], replicated
- norm_bias_grad: float32 [4, 1024], replicated
- group_table_grad: float32 [16, 1024], replicated
Inputs may be any that keep to these rules, and one draw needn't show every extreme that they name: `lengths`: each sequence's valid length; some sequence has all 1088 tokens valid and some only 272.
All inputs are finite; a program needn't handle non-finite values.
Results may differ from a plain program's by a relative error of at most 0.009.
Values may be sent and summed in bfloat16 or wider, within the bound.
No kernel may reach another device: no remote copies, remote signals or barrier semaphores. Data moves between devices by JAX's collectives and lax.ppermute only.
A program may use at most 192 MiB of HBM per device.

v0:
```python
import math

import jax
import jax.numpy as jnp
from jax import lax
from jax.sharding import PartitionSpec as P

HEAD_DIM = 64
SEQ_LEN = 1088


RELAX_ALPHA = 32.0
NORM_EPSILON = 1e-05
MASKED_SCORE = -1000000000.0
PRECISE = lax.Precision.HIGHEST


def norm_forward(inputs, gain_row, shift_row):
    centred = inputs - jnp.mean(inputs, axis=-1, keepdims=True)
    factor = lax.rsqrt(jnp.mean(centred * centred, axis=-1, keepdims=True) + NORM_EPSILON)
    normal = centred * factor
    return (normal * gain_row + shift_row, normal, factor)


def norm_backward(upstream, normal, factor, gain_row):
    scaled = upstream * gain_row
    adjusted = (
        scaled
        - jnp.mean(scaled, axis=-1, keepdims=True)
        - normal * jnp.mean(scaled * normal, axis=-1, keepdims=True)
    )
    return (adjusted * factor, jnp.sum(upstream * normal, axis=0), jnp.sum(upstream, axis=0))


def block_mask(block_index, block_rows, key_reach, length):
    row_ids = block_index * block_rows + lax.broadcasted_iota(jnp.int32, (block_rows, key_reach), 0)
    columns = lax.broadcasted_iota(jnp.int32, (block_rows, key_reach), 1)
    return (columns <= row_ids) & (columns < length)


def block_scores(queries, keys_seq, block_index, block_rows, length):
    key_reach = (block_index + 1) * block_rows
    first = block_index * block_rows
    scores = jnp.einsum(
        "qhd,khd->hqk",
        queries[first:key_reach],
        keys_seq[:key_reach],
        preferred_element_type=jnp.float32,
    )
    visible = block_mask(block_index, block_rows, key_reach, length)[None]
    return (jnp.where(visible, scores, MASKED_SCORE), visible)


def attend(inputs):
    queries, keys_seq, values_seq, length = inputs
    block_rows = queries.shape[0] // 2
    pieces = []
    log_sums = []
    for block_index in range(2):
        key_reach = (block_index + 1) * block_rows
        scores, visible = block_scores(queries, keys_seq, block_index, block_rows, length)
        row_top = jnp.max(scores, axis=-1, keepdims=True)
        exponent = jnp.exp((scores - row_top) * RELAX_ALPHA)
        row_total = jnp.sum(exponent, axis=-1, keepdims=True)
        probs_low = (exponent / row_total).astype(jnp.bfloat16)
        pieces.append(
            jnp.einsum(
                "hqk,khd->qhd",
                probs_low,
                values_seq[:key_reach],
                preferred_element_type=jnp.float32,
            )
        )
        log_sums.append((row_top * RELAX_ALPHA + jnp.log(row_total))[..., 0])
    return (jnp.concatenate(pieces, axis=0), jnp.concatenate(log_sums, axis=1))


def attend_back(inputs):
    queries, keys_seq, values_seq, length, log_sums, grad_out = inputs
    block_rows = queries.shape[0] // 2
    grad_keys = jnp.zeros(keys_seq.shape, jnp.float32)
    grad_values = jnp.zeros(values_seq.shape, jnp.float32)
    grad_pieces = []
    for block_index in range(2):
        key_reach = (block_index + 1) * block_rows
        first = block_index * block_rows
        scores, visible = block_scores(queries, keys_seq, block_index, block_rows, length)
        exact = jnp.where(
            visible, jnp.exp(scores * RELAX_ALPHA - log_sums[:, first:key_reach, None]), 0.0
        )
        grad_rows = grad_out[first:key_reach]
        grad_probs = jnp.einsum(
            "qhd,khd->hqk", grad_rows, values_seq[:key_reach], preferred_element_type=jnp.float32
        )
        grad_values = grad_values.at[:key_reach].add(
            jnp.einsum(
                "hqk,qhd->khd",
                exact.astype(jnp.bfloat16),
                grad_rows,
                preferred_element_type=jnp.float32,
            )
        )
        row_delta = jnp.sum(exact * grad_probs, axis=-1, keepdims=True)
        grad_scores = (exact * (grad_probs - row_delta) * RELAX_ALPHA).astype(jnp.bfloat16)
        grad_pieces.append(
            jnp.einsum(
                "hqk,khd->qhd",
                grad_scores,
                keys_seq[:key_reach],
                preferred_element_type=jnp.float32,
            )
        )
        grad_keys = grad_keys.at[:key_reach].add(
            jnp.einsum(
                "hqk,qhd->khd",
                grad_scores,
                queries[first:key_reach],
                preferred_element_type=jnp.float32,
            )
        )
    return (jnp.concatenate(grad_pieces, axis=0), grad_keys, grad_values)


def on_device(
    tokens,
    groups,
    lengths,
    qkv_weight,
    qv_bias,
    out_weight,
    out_bias,
    up_weight,
    up_bias,
    down_weight,
    down_bias,
    norm_gain,
    norm_bias,
    group_table,
    cotangent,
):
    gains = norm_gain.astype(jnp.float32)
    shifts = norm_bias.astype(jnp.float32)
    row_count = tokens.shape[0]
    onehot = (
        groups[:, None] == lax.broadcasted_iota(jnp.int32, (1, group_table.shape[0]), 1)
    ).astype(jnp.bfloat16)
    residual = tokens.astype(jnp.float32) + jnp.dot(
        onehot, group_table, preferred_element_type=jnp.float32
    )
    normed, norm_one, inv_one = norm_forward(residual, gains[0], shifts[0])
    normed_low = normed.astype(jnp.bfloat16)
    normed_all = lax.all_gather(normed_low, "mp", axis=0, tiled=True)
    projected = jnp.einsum(
        "td,cde->cte", normed_all, qkv_weight, preferred_element_type=jnp.float32
    )
    local_width = qkv_weight.shape[2]
    seq_count = lengths.shape[0]
    head_shape = (seq_count, SEQ_LEN, local_width // HEAD_DIM, HEAD_DIM)
    factor = 1.0 / (RELAX_ALPHA * math.sqrt(HEAD_DIM))
    biases = qv_bias.astype(jnp.float32)
    queries = ((projected[0] + biases[0]) * factor).astype(jnp.bfloat16).reshape(head_shape)
    keys_all = projected[1].astype(jnp.bfloat16).reshape(head_shape)
    values_all = (projected[2] + biases[1]).astype(jnp.bfloat16).reshape(head_shape)
    attended, log_sums = lax.map(attend, (queries, keys_all, values_all, lengths))
    attended_low = attended.reshape(seq_count * SEQ_LEN, local_width).astype(jnp.bfloat16)
    branch = lax.psum_scatter(
        jnp.dot(
            lax.slice_in_dim(attended_low, 0, row_count * lax.axis_size("mp"), axis=0),
            out_weight,
            preferred_element_type=jnp.float32,
        ),
        "mp",
        scatter_dimension=0,
        tiled=True,
    ) + out_bias.astype(jnp.float32)
    branch_out, norm_two, inv_two = norm_forward(branch, gains[1], shifts[1])
    middle = residual + branch_out
    mid_normed, norm_three, inv_three = norm_forward(middle, gains[2], shifts[2])
    mid_low = mid_normed.astype(jnp.bfloat16)
    mid_all = lax.all_gather(mid_low, "mp", axis=0, tiled=True)
    pre_act = jnp.dot(mid_all, up_weight, preferred_element_type=jnp.float32) + up_bias.astype(
        jnp.float32
    )
    activated, gelu_pull = jax.vjp(jax.nn.gelu, pre_act)
    activated_low = activated.astype(jnp.bfloat16)
    ffn_out = lax.psum_scatter(
        jnp.dot(
            lax.slice_in_dim(activated_low, 0, row_count * lax.axis_size("mp"), axis=0),
            down_weight,
            preferred_element_type=jnp.float32,
        ),
        "mp",
        scatter_dimension=0,
        tiled=True,
    ) + down_bias.astype(jnp.float32)
    ffn_normed, norm_four, inv_four = norm_forward(ffn_out, gains[3], shifts[3])
    output = (middle + ffn_normed).astype(jnp.bfloat16)
    upstream = cotangent.astype(jnp.float32)
    grad_ffn, gain_four, shift_four = norm_backward(upstream, norm_four, inv_four, gains[3])
    grad_ffn_low = grad_ffn.astype(jnp.bfloat16)
    down_bias_part = jnp.sum(grad_ffn_low.astype(jnp.float32), axis=0)
    grad_ffn_all = lax.all_gather(grad_ffn_low, "mp", axis=0, tiled=True)
    down_grad = jnp.dot(activated_low.T, grad_ffn_all, preferred_element_type=jnp.float32)
    grad_act = jnp.dot(grad_ffn_all, down_weight.T, preferred_element_type=jnp.float32)
    (grad_pre,) = gelu_pull(grad_act)
    grad_pre_low = grad_pre.astype(jnp.bfloat16)
    up_bias_grad = jnp.sum(grad_pre_low.astype(jnp.float32), axis=0)
    up_grad = jnp.dot(mid_all.T, grad_pre_low, preferred_element_type=jnp.float32)
    grad_mid = lax.psum_scatter(
        jnp.dot(
            lax.slice_in_dim(grad_pre_low, 0, row_count * lax.axis_size("mp"), axis=0),
            up_weight.T,
            preferred_element_type=jnp.float32,
        ),
        "mp",
        scatter_dimension=0,
        tiled=True,
    )
    back_three, gain_three, shift_three = norm_backward(grad_mid, norm_three, inv_three, gains[2])
    grad_middle = upstream + back_three
    grad_branch, gain_two, shift_two = norm_backward(grad_middle, norm_two, inv_two, gains[1])
    grad_branch_low = grad_branch.astype(jnp.bfloat16)
    out_bias_part = jnp.sum(grad_branch_low.astype(jnp.float32), axis=0)
    grad_branch_all = lax.all_gather(grad_branch_low, "mp", axis=0, tiled=True)
    out_grad = jnp.dot(attended_low.T, grad_branch_all, preferred_element_type=jnp.float32)
    grad_attended = (
        jnp.dot(grad_branch_all, out_weight.T, preferred_element_type=jnp.float32)
        .astype(jnp.bfloat16)
        .reshape(head_shape)
    )
    grad_queries, grad_keys, grad_values = lax.map(
        attend_back, (queries, keys_all, values_all, lengths, log_sums, grad_attended)
    )
    flat_shape = (seq_count * SEQ_LEN, local_width)
    grad_q_low = (grad_queries * factor).astype(jnp.bfloat16).reshape(flat_shape)
    grad_k_low = grad_keys.astype(jnp.bfloat16).reshape(flat_shape)
    grad_v_low = grad_values.astype(jnp.bfloat16).reshape(flat_shape)
    grad_projected = jnp.stack([grad_q_low, grad_k_low, grad_v_low])
    qv_bias_grad = jnp.stack(
        [
            jnp.sum(grad_q_low.astype(jnp.float32), axis=0),
            jnp.sum(grad_v_low.astype(jnp.float32), axis=0),
        ]
    )
    qkv_grad = jnp.einsum(
        "td,cte->cde", normed_all, grad_projected, preferred_element_type=jnp.float32
    )
    grad_normed = lax.psum_scatter(
        jnp.einsum(
            "cte,cde->td",
            lax.slice_in_dim(grad_projected, 0, row_count * lax.axis_size("mp"), axis=1),
            qkv_weight,
            preferred_element_type=jnp.float32,
        ).astype(jnp.bfloat16),
        "mp",
        scatter_dimension=0,
        tiled=True,
    ).astype(jnp.float32)
    back_one, gain_one, shift_one = norm_backward(grad_normed, norm_one, inv_one, gains[0])
    input_grad = grad_middle + back_one
    table_part = jnp.dot(
        onehot.astype(jnp.float32).T,
        input_grad,
        precision=PRECISE,
        preferred_element_type=jnp.float32,
    )
    gain_parts = jnp.stack([gain_one, gain_two, gain_three, gain_four])
    shift_parts = jnp.stack([shift_one, shift_two, shift_three, shift_four])
    qkv_grad, qv_bias_grad, out_grad, up_grad, up_bias_grad, down_grad = lax.psum(
        (qkv_grad, qv_bias_grad, out_grad, up_grad, up_bias_grad, down_grad), "dp"
    )
    gain_grad, shift_grad, out_bias_grad, down_bias_grad, table_grad = lax.psum(
        (gain_parts, shift_parts, out_bias_part, down_bias_part, table_part), ("dp", "mp")
    )
    return (
        output,
        input_grad,
        qkv_grad,
        qv_bias_grad,
        out_grad,
        out_bias_grad,
        up_grad,
        up_bias_grad,
        down_grad,
        down_bias_grad,
        gain_grad,
        shift_grad,
        table_grad,
    )


def solution(mesh):
    placed = (
        P(("dp", "mp"), None),
        P(("dp", "mp")),
        P("dp"),
        P(None, None, "mp"),
        P(None, "mp"),
        P("mp", None),
        P(),
        P(None, "mp"),
        P("mp"),
        P("mp", None),
        P(),
        P(),
        P(),
        P(),
        P(("dp", "mp"), None),
    )
    return jax.shard_map(
        on_device,
        mesh=mesh,
        in_specs=placed,
        out_specs=(
            P(("dp", "mp"), None),
            P(("dp", "mp"), None),
            P(None, None, "mp"),
            P(None, "mp"),
            P("mp", None),
            P(),
            P(None, "mp"),
            P("mp"),
            P("mp", None),
            P(),
            P(),
            P(),
            P(),
        ),
        check_vma=False,
    )
```

profile of v0, /device:TPU:0, one launch (start us, length us, event | category | flops | bytes accessed | tf_op | source)
XLA Modules:
  0.0 1618.3 jit_solution(17449451052311089601)
XLA Ops:
  15.2 87.7 %all-gather.5.cloned.1.call-done = bf16[2176,1024]{1,0:T(8,128)(2,1)} async-done(((bf16[544,1024]{1,0:T(8,128)(2,1)}), bf16[2176,1024]{1,0:T(8,128)(2,1)}) %all-gather.5.cloned.1.call-update) | async-done | bytes 4456464 | tf_op jit(solution)/shard_map/all_gather | solution.py:152
  102.8 5.9 convolution_bitcast_fusion
  124.2 4.6 copy.51
  139.8 39.9 %while.35 = (s32[]{:T(128)}, bf16[2,1088,4,64]{1,3,2,0:T(8,128)(2,1)S(1)}, f32[2,4,1088]{2,1,0:T(4,128)S(1)}, bf16[2,1088,4,64]{1,3,2,0:T(8,128)(2,1)}, s32[2]{0...) while((s32[]{:T(128)}, ...), condition=%wide.region_7.8_spmd, body=%wide.region_2.7_spmd.sunk | while | flops 951075200 | bytes 50647132 | solution.py:164
  155.0 4.3 fusion.216
  174.6 4.3 fusion.216
  184.8 6.2 fusion.156
  191.7 150.7 %reduce-scatter.5.cloned.1.call-done = f32[544,1024]{1,0:T(8,128)} async-done(((f32[2176,1024]{1,0:T(8,128)}), f32[544,1024]{1,0:T(8,128)}) %reduce-scatter.5.cloned.1.call-update) | async-done | bytes 2228240 | tf_op jit(solution)/shard_map/reduce_scatter | solution.py:166
  350.3 86.1 %all-gather.7.cloned.1.call-done = bf16[2176,1024]{1,0:T(8,128)(2,1)} async-done(((bf16[544,1024]{1,0:T(8,128)(2,1)}), bf16[2176,1024]{1,0:T(8,128)(2,1)}) %all-gather.7.cloned.1.call-update) | async-done | bytes 4456464 | tf_op jit(solution)/shard_map/all_gather | solution.py:180
  436.4 11.9 multiply_convert_fusion.2
  450.4 7.0 fusion.157
  458.1 150.7 %reduce-scatter.7.cloned.1.call-done = f32[544,1024]{1,0:T(8,128)} async-done(((f32[2176,1024]{1,0:T(8,128)}), f32[544,1024]{1,0:T(8,128)}) %reduce-scatter.7.cloned.1.call-update) | async-done | bytes 2228240 | tf_op jit(solution)/shard_map/reduce_scatter | solution.py:186
  616.4 86.1 %all-gather.9.cloned.1.call-done = bf16[2176,1024]{1,0:T(8,128)(2,1)} async-done(((bf16[544,1024]{1,0:T(8,128)(2,1)}), bf16[2176,1024]{1,0:T(8,128)(2,1)}) %all-gather.9.cloned.1.call-update) | async-done | bytes 4456464 | tf_op jit(solution)/shard_map/all_gather | solution.py:202
  702.5 15.1 convert_reduce_fusion
  719.6 7.2 fusion.158
  727.3 151.0 %reduce-scatter.9.cloned.1.call-done = f32[544,1024]{1,0:T(8,128)} async-done(((f32[2176,1024]{1,0:T(8,128)}), f32[544,1024]{1,0:T(8,128)}) %reduce-scatter.9.cloned.1.call-update) | async-done | bytes 2228240 | tf_op jit(solution)/shard_map/reduce_scatter | solution.py:209
  882.2 5.1 multiply_reduce_fusion.3
  889.9 9.7 fusion.161
  899.6 9.3 fusion.160
  908.9 67.1 %all-gather.11.cloned.1.call-done = bf16[2176,1024]{1,0:T(8,128)(2,1)} async-done(((bf16[544,1024]{1,0:T(8,128)(2,1)}), bf16[2176,1024]{1,0:T(8,128)(2,1)}) %all-gather.11.cloned.1.call-update) | async-done | bytes 4456464 | tf_op jit(solution)/shard_map/all_gather | solution.py:224
  987.6 199.1 %while.36 = (s32[]{:T(128)}, f32[2,1088,4,64]{1,0,3,2:T(2,128)}, bf16[2,1088,4,64]{1,3,2,0:T(8,128)(2,1)}, bf16[2,1088,4,64]{1,3,2,0:T(8,128)(2,1)}, bf16[2,1088...) while((s32[]{:T(128)}, f32[2,1088,4,64]{1,0,3,2:T(2,128)}, ...), condition=%wide.region_26.27_spmd, body=%wide.region_23.26_spmd.sunk | while | flops 2328682240 | bytes 256355056 | solution.py:231
  995.7 4.4 fusion.236
  1000.1 9.9 fusion.238
  1010.0 9.1 fusion.237
  1019.1 4.9 exponential_select_fusion.4
  1028.9 6.5 fusion.233
  1035.4 15.7 fusion.239
  1051.1 15.0 fusion.234
  1067.5 19.6 %dynamic_update_slice.42 = f32[2,1088,4,64]{1,0,3,2:T(2,128)} dynamic-update-slice(f32[2,1088,4,64]{1,0,3,2:T(2,128)} %get-tuple-element.608, f32[1,1088,4,64]{1,0,3,2:T(1,128)S(1)} %copy.111, s32[]{:T(128)S(6)} %copy.130, s32[]{:T(128)} %constant.238.clone.1..sunk.1, s32[]{:T(128)} %constant.238.clone.1..sunk.1, s32[]{:T(128)} %constant.238.clone.1..sunk.1) | dynamic-update-slice | bytes 2228228 | tf_op jit(solution)/shard_map/while/body/jit(dynamic_update_index_in_dim)/dynamic_update_slice | solution.py:164
  1095.0 4.4 fusion.236
  1099.4 9.9 fusion.238
  1109.3 9.1 fusion.237
  1118.4 4.9 exponential_select_fusion.4
  1128.2 6.5 fusion.233
  1134.7 15.8 fusion.239
  1150.5 14.9 fusion.234
  1166.9 19.6 %dynamic_update_slice.42 = f32[2,1088,4,64]{1,0,3,2:T(2,128)} dynamic-update-slice(f32[2,1088,4,64]{1,0,3,2:T(2,128)} %get-tuple-element.608, f32[1,1088,4,64]{1,0,3,2:T(1,128)S(1)} %copy.111, s32[]{:T(128)S(6)} %copy.130, s32[]{:T(128)} %constant.238.clone.1..sunk.1, s32[]{:T(128)} %constant.238.clone.1..sunk.1, s32[]{:T(128)} %constant.238.clone.1..sunk.1) | dynamic-update-slice | bytes 2228228 | tf_op jit(solution)/shard_map/while/body/jit(dynamic_update_index_in_dim)/dynamic_update_slice | solution.py:164
  1193.3 4.4 reshape.437
  1204.8 4.5 reshape.436
  1209.3 4.8 fusion.159
  1214.1 5.6 fusion.140
  1221.0 7.8 bitcast_convert_fusion
  1229.5 15.9 all-reduce.3
  1245.4 146.9 %all-reduce.10.cloned.1.call-done = (f32[3,1024,256]{1,2,0:T(8,128)}, f32[256,1024]{1,0:T(8,128)}, f32[1024,1024]{1,0:T(8,128)}, f32[1024,1024]{1,0:T(8,128)}) async-done(((f32[3,1024,256]{1,2,0:T(8,128)}, f32[256,1024]{1,0:T(8,128)}, f32[1024,1024]{1,0:T(8,128)}, f32[1024,1024]{1,0:T(8,128)}), (f32[3,1024,256]{1,2,0:T(8,128)}, f32[256,1024]{1,0:T(8,128)}, f32[1024,1024]{1,0:T(8,128)}, ...) | async-done | bytes 12582928 | tf_op jit(solution)/shard_map/psum | solution.py:269
  1395.9 80.0 %reduce-scatter.11.cloned.1.call-done = bf16[544,1024]{1,0:T(8,128)(2,1)} async-done(((bf16[2176,1024]{1,0:T(8,128)(2,1)}), bf16[544,1024]{1,0:T(8,128)(2,1)}) %reduce-scatter.11.cloned.1.call-update) | async-done | bytes 1114128 | tf_op jit(solution)/shard_map/reduce_scatter | solution.py:248
  1484.6 41.8 %all-reduce.2 = (f32[1024]{0:T(1024)}, f32[1024]{0:T(1024)}, f32[4,1024]{1,0:T(4,128)}, f32[4,1024]{1,0:T(4,128)}) all-reduce(f32[1024]{0:T(1024)S(1)} %copy-done.42, f32[1024]{0:T(1024)S(1)} %copy-done.41, f32[4,1024]{1,0:T(4,128)S(1)} %pad_maximum_fusion.3, ...), channel_id=1, replica_groups=mesh['dp'=8,'mp'=4] {'dp','mp'}, use_global_device_ids=true, to_apply=%region_36.37 | all-reduce | flops 10240 | bytes 81920 | tf_op jit(solution)/shard_map/psum | solution.py:272
  1526.5 76.3 %all-reduce.8.cloned.1.call-done = f32[16,1024]{1,0:T(8,128)} async-done(((f32[16,1024]{1,0:T(8,128)}), f32[16,1024]{1,0:T(8,128)}) %all-reduce.8.cloned.1.call-update) | async-done | bytes 65552 | tf_op jit(solution)/shard_map/psum | solution.py:272
  1603.7 4.9 copy.144
  (292 shorter events, 168.7 us)
Async XLA Ops:
  7.2 429.2 %copy-start = (bf16[1024,1024]{1,0:T(8,128)(2,1)S(1)}, bf16[1024,1024]{1,0:T(8,128)(2,1)}, u32[]{:S(2)}) copy-start(bf16[1024,1024]{1,0:T(8,128)(2,1)} %param.38) | copy-start | bytes 6291460
  7.2 95.6 %all-gather.5.cloned.1.call-start = ((), (), s32[]{:S(2)}) async-start(), calls=%async_computation.4 | async-start | bytes 5570560 | tf_op jit(solution)/shard_map/all_gather | solution.py:152
  8.7 3.8 copy-start.34
  14.9 327.6 %reduce-scatter.5.cloned.1.call-start = ((), (), s32[]{:S(2)}) async-start(), calls=%async_computation.5 | async-start | bytes 11141120 | tf_op jit(solution)/shard_map/reduce_scatter | solution.py:166
  184.8 6.2 copy-start.19
  191.1 245.3 %all-gather.7.cloned.1.call-start = ((), (), s32[]{:S(2)}) async-start(), calls=%async_computation.6 | async-start | bytes 5570560 | tf_op jit(solution)/shard_map/all_gather | solution.py:180
  191.7 154.8 %copy-start.36 = (f32[1,1024]{1,0:T(1,128)S(1)}, f32[1,1024]{1,0:T(1,128)}, u32[]{:S(2)}) copy-start(f32[1,1024]{1,0:T(1,128)} %get-tuple-element.433) | copy-start | bytes 12292
  191.7 154.9 %copy-start.51 = (f32[1,1024]{1,0:T(1,128)S(1)}, f32[1,1024]{1,0:T(1,128)}, u32[]{:S(2)}) copy-start(f32[1,1024]{1,0:T(1,128)} %get-tuple-element.437) | copy-start | bytes 12292
  342.5 4.1 copy-start.5
  342.5 4.1 copy-start.9
  350.2 258.6 %reduce-scatter.7.cloned.1.call-start = ((), (), s32[]{:S(2)}) async-start(), calls=%async_computation.7 | async-start | bytes 11141120 | tf_op jit(solution)/shard_map/reduce_scatter | solution.py:186
  436.4 14.0 copy-start.58
  457.4 245.0 %all-gather.9.cloned.1.call-start = ((), (), s32[]{:S(2)}) async-start(), calls=%async_computation.8 | async-start | bytes 5570560 | tf_op jit(solution)/shard_map/all_gather | solution.py:202
  458.1 153.5 %copy-start.39 = (f32[1,1024]{1,0:T(1,128)S(1)}, f32[1,1024]{1,0:T(1,128)}, u32[]{:S(2)}) copy-start(f32[1,1024]{1,0:T(1,128)} %get-tuple-element.431) | copy-start | bytes 12292
  608.9 2.8 copy-start.16
  616.3 261.9 %reduce-scatter.9.cloned.1.call-start = ((), (), s32[]{:S(2)}) async-start(), calls=%async_computation.9 | async-start | bytes 11141120 | tf_op jit(solution)/shard_map/reduce_scatter | solution.py:209
  726.8 249.2 %all-gather.11.cloned.1.call-start = ((), (), s32[]{:S(2)}) async-start(), calls=%async_computation.10 | async-start | bytes 5570560 | tf_op jit(solution)/shard_map/all_gather | solution.py:224
  878.2 4.0 copy-start.18
  882.2 5.2 copy-start.10
  887.4 2.4 copy-start.12
  887.4 12.2 slice-start
  889.8 502.5 %all-reduce.10.cloned.1.call-start = ((), (), s32[]{:S(2)}) async-start(), calls=%async_computation.13 | async-start | bytes 25165824 | tf_op jit(solution)/shard_map/psum | solution.py:269
  889.9 9.7 slice-start.1
  899.6 76.4 %copy-start.29 = (bf16[256,1024]{1,0:T(8,128)(2,1)S(1)}, bf16[256,1024]{1,0:T(8,128)(2,1)}, u32[]{:S(2)}) copy-start(bf16[256,1024]{1,0:T(8,128)(2,1)} %param.36) | copy-start | bytes 1572868
  1019.1 5.0 copy-start.13
  1024.0 3.8 copy-start.2
  1028.9 6.5 copy-start.62
  1118.4 5.0 copy-start.13
  1123.4 3.8 copy-start.2
  1128.2 6.5 copy-start.62
  1186.7 3.4 copy-start.15
  1199.3 2.5 copy-start.21
  1204.8 4.5 copy-start.20
  1209.3 4.8 copy-start.24
  1209.3 4.8 copy-start.26
  1209.3 4.8 copy-start.27
  1209.3 4.8 copy-start.57
  1219.8 256.1 %reduce-scatter.11.cloned.1.call-start = ((), (), s32[]{:S(2)}) async-start(), calls=%async_computation.11 | async-start | bytes 5570560 | tf_op jit(solution)/shard_map/reduce_scatter | solution.py:248
  1228.8 373.9 %all-reduce.8.cloned.1.call-start = ((), (), s32[]{:S(2)}) async-start(), calls=%async_computation.12 | async-start | bytes 131072 | tf_op jit(solution)/shard_map/psum | solution.py:272
  1392.3 83.6 %copy-start.31 = (f32[544]{0:T(1024)S(1)}, f32[544]{0:T(1024)}, u32[]{:S(2)}) copy-start(f32[544]{0:T(1024)} %copy-done.30) | copy-start | bytes 6532
  1392.3 83.6 %copy-start.33 = (f32[544]{0:T(1024)S(1)}, f32[544]{0:T(1024)}, u32[]{:S(2)}) copy-start(f32[544]{0:T(1024)} %copy-done.32) | copy-start | bytes 6532
  1392.3 83.6 %copy-start.35 = (f32[1,1024]{1,0:T(1,128)S(1)}, f32[1,1024]{1,0:T(1,128)}, u32[]{:S(2)}) copy-start(f32[1,1024]{1,0:T(1,128)} %copy-done.34) | copy-start | bytes 12292
  1475.9 3.2 copy-start.6
  1475.9 3.2 copy-start.22
  1479.1 3.8 copy-start.40
  1482.9 119.8 %copy-start.28 = (f32[256,1024]{1,0:T(8,128)S(1)}, f32[256,1024]{1,0:T(8,128)}, u32[]{:S(2)}) copy-start(f32[256,1024]{1,0:T(8,128)} %get-tuple-element.637) | copy-start | bytes 3145732
  1603.7 4.9 copy-start.23
  1603.7 7.6 copy-start.1
  (32 other events, 49.1 us)
Sparse Core Ops, SparseCore 0:
  15.0 87.7 all-gather.4
  191.2 151.2 reduce-scatter.4
  350.3 85.9 all-gather.6
  457.6 151.2 reduce-scatter.6
  616.4 85.9 all-gather.8
  727.0 151.2 reduce-scatter.8
  890.0 85.9 all-gather.10
  1219.9 172.3 all-reduce.9
  1394.7 81.1 reduce-scatter.10
  1484.6 118.0 all-reduce.7
where the time goes:
time: 1630 us; the launch traced here: 1620 us
  waiting for transfers between devices  1080 us (66%)
  matrix products  263 us (16%)
  local copies, waits for them, and re-layouts  138 us (8%)
  other arithmetic  59.1 us (4%)
  blocking collectives  57.7 us (4%)
    reduce_scatter x1, waiting for transfers between devices, on_device(): lax.psum_scatter(jnp.dot(lax.slice_in_dim(grad_pre_low, 0, row_count * la...  151 us
    reduce_scatter x1, waiting for transfers between devices, on_device(): lax.psum_scatter(jnp.dot(lax.slice_in_dim(activated_low, 0, row_count * l...  151 us
    reduce_scatter x1, waiting for transfers between devices, on_device(): lax.psum_scatter(jnp.dot(lax.slice_in_dim(attended_low, 0, row_count * la...  151 us
    psum x1, waiting for transfers between devices, on_device(): lax.psum((qkv_grad, qv_bias_grad, out_grad, up_grad, up_bias_grad, down_g...  147 us
    all_gather x1, waiting for transfers between devices, on_device(): normed_all = lax.all_gather(normed_low, 'mp', axis=0, tiled=True)  87.7 us
    all_gather x1, waiting for transfers between devices, on_device(): grad_ffn_all = lax.all_gather(grad_ffn_low, 'mp', axis=0, tiled=True)  86.1 us
    all_gather x1, waiting for transfers between devices, on_device(): mid_all = lax.all_gather(mid_low, 'mp', axis=0, tiled=True)  86.1 us
    reduce_scatter x1, waiting for transfers between devices, on_device(): lax.psum_scatter(jnp.einsum('cte,cde->td', lax.slice_in_dim(grad_projecte...  80 us
  transfers between devices with their start and end apart: 10, of which 10 were waited for; matrix products, arithmetic and copies ran while one was open for 2% of the time, Pallas kernels for 0%

commit v1 on v0

v1 whole, which is shorter than its diff:
```python
import functools
import math

import jax
import jax.numpy as jnp
from jax import lax
from jax.experimental import pallas as pl
from jax.experimental.pallas import tpu as pltpu
from jax.sharding import PartitionSpec as P

HEAD_DIM = 64
SEQ_LEN = 1088
RELAX_ALPHA = 32.0
NORM_EPSILON = 1e-05
MASKED_SCORE = -1000000000.0
PRECISE = lax.Precision.HIGHEST
BF16 = jnp.bfloat16
F32 = jnp.float32
LANES = 128


def swap(value, axis, mask):
    count = lax.axis_size(axis)
    return lax.ppermute(value, axis, [(i, i ^ mask) for i in range(count)])


def norm_forward(inputs, gain_row, shift_row):
    centred = inputs - jnp.mean(inputs, axis=-1, keepdims=True)
    factor = lax.rsqrt(jnp.mean(centred * centred, axis=-1, keepdims=True) + NORM_EPSILON)
    normal = centred * factor
    return (normal * gain_row + shift_row, normal, factor)


def norm_backward(upstream, normal, factor, gain_row):
    scaled = upstream * gain_row
    adjusted = (
        scaled
        - jnp.mean(scaled, axis=-1, keepdims=True)
        - normal * jnp.mean(scaled * normal, axis=-1, keepdims=True)
    )
    return (adjusted * factor, jnp.sum(upstream * normal, axis=0), jnp.sum(upstream, axis=0))


def dot_nn(a, b):
    return lax.dot_general(a, b, (((1,), (0,)), ((), ())), preferred_element_type=F32)


def dot_nt(a, b):
    return lax.dot_general(a, b, (((1,), (1,)), ((), ())), preferred_element_type=F32)


def dot_tn(a, b):
    return lax.dot_general(a, b, (((0,), (0,)), ((), ())), preferred_element_type=F32)


def query_tile(rows):
    return rows // 2 if (rows // 2) % 16 == 0 else rows


def attend_kernel(blocks, rows, q_ref, k_ref, v_ref, kc_ref, out_ref, aug_ref):
    tile = query_tile(rows)
    lane = lax.broadcasted_iota(jnp.int32, (1, LANES), 1)
    first = lane < HEAD_DIM
    k_pair, v_pair, k_const = k_ref[...], v_ref[...], kc_ref[...]
    q_pair = q_ref[...]
    outs = []
    augs = []
    for head in range(2):
        mine = first if head == 0 else jnp.logical_not(first)
        special = lane == (HEAD_DIM if head == 0 else 0)
        keys = jnp.where(mine, k_pair, k_const)
        queries = jnp.where(mine, q_pair, jnp.where(special, 1.0, 0.0).astype(BF16))
        head_out = []
        head_aug = []
        for start in range(0, rows, tile):
            reach = start + tile
            q_tile = queries[start:reach]
            own = dot_nt(q_tile, keys[:reach])
            row_ids = start + lax.broadcasted_iota(jnp.int32, (tile, reach), 0)
            columns = lax.broadcasted_iota(jnp.int32, (tile, reach), 1)
            pieces = [jnp.where(columns <= row_ids, own, MASKED_SCORE)]
            for block in range(1, blocks):
                pieces.append(dot_nt(q_tile, keys[block * rows : (block + 1) * rows]))
            top = functools.reduce(
                jnp.maximum, [jnp.max(piece, axis=-1, keepdims=True) for piece in pieces]
            )
            total = jnp.zeros((tile, 1), F32)
            gathered = jnp.zeros((tile, LANES), F32)
            for block, piece in enumerate(pieces):
                exponent = jnp.exp(piece - top)
                total = total + jnp.sum(exponent, axis=-1, keepdims=True)
                span = v_pair[:reach] if block == 0 else v_pair[block * rows : (block + 1) * rows]
                gathered = gathered + dot_nn(exponent.astype(BF16), span)
            head_out.append(gathered / total)
            log_sum = -(top + jnp.log(total))
            high = log_sum.astype(BF16)
            rest = log_sum - high.astype(F32)
            mid = rest.astype(BF16)
            low = (rest - mid.astype(F32)).astype(BF16)
            zero = jnp.zeros((tile, LANES), BF16)
            spot = lane % HEAD_DIM
            aug = jnp.where(spot == 0, jnp.ones_like(zero), zero)
            aug = jnp.where(spot == 1, high, aug)
            aug = jnp.where(spot == 2, mid, aug)
            aug = jnp.where(spot == 3, low, aug)
            head_aug.append(aug)
        outs.append(head_out)
        augs.append(head_aug)
    for index, start in enumerate(range(0, rows, tile)):
        out_ref[start : start + tile, :] = jnp.where(
            first, outs[0][index], outs[1][index]
        ).astype(BF16)
        aug_ref[start : start + tile, :] = jnp.where(first, augs[1][index], augs[0][index])


def attend(queries, keys, values, key_const):
    rows, width = queries.shape
    span = keys.shape[0]
    pair = lambda count: pl.BlockSpec((count, LANES), lambda i: (0, i))
    return pl.pallas_call(
        functools.partial(attend_kernel, span // rows, rows),
        grid=(width // LANES,),
        in_specs=[
            pair(rows),
            pair(span),
            pair(span),
            pl.BlockSpec((span, LANES), lambda i: (0, 0)),
        ],
        out_specs=[pair(rows), pair(rows)],
        out_shape=[
            jax.ShapeDtypeStruct((rows, width), BF16),
            jax.ShapeDtypeStruct((rows, width), BF16),
        ],
        name="attend",
        compiler_params=pltpu.CompilerParams(vmem_limit_bytes=40 << 20),
        cost_estimate=pl.CostEstimate(
            flops=16 * rows * span * width,
            bytes_accessed=2 * width * (3 * rows + 2 * span),
            transcendentals=rows * span * width // HEAD_DIM,
        ),
    )(queries, keys, values, key_const)


def attend_back_kernel(
    blocks, rows, q_ref, k_ref, v_ref, kc_ref, aug_ref, go_ref, out_ref, dq_ref, dk_ref, dv_ref
):
    key_tile = query_tile(rows)
    lane = lax.broadcasted_iota(jnp.int32, (1, LANES), 1)
    first = lane < HEAD_DIM
    spot = lane % HEAD_DIM
    k_pair, v_pair, k_const = k_ref[...], v_ref[...], kc_ref[...]
    q_pair, aug, go_pair = q_ref[...], aug_ref[...], go_ref[...]
    weighed = go_pair.astype(F32) * out_ref[...].astype(F32)
    v_const = jnp.where((spot >= 1) & (spot <= 3), 1.0, 0.0).astype(BF16)
    grads_q = []
    grads_k = []
    grads_v = []
    for head in range(2):
        mine = first if head == 0 else jnp.logical_not(first)
        keys = jnp.where(mine, k_pair, k_const)
        queries = jnp.where(mine, q_pair, aug)
        values = jnp.where(mine, v_pair, v_const)
        delta = -jnp.sum(jnp.where(mine, weighed, 0.0), axis=-1, keepdims=True)
        high = delta.astype(BF16)
        rest = delta - high.astype(F32)
        mid = rest.astype(BF16)
        low = (rest - mid.astype(F32)).astype(BF16)
        go_aug = jnp.where(spot == 1, high, jnp.zeros((rows, LANES), BF16))
        go_aug = jnp.where(spot == 2, mid, go_aug)
        go_aug = jnp.where(spot == 3, low, go_aug)
        grads = jnp.where(mine, go_pair, go_aug)
        grad_q = jnp.zeros((rows, LANES), F32)
        head_k = []
        head_v = []
        for start in range(0, blocks * rows, key_tile):
            stop = start + key_tile
            scores = dot_nt(keys[start:stop], queries)
            exact = jnp.exp(scores)
            if start < rows:
                key_ids = start + lax.broadcasted_iota(jnp.int32, (key_tile, rows), 0)
                query_ids = lax.broadcasted_iota(jnp.int32, (key_tile, rows), 1)
                exact = jnp.where(key_ids <= query_ids, exact, 0.0)
            centred = dot_nt(values[start:stop], grads)
            grad_scores = (exact * centred).astype(BF16)
            head_v.append(dot_nn(exact.astype(BF16), go_pair))
            head_k.append(dot_nn(grad_scores, q_pair))
            grad_q = grad_q + dot_tn(grad_scores, k_pair[start:stop])
        grads_q.append(grad_q)
        grads_k.append(head_k)
        grads_v.append(head_v)
    dq_ref[...] = (jnp.where(first, grads_q[0], grads_q[1]) * 0.125).astype(BF16)
    for index, start in enumerate(range(0, blocks * rows, key_tile)):
        dk_ref[start : start + key_tile, :] = jnp.where(
            first, grads_k[0][index], grads_k[1][index]
        ).astype(BF16)
        dv_ref[start : start + key_tile, :] = jnp.where(
            first, grads_v[0][index], grads_v[1][index]
        ).astype(BF16)


def attend_back(queries, keys, values, key_const, aug, grad_out, out):
    rows, width = queries.shape
    span = keys.shape[0]
    pair = lambda count: pl.BlockSpec((count, LANES), lambda i: (0, i))
    return pl.pallas_call(
        functools.partial(attend_back_kernel, span // rows, rows),
        grid=(width // LANES,),
        in_specs=[
            pair(rows),
            pair(span),
            pair(span),
            pl.BlockSpec((span, LANES), lambda i: (0, 0)),
            pair(rows),
            pair(rows),
            pair(rows),
        ],
        out_specs=[pair(rows), pair(span), pair(span)],
        out_shape=[
            jax.ShapeDtypeStruct((rows, width), BF16),
            jax.ShapeDtypeStruct((span, width), BF16),
            jax.ShapeDtypeStruct((span, width), BF16),
        ],
        name="attend_back",
        compiler_params=pltpu.CompilerParams(vmem_limit_bytes=48 << 20),
        cost_estimate=pl.CostEstimate(
            flops=40 * rows * span * width,
            bytes_accessed=2 * width * (5 * rows + 4 * span),
            transcendentals=rows * span * width // HEAD_DIM,
        ),
    )(queries, keys, values, key_const, aug, grad_out, out)


def chip_masks(dp):
    bits = dp.bit_length() - 2
    low = bits // 2
    along_x = [2 << i for i in range(low)]
    along_y = [2 << i for i in range(low, bits)]
    return along_x, along_y


def pack(weight):
    width, full = weight.shape
    if width == full:
        return weight
    return weight.reshape(width, full // width, width).transpose(1, 0, 2).reshape(full, width)


def spread(own):
    along_x, along_y = chip_masks(lax.axis_size("dp"))
    found = []
    for half, order in zip(own, (along_x + along_y, along_y + along_x)):
        masks, held = [0], half[None]
        arrays = []
        for step, mask in enumerate(order):
            got = swap(held, "dp", mask)
            got_masks = [m ^ mask for m in masks]
            if step + 1 < len(order):
                held = jnp.concatenate([held, got], axis=0)
                masks = masks + got_masks
            else:
                arrays += [(masks, held), (got_masks, got)]
        if not order:
            arrays = [(masks, held)]
        arrays += [([m ^ 1 for m in masks], swap(held, "dp", 1)) for masks, held in arrays]
        found.append(arrays)
    return found


def place_kernel(plan, counts, scal_ref, *refs):
    n_in, n_out = counts
    ins, outs, sems = refs[:n_in], refs[n_in : n_in + n_out], refs[n_in + n_out]
    device = scal_ref[0]
    copies = [
        pltpu.make_async_copy(source(ins), target(outs, device), sems.at[index])
        for index, (source, target) in enumerate(plan)
    ]
    for copy in copies:
        copy.start()
    for copy in copies:
        copy.wait()


def place(plan, inputs, out_shapes, device, name):
    return pl.pallas_call(
        functools.partial(place_kernel, plan, (len(inputs), len(out_shapes))),
        grid_spec=pltpu.PrefetchScalarGridSpec(
            num_scalar_prefetch=1,
            grid=(),
            in_specs=[pl.BlockSpec(memory_space=pl.ANY)] * len(inputs),
            out_specs=[pl.BlockSpec(memory_space=pltpu.VMEM)] * len(out_shapes),
            scratch_shapes=[pltpu.SemaphoreType.DMA((len(plan),))],
        ),
        out_shape=out_shapes,
        name=name,
        compiler_params=pltpu.CompilerParams(vmem_limit_bytes=40 << 20),
        cost_estimate=pl.CostEstimate(
            flops=0,
            transcendentals=0,
            bytes_accessed=2 * sum(math.prod(s.shape) * 2 for s in out_shapes),
        ),
    )(device.reshape(1), *inputs)


def position(device, mask, dp):
    other = device ^ mask
    return (other & 1) * (dp // 2) + (other >> 1)


def gather_group(parts, kinds, device, name):
    dp, mp = lax.axis_size("dp"), lax.axis_size("mp")
    full, width = parts[0].shape
    rows = full // dp
    half = len(parts) // 2
    stacked = jnp.stack(
        [
            lax.dynamic_slice_in_dim(part, position(device, 0, dp) * rows, rows, axis=0)
            for part in parts
        ]
    )
    across = jnp.stack([swap(stacked, "mp", r) for r in range(1, mp)])
    found = spread((across[:, :half], across[:, half:]))
    inputs = list(parts)
    plan = []

    def target_of(which, kind, r, start, count):
        def target(outs, device):
            begin = start(device)
            if kind == "c":
                return outs[which].at[pl.ds(begin, count), pl.ds(r * width, width)]
            if count == full:
                raise ValueError
            block = begin // width
            return outs[which].at[
                pl.ds(pl.multiple_of(r * width + begin % width, count), count),
                pl.ds(pl.multiple_of(block * width, width), width),
            ]

        return target

    for which, kind in enumerate(kinds):
        if kind == "c":
            plan.append(
                (
                    lambda ins, which=which: ins[which],
                    lambda outs, device, which=which: outs[which].at[:, pl.ds(0, width)],
                )
            )
        else:
            for block in range(full // width):
                plan.append(
                    (
                        lambda ins, which=which, block=block: ins[which].at[
                            pl.ds(block * width, width), :
                        ],
                        lambda outs, device, which=which, block=block: outs[which].at[
                            pl.ds(0, width), pl.ds(block * width, width)
                        ],
                    )
                )
    for side, arrays in enumerate(found):
        for masks, held in arrays:
            spot = len(inputs)
            inputs.append(held)
            for index, mask in enumerate(masks):
                for r in range(1, mp):
                    for inner in range(half):
                        which = side * half + inner
                        start = lambda device, mask=mask: pl.multiple_of(
                            position(device, mask, dp) * rows, rows
                        )
                        plan.append(
                            (
                                lambda ins, spot=spot, index=index, r=r, inner=inner: ins[
                                    spot
                                ].at[index, r - 1, inner],
                                target_of(which, kinds[which], r, start, rows),
                            )
                        )
    shapes = [
        jax.ShapeDtypeStruct((full, mp * width) if kind == "c" else (mp * width, full), BF16)
        for kind in kinds
    ]
    return place(plan, inputs, shapes, device, name)


def halve(value, axis, bit):
    return (
        lax.dynamic_index_in_dim(value, 1 - bit, axis, keepdims=False),
        lax.dynamic_index_in_dim(value, bit, axis, keepdims=False),
    )


def sum_chips(value, order, device):
    lead, quarters, rows, columns = value.shape
    bits = quarters.bit_length() - 1
    value = value.reshape((lead,) + (2,) * bits + (rows, columns))
    left = list(range(bits - 1, -1, -1))
    for mask in order:
        which = mask.bit_length() - 2
        axis = 1 + left.index(which)
        left.remove(which)
        send, keep = halve(value, axis, (device >> (which + 1)) & 1)
        got = swap(send, "dp", mask)
        value = (keep.astype(F32) + got.astype(F32)).astype(BF16)
    return value.reshape(lead, rows, columns)


def sum_layers(pieces):
    total = pieces[0].astype(F32)
    for r in range(1, len(pieces)):
        total = total + swap(pieces[r], "mp", r).astype(F32)
    return total.astype(BF16)


def fill(shape, arrays, where):
    out = jnp.zeros(shape, F32)
    for masks, held in arrays:
        for index, mask in enumerate(masks):
            out = lax.dynamic_update_slice(out, held[index].astype(F32), where(mask))
    return out


def sum_small(value):
    for mask in [1 << i for i in range(lax.axis_size("dp").bit_length() - 1)]:
        value = value + swap(value, "dp", mask)
    for mask in [1 << i for i in range(lax.axis_size("mp").bit_length() - 1)]:
        value = value + swap(value, "mp", mask)
    return value


def on_device(
    tokens,
    groups,
    lengths,
    qkv_weight,
    qv_bias,
    out_weight,
    out_bias,
    up_weight,
    up_bias,
    down_weight,
    down_bias,
    norm_gain,
    norm_bias,
    group_table,
    cotangent,
):
    dp, mp = lax.axis_size("dp"), lax.axis_size("mp")
    device, layer = lax.axis_index("dp"), lax.axis_index("mp")
    core = device & 1
    rows, full = tokens.shape
    width = qkv_weight.shape[2]
    hidden = up_weight.shape[1]
    blocks = SEQ_LEN // rows
    place_in_seq = layer % blocks
    length = lax.dynamic_index_in_dim(lengths, layer // blocks, keepdims=False)
    along_x, along_y = chip_masks(dp)
    quarters = dp // 2
    gains = norm_gain.astype(F32)
    shifts = norm_bias.astype(F32)

    wq, wk, wv, wo = gather_group(
        [qkv_weight[0], qkv_weight[1], qkv_weight[2], pack(out_weight)],
        "cccr",
        device,
        "place_attention",
    )
    w_up, w_down = gather_group([up_weight, pack(down_weight)], "cr", device, "place_ffn")
    order_of = layer ^ jnp.arange(mp)
    small_here = jnp.concatenate([qv_bias[0], qv_bias[1], up_bias])
    small_all = jnp.stack([small_here] + [swap(small_here, "mp", r) for r in range(1, mp)])
    small_all = small_all.astype(F32)
    q_bias = small_all[:, :width].reshape(-1)
    v_bias = small_all[:, width : 2 * width].reshape(-1)
    u_bias = small_all[:, 2 * width :].reshape(-1)

    onehot = (
        groups[:, None] == lax.broadcasted_iota(jnp.int32, (1, group_table.shape[0]), 1)
    ).astype(BF16)
    residual = tokens.astype(F32) + jnp.dot(onehot, group_table, preferred_element_type=F32)
    normed, norm_one, inv_one = norm_forward(residual, gains[0], shifts[0])
    normed_low = normed.astype(BF16)
    seq_normed = jnp.concatenate(
        [normed_low] + [swap(normed_low, "mp", m) for m in range(1, blocks)], axis=0
    )
    factor = 1.0 / math.sqrt(HEAD_DIM) / RELAX_ALPHA
    queries = (((dot_nn(normed_low, wq) + q_bias) * factor).astype(BF16) * RELAX_ALPHA).astype(BF16)
    keys = dot_nn(seq_normed, wk).astype(BF16)
    values = (dot_nn(seq_normed, wv) + v_bias).astype(BF16)

    key_ids = lax.broadcasted_iota(jnp.int32, (blocks, rows, 1), 1)
    block_ids = place_in_seq ^ lax.broadcasted_iota(jnp.int32, (blocks, rows, 1), 0)
    shown = (block_ids <= place_in_seq) & (block_ids * rows + key_ids < length)
    spot = lax.broadcasted_iota(jnp.int32, (blocks, rows, LANES), 2) % HEAD_DIM
    key_const = jnp.where(
        spot == 0,
        jnp.where(shown, 0.0, MASKED_SCORE),
        jnp.where(spot <= 3, 1.0, 0.0),
    )
    key_const = key_const.astype(BF16).reshape(blocks * rows, LANES)
    attended, aug = attend(queries, keys, values, key_const)

    branch = dot_nn(attended, wo) + out_bias.astype(F32)
    branch_out, norm_two, inv_two = norm_forward(branch, gains[1], shifts[1])
    middle = residual + branch_out
    mid_normed, norm_three, inv_three = norm_forward(middle, gains[2], shifts[2])
    mid_low = mid_normed.astype(BF16)
    pre_act = dot_nn(mid_low, w_up) + u_bias
    activated, gelu_pull = jax.vjp(jax.nn.gelu, pre_act)
    activated_low = activated.astype(BF16)
    ffn_out = dot_nn(activated_low, w_down) + down_bias.astype(F32)
    ffn_normed, norm_four, inv_four = norm_forward(ffn_out, gains[3], shifts[3])
    output = (middle + ffn_normed).astype(BF16)

    upstream = cotangent.astype(F32)
    grad_ffn, gain_four, shift_four = norm_backward(upstream, norm_four, inv_four, gains[3])
    grad_ffn_low = grad_ffn.astype(BF16)
    down_bias_part = jnp.sum(grad_ffn_low.astype(F32), axis=0)
    half = full // 2

    def split(value):
        return (
            lax.dynamic_slice_in_dim(value, (1 - core) * half, half, axis=1),
            lax.dynamic_slice_in_dim(value, core * half, half, axis=1),
        )

    def both_cores(send, keep):
        return (keep() + swap(send().astype(BF16), "dp", 1).astype(F32)).astype(BF16)

    gf_send, gf_keep = split(grad_ffn_low)
    down_sum = both_cores(
        lambda: dot_tn(activated_low, gf_send), lambda: dot_tn(activated_low, gf_keep)
    ).reshape(mp, quarters, hidden // quarters, half)
    grad_act = dot_nt(grad_ffn_low, w_down)
    (grad_pre,) = gelu_pull(grad_act)
    grad_pre_low = grad_pre.astype(BF16)
    up_bias_part = jnp.sum(grad_pre_low.astype(F32), axis=0)
    mid_send, mid_keep = split(mid_low)
    up_sum = both_cores(
        lambda: dot_tn(mid_send, grad_pre_low), lambda: dot_tn(mid_keep, grad_pre_low)
    ).reshape(1, quarters, half // quarters, mp * hidden)
    down_piece = sum_chips(down_sum, along_x + along_y, device)
    up_piece = sum_chips(up_sum, along_y + along_x, device)[0]
    down_mine = sum_layers([down_piece[r] for r in range(mp)])
    up_mine = sum_layers([up_piece[:, r * hidden : (r + 1) * hidden] for r in range(mp)])
    up_all, down_all = spread((up_mine, down_mine))

    def quarter_of(mask):
        return (device ^ mask) >> 1

    def core_of(mask):
        return (device ^ mask) & 1

    up_rows = half // quarters
    up_grad = fill(
        (full, hidden), up_all, lambda m: (core_of(m) * half + quarter_of(m) * up_rows, 0)
    )
    down_rows = hidden // quarters
    down_grad = fill(
        (hidden, full), down_all, lambda m: (quarter_of(m) * down_rows, core_of(m) * half)
    )

    grad_mid = dot_nt(grad_pre_low, w_up)
    back_three, gain_three, shift_three = norm_backward(grad_mid, norm_three, inv_three, gains[2])
    grad_middle = upstream + back_three
    grad_branch, gain_two, shift_two = norm_backward(grad_middle, norm_two, inv_two, gains[1])
    grad_branch_low = grad_branch.astype(BF16)
    out_bias_part = jnp.sum(grad_branch_low.astype(F32), axis=0)
    gb_send, gb_keep = split(grad_branch_low)
    out_sum = both_cores(
        lambda: dot_tn(attended, gb_send), lambda: dot_tn(attended, gb_keep)
    ).reshape(mp, quarters, width // quarters, half)
    grad_attended = dot_nt(grad_branch_low, wo).astype(BF16)
    grad_q, grad_k, grad_v = attend_back(
        queries, keys, values, key_const, aug, grad_attended, attended
    )
    q_bias_part = jnp.sum(grad_q.astype(F32), axis=0)
    v_bias_part = jnp.sum(grad_v.astype(F32), axis=0)
    grad_seq = dot_nt(grad_k, wk) + dot_nt(grad_v, wv)
    grad_normed = dot_nt(grad_q, wq) + grad_seq[:rows]
    for m in range(1, blocks):
        grad_normed = grad_normed + swap(
            grad_seq[m * rows : (m + 1) * rows].astype(BF16), "mp", m
        ).astype(F32)
    seq_send, seq_keep = split(seq_normed)
    qkv_sum = both_cores(
        lambda: jnp.concatenate(
            [dot_tn(seq_send[:rows], grad_q), dot_tn(seq_send, grad_k), dot_tn(seq_send, grad_v)],
            axis=1,
        ),
        lambda: jnp.concatenate(
            [dot_tn(seq_keep[:rows], grad_q), dot_tn(seq_keep, grad_k), dot_tn(seq_keep, grad_v)],
            axis=1,
        ),
    ).reshape(1, quarters, half // quarters, 3 * full)
    out_piece = sum_chips(out_sum, along_x + along_y, device)
    qkv_piece = sum_chips(qkv_sum, along_y + along_x, device)[0]
    out_mine = sum_layers([out_piece[r] for r in range(mp)])
    qkv_mine = sum_layers(
        [
            jnp.stack(
                [
                    qkv_piece[:, c * full + r * width : c * full + (r + 1) * width]
                    for c in range(3)
                ]
            )
            for r in range(mp)
        ]
    )
    qkv_all, out_all = spread((qkv_mine, out_mine))
    qkv_grad = fill(
        (3, full, width), qkv_all, lambda m: (0, core_of(m) * half + quarter_of(m) * up_rows, 0)
    )
    out_rows = width // quarters
    out_grad = fill(
        (width, full), out_all, lambda m: (quarter_of(m) * out_rows, core_of(m) * half)
    )

    back_one, gain_one, shift_one = norm_backward(grad_normed, norm_one, inv_one, gains[0])
    input_grad = grad_middle + back_one
    table_part = jnp.dot(
        onehot.astype(F32).T, input_grad, precision=PRECISE, preferred_element_type=F32
    )
    by_layer = jnp.concatenate(
        [q_bias_part.reshape(mp, -1), v_bias_part.reshape(mp, -1), up_bias_part.reshape(mp, -1)],
        axis=1,
    )
    by_layer = jnp.take(by_layer, order_of, axis=0)
    wide = by_layer.shape[1]
    by_layer = jnp.pad(by_layer, ((0, 0), (0, -wide % full))).reshape(-1, full)
    parts = jnp.concatenate(
        [
            jnp.stack([gain_one, gain_two, gain_three, gain_four]),
            jnp.stack([shift_one, shift_two, shift_three, shift_four]),
            jnp.stack([out_bias_part, down_bias_part]),
            table_part,
            by_layer,
        ]
    )
    parts = sum_small(parts)
    gain_grad, shift_grad = parts[:4], parts[4:8]
    out_bias_grad, down_bias_grad = parts[8], parts[9]
    n_groups = group_table.shape[0]
    table_grad = parts[10 : 10 + n_groups]
    by_layer = parts[10 + n_groups :].reshape(mp, -1)
    mine = lax.dynamic_index_in_dim(by_layer, layer, keepdims=False)
    qv_bias_grad = mine[: 2 * width].reshape(2, width)
    up_bias_grad = mine[2 * width : 2 * width + hidden]
    return (
        output,
        input_grad,
        qkv_grad,
        qv_bias_grad,
        out_grad,
        out_bias_grad,
        up_grad,
        up_bias_grad,
        down_grad,
        down_bias_grad,
        gain_grad,
        shift_grad,
        table_grad,
    )


def solution(mesh):
    placed = (
        P(("dp", "mp"), None),
        P(("dp", "mp")),
        P("dp"),
        P(None, None, "mp"),
        P(None, "mp"),
        P("mp", None),
        P(),
        P(None, "mp"),
        P("mp"),
        P("mp", None),
        P(),
        P(),
        P(),
        P(),
        P(("dp", "mp"), None),
    )
    return jax.shard_map(
        on_device,
        mesh=mesh,
        in_specs=placed,
        out_specs=(
            P(("dp", "mp"), None),
            P(("dp", "mp"), None),
            P(None, None, "mp"),
            P(None, "mp"),
            P("mp", None),
            P(),
            P(None, "mp"),
            P("mp"),
            P("mp", None),
            P(),
            P(),
            P(),
            P(),
        ),
        check_vma=False,
    )
```

time: 1630 us -> 618 us (0.38)
  waiting for transfers between devices: 1080 us -> 274 us
  matrix products: 263 us -> 116 us
  local copies, waits for them, and re-layouts: 138 us -> 27.5 us
  Pallas kernels: 0 us -> 79.3 us
  starting transfers between devices: 1.4 us -> 75 us
  blocking collectives: 57.7 us -> 0 us
  other arithmetic: 59.1 us -> 37.3 us
    reduce_scatter x4 -> x0, waiting for transfers between devices: 532 us -> none  [the longest x1 151 us: on_device(): lax.psum_scatter(jnp.dot(lax.slice_in_dim(grad_pre_low, 0, row_count * la...]
    all_gather x4 -> x0, waiting for transfers between devices: 327 us -> none  [the longest x1 87.7 us: on_device(): normed_all = lax.all_gather(normed_low, 'mp', axis=0, tiled=True)]
    ppermute x0 -> x72, waiting for transfers between devices: none -> 274 us  [swap(): return lax.ppermute(value, axis, [(i, i ^ mask) for i in range(count)])]
    psum x2 -> x0, waiting for transfers between devices: 223 us -> none  [the longest x1 147 us: on_device(): lax.psum((qkv_grad, qv_bias_grad, out_grad, up_grad, up_bias_grad, down_g...]
    dot_general x42 -> x26, matrix products: 263 us -> 116 us  [the longest x12 44.5 us: dot_tn(): lax.dot_general(a, b, (((0,), (0,)), ((), ())), preferred_element_type=F32)]
    pallas_call x0 -> x4, Pallas kernels: none -> 79.3 us  [the longest x1 40.4 us: attend_back(): pl.pallas_call(functools.partial(attend_back_kernel, span // rows, rows),...]
    ppermute x0 -> x72, starting transfers between devices: none -> 75 us  [swap(): return lax.ppermute(value, axis, [(i, i ^ mask) for i in range(count)])]
    psum x2 -> x0, blocking collectives: 57.7 us -> none  [the longest x1 41.8 us: on_device(): lax.psum((gain_parts, shift_parts, out_bias_part, down_bias_part, table_p...]
  transfers between devices with their start and end apart: 10 -> 72, of which waited for: 10 -> 35; matrix products, arithmetic and copies ran while one was open for 2% -> 15% of each run, Pallas kernels for 0% -> 5%
where the time goes in v1:
time: 618 us; the launch traced here: 612 us
  waiting for transfers between devices  274 us (44%)
  matrix products  116 us (19%)
  Pallas kernels  79.3 us (13%)
  starting transfers between devices  75 us (12%)
  other arithmetic  37.3 us (6%)
  local copies, waits for them, and re-layouts  27.5 us (4%)
    ppermute x72, waiting for transfers between devices, swap(): return lax.ppermute(value, axis, [(i, i ^ mask) for i in range(count)])  274 us
    ppermute x72, starting transfers between devices, swap(): return lax.ppermute(value, axis, [(i, i ^ mask) for i in range(count)])  75 us
    dot_general x12, matrix products, dot_tn(): lax.dot_general(a, b, (((0,), (0,)), ((), ())), preferred_element_type=F32)  44.5 us
    pallas_call x1, Pallas kernels, attend_back(): pl.pallas_call(functools.partial(attend_back_kernel, span // rows, rows),...  40.4 us
    dot_general x6, matrix products, dot_nt(): lax.dot_general(a, b, (((1,), (1,)), ((), ())), preferred_element_type=F32)  35.4 us
    dot_general x6, matrix products, dot_nn(): lax.dot_general(a, b, (((1,), (0,)), ((), ())), preferred_element_type=F32)  34.5 us
    pallas_call x1, Pallas kernels, attend(): pl.pallas_call(functools.partial(attend_kernel, span // rows, rows), grid...  24.8 us
    pallas_call x2, Pallas kernels, place(): pl.pallas_call(functools.partial(place_kernel, plan, (len(inputs), len(ou...  14.2 us
  transfers between devices with their start and end apart: 72, of which 35 were waited for; matrix products, arithmetic and copies ran while one was open for 15% of the time, Pallas kernels for 5%

profile of v1, /device:TPU:0, one launch (start us, length us, event | category | flops | bytes accessed | tf_op | source)
XLA Modules:
  0.0 612.1 jit_solution(7405898713185304592)
XLA Ops:
  4.5 5.1 collective-permute-start.2
  11.3 3.8 collective-permute-start.17
  22.6 6.1 %collective-permute-start.15 = (bf16[2,128,1024]{2,1,0:T(8,128)(2,1)S(1)}, bf16[2,128,1024]{2,1,0:T(8,128)(2,1)S(1)}, u32[]{:S(2)}, u32[]{:S(2)}) collective-permute-start(bf16[2,128,1024]{2,1,0:T(8,128)(2,1)S(1)} %pad_maximum_fusion.10), channel_id=1, source_target_pairs={{0,1},{1,0},{2,3},{3,2},{4,5},{5,4},{6,7},{7,6},{8,9},{9,8},{10,11... | collective-permute-start | bytes 1572872 | tf_op jit(solution)/shard_map/ppermute | solution.py:24
  28.8 26.6 %collective-permute-done.1 = bf16[4,128,256]{2,1,0:T(8,128)(2,1)} collective-permute-done((bf16[4,128,256]{2,1,0:T(8,128)(2,1)S(1)}, bf16[4,128,256]{2,1,0:T(8,128)(2,1)}, u32[]{:S(2)}, u32[]{:S(2)}) %collective-permute-start.1) | collective-permute-done | bytes 262176 | tf_op jit(solution)/shard_map/ppermute | solution.py:24
  60.9 16.2 %collective-permute-done.16 = bf16[2,128,1024]{2,1,0:T(8,128)(2,1)} collective-permute-done((bf16[2,128,1024]{2,1,0:T(8,128)(2,1)S(1)}, bf16[2,128,1024]{2,1,0:T(8,128)(2,1)}, u32[]{:S(2)}, u32[]{:S(2)}) %collective-permute-start.16) | collective-permute-done | bytes 524320 | tf_op jit(solution)/shard_map/ppermute | solution.py:24
  83.5 5.7 collective-permute-done.7
  91.2 4.5 collective-permute-done.12
  102.1 4.0 collective-permute-done.4.refs_5_
  106.2 10.5 %collective-permute-done.8.refs_9_ = bf16[2,3,2,128,256]{4,3,2,1,0:T(8,128)(2,1)} collective-permute-done((bf16[2,3,2,128,256]{4,3,2,1,0:T(8,128)(2,1)S(1)}, bf16[2,3,2,128,256]{4,3,2,1,0:T(8,128)(2,1)}, u32[]{:S(2)}, u32[]{:S(2)}) %collective-permute-start.8) | collective-permute-done | bytes 786464 | tf_op jit(solution)/shard_map/ppermute | solution.py:24
  116.8 3.1 fusion.26
  125.9 5.1 place_attention.1
  131.0 3.4 fusion.24.q_ref
  134.5 4.5 convolution_convert_fusion.2.k_ref
  139.0 4.9 fusion.10.v_ref
  144.0 24.8 %attend.1 = (bf16[544,1024]{1,0:T(8,128)(2,1)S(1)}, bf16[544,1024]{1,0:T(8,128)(2,1)S(1)}) custom-call(bf16[544,1024]{1,0:T(8,128)(2,1)S(1)} %fusion.24.q_ref, bf16[1088,1024]{1,0:T(8,128)(2,1)S(1)} %convolution_convert_fusion.2.k_ref, bf16[1088,1024]{1,0:T(8,128)(2,1)S(1)} %fusion.10.v_ref, bf16[1088,128]{1,0:T(8,128)(2,1)S(1)} %select_convert_fusion.kc_ref), custom_call_target="tpu_custom_call" | custom-call | flops 9697230848 | bytes 7798784 | tf_op jit(solution)/shard_map/attend/pallas_call | solution.py:120
  168.8 3.4 add_reduce_fusion.1
  178.4 9.1 %place_ffn.1 = (bf16[1024,4096]{1,0:T(8,128)(2,1)}, bf16[4096,1024]{1,0:T(8,128)(2,1)}) custom-call(s32[1]{0:T(128)} %bitcast.2.scal_ref, bf16[1024,1024]{1,0:T(8,128)(2,1)} %refs_0_.1, bf16[1024,1024]{1,0:T(8,128)(2,1)} %refs_1_.1, bf16[2,3,1,128,1024]{4,3,2,1,0:T(8,128)(2,1)S(1)} %get-tuple-element.78.refs_2_, bf16[2,3,1,128,1024]{4,3,2,1,0:T(8,128)(2,1)S(1)} %bitcast.358, ...), custom_call_target="tpu_custom_call" | custom-call | bytes 33554432 | tf_op jit(solution)/shard_map/place_ffn/pallas_call | solution.py:284
  187.5 13.3 %multiply_convert_fusion = (bf16[544,4096]{1,0:T(8,128)(2,1)S(1)}, f32[544,4096]{1,0:T(8,128)}) fusion(f32[4096]{0:T(1024)S(1)} %bitcast.404, bf16[544,1024]{1,0:T(8,128)(2,1)S(1)} %add_convert_fusion.3, bf16[1024,4096]{1,0:T(8,128)(2,1)} %get-tuple-element.29), kind=kOutput, calls=%fused_computation.11 | convolution fusion | flops 4585684992 | bytes 22888448 | tf_op jit(solution)/shard_map/dot_general | solution.py:45
  200.8 5.0 add_reduce_fusion
  210.4 14.2 %convert_reduce_fusion = (f32[4096]{0:T(1024)S(1)}, bf16[544,4096]{1,0:T(8,128)(2,1)S(1)}) fusion(f32[544,4096]{1,0:T(8,128)} %get-tuple-element.129, f32[4096]{0:T(1024)S(1)} %bitcast.405, bf16[544,1024]{1,0:T(8,128)(2,1)S(1)} %get-tuple-element.62, bf16[4096,1024]{1,0:T(8,128)(2,1)} %get-tuple-element.30), kind=kOutput, calls=%fused_computation.10 | convolution fusion | flops 4614647808 | bytes 22904832 | tf_op jit(solution)/shard_map/dot_general | solution.py:49
  224.6 9.6 %multiply_reduce_fusion = (f32[1024]{0:T(1024)S(1)}, f32[544]{0:T(1024)S(1)}, f32[544]{0:T(1024)S(1)}, f32[1024]{0:T(1024)S(1)}, f32[544,1024]{1,0:T(8,128)S(1)}) fusion(f32[544,1024]{1,0:T(8,128)S(1)} %get-tuple-element.69, f32[544]{0:T(1024)S(1)} %add_rsqrt_fusion.1, f32[544]{0:T(1024)S(1)} %broadcast_multiply_fusion.9, f32[1024]{0:T(1024)S(1)} %bitcast.390, ...), kind=kOutput, calls=%fused_computation.53 | convolution fusion | flops 4568413184 | bytes 17322496 | tf_op jit(solution)/shard_map/dot_general | solution.py:49
  240.6 40.4 %attend_back.1 = (bf16[544,1024]{1,0:T(8,128)(2,1)S(1)}, bf16[1088,1024]{1,0:T(8,128)(2,1)}, bf16[1088,1024]{1,0:T(8,128)(2,1)}) custom-call(bf16[544,1024]{1,0:T(8,128)(2,1)S(1)} %copy-done.8, bf16[1088,1024]{1,0:T(8,128)(2,1)} %copy-done.9, bf16[1088,1024]{1,0:T(8,128)(2,1)} %copy-done.10, bf16[1088,128]{1,0:T(8,128)(2,1)S(1)} %select_convert_fusion.kc_ref, ...), custom_call_target="tpu_custom_call" | custom-call | flops 24243077120 | bytes 14483456 | tf_op jit(solution)/shard_map/attend_back/pallas_call | solution.py:205
  281.0 4.3 fusion.83
  291.3 5.1 convolution_convert_fusion.1
  309.0 3.3 pad_maximum_fusion
  312.3 8.0 %convolution_convert_fusion = bf16[4096,512]{1,0:T(8,128)(2,1)} fusion(bf16[544,4096]{1,0:T(8,128)(2,1)} %copy-done.63, bf16[544,1024]{1,0:T(8,128)(2,1)S(1)} %copy-done.37, s32[]{:T(128)S(6)} %select_n.242), kind=kOutput, calls=%fused_computation.16 | convolution fusion | flops 2283798528 | bytes 9207812 | tf_op jit(solution)/shard_map/dot_general | solution.py:53
  320.3 11.5 %collective-permute-done.26 = bf16[544,1024]{1,0:T(8,128)(2,1)} collective-permute-done((bf16[544,1024]{1,0:T(8,128)(2,1)}, bf16[544,1024]{1,0:T(8,128)(2,1)}, u32[]{:S(2)}, u32[]{:S(2)}) %collective-permute-start.26) | collective-permute-done | bytes 1114144 | tf_op jit(solution)/shard_map/ppermute | solution.py:24
  331.9 3.5 multiply_reduce_fusion.2
  346.6 12.7 %collective-permute-done.38 = f32[34,1024]{1,0:T(8,128)S(1)} collective-permute-done((f32[34,1024]{1,0:T(8,128)S(1)}, f32[34,1024]{1,0:T(8,128)S(1)}, u32[]{:S(2)}, u32[]{:S(2)}) %collective-permute-start.38) | collective-permute-done | bytes 139296 | tf_op jit(solution)/shard_map/ppermute | solution.py:24
  367.0 3.6 collective-permute-done.40
  374.1 5.2 collective-permute-done.41
  392.1 4.4 collective-permute-done.49
  396.7 3.7 fusion.7
  402.5 5.5 add_convert_fusion.1
  409.4 28.4 %collective-permute-done.28 = bf16[1,2,128,3072]{3,2,1,0:T(8,128)(2,1)S(1)} collective-permute-done((bf16[1,2,128,3072]{3,2,1,0:T(8,128)(2,1)S(1)}, bf16[1,2,128,3072]{3,2,1,0:T(8,128)(2,1)S(1)}, u32[]{:S(2)}, u32[]{:S(2)}) %collective-permute-start.28) | collective-permute-done | bytes 1572896 | tf_op jit(solution)/shard_map/ppermute | solution.py:24
  439.1 5.4 add_convert_fusion
  444.5 12.9 %collective-permute-done.29 = bf16[1,128,3072]{2,1,0:T(8,128)(2,1)S(1)} collective-permute-done((bf16[1,128,3072]{2,1,0:T(8,128)(2,1)S(1)}, bf16[1,128,3072]{2,1,0:T(8,128)(2,1)S(1)}, u32[]{:S(2)}, u32[]{:S(2)}) %collective-permute-start.29) | collective-permute-done | bytes 786464 | tf_op jit(solution)/shard_map/ppermute | solution.py:24
  463.5 3.9 collective-permute-done.32
  467.4 8.8 %collective-permute-done.31 = bf16[3,128,256]{2,1,0:T(8,128)(2,1)S(1)} collective-permute-done((bf16[3,128,256]{2,1,0:T(8,128)(2,1)S(1)}, bf16[3,128,256]{2,1,0:T(8,128)(2,1)S(1)}, u32[]{:S(2)}, u32[]{:S(2)}) %collective-permute-start.31) | collective-permute-done | bytes 196640 | tf_op jit(solution)/shard_map/ppermute | solution.py:24
  477.2 35.1 %collective-permute-done.33 = bf16[1,3,128,256]{3,2,1,0:T(8,128)(2,1)S(1)} collective-permute-done((bf16[1,3,128,256]{3,2,1,0:T(8,128)(2,1)S(1)}, bf16[1,3,128,256]{3,2,1,0:T(8,128)(2,1)S(1)}, u32[]{:S(2)}, u32[]{:S(2)}) %collective-permute-start.33) | collective-permute-done | bytes 196640 | tf_op jit(solution)/shard_map/ppermute | solution.py:24
  516.7 4.9 collective-permute-done.34
  523.4 16.7 %collective-permute-done.54 = bf16[1,128,4096]{2,1,0:T(8,128)(2,1)S(1)} collective-permute-done((bf16[1,128,4096]{2,1,0:T(8,128)(2,1)S(1)}, bf16[1,128,4096]{2,1,0:T(8,128)(2,1)S(1)}, u32[]{:S(2)}, u32[]{:S(2)}) %collective-permute-start.54) | collective-permute-done | bytes 1048608 | tf_op jit(solution)/shard_map/ppermute | solution.py:24
  547.6 4.0 collective-permute-done.57
  551.6 10.0 %collective-permute-start.65 = (bf16[256,512]{1,0:T(8,128)(2,1)S(1)}, bf16[256,512]{1,0:T(8,128)(2,1)S(1)}, u32[]{:S(2)}, u32[]{:S(2)}) collective-permute-start(bf16[256,512]{1,0:T(8,128)(2,1)S(1)} %get-tuple-element.85), channel_id=1, source_target_pairs={{0,1},{1,0},{2,3},{3,2},{4,5},{5,4},{6,7},{7,6},{8,9},{9,8},{10,11... | collective-permute-start | bytes 786440 | tf_op jit(solution)/shard_map/ppermute | solution.py:24
  561.6 15.9 %collective-permute-done.56 = bf16[128,1024]{1,0:T(8,128)(2,1)S(1)} collective-permute-done((bf16[128,1024]{1,0:T(8,128)(2,1)S(1)}, bf16[128,1024]{1,0:T(8,128)(2,1)S(1)}, u32[]{:S(2)}, u32[]{:S(2)}) %collective-permute-start.56) | collective-permute-done | bytes 262176 | tf_op jit(solution)/shard_map/ppermute | solution.py:24
  578.8 8.7 %collective-permute-done.66 = bf16[256,512]{1,0:T(8,128)(2,1)S(1)} collective-permute-done((bf16[256,512]{1,0:T(8,128)(2,1)S(1)}, bf16[256,512]{1,0:T(8,128)(2,1)S(1)}, u32[]{:S(2)}, u32[]{:S(2)}) %collective-permute-start.66) | collective-permute-done | bytes 262176 | tf_op jit(solution)/shard_map/ppermute | solution.py:24
  590.4 7.0 %collective-permute-done.68 = bf16[1,256,512]{2,1,0:T(8,128)(2,1)S(1)} collective-permute-done((bf16[1,256,512]{2,1,0:T(8,128)(2,1)S(1)}, bf16[1,256,512]{2,1,0:T(8,128)(2,1)S(1)}, u32[]{:S(2)}, u32[]{:S(2)}) %collective-permute-start.68) | collective-permute-done | bytes 262176 | tf_op jit(solution)/shard_map/ppermute | solution.py:24
  598.2 8.3 %collective-permute-done.59 = bf16[2,128,1024]{2,1,0:T(8,128)(2,1)S(1)} collective-permute-done((bf16[2,128,1024]{2,1,0:T(8,128)(2,1)S(1)}, bf16[2,128,1024]{2,1,0:T(8,128)(2,1)S(1)}, u32[]{:S(2)}, u32[]{:S(2)}) %collective-permute-start.59) | collective-permute-done | bytes 524320 | tf_op jit(solution)/shard_map/ppermute | solution.py:24
  (432 shorter events, 145.0 us)
Async XLA Ops:
  4.5 18.1 %collective-permute-start.2 = (bf16[4,128,256]{2,1,0:T(8,128)(2,1)S(1)}, bf16[4,128,256]{2,1,0:T(8,128)(2,1)}, u32[]{:S(2)}, u32[]{:S(2)}) collective-permute-start(bf16[4,128,256]{2,1,0:T(8,128)(2,1)S(1)} %pad_maximum_fusion.14), channel_id=1, source_target_pairs={{0,3},{1,2},{2,1},{3,0},{4,7},{5,6},{6,5},{7,4},{8,11},{9,10},{10,... | collective-permute-start | bytes 786440 | tf_op jit(solution)/shard_map/ppermute | solution.py:24
  9.6 45.8 %collective-permute-start.1 = (bf16[4,128,256]{2,1,0:T(8,128)(2,1)S(1)}, bf16[4,128,256]{2,1,0:T(8,128)(2,1)}, u32[]{:S(2)}, u32[]{:S(2)}) collective-permute-start(bf16[4,128,256]{2,1,0:T(8,128)(2,1)S(1)} %pad_maximum_fusion.14), channel_id=1, source_target_pairs={{0,2},{1,3},{2,0},{3,1},{4,6},{5,7},{6,4},{7,5},{8,10},{9,11},{10,... | collective-permute-start | bytes 786440 | tf_op jit(solution)/shard_map/ppermute | solution.py:24
  9.6 48.5 %collective-permute-start = (bf16[4,128,256]{2,1,0:T(8,128)(2,1)S(1)}, bf16[4,128,256]{2,1,0:T(8,128)(2,1)}, u32[]{:S(2)}, u32[]{:S(2)}) collective-permute-start(bf16[4,128,256]{2,1,0:T(8,128)(2,1)S(1)} %pad_maximum_fusion.14), channel_id=1, source_target_pairs={{0,1},{1,0},{2,3},{3,2},{4,5},{5,4},{6,7},{7,6},{8,9},{9,8},{10,11... | collective-permute-start | bytes 786440 | tf_op jit(solution)/shard_map/ppermute | solution.py:24
  11.3 48.0 %collective-permute-start.17 = (bf16[2,128,1024]{2,1,0:T(8,128)(2,1)S(1)}, bf16[2,128,1024]{2,1,0:T(8,128)(2,1)}, u32[]{:S(2)}, u32[]{:S(2)}) collective-permute-start(bf16[2,128,1024]{2,1,0:T(8,128)(2,1)S(1)} %pad_maximum_fusion.10), channel_id=1, source_target_pairs={{0,3},{1,2},{2,1},{3,0},{4,7},{5,6},{6,5},{7,4},{8,11},{9,10},{10,... | collective-permute-start | bytes 1572872 | tf_op jit(solution)/shard_map/ppermute | solution.py:24
  15.1 62.0 %collective-permute-start.16 = (bf16[2,128,1024]{2,1,0:T(8,128)(2,1)S(1)}, bf16[2,128,1024]{2,1,0:T(8,128)(2,1)}, u32[]{:S(2)}, u32[]{:S(2)}) collective-permute-start(bf16[2,128,1024]{2,1,0:T(8,128)(2,1)S(1)} %pad_maximum_fusion.10), channel_id=1, source_target_pairs={{0,2},{1,3},{2,0},{3,1},{4,6},{5,7},{6,4},{7,5},{8,10},{9,11},{10,... | collective-permute-start | bytes 1572872 | tf_op jit(solution)/shard_map/ppermute | solution.py:24
  22.6 56.1 %collective-permute-start.15 = (bf16[2,128,1024]{2,1,0:T(8,128)(2,1)S(1)}, bf16[2,128,1024]{2,1,0:T(8,128)(2,1)S(1)}, u32[]{:S(2)}, u32[]{:S(2)}) collective-permute-start(bf16[2,128,1024]{2,1,0:T(8,128)(2,1)S(1)} %pad_maximum_fusion.10), channel_id=1, source_target_pairs={{0,1},{1,0},{2,3},{3,2},{4,5},{5,4},{6,7},{7,6},{8,9},{9,8},{10,11... | collective-permute-start | bytes 1572872 | tf_op jit(solution)/shard_map/ppermute | solution.py:24
  55.4 35.6 %collective-permute-start.13 = (bf16[1536]{0:T(1024)(128)(2,1)S(1)}, bf16[1536]{0:T(1024)(128)(2,1)S(1)}, u32[]{:S(2)}, u32[]{:S(2)}) collective-permute-start(bf16[1536]{0:T(1024)(128)(2,1)S(1)} %pad_maximum_fusion.23), channel_id=1, source_target_pairs={{0,3},{1,2},{2,1},{3,0},{4,7},{5,6},{6,5},{7,4},{8,11},{9,10},{10,... | collective-permute-start | bytes 9224 | tf_op jit(solution)/shard_map/ppermute | solution.py:24
  58.1 43.5 %collective-permute-start.14 = (bf16[544,1024]{1,0:T(8,128)(2,1)}, bf16[544,1024]{1,0:T(8,128)(2,1)}, u32[]{:S(2)}, u32[]{:S(2)}) collective-permute-start(bf16[544,1024]{1,0:T(8,128)(2,1)} %add_convert_fusion.4), channel_id=1, source_target_pairs={{0,1},{1,0},{2,3},{3,2},{4,5},{5,4},{6,7},{7,6},{8,9},{9,8},{10,11... | collective-permute-start | bytes 3342344 | tf_op jit(solution)/shard_map/ppermute | solution.py:24
  59.4 23.5 %collective-permute-start.3 = (bf16[1,3,2,128,256]{4,3,2,1,0:T(8,128)(2,1)S(1)}, bf16[1,3,2,128,256]{4,3,2,1,0:T(8,128)(2,1)S(1)}, u32[]{:S(2)}, u32[]{:S(2)}) collective-permute-start(bf16[1,3,2,128,256]{4,3,2,1,0:T(8,128)(2,1)S(1)} %get-tuple-element.106), channel_id=1, source_target_pairs={{0,8},{4,12},{8,0},{12,4},{16,24},{20,28},{24,16},{28,20},{1,9},{5... | collective-permute-start | bytes 1179656 | tf_op jit(solution)/shard_map/ppermute | solution.py:24
  77.2 12.1 %collective-permute-start.7 = (bf16[1,3,2,128,256]{4,3,2,1,0:T(8,128)(2,1)S(1)}, bf16[1,3,2,128,256]{4,3,2,1,0:T(8,128)(2,1)S(1)}, u32[]{:S(2)}, u32[]{:S(2)}) collective-permute-start(bf16[1,3,2,128,256]{4,3,2,1,0:T(8,128)(2,1)S(1)} %get-tuple-element.105), channel_id=1, source_target_pairs={{0,16},{4,20},{8,24},{12,28},{16,0},{20,4},{24,8},{28,12},{1,17},{... | collective-permute-start | bytes 1179656 | tf_op jit(solution)/shard_map/ppermute | solution.py:24
  81.3 20.8 %collective-permute-start.18 = (bf16[1,3,1,128,1024]{4,3,1,2,0:T(8,128)(2,1)}, bf16[1,3,1,128,1024]{4,3,1,2,0:T(8,128)(2,1)}, u32[]{:S(2)}, u32[]{:S(2)}) collective-permute-start(bf16[1,3,1,128,1024]{4,3,1,2,0:T(8,128)(2,1)} %get-tuple-element.76), channel_id=1, source_target_pairs={{0,8},{4,12},{8,0},{12,4},{16,24},{20,28},{24,16},{28,20},{1,9},{5... | collective-permute-start | bytes 2359304 | tf_op jit(solution)/shard_map/ppermute | solution.py:24
  82.9 23.3 %collective-permute-start.4 = (bf16[2,3,2,128,256]{4,3,2,1,0:T(8,128)(2,1)S(1)}, bf16[2,3,2,128,256]{4,3,2,1,0:T(8,128)(2,1)}, u32[]{:S(2)}, u32[]{:S(2)}) collective-permute-start(bf16[2,3,2,128,256]{4,3,2,1,0:T(8,128)(2,1)S(1)} %pad_maximum_fusion.8.refs_4_), channel_id=1, source_target_pairs={{0,16},{4,20},{8,24},{12,28},{16,0},{20,4},{24,8},{28,12},{1,17},{... | collective-permute-start | bytes 2359304 | tf_op jit(solution)/shard_map/ppermute | solution.py:24
  89.3 27.4 %collective-permute-start.8 = (bf16[2,3,2,128,256]{4,3,2,1,0:T(8,128)(2,1)S(1)}, bf16[2,3,2,128,256]{4,3,2,1,0:T(8,128)(2,1)}, u32[]{:S(2)}, u32[]{:S(2)}) collective-permute-start(bf16[2,3,2,128,256]{4,3,2,1,0:T(8,128)(2,1)S(1)} %pad_maximum_fusion.9.refs_8_), channel_id=1, source_target_pairs={{0,8},{4,12},{8,0},{12,4},{16,24},{20,28},{24,16},{28,20},{1,9},{5... | collective-permute-start | bytes 2359304 | tf_op jit(solution)/shard_map/ppermute | solution.py:24
  99.2 22.2 %collective-permute-start.22 = (bf16[1,3,1,128,1024]{4,3,2,1,0:T(8,128)(2,1)}, bf16[1,3,1,128,1024]{4,3,2,1,0:T(8,128)(2,1)}, u32[]{:S(2)}, u32[]{:S(2)}) collective-permute-start(bf16[1,3,1,128,1024]{4,3,2,1,0:T(8,128)(2,1)} %get-tuple-element.75), channel_id=1, source_target_pairs={{0,16},{4,20},{8,24},{12,28},{16,0},{20,4},{24,8},{28,12},{1,17},{... | collective-permute-start | bytes 2359304 | tf_op jit(solution)/shard_map/ppermute | solution.py:24
  101.5 22.5 %collective-permute-start.5 = (bf16[2,3,2,128,256]{4,3,2,1,0:T(8,128)(2,1)S(1)}, bf16[2,3,2,128,256]{4,3,2,1,0:T(8,128)(2,1)S(1)}, u32[]{:S(2)}, u32[]{:S(2)}) collective-permute-start(bf16[2,3,2,128,256]{4,3,2,1,0:T(8,128)(2,1)S(1)} %pad_maximum_fusion.8.refs_4_), channel_id=1, source_target_pairs={{0,4},{4,0},{8,12},{12,8},{16,20},{20,16},{24,28},{28,24},{1,5},{5... | collective-permute-start | bytes 2359304 | tf_op jit(solution)/shard_map/ppermute | solution.py:24
  102.1 22.0 %collective-permute-start.9 = (bf16[2,3,2,128,256]{4,3,2,1,0:T(8,128)(2,1)S(1)}, bf16[2,3,2,128,256]{4,3,2,1,0:T(8,128)(2,1)S(1)}, u32[]{:S(2)}, u32[]{:S(2)}) collective-permute-start(bf16[2,3,2,128,256]{4,3,2,1,0:T(8,128)(2,1)S(1)} %pad_maximum_fusion.9.refs_8_), channel_id=1, source_target_pairs={{0,4},{4,0},{8,12},{12,8},{16,20},{20,16},{24,28},{28,24},{1,5},{5... | collective-permute-start | bytes 2359304 | tf_op jit(solution)/shard_map/ppermute | solution.py:24
  106.2 19.6 %collective-permute-start.6 = (bf16[2,3,2,128,256]{4,3,2,1,0:T(8,128)(2,1)}, bf16[2,3,2,128,256]{4,3,2,1,0:T(8,128)(2,1)S(1)}, u32[]{:S(2)}, u32[]{:S(2)}) collective-permute-start(bf16[2,3,2,128,256]{4,3,2,1,0:T(8,128)(2,1)} %collective-permute-done.4.refs_5_), channel_id=1, source_target_pairs={{0,4},{4,0},{8,12},{12,8},{16,20},{20,16},{24,28},{28,24},{1,5},{5... | collective-permute-start | bytes 2359304 | tf_op jit(solution)/shard_map/ppermute | solution.py:24
  121.5 51.2 %collective-permute-start.19 = (bf16[2,3,1,128,1024]{4,3,1,2,0:T(8,128)(2,1)S(1)}, bf16[2,3,1,128,1024]{4,3,1,2,0:T(8,128)(2,1)S(1)}, u32[]{:S(2)}, u32[]{:S(2)}) collective-permute-start(bf16[2,3,1,128,1024]{4,3,1,2,0:T(8,128)(2,1)S(1)} %get-tuple-element.77), channel_id=1, source_target_pairs={{0,16},{4,20},{8,24},{12,28},{16,0},{20,4},{24,8},{28,12},{1,17},{... | collective-permute-start | bytes 4718600 | tf_op jit(solution)/shard_map/ppermute | solution.py:24
  124.1 51.4 %collective-permute-start.20 = (bf16[2,3,1,128,1024]{4,3,1,2,0:T(8,128)(2,1)S(1)}, bf16[2,3,1,128,1024]{4,3,1,2,0:T(8,128)(2,1)S(1)}, u32[]{:S(2)}, u32[]{:S(2)}) collective-permute-start(bf16[2,3,1,128,1024]{4,3,1,2,0:T(8,128)(2,1)S(1)} %get-tuple-element.77), channel_id=1, source_target_pairs={{0,4},{4,0},{8,12},{12,8},{16,20},{20,16},{24,28},{28,24},{1,5},{5... | collective-permute-start | bytes 4718600 | tf_op jit(solution)/shard_map/ppermute | solution.py:24
  124.2 48.9 %collective-permute-start.23 = (bf16[2,3,1,128,1024]{4,3,2,1,0:T(8,128)(2,1)S(1)}, bf16[2,3,1,128,1024]{4,3,2,1,0:T(8,128)(2,1)S(1)}, u32[]{:S(2)}, u32[]{:S(2)}) collective-permute-start(bf16[2,3,1,128,1024]{4,3,2,1,0:T(8,128)(2,1)S(1)} %pad_maximum_fusion.4.refs_6_), channel_id=1, source_target_pairs={{0,8},{4,12},{8,0},{12,4},{16,24},{20,28},{24,16},{28,20},{1,9},{5... | collective-permute-start | bytes 4718600 | tf_op jit(solution)/shard_map/ppermute | solution.py:24
  125.7 49.8 %collective-permute-start.24 = (bf16[2,3,1,128,1024]{4,3,2,1,0:T(8,128)(2,1)S(1)}, bf16[2,3,1,128,1024]{4,3,2,1,0:T(8,128)(2,1)}, u32[]{:S(2)}, u32[]{:S(2)}) collective-permute-start(bf16[2,3,1,128,1024]{4,3,2,1,0:T(8,128)(2,1)S(1)} %pad_maximum_fusion.4.refs_6_), channel_id=1, source_target_pairs={{0,4},{4,0},{8,12},{12,8},{16,20},{20,16},{24,28},{28,24},{1,5},{5... | collective-permute-start | bytes 4718600 | tf_op jit(solution)/shard_map/ppermute | solution.py:24
  304.7 27.1 %collective-permute-start.26 = (bf16[544,1024]{1,0:T(8,128)(2,1)}, bf16[544,1024]{1,0:T(8,128)(2,1)}, u32[]{:S(2)}, u32[]{:S(2)}) collective-permute-start(bf16[544,1024]{1,0:T(8,128)(2,1)} %slice.516), channel_id=1, source_target_pairs={{0,1},{1,0},{2,3},{3,2},{4,5},{5,4},{6,7},{7,6},{8,9},{9,8},{10,11... | collective-permute-start | bytes 3342344 | tf_op jit(solution)/shard_map/ppermute | solution.py:24
  308.6 30.2 %collective-permute-start.42 = (bf16[1024,512]{1,0:T(8,128)(2,1)}, bf16[1024,512]{1,0:T(8,128)(2,1)}, u32[]{:S(2)}, u32[]{:S(2)}) collective-permute-start(bf16[1024,512]{1,0:T(8,128)(2,1)} %convolution_convert_fusion.4), channel_id=1, source_target_pairs={{0,4},{4,0},{8,12},{12,8},{16,20},{20,16},{24,28},{28,24},{1,5},{5... | collective-permute-start | bytes 3145736 | tf_op jit(solution)/shard_map/ppermute | solution.py:24
  341.4 24.1 %collective-permute-start.43 = (bf16[4,2,64,512]{3,2,0,1:T(8,128)(2,1)S(1)}, bf16[4,2,64,512]{3,2,0,1:T(8,128)(2,1)S(1)}, u32[]{:S(2)}, u32[]{:S(2)}) collective-permute-start(bf16[4,2,64,512]{3,2,0,1:T(8,128)(2,1)S(1)} %bitcast.377), channel_id=1, source_target_pairs={{0,8},{4,12},{8,0},{12,4},{16,24},{20,28},{24,16},{28,20},{1,9},{5... | collective-permute-start | bytes 1572872 | tf_op jit(solution)/shard_map/ppermute | solution.py:24
  342.1 17.2 %collective-permute-start.38 = (f32[34,1024]{1,0:T(8,128)S(1)}, f32[34,1024]{1,0:T(8,128)S(1)}, u32[]{:S(2)}, u32[]{:S(2)}) collective-permute-start(f32[34,1024]{1,0:T(8,128)S(1)} %add.563), channel_id=1, source_target_pairs={{0,8},{4,12},{8,0},{12,4},{16,24},{20,28},{24,16},{28,20},{1,9},{5... | collective-permute-start | bytes 417800 | tf_op jit(solution)/shard_map/ppermute | solution.py:24
  346.5 50.2 %collective-permute-start.27 = (bf16[512,3072]{1,0:T(8,128)(2,1)}, bf16[512,3072]{1,0:T(8,128)(2,1)}, u32[]{:S(2)}, u32[]{:S(2)}) collective-permute-start(bf16[512,3072]{1,0:T(8,128)(2,1)} %pad_maximum_fusion), channel_id=1, source_target_pairs={{0,4},{4,0},{8,12},{12,8},{16,20},{20,16},{24,28},{28,24},{1,5},{5... | collective-permute-start | bytes 9437192 | tf_op jit(solution)/shard_map/ppermute | solution.py:24
  363.5 38.3 %collective-permute-start.52 = (bf16[512,4096]{1,0:T(8,128)(2,1)}, bf16[512,4096]{1,0:T(8,128)(2,1)}, u32[]{:S(2)}, u32[]{:S(2)}) collective-permute-start(bf16[512,4096]{1,0:T(8,128)(2,1)} %convolution_convert_fusion.1), channel_id=1, source_target_pairs={{0,4},{4,0},{8,12},{12,8},{16,20},{20,16},{24,28},{28,24},{1,5},{5... | collective-permute-start | bytes 12582920 | tf_op jit(solution)/shard_map/ppermute | solution.py:24
  365.8 13.6 %collective-permute-start.44 = (bf16[4,64,512]{2,1,0:T(8,128)(2,1)S(1)}, bf16[4,64,512]{2,1,0:T(8,128)(2,1)S(1)}, u32[]{:S(2)}, u32[]{:S(2)}) collective-permute-start(bf16[4,64,512]{2,1,0:T(8,128)(2,1)S(1)} %dynamic-slice_bitcast_fusion.5), channel_id=1, source_target_pairs={{0,16},{4,20},{8,24},{12,28},{16,0},{20,4},{24,8},{28,12},{1,17},{... | collective-permute-start | bytes 786440 | tf_op jit(solution)/shard_map/ppermute | solution.py:24
  385.6 53.5 %collective-permute-start.62 = (bf16[4096,512]{1,0:T(8,128)(2,1)}, bf16[4096,512]{1,0:T(8,128)(2,1)}, u32[]{:S(2)}, u32[]{:S(2)}) collective-permute-start(bf16[4096,512]{1,0:T(8,128)(2,1)} %convolution_convert_fusion), channel_id=1, source_target_pairs={{0,4},{4,0},{8,12},{12,8},{16,20},{20,16},{24,28},{28,24},{1,5},{5... | collective-permute-start | bytes 12582920 | tf_op jit(solution)/shard_map/ppermute | solution.py:24
  400.6 37.3 %collective-permute-start.28 = (bf16[1,2,128,3072]{3,2,1,0:T(8,128)(2,1)S(1)}, bf16[1,2,128,3072]{3,2,1,0:T(8,128)(2,1)S(1)}, u32[]{:S(2)}, u32[]{:S(2)}) collective-permute-start(bf16[1,2,128,3072]{3,2,1,0:T(8,128)(2,1)S(1)} %dynamic-slice_bitcast_fusion.1), channel_id=1, source_target_pairs={{0,16},{4,20},{8,24},{12,28},{16,0},{20,4},{24,8},{28,12},{1,17},{... | collective-permute-start | bytes 4718600 | tf_op jit(solution)/shard_map/ppermute | solution.py:24
  408.2 105.3 %collective-permute-start.53 = (bf16[1,2,128,4096]{3,2,1,0:T(8,128)(2,1)S(1)}, bf16[1,2,128,4096]{3,2,1,0:T(8,128)(2,1)S(1)}, u32[]{:S(2)}, u32[]{:S(2)}) collective-permute-start(bf16[1,2,128,4096]{3,2,1,0:T(8,128)(2,1)S(1)} %dynamic-slice_bitcast_fusion), channel_id=1, source_target_pairs={{0,16},{4,20},{8,24},{12,28},{16,0},{20,4},{24,8},{28,12},{1,17},{... | collective-permute-start | bytes 6291464 | tf_op jit(solution)/shard_map/ppermute | solution.py:24
  438.5 18.9 %collective-permute-start.29 = (bf16[1,128,3072]{2,1,0:T(8,128)(2,1)S(1)}, bf16[1,128,3072]{2,1,0:T(8,128)(2,1)S(1)}, u32[]{:S(2)}, u32[]{:S(2)}) collective-permute-start(bf16[1,128,3072]{2,1,0:T(8,128)(2,1)S(1)} %dynamic-slice_bitcast_fusion.4), channel_id=1, source_target_pairs={{0,8},{4,12},{8,0},{12,4},{16,24},{20,28},{24,16},{28,20},{1,9},{5... | collective-permute-start | bytes 2359304 | tf_op jit(solution)/shard_map/ppermute | solution.py:24
  457.7 9.7 %collective-permute-start.32 = (bf16[3,128,256]{2,1,0:T(8,128)(2,1)S(1)}, bf16[3,128,256]{2,1,0:T(8,128)(2,1)S(1)}, u32[]{:S(2)}, u32[]{:S(2)}) collective-permute-start(bf16[3,128,256]{2,1,0:T(8,128)(2,1)S(1)} %pad_maximum_fusion.17), channel_id=1, source_target_pairs={{0,3},{1,2},{2,1},{3,0},{4,7},{5,6},{6,5},{7,4},{8,11},{9,10},{10,... | collective-permute-start | bytes 589832 | tf_op jit(solution)/shard_map/ppermute | solution.py:24
  460.0 16.2 %collective-permute-start.31 = (bf16[3,128,256]{2,1,0:T(8,128)(2,1)S(1)}, bf16[3,128,256]{2,1,0:T(8,128)(2,1)S(1)}, u32[]{:S(2)}, u32[]{:S(2)}) collective-permute-start(bf16[3,128,256]{2,1,0:T(8,128)(2,1)S(1)} %pad_maximum_fusion.16), channel_id=1, source_target_pairs={{0,2},{1,3},{2,0},{3,1},{4,6},{5,7},{6,4},{7,5},{8,10},{9,11},{10,... | collective-permute-start | bytes 589832 | tf_op jit(solution)/shard_map/ppermute | solution.py:24
  460.5 15.7 %collective-permute-start.30 = (bf16[3,128,256]{2,1,0:T(8,128)(2,1)S(1)}, bf16[3,128,256]{2,1,0:T(8,128)(2,1)S(1)}, u32[]{:S(2)}, u32[]{:S(2)}) collective-permute-start(bf16[3,128,256]{2,1,0:T(8,128)(2,1)S(1)} %pad_maximum_fusion.15), channel_id=1, source_target_pairs={{0,1},{1,0},{2,3},{3,2},{4,5},{5,4},{6,7},{7,6},{8,9},{9,8},{10,11... | collective-permute-start | bytes 589832 | tf_op jit(solution)/shard_map/ppermute | solution.py:24
  462.9 52.2 %collective-permute-start.63 = (bf16[4,2,256,512]{3,2,0,1:T(8,128)(2,1)S(1)}, bf16[4,2,256,512]{3,2,0,1:T(8,128)(2,1)S(1)}, u32[]{:S(2)}, u32[]{:S(2)}) collective-permute-start(bf16[4,2,256,512]{3,2,0,1:T(8,128)(2,1)S(1)} %bitcast.368), channel_id=1, source_target_pairs={{0,8},{4,12},{8,0},{12,4},{16,24},{20,28},{24,16},{28,20},{1,9},{5... | collective-permute-start | bytes 6291464 | tf_op jit(solution)/shard_map/ppermute | solution.py:24
  476.6 35.7 %collective-permute-start.33 = (bf16[1,3,128,256]{3,2,1,0:T(8,128)(2,1)S(1)}, bf16[1,3,128,256]{3,2,1,0:T(8,128)(2,1)S(1)}, u32[]{:S(2)}, u32[]{:S(2)}) collective-permute-start(bf16[1,3,128,256]{3,2,1,0:T(8,128)(2,1)S(1)} %bitcast.374), channel_id=1, source_target_pairs={{0,8},{4,12},{8,0},{12,4},{16,24},{20,28},{24,16},{28,20},{1,9},{5... | collective-permute-start | bytes 589832 | tf_op jit(solution)/shard_map/ppermute | solution.py:24
  514.4 25.6 %collective-permute-start.54 = (bf16[1,128,4096]{2,1,0:T(8,128)(2,1)S(1)}, bf16[1,128,4096]{2,1,0:T(8,128)(2,1)S(1)}, u32[]{:S(2)}, u32[]{:S(2)}) collective-permute-start(bf16[1,128,4096]{2,1,0:T(8,128)(2,1)S(1)} %dynamic-slice_bitcast_fusion.3), channel_id=1, source_target_pairs={{0,8},{4,12},{8,0},{12,4},{16,24},{20,28},{24,16},{28,20},{1,9},{5... | collective-permute-start | bytes 3145736 | tf_op jit(solution)/shard_map/ppermute | solution.py:24
  515.8 29.1 %collective-permute-start.64 = (bf16[4,256,512]{2,1,0:T(8,128)(2,1)S(1)}, bf16[4,256,512]{2,1,0:T(8,128)(2,1)S(1)}, u32[]{:S(2)}, u32[]{:S(2)}) collective-permute-start(bf16[4,256,512]{2,1,0:T(8,128)(2,1)S(1)} %dynamic-slice_bitcast_fusion.2), channel_id=1, source_target_pairs={{0,16},{4,20},{8,24},{12,28},{16,0},{20,4},{24,8},{28,12},{1,17},{... | collective-permute-start | bytes 3145736 | tf_op jit(solution)/shard_map/ppermute | solution.py:24
  540.4 11.2 %collective-permute-start.57 = (bf16[128,1024]{1,0:T(8,128)(2,1)S(1)}, bf16[128,1024]{1,0:T(8,128)(2,1)S(1)}, u32[]{:S(2)}, u32[]{:S(2)}) collective-permute-start(bf16[128,1024]{1,0:T(8,128)(2,1)S(1)} %get-tuple-element.89), channel_id=1, source_target_pairs={{0,3},{1,2},{2,1},{3,0},{4,7},{5,6},{6,5},{7,4},{8,11},{9,10},{10,... | collective-permute-start | bytes 786440 | tf_op jit(solution)/shard_map/ppermute | solution.py:24
  542.8 34.7 %collective-permute-start.56 = (bf16[128,1024]{1,0:T(8,128)(2,1)S(1)}, bf16[128,1024]{1,0:T(8,128)(2,1)S(1)}, u32[]{:S(2)}, u32[]{:S(2)}) collective-permute-start(bf16[128,1024]{1,0:T(8,128)(2,1)S(1)} %get-tuple-element.90), channel_id=1, source_target_pairs={{0,2},{1,3},{2,0},{3,1},{4,6},{5,7},{6,4},{7,5},{8,10},{9,11},{10,... | collective-permute-start | bytes 786440 | tf_op jit(solution)/shard_map/ppermute | solution.py:24
  542.8 34.7 %collective-permute-start.55 = (bf16[128,1024]{1,0:T(8,128)(2,1)S(1)}, bf16[128,1024]{1,0:T(8,128)(2,1)S(1)}, u32[]{:S(2)}, u32[]{:S(2)}) collective-permute-start(bf16[128,1024]{1,0:T(8,128)(2,1)S(1)} %get-tuple-element.88), channel_id=1, source_target_pairs={{0,1},{1,0},{2,3},{3,2},{4,5},{5,4},{6,7},{7,6},{8,9},{9,8},{10,11... | collective-permute-start | bytes 786440 | tf_op jit(solution)/shard_map/ppermute | solution.py:24
  545.2 33.6 %collective-permute-start.67 = (bf16[256,512]{1,0:T(8,128)(2,1)S(1)}, bf16[256,512]{1,0:T(8,128)(2,1)S(1)}, u32[]{:S(2)}, u32[]{:S(2)}) collective-permute-start(bf16[256,512]{1,0:T(8,128)(2,1)S(1)} %get-tuple-element.86), channel_id=1, source_target_pairs={{0,3},{1,2},{2,1},{3,0},{4,7},{5,6},{6,5},{7,4},{8,11},{9,10},{10,... | collective-permute-start | bytes 786440 | tf_op jit(solution)/shard_map/ppermute | solution.py:24
  547.6 39.9 %collective-permute-start.66 = (bf16[256,512]{1,0:T(8,128)(2,1)S(1)}, bf16[256,512]{1,0:T(8,128)(2,1)S(1)}, u32[]{:S(2)}, u32[]{:S(2)}) collective-permute-start(bf16[256,512]{1,0:T(8,128)(2,1)S(1)} %get-tuple-element.87), channel_id=1, source_target_pairs={{0,2},{1,3},{2,0},{3,1},{4,6},{5,7},{6,4},{7,5},{8,10},{9,11},{10,... | collective-permute-start | bytes 786440 | tf_op jit(solution)/shard_map/ppermute | solution.py:24
  551.6 35.9 %collective-permute-start.65 = (bf16[256,512]{1,0:T(8,128)(2,1)S(1)}, bf16[256,512]{1,0:T(8,128)(2,1)S(1)}, u32[]{:S(2)}, u32[]{:S(2)}) collective-permute-start(bf16[256,512]{1,0:T(8,128)(2,1)S(1)} %get-tuple-element.85), channel_id=1, source_target_pairs={{0,1},{1,0},{2,3},{3,2},{4,5},{5,4},{6,7},{7,6},{8,9},{9,8},{10,11... | collective-permute-start | bytes 786440 | tf_op jit(solution)/shard_map/ppermute | solution.py:24
  578.2 11.0 %collective-permute-start.58 = (bf16[1,128,1024]{2,1,0:T(8,128)(2,1)S(1)}, bf16[1,128,1024]{2,1,0:T(8,128)(2,1)S(1)}, u32[]{:S(2)}, u32[]{:S(2)}) collective-permute-start(bf16[1,128,1024]{2,1,0:T(8,128)(2,1)S(1)} %bitcast.372), channel_id=1, source_target_pairs={{0,8},{4,12},{8,0},{12,4},{16,24},{20,28},{24,16},{28,20},{1,9},{5... | collective-permute-start | bytes 786440 | tf_op jit(solution)/shard_map/ppermute | solution.py:24
  589.3 17.3 %collective-permute-start.59 = (bf16[2,128,1024]{2,1,0:T(8,128)(2,1)S(1)}, bf16[2,128,1024]{2,1,0:T(8,128)(2,1)S(1)}, u32[]{:S(2)}, u32[]{:S(2)}) collective-permute-start(bf16[2,128,1024]{2,1,0:T(8,128)(2,1)S(1)} %pad_maximum_fusion.11), channel_id=1, source_target_pairs={{0,16},{4,20},{8,24},{12,28},{16,0},{20,4},{24,8},{28,12},{1,17},{... | collective-permute-start | bytes 1572872 | tf_op jit(solution)/shard_map/ppermute | solution.py:24
  590.4 16.2 %collective-permute-start.60 = (bf16[2,128,1024]{2,1,0:T(8,128)(2,1)S(1)}, bf16[2,128,1024]{2,1,0:T(8,128)(2,1)S(1)}, u32[]{:S(2)}, u32[]{:S(2)}) collective-permute-start(bf16[2,128,1024]{2,1,0:T(8,128)(2,1)S(1)} %pad_maximum_fusion.11), channel_id=1, source_target_pairs={{0,4},{4,0},{8,12},{12,8},{16,20},{20,16},{24,28},{28,24},{1,5},{5... | collective-permute-start | bytes 1572872 | tf_op jit(solution)/shard_map/ppermute | solution.py:24
  (94 other events, 950.1 us)

commit v2 on v1

v2 whole, which is shorter than its diff:
```python
import functools
import math

import jax
import jax.numpy as jnp
from jax import lax
from jax.experimental import pallas as pl
from jax.experimental.pallas import tpu as pltpu
from jax.sharding import PartitionSpec as P

HEAD_DIM = 64
SEQ_LEN = 1088
RELAX_ALPHA = 32.0
NORM_EPSILON = 1e-05
MASKED_SCORE = -1000000000.0
PRECISE = lax.Precision.HIGHEST
BF16 = jnp.bfloat16
F32 = jnp.float32
LANES = 128
LIGHT = pl.CostEstimate(flops=1000, bytes_accessed=1000, transcendentals=0)


def swap(value, axis, mask):
    count = lax.axis_size(axis)
    return lax.ppermute(value, axis, [(i, i ^ mask) for i in range(count)])


def normalize(inputs):
    centred = inputs - jnp.mean(inputs, axis=-1, keepdims=True)
    factor = lax.rsqrt(jnp.mean(centred * centred, axis=-1, keepdims=True) + NORM_EPSILON)
    return centred * factor, factor


def norm_forward(inputs, gain_row, shift_row):
    centred = inputs - jnp.mean(inputs, axis=-1, keepdims=True)
    factor = lax.rsqrt(jnp.mean(centred * centred, axis=-1, keepdims=True) + NORM_EPSILON)
    normal = centred * factor
    return (normal * gain_row + shift_row, normal, factor)


def norm_backward(upstream, normal, factor, gain_row):
    scaled = upstream * gain_row
    adjusted = (
        scaled
        - jnp.mean(scaled, axis=-1, keepdims=True)
        - normal * jnp.mean(scaled * normal, axis=-1, keepdims=True)
    )
    return (adjusted * factor, jnp.sum(upstream * normal, axis=0), jnp.sum(upstream, axis=0))


def dot_nn(a, b):
    return lax.dot_general(a, b, (((1,), (0,)), ((), ())), preferred_element_type=F32)


def dot_nt(a, b):
    return lax.dot_general(a, b, (((1,), (1,)), ((), ())), preferred_element_type=F32)


def dot_tn(a, b):
    return lax.dot_general(a, b, (((0,), (0,)), ((), ())), preferred_element_type=F32)


def query_tile(rows):
    return rows // 2 if (rows // 2) % 16 == 0 else rows


def attend_kernel(blocks, rows, q_ref, k_ref, v_ref, kc_ref, out_ref, aug_ref):
    tile = query_tile(rows)
    lane = lax.broadcasted_iota(jnp.int32, (1, LANES), 1)
    first = lane < HEAD_DIM
    k_pair, v_pair, k_const = k_ref[...], v_ref[...], kc_ref[...]
    q_pair = q_ref[...]
    outs = []
    augs = []
    for head in range(2):
        mine = first if head == 0 else jnp.logical_not(first)
        special = lane == (HEAD_DIM if head == 0 else 0)
        keys = jnp.where(mine, k_pair, k_const)
        queries = jnp.where(mine, q_pair, jnp.where(special, 1.0, 0.0).astype(BF16))
        head_out = []
        head_aug = []
        for start in range(0, rows, tile):
            reach = start + tile
            q_tile = queries[start:reach]
            own = dot_nt(q_tile, keys[:reach])
            row_ids = start + lax.broadcasted_iota(jnp.int32, (tile, reach), 0)
            columns = lax.broadcasted_iota(jnp.int32, (tile, reach), 1)
            pieces = [jnp.where(columns <= row_ids, own, MASKED_SCORE)]
            for block in range(1, blocks):
                pieces.append(dot_nt(q_tile, keys[block * rows : (block + 1) * rows]))
            top = functools.reduce(
                jnp.maximum, [jnp.max(piece, axis=-1, keepdims=True) for piece in pieces]
            )
            total = jnp.zeros((tile, 1), F32)
            gathered = jnp.zeros((tile, LANES), F32)
            for block, piece in enumerate(pieces):
                exponent = jnp.exp(piece - top)
                total = total + jnp.sum(exponent, axis=-1, keepdims=True)
                span = v_pair[:reach] if block == 0 else v_pair[block * rows : (block + 1) * rows]
                gathered = gathered + dot_nn(exponent.astype(BF16), span)
            head_out.append(gathered / total)
            log_sum = -(top + jnp.log(total))
            high = log_sum.astype(BF16)
            rest = log_sum - high.astype(F32)
            mid = rest.astype(BF16)
            low = (rest - mid.astype(F32)).astype(BF16)
            zero = jnp.zeros((tile, LANES), BF16)
            spot = lane % HEAD_DIM
            aug = jnp.where(spot == 0, jnp.ones_like(zero), zero)
            aug = jnp.where(spot == 1, high, aug)
            aug = jnp.where(spot == 2, mid, aug)
            aug = jnp.where(spot == 3, low, aug)
            head_aug.append(aug)
        outs.append(head_out)
        augs.append(head_aug)
    for index, start in enumerate(range(0, rows, tile)):
        out_ref[start : start + tile, :] = jnp.where(
            first, outs[0][index], outs[1][index]
        ).astype(BF16)
        aug_ref[start : start + tile, :] = jnp.where(first, augs[1][index], augs[0][index])


def attend(queries, keys, values, key_const, begin, count):
    rows = queries.shape[0]
    span = keys.shape[0]
    first = begin // LANES
    pair = lambda height: pl.BlockSpec((height, LANES), lambda i: (0, first + i))
    made = lambda height: pl.BlockSpec((height, LANES), lambda i: (0, i))
    return pl.pallas_call(
        functools.partial(attend_kernel, span // rows, rows),
        grid=(count // LANES,),
        in_specs=[
            pair(rows),
            pair(span),
            pair(span),
            pl.BlockSpec((span, LANES), lambda i: (0, 0)),
        ],
        out_specs=[made(rows), made(rows)],
        out_shape=[
            jax.ShapeDtypeStruct((rows, count), BF16),
            jax.ShapeDtypeStruct((rows, count), BF16),
        ],
        name="attend",
        compiler_params=pltpu.CompilerParams(vmem_limit_bytes=40 << 20),
        cost_estimate=LIGHT,
    )(queries, keys, values, key_const)


def attend_back_kernel(
    blocks, rows, q_ref, k_ref, v_ref, kc_ref, aug_ref, go_ref, out_ref, dq_ref, dk_ref, dv_ref
):
    key_tile = query_tile(rows)
    lane = lax.broadcasted_iota(jnp.int32, (1, LANES), 1)
    first = lane < HEAD_DIM
    spot = lane % HEAD_DIM
    k_pair, v_pair, k_const = k_ref[...], v_ref[...], kc_ref[...]
    q_pair, aug, go_pair = q_ref[...], aug_ref[...], go_ref[...]
    weighed = go_pair.astype(F32) * out_ref[...].astype(F32)
    v_const = jnp.where((spot >= 1) & (spot <= 3), 1.0, 0.0).astype(BF16)
    grads_q = []
    grads_k = []
    grads_v = []
    for head in range(2):
        mine = first if head == 0 else jnp.logical_not(first)
        keys = jnp.where(mine, k_pair, k_const)
        queries = jnp.where(mine, q_pair, aug)
        values = jnp.where(mine, v_pair, v_const)
        delta = -jnp.sum(jnp.where(mine, weighed, 0.0), axis=-1, keepdims=True)
        high = delta.astype(BF16)
        rest = delta - high.astype(F32)
        mid = rest.astype(BF16)
        low = (rest - mid.astype(F32)).astype(BF16)
        go_aug = jnp.where(spot == 1, high, jnp.zeros((rows, LANES), BF16))
        go_aug = jnp.where(spot == 2, mid, go_aug)
        go_aug = jnp.where(spot == 3, low, go_aug)
        grads = jnp.where(mine, go_pair, go_aug)
        grad_q = jnp.zeros((rows, LANES), F32)
        head_k = []
        head_v = []
        for start in range(0, blocks * rows, key_tile):
            stop = start + key_tile
            scores = dot_nt(keys[start:stop], queries)
            exact = jnp.exp(scores)
            if start < rows:
                key_ids = start + lax.broadcasted_iota(jnp.int32, (key_tile, rows), 0)
                query_ids = lax.broadcasted_iota(jnp.int32, (key_tile, rows), 1)
                exact = jnp.where(key_ids <= query_ids, exact, 0.0)
            centred = dot_nt(values[start:stop], grads)
            grad_scores = (exact * centred).astype(BF16)
            head_v.append(dot_nn(exact.astype(BF16), go_pair))
            head_k.append(dot_nn(grad_scores, q_pair))
            grad_q = grad_q + dot_tn(grad_scores, k_pair[start:stop])
        grads_q.append(grad_q)
        grads_k.append(head_k)
        grads_v.append(head_v)
    dq_ref[...] = (jnp.where(first, grads_q[0], grads_q[1]) * 0.125).astype(BF16)
    for index, start in enumerate(range(0, blocks * rows, key_tile)):
        dk_ref[start : start + key_tile, :] = jnp.where(
            first, grads_k[0][index], grads_k[1][index]
        ).astype(BF16)
        dv_ref[start : start + key_tile, :] = jnp.where(
            first, grads_v[0][index], grads_v[1][index]
        ).astype(BF16)


def attend_back(queries, keys, values, key_const, aug, grad_out, out, begin):
    rows = queries.shape[0]
    count = aug.shape[1]
    span = keys.shape[0]
    first = begin // LANES
    pair = lambda height: pl.BlockSpec((height, LANES), lambda i: (0, first + i))
    made = lambda height: pl.BlockSpec((height, LANES), lambda i: (0, i))
    return pl.pallas_call(
        functools.partial(attend_back_kernel, span // rows, rows),
        grid=(count // LANES,),
        in_specs=[
            pair(rows),
            pair(span),
            pair(span),
            pl.BlockSpec((span, LANES), lambda i: (0, 0)),
            made(rows),
            pair(rows),
            made(rows),
        ],
        out_specs=[made(rows), made(span), made(span)],
        out_shape=[
            jax.ShapeDtypeStruct((rows, count), BF16),
            jax.ShapeDtypeStruct((span, count), BF16),
            jax.ShapeDtypeStruct((span, count), BF16),
        ],
        name="attend_back",
        compiler_params=pltpu.CompilerParams(vmem_limit_bytes=48 << 20),
        cost_estimate=LIGHT,
    )(queries, keys, values, key_const, aug, grad_out, out)


def chip_masks(dp):
    bits = dp.bit_length() - 2
    low = bits // 2
    along_x = [2 << i for i in range(low)]
    along_y = [2 << i for i in range(low, bits)]
    return along_x, along_y


def position(device, mask, dp):
    other = device ^ mask
    return (other & 1) * (dp // 2) + (other >> 1)


def own_slice(weight, by_rows, device, width):
    dp = lax.axis_size("dp")
    if by_rows:
        full = weight.shape[1]
        start = position(device, 0, dp) * (full // dp)
        piece = lax.dynamic_slice(weight, (start % width, start // width * width), (full // dp, width))
        return piece[None]
    rows = weight.shape[1] // dp
    return lax.dynamic_slice_in_dim(weight, position(device, 0, dp) * rows, rows, axis=1)


class Flow:
    def __init__(self, steps):
        self.steps = steps
        self.result = None
        self.over = False
        self.held = None
        self.move(None)

    def move(self, value):
        try:
            self.held = self.steps.send(value)
        except StopIteration as stop:
            self.result, self.over, self.held = stop.value, True, None


def ordered(flows, values):
    live = [flow for flow in flows if not flow.over]
    values, held = lax.optimization_barrier((values, [flow.held for flow in live]))
    for flow, item in zip(live, held):
        flow.move(item)
    return values


def begin(flows, *values):
    values = ordered(flows, values)
    return values if len(values) > 1 else values[0]


def meet(flows, *values):
    values = ordered(flows, values)
    return begin(flows, *values)


def layer_steps(value):
    mp = lax.axis_size("mp")
    got = {0: value}
    for count in range(1, mp.bit_length()):
        ranks = [r for r in range(mp) if r.bit_count() == count]
        sent = [got[r & (r - 1)] for r in ranks]
        if count > 1:
            sent = yield tuple(sent)
        found = yield tuple(swap(item, "mp", r & -r) for r, item in zip(ranks, sent))
        got.update(zip(ranks, found))
    return [got[r] for r in range(mp)]


def spread_steps(sides):
    along_x, along_y = chip_masks(lax.axis_size("dp"))
    orders = (along_x + along_y, along_y + along_x)
    masks = [[0], [0]]
    held = [side[None] for side in sides]
    arrays = []
    for step in range(len(along_x + along_y)):
        held = yield tuple(held)
        got = yield tuple(swap(value, "dp", order[step]) for value, order in zip(held, orders))
        for side, order in enumerate(orders):
            moved = [m ^ order[step] for m in masks[side]]
            if step + 1 < len(order):
                masks[side] = masks[side] + moved
            else:
                arrays += [(side, masks[side], held[side]), (side, moved, got[side])]
        held = [jnp.concatenate([one, two], axis=0) for one, two in zip(held, got)]
    own = yield tuple(value for _, _, value in arrays)
    other = yield tuple(swap(value, "dp", 1) for value in own)
    return [(side, m, value) for (side, m, _), value in zip(arrays, own)] + [
        (side, [k ^ 1 for k in m], value) for (side, m, _), value in zip(arrays, other)
    ]


def gather_flow(stacked, extra=None):
    count, rows, width = stacked.shape
    flat = stacked.reshape(count * rows, width)
    if extra is not None:
        flat = jnp.concatenate([flat, extra], axis=0)
    (flat,) = yield (flat,)
    found = yield from layer_steps(flat)
    across = jnp.stack([item[: count * rows].reshape(count, rows, width) for item in found[1:]])
    half = rows // 2
    arrays = yield from spread_steps((across[:, :, :half], across[:, :, half:]))
    return arrays, [item[count * rows :] for item in found]


class Weights:
    def __init__(self, own, arrays):
        self.own, self.arrays = own, arrays
        sample = arrays[0][2]
        self.full, self.width = sample.shape[3] * 2 * lax.axis_size("dp"), sample.shape[4]
        self.inputs = [shard for shard, _, _ in own] + [value for _, _, value in arrays]
        self.n_own = len(own)

    def specs(self):
        return [pl.BlockSpec(memory_space=pl.ANY)] * len(self.inputs)

    def scratch(self, mp, which):
        count = self.full // self.width + (mp - 1) * sum(len(m) for _, m, _ in self.arrays)
        return [
            pltpu.VMEM((mp, len(which), self.full, self.width), BF16),
            pltpu.SemaphoreType.DMA((count + 4,)),
        ]

    def copies(self, refs, held, sems, device, mp, dp, which):
        made = [[] for _ in range(mp)]
        spot = 0

        def add(r, source, target):
            nonlocal spot
            made[r].append((source, target, sems.at[spot]))
            spot += 1

        first, last = which[0], which[-1] + 1
        for ref, (_, index, by_rows) in zip(refs, self.own):
            if by_rows and first <= index < last:
                for block in range(self.full // self.width):
                    columns = pl.ds(block * self.width, self.width)
                    add(0, ref.at[:, columns], held.at[0, index - first, columns, :])
            elif not by_rows and first == index:
                add(0, ref, held.at[0, 0 : ref.shape[0]])
        half = self.full // dp // 2
        for r in range(1, mp):
            for ref, (side, masks, _) in zip(refs[self.n_own :], self.arrays):
                for index, mask in enumerate(masks):
                    start = pl.multiple_of((position(device, mask, dp) * 2 + side) * half, half)
                    add(
                        r,
                        ref.at[index, r - 1, first:last],
                        held.at[r, :, pl.ds(start, half), :],
                    )
        return made


def start_all(copies):
    for copy in copies:
        pltpu.make_async_copy(*copy).start()


def wait_all(copies):
    for copy in copies:
        pltpu.make_async_copy(*copy).wait()


def wait_step(step, copies, begin=0):
    for r in range(begin, len(copies)):

        @pl.when(step == r)
        def _():
            wait_all(copies[r])


def tiles(count, size, body):
    if count == size:
        body(0)
    else:

        for i in range(count // size):
            body(i * size)


def row_tile(rows):
    return 272 if rows % 272 == 0 else 16


COLUMNS = 256


def column_tile(width):
    return min(COLUMNS, width)


def whole(shape):
    return pl.BlockSpec(shape, lambda i, *_: (0,) * len(shape))


def project_kernel(group, blocks, scale, scal, *refs):
    n_in = len(group.inputs)
    x_refs, bias_ref = refs[:blocks], refs[blocks]
    w_refs = refs[blocks + 1 : blocks + 1 + n_in]
    q_ref, k_ref, v_ref, held, sems = refs[blocks + 1 + n_in :]
    r = pl.program_id(0)
    mp, dp = lax.axis_size("mp"), lax.axis_size("dp")
    copies = group.copies(w_refs, held, sems, scal[0], mp, dp, [0, 1, 2])
    rows = q_ref.shape[0]

    @pl.when(r == 0)
    def _():
        start_all(sum(copies, []))

    wait_step(r, copies)

    size = column_tile(group.width)
    for begin in range(0, group.width, size):
        columns = slice(begin, begin + size)
        q = dot_nn(x_refs[0][...], held[r, 0, :, columns]) + bias_ref[0:1, columns].astype(F32)
        q_ref[:, columns] = ((q * scale).astype(BF16) * RELAX_ALPHA).astype(BF16)
        for block in range(blocks):
            x = x_refs[block][...]
            place = slice(block * rows, (block + 1) * rows)
            k_ref[place, columns] = dot_nn(x, held[r, 1, :, columns]).astype(BF16)
            v = dot_nn(x, held[r, 2, :, columns]) + bias_ref[1:2, columns].astype(F32)
            v_ref[place, columns] = v.astype(BF16)


def project(normed, biases, group, device):
    mp = lax.axis_size("mp")
    rows, full = normed[0].shape
    blocks = len(normed)
    width = group.width
    made = lambda height: pl.BlockSpec((height, width), lambda i, *_: (0, i))
    return pl.pallas_call(
        functools.partial(project_kernel, group, blocks, 1.0 / math.sqrt(HEAD_DIM) / RELAX_ALPHA),
        grid_spec=pltpu.PrefetchScalarGridSpec(
            num_scalar_prefetch=1,
            grid=(mp,),
            in_specs=[whole((rows, full))] * blocks
            + [pl.BlockSpec((8, width), lambda i, *_: (0, i))]
            + group.specs(),
            out_specs=[made(rows), made(blocks * rows), made(blocks * rows)],
            scratch_shapes=group.scratch(mp, [0, 1, 2]),
        ),
        out_shape=[
            jax.ShapeDtypeStruct((rows, full), BF16),
            jax.ShapeDtypeStruct((blocks * rows, full), BF16),
            jax.ShapeDtypeStruct((blocks * rows, full), BF16),
        ],
        name="project",
        compiler_params=pltpu.CompilerParams(vmem_limit_bytes=48 << 20),
        cost_estimate=LIGHT,
    )(device.reshape(1), *normed, biases, *group.inputs)


def up_kernel(group_a, group_u, scal, *refs):
    (att_a, att_b, residual_ref, rows_ref, bias_ref), refs = refs[:5], refs[5:]
    wa, refs = refs[: len(group_a.inputs)], refs[len(group_a.inputs) :]
    wu, refs = refs[: len(group_u.inputs)], refs[len(group_u.inputs) :]
    branch_ref, middle_ref, mid_ref, act_ref, slope_ref, held_o, sem_o, held_u, sem_u = refs
    r = pl.program_id(0)
    mp, dp = lax.axis_size("mp"), lax.axis_size("dp")
    copies_o = sum(group_a.copies(wa, held_o, sem_o, scal[0], mp, dp, [3]), [])
    copies_u = group_u.copies(wu, held_u, sem_u, scal[0], mp, dp, [0])
    rows, full = middle_ref.shape
    width = group_a.width
    part = att_a.shape[1]

    @pl.when(r == 0)
    def _():
        start_all(copies_o)
        start_all(sum(copies_u, []))
        wait_all(copies_o)
        for block in range(full // width):
            columns = slice(block * width, (block + 1) * width)
            total = jnp.zeros((rows, width), F32)
            for layer in range(mp):
                source = att_a if layer * width < part else att_b
                first = layer * width % part
                total = total + dot_nn(source[:, first : first + width], held_o[layer, 0, columns, :])
            branch_ref[:, columns] = total + rows_ref[0:1, columns]

        def norm_rows(start):
            place = pl.ds(start, row_tile(rows))
            normal, _ = normalize(branch_ref[place, :])
            middle = residual_ref[place, :] + normal * rows_ref[1:2, :] + rows_ref[2:3, :]
            middle_ref[place, :] = middle
            normal, _ = normalize(middle)
            mid_ref[place, :] = (normal * rows_ref[3:4, :] + rows_ref[4:5, :]).astype(BF16)

        tiles(rows, row_tile(rows), norm_rows)

    wait_step(r, copies_u)

    size = column_tile(group_u.width)

    def activate(start):
        columns = pl.ds(start, size)
        u = dot_nn(mid_ref[...], held_u[r, 0, :, columns]) + bias_ref[0:1, columns]
        scale = math.sqrt(2.0 / math.pi)
        square = u * u
        bent = jnp.tanh(scale * u * (1.0 + 0.044715 * square))
        lifted = 0.5 + 0.5 * bent
        act_ref[:, columns] = (u * lifted).astype(BF16)
        slope = lifted + (0.5 * scale) * u * (1.0 - bent * bent) * (
            1.0 + (3.0 * 0.044715) * square
        )
        slope_ref[:, columns] = slope.astype(BF16)

    tiles(group_u.width, size, activate)


def feed_up(att_a, att_b, residual, vectors, u_bias, group_a, group_u, device):
    mp = lax.axis_size("mp")
    rows, full = residual.shape
    hidden = group_u.width
    made = pl.BlockSpec((rows, hidden), lambda i, *_: (0, i))
    return pl.pallas_call(
        functools.partial(up_kernel, group_a, group_u),
        grid_spec=pltpu.PrefetchScalarGridSpec(
            num_scalar_prefetch=1,
            grid=(mp,),
            in_specs=[whole(att_a.shape), whole(att_b.shape), whole((rows, full)), whole((8, full))]
            + [pl.BlockSpec((8, hidden), lambda i, *_: (0, i))]
            + group_a.specs()
            + group_u.specs(),
            out_specs=[whole((rows, full)), whole((rows, full)), whole((rows, full)), made, made],
            scratch_shapes=group_a.scratch(mp, [3]) + group_u.scratch(mp, [0]),
        ),
        out_shape=[
            jax.ShapeDtypeStruct((rows, full), F32),
            jax.ShapeDtypeStruct((rows, full), F32),
            jax.ShapeDtypeStruct((rows, full), BF16),
            jax.ShapeDtypeStruct((rows, mp * hidden), BF16),
            jax.ShapeDtypeStruct((rows, mp * hidden), BF16),
        ],
        name="feed_up",
        compiler_params=pltpu.CompilerParams(vmem_limit_bytes=56 << 20),
        cost_estimate=LIGHT,
    )(
        device.reshape(1), att_a, att_b, residual, vectors, u_bias, *group_a.inputs, *group_u.inputs
    )


def down_kernel(group_d, scal, *refs):
    (act_ref, middle_ref, cot_ref, rows_ref), refs = refs[:4], refs[4:]
    wd, refs = refs[: len(group_d.inputs)], refs[len(group_d.inputs) :]
    out_ref, grad_ref, sums_ref, held, sems, total = refs
    r = pl.program_id(0)
    mp, dp = lax.axis_size("mp"), lax.axis_size("dp")
    copies = group_d.copies(wd, held, sems, scal[0], mp, dp, [0])
    rows, full = middle_ref.shape
    width = group_d.width

    @pl.when(r == 0)
    def _():
        start_all(sum(copies, []))
        total[...] = jnp.zeros_like(total)

    wait_step(r, copies)

    size = column_tile(width)
    for block in range(full // width):

        def add(start):
            columns = pl.ds(block * width + start, size)
            total[:, columns] += dot_nn(
                act_ref[...], held[r, 0, block * width : (block + 1) * width, pl.ds(start, size)]
            )

        tiles(width, size, add)

    @pl.when(r == mp - 1)
    def _():
        sums_ref[...] = jnp.zeros_like(sums_ref)

        def norm_rows(start):
            place = pl.ds(start, row_tile(rows))
            normal, factor = normalize(total[place, :] + rows_ref[0:1, :])
            gain = rows_ref[1:2, :]
            out_ref[place, :] = (
                middle_ref[place, :] + (normal * gain + rows_ref[2:3, :])
            ).astype(BF16)
            upstream = cot_ref[place, :].astype(F32)
            scaled = upstream * gain
            grad = (
                scaled
                - jnp.mean(scaled, axis=-1, keepdims=True)
                - normal * jnp.mean(scaled * normal, axis=-1, keepdims=True)
            ) * factor
            grad = grad.astype(BF16)
            grad_ref[place, :] = grad
            sums_ref[0:8, :] += fold(upstream * normal)
            sums_ref[8:16, :] += fold(upstream)
            sums_ref[16:24, :] += fold(grad.astype(F32))

        tiles(rows, row_tile(rows), norm_rows)


def fold(value):
    return functools.reduce(jnp.add, [value[i : i + 8] for i in range(0, value.shape[0], 8)])


def feed_down(act, middle, cotangent, vectors, group_d, device):
    mp = lax.axis_size("mp")
    rows, full = middle.shape
    hidden = group_d.width
    return pl.pallas_call(
        functools.partial(down_kernel, group_d),
        grid_spec=pltpu.PrefetchScalarGridSpec(
            num_scalar_prefetch=1,
            grid=(mp,),
            in_specs=[pl.BlockSpec((rows, hidden), lambda i, *_: (0, i))]
            + [whole((rows, full)), whole((rows, full)), whole((8, full))]
            + group_d.specs(),
            out_specs=[whole((rows, full)), whole((rows, full)), whole((24, full))],
            scratch_shapes=group_d.scratch(mp, [0]) + [pltpu.VMEM((rows, full), F32)],
        ),
        out_shape=[
            jax.ShapeDtypeStruct((rows, full), BF16),
            jax.ShapeDtypeStruct((rows, full), BF16),
            jax.ShapeDtypeStruct((24, full), F32),
        ],
        name="feed_down",
        compiler_params=pltpu.CompilerParams(vmem_limit_bytes=48 << 20),
        cost_estimate=LIGHT,
    )(device.reshape(1), act, middle, cotangent, vectors, *group_d.inputs)


def back_kernel(group_a, group_u, group_d, scal, *refs):
    (grad_ref, slope_ref, branch_ref, middle_ref, cot_ref, rows_ref), refs = refs[:6], refs[6:]
    wa, refs = refs[: len(group_a.inputs)], refs[len(group_a.inputs) :]
    wu, refs = refs[: len(group_u.inputs)], refs[len(group_u.inputs) :]
    wd, refs = refs[: len(group_d.inputs)], refs[len(group_d.inputs) :]
    (pre_ref, mid_ref, low_ref, att_ref, sums_ref, u_sum_ref), refs = refs[:6], refs[6:]
    held_o, sem_o, held_u, sem_u, held_d, sem_d, total = refs
    r = pl.program_id(0)
    mp, dp = lax.axis_size("mp"), lax.axis_size("dp")
    copies_o = sum(group_a.copies(wa, held_o, sem_o, scal[0], mp, dp, [3]), [])
    copies_u = group_u.copies(wu, held_u, sem_u, scal[0], mp, dp, [0])
    copies_d = group_d.copies(wd, held_d, sem_d, scal[0], mp, dp, [0])
    copies = [one + two for one, two in zip(copies_d, copies_u)]
    rows, full = middle_ref.shape
    hidden = group_d.width
    size = column_tile(hidden)

    @pl.when(r == 0)
    def _():
        start_all(sum(copies, []) + copies_o)
        total[...] = jnp.zeros_like(total)

    wait_step(r, copies)

    def slopes(start):
        columns = pl.ds(start, size)
        grad = jnp.zeros((rows, size), F32)
        for block in range(full // hidden):
            grad = grad + dot_nt(
                grad_ref[:, block * hidden : (block + 1) * hidden],
                held_d[r, 0, pl.ds(block * hidden + start, size), :],
            )
        pre = (grad * slope_ref[:, columns].astype(F32)).astype(BF16)
        pre_ref[:, columns] = pre
        u_sum_ref[:, columns] = fold(pre.astype(F32))

    tiles(hidden, size, slopes)
    wide = column_tile(full)

    def add(start):
        columns = pl.ds(start, wide)
        total[:, columns] += dot_nt(pre_ref[...], held_u[r, 0, columns, :])

    tiles(full, wide, add)

    @pl.when(r == mp - 1)
    def _():
        sums_ref[...] = jnp.zeros_like(sums_ref)

        def norm_rows(start):
            place = pl.ds(start, row_tile(rows))

            def backward(upstream, inputs, gain):
                normal, factor = normalize(inputs)
                scaled = upstream * gain
                grad = (
                    scaled
                    - jnp.mean(scaled, axis=-1, keepdims=True)
                    - normal * jnp.mean(scaled * normal, axis=-1, keepdims=True)
                ) * factor
                return grad, fold(upstream * normal), fold(upstream)

            grad_mid, gain_sum, shift_sum = backward(
                total[place, :], middle_ref[place, :], rows_ref[0:1, :]
            )
            sums_ref[0:8, :] += gain_sum
            sums_ref[8:16, :] += shift_sum
            grad_middle = cot_ref[place, :].astype(F32) + grad_mid
            mid_ref[place, :] = grad_middle
            grad_branch, gain_sum, shift_sum = backward(
                grad_middle, branch_ref[place, :], rows_ref[1:2, :]
            )
            sums_ref[16:24, :] += gain_sum
            sums_ref[24:32, :] += shift_sum
            low = grad_branch.astype(BF16)
            low_ref[place, :] = low
            sums_ref[32:40, :] += fold(low.astype(F32))

        tiles(rows, row_tile(rows), norm_rows)
        wait_all(copies_o)
        width = group_a.width
        for layer in range(mp):
            grad = jnp.zeros((rows, width), F32)
            for block in range(full // width):
                columns = slice(block * width, (block + 1) * width)
                grad = grad + dot_nt(low_ref[:, columns], held_o[layer, 0, columns, :])
            att_ref[:, layer * width : (layer + 1) * width] = grad.astype(BF16)


def feed_back(grad, slope, branch, middle, cotangent, vectors, group_a, group_u, group_d, device):
    mp = lax.axis_size("mp")
    rows, full = middle.shape
    hidden = group_d.width
    step = pl.BlockSpec((rows, hidden), lambda i, *_: (0, i))
    return pl.pallas_call(
        functools.partial(back_kernel, group_a, group_u, group_d),
        grid_spec=pltpu.PrefetchScalarGridSpec(
            num_scalar_prefetch=1,
            grid=(mp,),
            in_specs=[whole((rows, full)), step]
            + [whole((rows, full))] * 3
            + [whole((8, full))]
            + group_a.specs()
            + group_u.specs()
            + group_d.specs(),
            out_specs=[step]
            + [whole((rows, full))] * 3
            + [whole((40, full)), pl.BlockSpec((8, hidden), lambda i, *_: (0, i))],
            scratch_shapes=group_a.scratch(mp, [3])
            + group_u.scratch(mp, [0])
            + group_d.scratch(mp, [0])
            + [pltpu.VMEM((rows, full), F32)],
        ),
        out_shape=[
            jax.ShapeDtypeStruct((rows, mp * hidden), BF16),
            jax.ShapeDtypeStruct((rows, full), F32),
            jax.ShapeDtypeStruct((rows, full), BF16),
            jax.ShapeDtypeStruct((rows, full), BF16),
            jax.ShapeDtypeStruct((40, full), F32),
            jax.ShapeDtypeStruct((8, mp * hidden), F32),
        ],
        name="feed_back",
        compiler_params=pltpu.CompilerParams(vmem_limit_bytes=58 << 20),
        cost_estimate=LIGHT,
    )(
        device.reshape(1),
        grad,
        slope,
        branch,
        middle,
        cotangent,
        vectors,
        *group_a.inputs,
        *group_u.inputs,
        *group_d.inputs,
    )


def unproject_kernel(group, begin, steps, scal, *refs):
    (dq_ref, dk_ref, dv_ref), refs = refs[:3], refs[3:]
    w_refs, refs = refs[: len(group.inputs)], refs[len(group.inputs) :]
    near_ref, far_ref, held, sems, total = refs
    step = pl.program_id(0)
    mp, dp = lax.axis_size("mp"), lax.axis_size("dp")
    copies = group.copies(w_refs, held, sems, scal[0], mp, dp, [0, 1, 2])
    copies = copies[begin : begin + steps]
    rows, full = near_ref.shape

    @pl.when(step == 0)
    def _():
        start_all(sum(copies, []))
        total[...] = jnp.zeros_like(total)

    wait_step(step, copies)
    r = begin + step
    size = column_tile(full)

    def add(start):
        columns = pl.ds(start, size)
        grad = dot_nt(dk_ref[...], held[r, 1, columns, :]) + dot_nt(
            dv_ref[...], held[r, 2, columns, :]
        )
        total[:, columns] += grad
        total[0:rows, columns] += dot_nt(dq_ref[...], held[r, 0, columns, :])

    tiles(full, size, add)

    @pl.when(step == pl.num_programs(0) - 1)
    def _():
        near_ref[...] = total[0:rows, :]
        far_ref[...] = total[rows:, :].astype(BF16)


def unproject(grads, group, begin, device):
    grad_q, grad_k, grad_v = grads
    mp = lax.axis_size("mp")
    rows, count = grad_q.shape
    span = grad_k.shape[0]
    full, width = group.full, group.width
    made = lambda height: pl.BlockSpec((height, width), lambda i, *_: (0, i))
    return pl.pallas_call(
        functools.partial(unproject_kernel, group, begin, count // width),
        grid_spec=pltpu.PrefetchScalarGridSpec(
            num_scalar_prefetch=1,
            grid=(count // width,),
            in_specs=[made(rows), made(span), made(span)] + group.specs(),
            out_specs=[whole((rows, full)), whole((span - rows, full))],
            scratch_shapes=group.scratch(mp, [0, 1, 2]) + [pltpu.VMEM((span, full), F32)],
        ),
        out_shape=[
            jax.ShapeDtypeStruct((rows, full), F32),
            jax.ShapeDtypeStruct((span - rows, full), BF16),
        ],
        name="unproject",
        compiler_params=pltpu.CompilerParams(vmem_limit_bytes=48 << 20),
        cost_estimate=LIGHT,
    )(device.reshape(1), grad_q, grad_k, grad_v, *group.inputs)


def other_half_kernel(scal, left_ref, right_ref, out_ref):
    out_ref[...] = dot_tn(left_ref[...], right_ref[...]).astype(BF16)


def split_rows(total, bit_at, bit, outs):
    send_ref, keep_ref = outs
    count, rows, _ = send_ref.shape
    for j in range(count):
        base = ((j >> bit_at) << (bit_at + 1)) | (j & ((1 << bit_at) - 1))
        for ref, value in ((send_ref, 1 - bit), (keep_ref, bit)):
            start = pl.multiple_of((base + (value << bit_at)) * rows, rows)
            ref[j] = total[pl.ds(start, rows), :].astype(BF16)


def this_half_kernel(bits_at, scal, left_ref, right_ref, got_ref, *refs):
    outs, total = refs[:-1], refs[-1]
    total[...] = dot_tn(left_ref[...], right_ref[...]) + got_ref[...].astype(F32)
    step = pl.program_id(0)
    count = pl.num_programs(0) // 2
    for side in range(2):

        @pl.when(step // count == side)
        def _():
            split_rows(
                total,
                bits_at[side],
                (scal[0] >> (bits_at[side] + 1)) & 1,
                outs[2 * side : 2 * side + 2],
            )


def first_bits():
    along_x, along_y = chip_masks(lax.axis_size("dp"))
    return [order[0].bit_length() - 2 for order in (along_x + along_y, along_y + along_x)]


def other_half(left, right, device):
    rows, full = left.shape
    size = right.shape[1] // lax.axis_size("mp")
    return pl.pallas_call(
        other_half_kernel,
        grid_spec=pltpu.PrefetchScalarGridSpec(
            num_scalar_prefetch=1,
            grid=(right.shape[1] // size,),
            in_specs=[
                pl.BlockSpec((rows, full // 2), lambda i, scal: (0, 1 - scal[0] % 2)),
                pl.BlockSpec((rows, size), lambda i, scal: (0, i)),
            ],
            out_specs=pl.BlockSpec((full // 2, size), lambda i, scal: (0, i)),
        ),
        out_shape=jax.ShapeDtypeStruct((full // 2, right.shape[1]), BF16),
        name="other_half",
        compiler_params=pltpu.CompilerParams(vmem_limit_bytes=32 << 20),
        cost_estimate=LIGHT,
    )(device.reshape(1), left, right)


def this_half(left, right, got, device):
    rows, full = left.shape
    mp = lax.axis_size("mp")
    size = right.shape[1] // mp
    quarters = lax.axis_size("dp") // 2
    shape = (quarters // 2, full // 2 // quarters, mp // 2 * size)
    block = (quarters // 2, full // 2 // quarters, size)
    last = mp // 2 - 1
    sides = [lambda i, scal: (0, 0, jnp.minimum(i, last))] * 2 + [
        lambda i, scal: (0, 0, jnp.maximum(i - last - 1, 0))
    ] * 2
    return pl.pallas_call(
        functools.partial(this_half_kernel, first_bits()),
        grid_spec=pltpu.PrefetchScalarGridSpec(
            num_scalar_prefetch=1,
            grid=(mp,),
            in_specs=[
                pl.BlockSpec((rows, full // 2), lambda i, scal: (0, scal[0] % 2)),
                pl.BlockSpec((rows, size), lambda i, scal: (0, i)),
                pl.BlockSpec((full // 2, size), lambda i, scal: (0, i)),
            ],
            out_specs=[pl.BlockSpec(block, index) for index in sides],
            scratch_shapes=[pltpu.VMEM((full // 2, size), F32)],
        ),
        out_shape=[jax.ShapeDtypeStruct(shape, BF16)] * 4,
        name="this_half",
        compiler_params=pltpu.CompilerParams(vmem_limit_bytes=40 << 20),
        cost_estimate=LIGHT,
    )(device.reshape(1), left, right, got)


def attention_dots(width, lefts, branch, grads, attended, layer, put):
    grad_q, grad_k, grad_v = grads
    rows = grad_q.shape[0]
    columns = slice(layer * width, (layer + 1) * width)
    put(0, dot_tn(lefts[0][...], grad_q[:, columns]))
    for index, grad in ((1, grad_k), (2, grad_v)):
        total = dot_tn(lefts[0][...], grad[0:rows, columns])
        for block in range(1, len(lefts)):
            total = total + dot_tn(
                lefts[block][...], grad[block * rows : (block + 1) * rows, columns]
            )
        put(index, total)
    put(3, dot_tn(branch[...], attended[:, columns]))


def attention_other_kernel(width, blocks, scal, *refs):
    lefts, (branch, *grads, attended, out_ref) = refs[:blocks], refs[blocks:]
    for layer in range(attended.shape[1] // width):

        def put(index, value):
            place = (layer * 4 + index) * width
            out_ref[:, place : place + width] = value.astype(BF16)

        attention_dots(width, lefts, branch, grads, attended, layer, put)


def attention_this_kernel(width, blocks, bits_at, scal, *refs):
    lefts, (branch, *grads, attended, got_ref) = refs[:blocks], refs[blocks : blocks + 6]
    outs, total = refs[blocks + 6 : -1], refs[-1]
    layers = attended.shape[1] // width
    for side in range(2):
        for local in range(layers // 2):
            layer = side * (layers // 2) + local

            def put(index, value):
                place = (layer * 4 + index) * width
                total[:, index * width : (index + 1) * width] = value + got_ref[
                    :, place : place + width
                ].astype(F32)

            attention_dots(width, lefts, branch, grads, attended, layer, put)
            columns = pl.ds(local * 4 * width, 4 * width)
            split_rows(
                total,
                bits_at[side],
                (scal[0] >> (bits_at[side] + 1)) & 1,
                [ref.at[:, :, columns] for ref in outs[2 * side : 2 * side + 2]],
            )


def attention_specs(normed, branch, grads, attended, core_of):
    rows, full = branch.shape
    left = pl.BlockSpec((rows, full // 2), lambda i, scal: (0, core_of(scal)))
    return [left] * (len(normed) + 1) + [whole(g.shape) for g in grads] + [whole(attended.shape)]


def attention_other(normed, branch, grads, attended, width, device):
    full = branch.shape[1]
    out = (full // 2, 4 * attended.shape[1])
    return pl.pallas_call(
        functools.partial(attention_other_kernel, width, len(normed)),
        grid_spec=pltpu.PrefetchScalarGridSpec(
            num_scalar_prefetch=1,
            grid=(1,),
            in_specs=attention_specs(normed, branch, grads, attended, lambda s: 1 - s[0] % 2),
            out_specs=whole(out),
        ),
        out_shape=jax.ShapeDtypeStruct(out, BF16),
        name="attention_other",
        compiler_params=pltpu.CompilerParams(vmem_limit_bytes=40 << 20),
        cost_estimate=LIGHT,
    )(device.reshape(1), *normed, branch, *grads, attended)


def attention_this(normed, branch, grads, attended, got, width, device):
    full = branch.shape[1]
    quarters = lax.axis_size("dp") // 2
    shape = (quarters // 2, full // 2 // quarters, 2 * attended.shape[1])
    return pl.pallas_call(
        functools.partial(attention_this_kernel, width, len(normed), first_bits()),
        grid_spec=pltpu.PrefetchScalarGridSpec(
            num_scalar_prefetch=1,
            grid=(1,),
            in_specs=attention_specs(normed, branch, grads, attended, lambda s: s[0] % 2)
            + [whole(got.shape)],
            out_specs=[whole(shape)] * 4,
            scratch_shapes=[pltpu.VMEM((full // 2, 4 * width), F32)],
        ),
        out_shape=[jax.ShapeDtypeStruct(shape, BF16)] * 4,
        name="attention_this",
        compiler_params=pltpu.CompilerParams(vmem_limit_bytes=48 << 20),
        cost_estimate=LIGHT,
    )(device.reshape(1), *normed, branch, *grads, attended, got)


def reduce_flow(send, add, layers, device):
    (send,) = yield (send,)
    (got,) = yield (swap(send, "dp", 1),)
    send_a, keep_a, send_b, keep_b = add(got)
    along_x, along_y = chip_masks(lax.axis_size("dp"))
    orders = (along_x + along_y, along_y + along_x)
    bits = len(orders[0])
    sends, keeps = [send_a, send_b], [keep_a, keep_b]
    lefts = []
    for side, order in enumerate(orders):
        left = list(range(bits - 1, -1, -1))
        left.remove(order[0].bit_length() - 2)
        lefts.append(left)
        keeps[side] = keeps[side].reshape((2,) * (bits - 1) + keeps[side].shape[1:])
    for step in range(bits):
        sends = yield tuple(sends)
        gots = yield tuple(swap(value, "dp", order[step]) for value, order in zip(sends, orders))
        gots = [got.reshape(keep.shape) for got, keep in zip(gots, keeps)]
        if step + 1 == bits:
            break
        sends, next_keeps = [], []
        for side, order in enumerate(orders):
            which = order[step + 1].bit_length() - 2
            axis = lefts[side].index(which)
            lefts[side].remove(which)
            bit = (device >> (which + 1)) & 1

            def part(value):
                summed = [
                    lax.dynamic_index_in_dim(item, value, axis, keepdims=False).astype(F32)
                    for item in (keeps[side], gots[side])
                ]
                return (summed[0] + summed[1]).astype(BF16)

            sends.append(part(1 - bit))
            next_keeps.append(part(bit))
        keeps = next_keeps
    each = len(layers) // 2
    size = keeps[0].shape[-1] // each
    pieces = []
    for side in range(2):
        for local in range(each):
            columns = slice(local * size, (local + 1) * size)
            pieces.append(
                keeps[side][..., columns].astype(F32) + gots[side][..., columns].astype(F32)
            )
    away = [(r, piece.astype(BF16)) for r, piece in zip(layers, pieces) if r]
    sent = yield tuple(piece for _, piece in away)
    found = yield tuple(swap(piece, "mp", r) for (r, _), piece in zip(away, sent))
    return [piece for r, piece in zip(layers, pieces) if r == 0] + [
        piece.astype(F32) for piece in found
    ]


def fill_kernel(plan, rows, dp, scal, *refs):
    ins, (qkv_ref, out_ref, turned) = refs[:-3], refs[-3:]
    width = turned.shape[1]
    for ref, (side, masks) in zip(ins, plan):
        for index, mask in enumerate(masks):
            place = pl.ds(pl.multiple_of(position(scal[0], mask, dp) * rows, rows), rows)
            for inner in range(2):
                value = ref[index, :, inner * width : (inner + 1) * width].astype(F32)
                if side * 2 + inner < 3:
                    qkv_ref[side * 2 + inner, place, :] = value
                else:
                    turned[place, :] = value
    out_ref[...] = turned[...].T


def fill_attention(arrays, full, width, device):
    dp = lax.axis_size("dp")
    inputs = [value for _, _, value in arrays]
    vmem = pl.BlockSpec(memory_space=pltpu.VMEM)
    return pl.pallas_call(
        functools.partial(fill_kernel, [(side, m) for side, m, _ in arrays], full // dp, dp),
        grid_spec=pltpu.PrefetchScalarGridSpec(
            num_scalar_prefetch=1,
            grid=(),
            in_specs=[vmem] * len(inputs),
            out_specs=[vmem, vmem],
            scratch_shapes=[pltpu.VMEM((full, width), F32)],
        ),
        out_shape=[
            jax.ShapeDtypeStruct((3, full, width), F32),
            jax.ShapeDtypeStruct((width, full), F32),
        ],
        name="fill_attention",
        compiler_params=pltpu.CompilerParams(vmem_limit_bytes=32 << 20),
        cost_estimate=LIGHT,
    )(device.reshape(1), *inputs)


def fill_ffn_kernel(turn, in_ref, out_ref):
    group, _, rows, hidden = in_ref.shape
    value = in_ref[...].astype(F32).reshape(group * rows, hidden)
    out_ref[...] = value.T if turn else value


def fill_ffn(gathered, turn):
    dp, rows, hidden = gathered.shape
    quarters = dp // 2
    group = quarters
    count = quarters // group
    full = dp * rows
    block = (hidden, group * rows) if turn else (group * rows, hidden)
    shape = (hidden, full) if turn else (full, hidden)
    where = (lambda c, j: (0, c * count + j)) if turn else (lambda c, j: (c * count + j, 0))
    return pl.pallas_call(
        functools.partial(fill_ffn_kernel, turn),
        grid=(2, count),
        in_specs=[pl.BlockSpec((group, 1, rows, hidden), lambda c, j: (j, c, 0, 0))],
        out_specs=pl.BlockSpec(block, where),
        out_shape=jax.ShapeDtypeStruct(shape, F32),
        name="fill_ffn",
        compiler_params=pltpu.CompilerParams(vmem_limit_bytes=24 << 20),
        cost_estimate=LIGHT,
    )(gathered.reshape(quarters, 2, rows, hidden))


def small_flow(value):
    for axis in ("dp", "mp"):
        for bit in range(lax.axis_size(axis).bit_length() - 1):
            (value,) = yield (value,)
            (got,) = yield (swap(value, axis, 1 << bit),)
            value = value + got
    return value


def spread_flow(sides):
    return (yield from spread_steps(sides))


def finish(flows, *values):
    while any(not flow.over for flow in flows):
        out = meet(flows, *values)
        values = out if len(values) > 1 else (out,)
    return values


def drain(*flows):
    for flow in flows:
        while not flow.over:
            flow.move(flow.held)


def eight_rows(*rows):
    stacked = jnp.stack([row.astype(F32) for row in rows])
    return jnp.pad(stacked, ((0, 8 - stacked.shape[0]), (0, 0)))


def on_device(
    tokens,
    groups,
    lengths,
    qkv_weight,
    qv_bias,
    out_weight,
    out_bias,
    up_weight,
    up_bias,
    down_weight,
    down_bias,
    norm_gain,
    norm_bias,
    group_table,
    cotangent,
):
    dp, mp = lax.axis_size("dp"), lax.axis_size("mp")
    device, layer = lax.axis_index("dp"), lax.axis_index("mp")
    core = device & 1
    rows, full = tokens.shape
    width = qkv_weight.shape[2]
    hidden = up_weight.shape[1]
    blocks = SEQ_LEN // rows
    place_in_seq = layer % blocks
    length = lax.dynamic_index_in_dim(lengths, layer // blocks, keepdims=False)
    along_x, along_y = chip_masks(dp)
    stages = len(along_x + along_y)
    gains = norm_gain.astype(F32)
    shifts = norm_bias.astype(F32)
    part, half = full // 2, full // 2

    shard_a = [(qkv_weight, 0, False), (out_weight, 3, True)]
    shard_u, shard_d = [(up_weight[None], 0, False)], [(down_weight, 0, True)]
    small_here = jnp.concatenate([qv_bias[0], qv_bias[1], up_bias]).reshape(-1, width)
    n_small = small_here.shape[0]
    small_here = jnp.pad(small_here, ((0, -n_small % 16), (0, 0)))
    slice_a = jnp.concatenate(
        [
            own_slice(qkv_weight, False, device, width),
            own_slice(out_weight, True, device, width),
        ]
    )
    flow_a = Flow(gather_flow(slice_a, small_here))
    tokens = begin([flow_a], tokens)

    order_of = layer ^ jnp.arange(mp)
    onehot = (
        groups[:, None] == lax.broadcasted_iota(jnp.int32, (1, group_table.shape[0]), 1)
    ).astype(BF16)
    residual = tokens.astype(F32) + jnp.dot(onehot, group_table, preferred_element_type=F32)
    normed, norm_one, inv_one = norm_forward(residual, gains[0], shifts[0])
    normed_low = normed.astype(BF16)

    def rows_flow(value):
        (value,) = yield (value,)
        return (yield tuple(swap(value, "mp", m) for m in range(1, blocks)))

    key_ids = lax.broadcasted_iota(jnp.int32, (blocks, rows, 1), 1)
    block_ids = place_in_seq ^ lax.broadcasted_iota(jnp.int32, (blocks, rows, 1), 0)
    shown = (block_ids <= place_in_seq) & (block_ids * rows + key_ids < length)
    spot = lax.broadcasted_iota(jnp.int32, (blocks, rows, LANES), 2) % HEAD_DIM
    key_const = jnp.where(
        spot == 0,
        jnp.where(shown, 0.0, MASKED_SCORE),
        jnp.where(spot <= 3, 1.0, 0.0),
    )
    key_const = key_const.astype(BF16).reshape(blocks * rows, LANES)

    slice_u = own_slice(up_weight[None], False, device, hidden)
    slice_d = own_slice(down_weight, True, device, hidden)
    flow_r = Flow(rows_flow(normed_low))
    slice_u, slice_d = begin([flow_r], slice_u, slice_d)
    normed_low, slice_u, slice_d = meet([flow_a], normed_low, slice_u, slice_d)
    flow_u, flow_d = Flow(gather_flow(slice_u)), Flow(gather_flow(slice_d))
    layer_stages = mp.bit_length() - 1
    for _ in range(layer_stages - 1):
        normed_low = meet([flow_a], normed_low)
    normed_low = begin([flow_u], normed_low)
    for _ in range(stages - 1):
        normed_low = meet([flow_a], normed_low)
    normed_low = meet([flow_a, flow_r, flow_u], normed_low)
    normed_low = meet([flow_a], normed_low)
    for _ in range(layer_stages - 1):
        normed_low = meet([flow_u], normed_low)
    normed_low = begin([flow_d], normed_low)
    arrays_a, small_all = flow_a.result
    group_a = Weights(shard_a, arrays_a)
    small_all = jnp.stack(small_all)[:, :n_small].reshape(mp, -1).astype(F32)
    qv_rows = small_all[:, : 2 * width].reshape(mp, 2, width).transpose(1, 0, 2).reshape(2, full)
    u_rows = small_all[:, 2 * width :].reshape(1, -1)
    qv_rows = jnp.pad(qv_rows, ((0, 6), (0, 0)))
    u_rows = jnp.pad(u_rows, ((0, 7), (0, 0)))
    seq_normed = (normed_low,) + tuple(flow_r.result)
    queries, keys, values = project(seq_normed, qv_rows, group_a, device)
    for _ in range(stages - 1):
        queries, keys, values = meet([flow_u, flow_d], queries, keys, values)
    attended_a, aug_a = attend(queries, keys, values, key_const, 0, part)
    attended_a, queries = meet([flow_d], attended_a, queries)
    for _ in range(layer_stages - 2):
        attended_a, queries = meet([flow_d], attended_a, queries)
    attended_b, aug_b = attend(queries, keys, values, key_const, part, part)
    attended_b = meet([flow_u], attended_b)
    for _ in range(stages - 1):
        attended_b = meet([flow_d], attended_b)
    (attended_b,) = finish([flow_u], attended_b)
    group_u = Weights(shard_u, flow_u.result[0])
    branch, middle, mid_low, act, slope = feed_up(
        attended_a,
        attended_b,
        residual,
        eight_rows(out_bias, gains[1], shifts[1], gains[2], shifts[2]),
        u_rows,
        group_a,
        group_u,
        device,
    )
    (act,) = finish([flow_d], act)
    group_d = Weights(shard_d, flow_d.result[0])
    output, grad_ffn, sums_ffn = feed_down(
        act, middle, cotangent, eight_rows(down_bias, gains[3], shifts[3]), group_d, device
    )

    everyone = list(range(mp))

    def weight_flow(left, right):
        return Flow(
            reduce_flow(
                other_half(left, right, device),
                lambda got: this_half(left, right, got, device),
                everyone,
                device,
            )
        )

    flow_d = weight_flow(grad_ffn, act)
    grad_ffn = begin([flow_d], grad_ffn)
    grad_ffn = meet([flow_d], grad_ffn)
    grad_pre, grad_middle, grad_branch, grad_attended, sums_back, sums_up = feed_back(
        grad_ffn,
        slope,
        branch,
        middle,
        cotangent,
        eight_rows(gains[2], gains[1]),
        group_a,
        group_u,
        group_d,
        device,
    )
    grad_pre, grad_branch, grad_attended = meet([flow_d], grad_pre, grad_branch, grad_attended)
    flow_u = weight_flow(mid_low, grad_pre)
    grad_branch, grad_attended = begin([flow_u], grad_branch, grad_attended)
    grad_branch, grad_attended = meet([flow_u], grad_branch, grad_attended)

    def attention_flow(grads, attended, layers):
        return Flow(
            reduce_flow(
                attention_other(seq_normed, grad_branch, grads, attended, width, device),
                lambda got: attention_this(
                    seq_normed, grad_branch, grads, attended, got, width, device
                ),
                layers,
                device,
            )
        )

    layers_b, layers_a = everyone[: mp // 2], everyone[mp // 2 :]
    grads_a = attend_back(queries, keys, values, key_const, aug_b, grad_attended, attended_b, part)
    grads_a = meet([flow_d], *grads_a)
    flow_qa = attention_flow(grads_a, attended_b, layers_a)
    grads_a = meet([flow_u], *grads_a)
    queries, *grads_a = begin([flow_qa], queries, *grads_a)
    near_a, far_a = unproject(grads_a, group_a, mp // 2, device)
    queries, near_a, far_a = meet([flow_qa], queries, near_a, far_a)
    queries, near_a, far_a = meet([flow_u], queries, near_a, far_a)
    grads_b = attend_back(queries, keys, values, key_const, aug_a, grad_attended, attended_a, 0)
    grads_b = meet([flow_d, flow_u, flow_qa], *grads_b)
    flow_qb = attention_flow(grads_b, attended_a, layers_b)
    grads_b = begin([flow_qb], *grads_b)
    near_b, far_b = unproject(grads_b, group_a, 0, device)
    flow_f = Flow(rows_back(far_a, far_b, rows, blocks))
    near_b = begin([flow_f], near_b)
    near_b = meet([flow_qb], near_b)
    near_b = meet([flow_f, flow_qa], near_b)
    grad_normed = near_a + near_b
    for value in flow_f.result:
        grad_normed = grad_normed + value.astype(F32)
    back_one, gain_one, shift_one = norm_backward(grad_normed, norm_one, inv_one, gains[0])
    input_grad = grad_middle + back_one
    table_part = jnp.dot(
        onehot.astype(F32).T, input_grad, precision=PRECISE, preferred_element_type=F32
    )
    grad_q_sum = jnp.concatenate([jnp.sum(g[0].astype(F32), axis=0) for g in (grads_b, grads_a)])
    grad_v_sum = jnp.concatenate([jnp.sum(g[2].astype(F32), axis=0) for g in (grads_b, grads_a)])
    ffn_sums = jnp.sum(sums_ffn.reshape(3, 8, full), axis=1)
    back_sums = jnp.sum(sums_back.reshape(5, 8, full), axis=1)
    up_bias_part = jnp.sum(sums_up, axis=0)
    by_layer = jnp.concatenate(
        [grad_q_sum.reshape(mp, -1), grad_v_sum.reshape(mp, -1), up_bias_part.reshape(mp, -1)],
        axis=1,
    )
    by_layer = jnp.take(by_layer, order_of, axis=0)
    wide = by_layer.shape[1]
    by_layer = jnp.pad(by_layer, ((0, 0), (0, -wide % full))).reshape(-1, full)
    parts = jnp.concatenate(
        [
            jnp.stack([gain_one, back_sums[2], back_sums[0], ffn_sums[0]]),
            jnp.stack([shift_one, back_sums[3], back_sums[1], ffn_sums[1]]),
            jnp.stack([back_sums[4], ffn_sums[2]]),
            table_part,
            by_layer,
        ]
    )
    flow_s = Flow(small_flow(parts))
    drain(flow_s, flow_u, flow_d, flow_qa, flow_qb)
    down_mine = sum(flow_d.result).astype(BF16)
    down_grad = fill_ffn(lax.all_gather(down_mine, "dp", axis=0), True)
    up_mine = sum(flow_u.result).astype(BF16)
    up_grad = fill_ffn(lax.all_gather(up_mine, "dp", axis=0), False)
    mine = sum(flow_qa.result + flow_qb.result).astype(BF16)
    flow_o = Flow(spread_flow((mine[:, : 2 * width], mine[:, 2 * width :])))
    drain(flow_o)
    qkv_grad, out_grad = fill_attention(flow_o.result, full, width, device)

    parts = flow_s.result
    gain_grad, shift_grad = parts[:4], parts[4:8]
    out_bias_grad, down_bias_grad = parts[8], parts[9]
    n_groups = group_table.shape[0]
    table_grad = parts[10 : 10 + n_groups]
    by_layer = parts[10 + n_groups :].reshape(mp, -1)
    mine = lax.dynamic_index_in_dim(by_layer, layer, keepdims=False)
    qv_bias_grad = mine[: 2 * width].reshape(2, width)
    up_bias_grad = mine[2 * width : 2 * width + hidden]
    return (
        output,
        input_grad,
        qkv_grad,
        qv_bias_grad,
        out_grad,
        out_bias_grad,
        up_grad,
        up_bias_grad,
        down_grad,
        down_bias_grad,
        gain_grad,
        shift_grad,
        table_grad,
    )


def rows_back(far_a, far_b, rows, blocks):
    value = (far_a.astype(F32) + far_b.astype(F32)).astype(BF16)
    (value,) = yield (value,)
    return (
        yield tuple(swap(value[(m - 1) * rows : m * rows], "mp", m) for m in range(1, blocks))
    )


def solution(mesh):
    placed = (
        P(("dp", "mp"), None),
        P(("dp", "mp")),
        P("dp"),
        P(None, None, "mp"),
        P(None, "mp"),
        P("mp", None),
        P(),
        P(None, "mp"),
        P("mp"),
        P("mp", None),
        P(),
        P(),
        P(),
        P(),
        P(("dp", "mp"), None),
    )
    return jax.shard_map(
        on_device,
        mesh=mesh,
        in_specs=placed,
        out_specs=(
            P(("dp", "mp"), None),
            P(("dp", "mp"), None),
            P(None, None, "mp"),
            P(None, "mp"),
            P("mp", None),
            P(),
            P(None, "mp"),
            P("mp"),
            P("mp", None),
            P(),
            P(),
            P(),
            P(),
        ),
        check_vma=False,
    )
```

time: 618 us -> 534 us (0.86)
  waiting for transfers between devices: 274 us -> 123 us
  Pallas kernels: 79.3 us -> 210 us
  matrix products: 116 us -> 2.2 us
  local copies, waits for them, and re-layouts: 27.5 us -> 45.9 us
  starting transfers between devices: 75 us -> 90.5 us
  between operations: 2.97 us -> 16.1 us
    ppermute x72 -> x77, waiting for transfers between devices: 274 us -> 123 us  [swap(): return lax.ppermute(value, axis, [(i, i ^ mask) for i in range(count)])]
    pallas_call x2 -> x17, Pallas kernels: 14.2 us -> 145 us  [the longest x1 25.6 us: feed_back(): pl.pallas_call(functools.partial(back_kernel, group_a, group_u, group_d),...]
    dot_general x24 -> x0, matrix products: 114 us -> none  [the longest x12 44.5 us: dot_tn(): lax.dot_general(a, b, (((0,), (0,)), ((), ())), preferred_element_type=F32)]
    convert_element_type x10 -> x19, other arithmetic: 6.71 us -> 22.8 us  [the longest x8 10.4 us: part(): return (summed[0] + summed[1]).astype(BF16)]
    ppermute x72 -> x77, starting transfers between devices: 75 us -> 90.4 us  [swap(): return lax.ppermute(value, axis, [(i, i ^ mask) for i in range(count)])]
    unnamed x143 -> x226, local copies, waits for them, and re-layouts: 12.4 us -> 25.8 us
    concatenate x12, other arithmetic: 9.81 us -> 2.82 us  [the longest x8 1.37 us: spread_steps(): held = [jnp.concatenate([one, two], axis=0) for one, two in zip(held, got)]]
    pallas_call x1 -> x2, Pallas kernels: 40.4 us -> 41 us  [attend_back(): pl.pallas_call(functools.partial(attend_back_kernel, span // rows, rows),...]
  transfers between devices with their start and end apart: 72 -> 79, of which waited for: 35 -> 27; matrix products, arithmetic and copies ran while one was open for 15% -> 9% of each run, Pallas kernels for 5% -> 32%
where the time goes in v2:
time: 534 us; the launch traced here: 529 us
  Pallas kernels  210 us (39%)
  waiting for transfers between devices  123 us (23%)
  starting transfers between devices  90.5 us (17%)
  local copies, waits for them, and re-layouts  45.9 us (9%)
  other arithmetic  40.1 us (8%)
  between operations  16.1 us (3%)
    ppermute x77, waiting for transfers between devices, swap(): return lax.ppermute(value, axis, [(i, i ^ mask) for i in range(count)])  123 us
    ppermute x77, starting transfers between devices, swap(): return lax.ppermute(value, axis, [(i, i ^ mask) for i in range(count)])  90.4 us
    pallas_call x2, Pallas kernels, attend_back(): pl.pallas_call(functools.partial(attend_back_kernel, span // rows, rows),...  41 us
    unnamed x226, local copies, waits for them, and re-layouts  25.8 us
    pallas_call x1, Pallas kernels, feed_back(): pl.pallas_call(functools.partial(back_kernel, group_a, group_u, group_d),...  25.6 us
    pallas_call x2, Pallas kernels, attend(): pl.pallas_call(functools.partial(attend_kernel, span // rows, rows), grid...  24.5 us
    pallas_call x1, Pallas kernels, feed_up(): pl.pallas_call(functools.partial(up_kernel, group_a, group_u), grid_spec=...  21.3 us
    pallas_call x1, Pallas kernels, feed_down(): pl.pallas_call(functools.partial(down_kernel, group_d), grid_spec=pltpu.P...  18.3 us
  transfers between devices with their start and end apart: 79, of which 27 were waited for; matrix products, arithmetic and copies ran while one was open for 9% of the time, Pallas kernels for 32%

profile of v2, /device:TPU:0, one launch (start us, length us, event | category | flops | bytes accessed | tf_op | source)
XLA Modules:
  0.0 528.6 jit_solution(3529045620835446827)
XLA Ops:
  11.4 4.0 collective-permute-start.1
  24.3 3.8 collective-permute-done.1
  31.7 4.2 collective-permute-done.2
  41.3 4.7 collective-permute-done.3
  49.3 4.6 collective-permute-start.9
  55.4 15.9 %collective-permute-done.9 = bf16[128,1024]{1,0:T(8,128)(2,1)} collective-permute-done((bf16[128,1024]{1,0:T(8,128)(2,1)}, bf16[128,1024]{1,0:T(8,128)(2,1)}, u32[]{:S(2)}, u32[]{:S(2)}) %collective-permute-start.9) | collective-permute-done | bytes 262176 | tf_op jit(solution)/shard_map/ppermute | solution.py:25
  71.3 3.5 collective-permute-done.8
  80.7 5.8 %collective-permute-done.14 = bf16[128,1024]{1,0:T(8,128)(2,1)} collective-permute-done((bf16[128,1024]{1,0:T(8,128)(2,1)}, bf16[128,1024]{1,0:T(8,128)(2,1)}, u32[]{:S(2)}, u32[]{:S(2)}) %collective-permute-start.14) | collective-permute-done | bytes 262176 | tf_op jit(solution)/shard_map/ppermute | solution.py:25
  90.0 4.4 collective-permute-start.18
  97.3 11.8 %project.1 = (bf16[544,1024]{1,0:T(8,128)(2,1)}, bf16[1088,1024]{1,0:T(8,128)(2,1)}, bf16[1088,1024]{1,0:T(8,128)(2,1)}) custom-call(s32[1]{0:T(128)} %bitcast.scal, bf16[544,1024]{1,0:T(8,128)(2,1)} %copy-done.2, bf16[544,1024]{1,0:T(8,128)(2,1)} %collective-permute-done.7.refs_1_, f32[8,1024]{1,0:T(8,128)S(1)} %pad.28.refs_2_, ...), custom_call_target="tpu_custom_call" | custom-call | flops 1000 | bytes 1000 | tf_op jit(solution)/shard_map/project/pallas_call | solution.py:468
  115.7 12.2 %attend.2 = (bf16[544,512]{1,0:T(8,128)(2,1)S(1)}, bf16[544,512]{1,0:T(8,128)(2,1)S(1)}) custom-call(bf16[544,1024]{1,0:T(8,128)(2,1)S(1)} %copy-done.23, bf16[1088,1024]{1,0:T(8,128)(2,1)S(1)} %copy-done.5, bf16[1088,1024]{1,0:T(8,128)(2,1)S(1)} %copy-done.6, bf16[1088,128]{1,0:T(8,128)(2,1)S(1)} %select_convert_fusion.kc_ref), custom_call_target="tpu_custom_call" | custom-call | flops 1000 | bytes 1000 | tf_op jit(solution)/shard_map/attend/pallas_call | solution.py:129
  128.9 12.2 %attend.3 = (bf16[544,512]{1,0:T(8,128)(2,1)S(1)}, bf16[544,512]{1,0:T(8,128)(2,1)S(1)}) custom-call(bf16[544,1024]{1,0:T(8,128)(2,1)S(1)} %copy-done.23, bf16[1088,1024]{1,0:T(8,128)(2,1)S(1)} %copy-done.5, bf16[1088,1024]{1,0:T(8,128)(2,1)S(1)} %copy-done.6, bf16[1088,128]{1,0:T(8,128)(2,1)S(1)} %select_convert_fusion.kc_ref), custom_call_target="tpu_custom_call" | custom-call | flops 1000 | bytes 1000 | tf_op jit(solution)/shard_map/attend/pallas_call | solution.py:129
  143.2 10.4 %collective-permute-done.22 = bf16[1,3,1,64,1024]{4,3,1,2,0:T(8,128)(2,1)S(1)} collective-permute-done((bf16[1,3,1,64,1024]{4,3,1,2,0:T(8,128)(2,1)S(1)}, bf16[1,3,1,64,1024]{4,3,1,2,0:T(8,128)(2,1)S(1)}, u32[]{:S(2)}, u32[]{:S(2)}) %collective-permute-start.22) | collective-permute-done | bytes 393248 | tf_op jit(solution)/shard_map/ppermute | solution.py:25
  161.1 21.3 %feed_up.1 = (f32[544,1024]{1,0:T(8,128)}, f32[544,1024]{1,0:T(8,128)}, bf16[544,1024]{1,0:T(8,128)(2,1)}, bf16[544,4096]{1,0:T(8,128)(2,1)}, bf16[544,4096]{1,0:T(8,128)(2,1)}) custom-call(s32[1]{0:T(128)} %bitcast.scal, bf16[544,512]{1,0:T(8,128)(2,1)} %copy-done.38, bf16[544,512]{1,0:T(8,128)(2,1)} %copy-done.42, f32[544,1024]{1,0:T(8,128)} %copy-done.63, ...), custom_call_target="tpu_custom_call" | custom-call | flops 1000 | bytes 1000 | tf_op jit(solution)/shard_map/feed_up/pallas_call | solution.py:552
  189.2 18.3 %feed_down.1 = (bf16[544,1024]{1,0:T(8,128)(2,1)}, bf16[544,1024]{1,0:T(8,128)(2,1)}, f32[24,1024]{1,0:T(8,128)S(1)}) custom-call(s32[1]{0:T(128)} %bitcast.scal, bf16[544,4096]{1,0:T(8,128)(2,1)} %get-tuple-element.376.refs_0_.right_ref, f32[544,1024]{1,0:T(8,128)} %get-tuple-element.377.refs_1_.refs_3_, bf16[544,1024]{1,0:T(8,128)(2,1)} %refs_4_.7, ...), custom_call_target="tpu_custom_call" | custom-call | flops 1000 | bytes 1000 | tf_op jit(solution)/shard_map/feed_down/pallas_call | solution.py:642
  209.4 4.7 other_half.2
  214.3 7.0 %collective-permute-done.34.got_ref = bf16[512,4096]{1,0:T(8,128)(2,1)S(1)} collective-permute-done((bf16[512,4096]{1,0:T(8,128)(2,1)S(1)}, bf16[512,4096]{1,0:T(8,128)(2,1)S(1)}, u32[]{:S(2)}, u32[]{:S(2)}) %collective-permute-start.34) | collective-permute-done | bytes 4194336 | tf_op jit(solution)/shard_map/ppermute | solution.py:25
  221.3 6.3 %this_half.2 = (bf16[2,128,2048]{2,1,0:T(8,128)(2,1)}, bf16[2,128,2048]{2,1,0:T(8,128)(2,1)S(1)}, bf16[2,128,2048]{2,1,0:T(8,128)(2,1)}, bf16[2,128,2048]{2,1,0:T(8,128)(2,1)S(1)}) custom-call(s32[1]{0:T(128)} %bitcast.scal, bf16[544,1024]{1,0:T(8,128)(2,1)S(1)} %copy-done.29, bf16[544,4096]{1,0:T(8,128)(2,1)S(1)} %copy-done.4, ...), custom_call_target="tpu_custom_call" | custom-call | flops 1000 | bytes 1000 | tf_op jit(solution)/shard_map/this_half/pallas_call | solution.py:931
  230.7 25.6 %feed_back.1 = (bf16[544,4096]{1,0:T(8,128)(2,1)}, f32[544,1024]{1,0:T(8,128)}, bf16[544,1024]{1,0:T(8,128)(2,1)}, bf16[544,1024]{1,0:T(8,128)(2,1)}, f32[40,1024]{1,0:T(8,128)}, /*index=5*/f32[8,4096]{1,0:T(8,128)}) custom-call(s32[1]{0:T(128)} %bitcast.scal, bf16[544,1024]{1,0:T(8,128)(2,1)} %get-tuple-element.390.left_ref.refs_0_, ...), custom_call_target="tpu_custom_call" | custom-call | flops 1000 | bytes 1000 | tf_op jit(solution)/shard_map/feed_back/pallas_call | solution.py:758
  258.1 2.6 fusion.4
  260.7 4.7 other_half.3
  265.4 7.1 %collective-permute-done.37.got_ref = bf16[512,4096]{1,0:T(8,128)(2,1)S(1)} collective-permute-done((bf16[512,4096]{1,0:T(8,128)(2,1)S(1)}, bf16[512,4096]{1,0:T(8,128)(2,1)S(1)}, u32[]{:S(2)}, u32[]{:S(2)}) %collective-permute-start.37) | collective-permute-done | bytes 4194336 | tf_op jit(solution)/shard_map/ppermute | solution.py:25
  272.6 5.6 %this_half.3 = (bf16[2,128,2048]{2,1,0:T(8,128)(2,1)S(1)}, bf16[2,128,2048]{2,1,0:T(8,128)(2,1)S(1)}, bf16[2,128,2048]{2,1,0:T(8,128)(2,1)S(1)}, bf16[2,128,2048]{2,1,0:T(8,128)(2,1)S(1)}) custom-call(s32[1]{0:T(128)} %bitcast.scal, bf16[544,1024]{1,0:T(8,128)(2,1)S(1)} %copy-done.48, bf16[544,4096]{1,0:T(8,128)(2,1)S(1)} %copy-done.18, ...), custom_call_target="tpu_custom_call" | custom-call | flops 1000 | bytes 1000 | tf_op jit(solution)/shard_map/this_half/pallas_call | solution.py:931
  282.3 20.7 %attend_back.2 = (bf16[544,512]{1,0:T(8,128)(2,1)S(1)}, bf16[1088,512]{1,0:T(8,128)(2,1)S(1)}, bf16[1088,512]{1,0:T(8,128)(2,1)S(1)}) custom-call(bf16[544,1024]{1,0:T(8,128)(2,1)S(1)} %copy-done.23, bf16[1088,1024]{1,0:T(8,128)(2,1)} %get-tuple-element.333.k_ref, bf16[1088,1024]{1,0:T(8,128)(2,1)} %get-tuple-element.334.v_ref, ...), custom_call_target="tpu_custom_call" | custom-call | flops 1000 | bytes 1000 | tf_op jit(solution)/shard_map/attend_back/pallas_call | solution.py:213
  303.0 12.9 %collective-permute-done.38 = bf16[128,2048]{1,0:T(8,128)(2,1)S(1)} collective-permute-done((bf16[128,2048]{1,0:T(8,128)(2,1)S(1)}, bf16[128,2048]{1,0:T(8,128)(2,1)S(1)}, u32[]{:S(2)}, u32[]{:S(2)}) %collective-permute-start.38) | collective-permute-done | bytes 524320 | tf_op jit(solution)/shard_map/ppermute | solution.py:25
  317.7 3.8 attention_other.2
  325.9 8.8 %unproject.2 = (f32[544,1024]{1,0:T(8,128)}, bf16[544,1024]{1,0:T(8,128)(2,1)}) custom-call(s32[1]{0:T(128)} %bitcast.scal, bf16[544,512]{1,0:T(8,128)(2,1)S(1)} %get-tuple-element.447.refs_3_.refs_0_, bf16[1088,512]{1,0:T(8,128)(2,1)} %copy-done.32, bf16[1088,512]{1,0:T(8,128)(2,1)} %copy-done.19, bf16[3,1024,256]{2,1,0:T(8,128)(2,1)} %refs_3_.5, ...), custom_call_target="tpu_custom_call" | custom-call | flops 1000 | bytes 1000 | tf_op jit(solution)/shard_map/unproject/pallas_call | solution.py:844
  334.7 3.0 collective-permute-start.47
  337.7 6.3 %attention_this.2 = (bf16[2,128,1024]{2,1,0:T(8,128)(2,1)S(1)}, bf16[2,128,1024]{2,1,0:T(8,128)(2,1)S(1)}, bf16[2,128,1024]{2,1,0:T(8,128)(2,1)S(1)}, bf16[2,128,1024]{2,1,0:T(8,128)(2,1)S(1)}) custom-call(s32[1]{0:T(128)} %bitcast.scal, bf16[544,1024]{1,0:T(8,128)(2,1)S(1)} %copy-done.3, bf16[544,1024]{1,0:T(8,128)(2,1)} %collective-permute-done.7.refs_1_, ...), custom_call_target="tpu_custom_call" | custom-call | flops 1000 | bytes 1000 | tf_op jit(solution)/shard_map/attention_this/pallas_call | solution.py:1029
  349.4 2.6 collective-permute-start.50
  352.0 20.3 %attend_back.3 = (bf16[544,512]{1,0:T(8,128)(2,1)S(1)}, bf16[1088,512]{1,0:T(8,128)(2,1)S(1)}, bf16[1088,512]{1,0:T(8,128)(2,1)S(1)}) custom-call(bf16[544,1024]{1,0:T(8,128)(2,1)S(1)} %copy-done.24, bf16[1088,1024]{1,0:T(8,128)(2,1)} %get-tuple-element.333.k_ref, bf16[1088,1024]{1,0:T(8,128)(2,1)} %get-tuple-element.334.v_ref, ...), custom_call_target="tpu_custom_call" | custom-call | flops 1000 | bytes 1000 | tf_op jit(solution)/shard_map/attend_back/pallas_call | solution.py:213
  389.2 5.2 attention_other.3
  401.4 8.9 %unproject.3 = (f32[544,1024]{1,0:T(8,128)}, bf16[544,1024]{1,0:T(8,128)(2,1)}) custom-call(s32[1]{0:T(128)} %bitcast.scal, bf16[544,512]{1,0:T(8,128)(2,1)S(1)} %copy-done.36, bf16[1088,512]{1,0:T(8,128)(2,1)} %copy-done.30, bf16[1088,512]{1,0:T(8,128)(2,1)} %copy-done.20, bf16[3,1024,256]{2,1,0:T(8,128)(2,1)} %refs_3_.5, bf16[256,1024]{1,0:T(8,128)(2,1)S(1)} %copy-done.27, ...), custom_call_target="tpu_custom_call" | custom-call | flops 1000 | bytes 1000 | tf_op jit(solution)/shard_map/unproject/pallas_call | solution.py:844
  410.3 2.8 add_convert_fusion
  413.0 2.6 collective-permute-start.54
  415.7 2.6 collective-permute-start.55
  424.0 6.4 %attention_this.3 = (bf16[2,128,1024]{2,1,0:T(8,128)(2,1)}, bf16[2,128,1024]{2,1,0:T(8,128)(2,1)S(1)}, bf16[2,128,1024]{2,1,0:T(8,128)(2,1)S(1)}, bf16[2,128,1024]{2,1,0:T(8,128)(2,1)S(1)}) custom-call(s32[1]{0:T(128)} %bitcast.scal, bf16[544,1024]{1,0:T(8,128)(2,1)S(1)} %copy-done.3, bf16[544,1024]{1,0:T(8,128)(2,1)} %collective-permute-done.7.refs_1_, ...), custom_call_target="tpu_custom_call" | custom-call | flops 1000 | bytes 1000 | tf_op jit(solution)/shard_map/attention_this/pallas_call | solution.py:1029
  430.5 10.5 %collective-permute-done.54 = bf16[544,1024]{1,0:T(8,128)(2,1)} collective-permute-done((bf16[544,1024]{1,0:T(8,128)(2,1)}, bf16[544,1024]{1,0:T(8,128)(2,1)}, u32[]{:S(2)}, u32[]{:S(2)}) %collective-permute-start.54) | collective-permute-done | bytes 1114144 | tf_op jit(solution)/shard_map/ppermute | solution.py:25
  443.2 2.6 collective-permute-start.61
  445.9 3.2 multiply_reduce_fusion
  449.1 2.6 collective-permute-start.59
  452.5 7.2 %collective-permute-done.61 = bf16[2,128,1024]{2,1,0:T(8,128)(2,1)S(1)} collective-permute-done((bf16[2,128,1024]{2,1,0:T(8,128)(2,1)S(1)}, bf16[2,128,1024]{2,1,0:T(8,128)(2,1)S(1)}, u32[]{:S(2)}, u32[]{:S(2)}) %collective-permute-start.61) | collective-permute-done | bytes 524320 | tf_op jit(solution)/shard_map/ppermute | solution.py:25
  474.1 3.6 collective-permute-done.73
  478.2 6.6 %collective-permute-done.57 = bf16[128,1024]{1,0:T(8,128)(2,1)S(1)} collective-permute-done((bf16[128,1024]{1,0:T(8,128)(2,1)S(1)}, bf16[128,1024]{1,0:T(8,128)(2,1)S(1)}, u32[]{:S(2)}, u32[]{:S(2)}) %collective-permute-start.57) | collective-permute-done | bytes 262176 | tf_op jit(solution)/shard_map/ppermute | solution.py:25
  484.8 3.7 collective-permute-done.63
  496.3 3.9 collective-permute-start.76
  500.1 6.5 %collective-permute-done.76 = f32[34,1024]{1,0:T(8,128)S(1)} collective-permute-done((f32[34,1024]{1,0:T(8,128)S(1)}, f32[34,1024]{1,0:T(8,128)S(1)}, u32[]{:S(2)}, u32[]{:S(2)}) %collective-permute-start.76) | collective-permute-done | bytes 139296 | tf_op jit(solution)/shard_map/ppermute | solution.py:25
  512.5 2.6 fill_ffn.3
  (473 shorter events, 152.0 us)
Async XLA Ops:
  7.2 503.7 %all-gather.7.cloned.1.call-start = ((), (), s32[]{:S(2)}) async-start(), calls=%async_computation.1 | async-start | bytes 2359296 | tf_op jit(solution)/shard_map/all_gather | solution.py:1413
  11.4 16.7 %collective-permute-start.1 = (bf16[528,256]{1,0:T(8,128)(2,1)}, bf16[528,256]{1,0:T(8,128)(2,1)}, u32[]{:S(2)}, u32[]{:S(2)}) collective-permute-start(bf16[528,256]{1,0:T(8,128)(2,1)} %fusion.16), channel_id=1, source_target_pairs={{0,2},{1,3},{2,0},{3,1},{4,6},{5,7},{6,4},{7,5},{8,10},{9,11},{10,... | collective-permute-start | bytes 811016 | tf_op jit(solution)/shard_map/ppermute | solution.py:25
  15.4 12.9 %collective-permute-start = (bf16[528,256]{1,0:T(8,128)(2,1)}, bf16[528,256]{1,0:T(8,128)(2,1)}, u32[]{:S(2)}, u32[]{:S(2)}) collective-permute-start(bf16[528,256]{1,0:T(8,128)(2,1)} %fusion.16), channel_id=1, source_target_pairs={{0,1},{1,0},{2,3},{3,2},{4,5},{5,4},{6,7},{7,6},{8,9},{9,8},{10,11... | collective-permute-start | bytes 811016 | tf_op jit(solution)/shard_map/ppermute | solution.py:25
  39.6 35.2 %collective-permute-start.7 = (bf16[544,1024]{1,0:T(8,128)(2,1)S(1)}, bf16[544,1024]{1,0:T(8,128)(2,1)}, u32[]{:S(2)}, u32[]{:S(2)}) collective-permute-start(bf16[544,1024]{1,0:T(8,128)(2,1)S(1)} %add_convert_fusion.1.refs_0_), channel_id=1, source_target_pairs={{0,1},{1,0},{2,3},{3,2},{4,5},{5,4},{6,7},{7,6},{8,9},{9,8},{10,11... | collective-permute-start | bytes 3342344 | tf_op jit(solution)/shard_map/ppermute | solution.py:25
  47.3 27.5 %collective-permute-start.5 = (bf16[2,3,4,64,256]{4,3,2,1,0:T(8,128)(2,1)S(1)}, bf16[2,3,4,64,256]{4,3,2,1,0:T(8,128)(2,1)S(1)}, u32[]{:S(2)}, u32[]{:S(2)}) collective-permute-start(bf16[2,3,4,64,256]{4,3,2,1,0:T(8,128)(2,1)S(1)} %pad_maximum_fusion.1.refs_5_.refs_7_.refs_8_), channel_id=1, source_target_pairs={{0,16},{4,20},{8,24},{12,28},{16,0},{20,4},{24,8},{28,12},{1,17},{... | collective-permute-start | bytes 2359304 | tf_op jit(solution)/shard_map/ppermute | solution.py:25
  48.8 26.1 %collective-permute-start.6 = (bf16[2,3,4,64,256]{4,3,2,1,0:T(8,128)(2,1)S(1)}, bf16[2,3,4,64,256]{4,3,2,1,0:T(8,128)(2,1)}, u32[]{:S(2)}, u32[]{:S(2)}) collective-permute-start(bf16[2,3,4,64,256]{4,3,2,1,0:T(8,128)(2,1)S(1)} %pad_maximum_fusion.2.refs_7_.refs_9_.refs_10_), channel_id=1, source_target_pairs={{0,8},{4,12},{8,0},{12,4},{16,24},{20,28},{24,16},{28,20},{1,9},{5... | collective-permute-start | bytes 2359304 | tf_op jit(solution)/shard_map/ppermute | solution.py:25
  49.3 22.0 %collective-permute-start.9 = (bf16[128,1024]{1,0:T(8,128)(2,1)}, bf16[128,1024]{1,0:T(8,128)(2,1)}, u32[]{:S(2)}, u32[]{:S(2)}) collective-permute-start(bf16[128,1024]{1,0:T(8,128)(2,1)} %bitcast.12), channel_id=1, source_target_pairs={{0,2},{1,3},{2,0},{3,1},{4,6},{5,7},{6,4},{7,5},{8,10},{9,11},{10,... | collective-permute-start | bytes 786440 | tf_op jit(solution)/shard_map/ppermute | solution.py:25
  53.9 20.9 %collective-permute-start.8 = (bf16[128,1024]{1,0:T(8,128)(2,1)}, bf16[128,1024]{1,0:T(8,128)(2,1)}, u32[]{:S(2)}, u32[]{:S(2)}) collective-permute-start(bf16[128,1024]{1,0:T(8,128)(2,1)} %bitcast.12), channel_id=1, source_target_pairs={{0,1},{1,0},{2,3},{3,2},{4,5},{5,4},{6,7},{7,6},{8,9},{9,8},{10,11... | collective-permute-start | bytes 786440 | tf_op jit(solution)/shard_map/ppermute | solution.py:25
  87.8 21.3 %collective-permute-start.15 = (bf16[1,3,1,64,1024]{4,3,1,2,0:T(8,128)(2,1)S(1)}, bf16[1,3,1,64,1024]{4,3,1,2,0:T(8,128)(2,1)S(1)}, u32[]{:S(2)}, u32[]{:S(2)}) collective-permute-start(bf16[1,3,1,64,1024]{4,3,1,2,0:T(8,128)(2,1)S(1)} %get-tuple-element.323), channel_id=1, source_target_pairs={{0,8},{4,12},{8,0},{12,4},{16,24},{20,28},{24,16},{28,20},{1,9},{5... | collective-permute-start | bytes 1179656 | tf_op jit(solution)/shard_map/ppermute | solution.py:25
  88.4 20.7 %collective-permute-start.16 = (bf16[1,3,1,64,1024]{4,3,2,1,0:T(8,128)(2,1)S(1)}, bf16[1,3,1,64,1024]{4,3,2,1,0:T(8,128)(2,1)S(1)}, u32[]{:S(2)}, u32[]{:S(2)}) collective-permute-start(bf16[1,3,1,64,1024]{4,3,2,1,0:T(8,128)(2,1)S(1)} %get-tuple-element.324), channel_id=1, source_target_pairs={{0,16},{4,20},{8,24},{12,28},{16,0},{20,4},{24,8},{28,12},{1,17},{... | collective-permute-start | bytes 1179656 | tf_op jit(solution)/shard_map/ppermute | solution.py:25
  90.0 19.1 %collective-permute-start.18 = (bf16[128,1024]{1,0:T(8,128)(2,1)S(1)}, bf16[128,1024]{1,0:T(8,128)(2,1)S(1)}, u32[]{:S(2)}, u32[]{:S(2)}) collective-permute-start(bf16[128,1024]{1,0:T(8,128)(2,1)S(1)} %bitcast.162), channel_id=1, source_target_pairs={{0,2},{1,3},{2,0},{3,1},{4,6},{5,7},{6,4},{7,5},{8,10},{9,11},{10,... | collective-permute-start | bytes 786440 | tf_op jit(solution)/shard_map/ppermute | solution.py:25
  94.5 14.7 %collective-permute-start.17 = (bf16[128,1024]{1,0:T(8,128)(2,1)S(1)}, bf16[128,1024]{1,0:T(8,128)(2,1)S(1)}, u32[]{:S(2)}, u32[]{:S(2)}) collective-permute-start(bf16[128,1024]{1,0:T(8,128)(2,1)S(1)} %bitcast.163), channel_id=1, source_target_pairs={{0,1},{1,0},{2,3},{3,2},{4,5},{5,4},{6,7},{7,6},{8,9},{9,8},{10,11... | collective-permute-start | bytes 786440 | tf_op jit(solution)/shard_map/ppermute | solution.py:25
  110.2 18.5 %collective-permute-start.19 = (bf16[128,1024]{1,0:T(8,128)(2,1)S(1)}, bf16[128,1024]{1,0:T(8,128)(2,1)S(1)}, u32[]{:S(2)}, u32[]{:S(2)}) collective-permute-start(bf16[128,1024]{1,0:T(8,128)(2,1)S(1)} %collective-permute-done.18), channel_id=1, source_target_pairs={{0,1},{1,0},{2,3},{3,2},{4,5},{5,4},{6,7},{7,6},{8,9},{9,8},{10,11... | collective-permute-start | bytes 786440 | tf_op jit(solution)/shard_map/ppermute | solution.py:25
  110.8 31.2 %collective-permute-start.20 = (bf16[2,3,1,64,1024]{4,3,1,2,0:T(8,128)(2,1)S(1)}, bf16[2,3,1,64,1024]{4,3,1,2,0:T(8,128)(2,1)}, u32[]{:S(2)}, u32[]{:S(2)}) collective-permute-start(bf16[2,3,1,64,1024]{4,3,1,2,0:T(8,128)(2,1)S(1)} %pad_maximum_fusion.4), channel_id=1, source_target_pairs={{0,16},{4,20},{8,24},{12,28},{16,0},{20,4},{24,8},{28,12},{1,17},{... | collective-permute-start | bytes 2359304 | tf_op jit(solution)/shard_map/ppermute | solution.py:25
  112.3 29.7 %collective-permute-start.21 = (bf16[2,3,1,64,1024]{4,3,2,1,0:T(8,128)(2,1)}, bf16[2,3,1,64,1024]{4,3,2,1,0:T(8,128)(2,1)}, u32[]{:S(2)}, u32[]{:S(2)}) collective-permute-start(bf16[2,3,1,64,1024]{4,3,2,1,0:T(8,128)(2,1)} %pad_maximum_fusion.5.refs_18_.refs_19_), channel_id=1, source_target_pairs={{0,8},{4,12},{8,0},{12,4},{16,24},{20,28},{24,16},{28,20},{1,9},{5... | collective-permute-start | bytes 2359304 | tf_op jit(solution)/shard_map/ppermute | solution.py:25
  142.0 13.1 %collective-permute-start.24 = (bf16[2,3,1,64,1024]{4,3,1,2,0:T(8,128)(2,1)S(1)}, bf16[2,3,1,64,1024]{4,3,1,2,0:T(8,128)(2,1)S(1)}, u32[]{:S(2)}, u32[]{:S(2)}) collective-permute-start(bf16[2,3,1,64,1024]{4,3,1,2,0:T(8,128)(2,1)S(1)} %pad_maximum_fusion.4), channel_id=1, source_target_pairs={{0,4},{4,0},{8,12},{12,8},{16,20},{20,16},{24,28},{28,24},{1,5},{5... | collective-permute-start | bytes 2359304 | tf_op jit(solution)/shard_map/ppermute | solution.py:25
  154.6 27.7 %collective-permute-start.28 = (bf16[2,3,1,64,1024]{4,3,1,2,0:T(8,128)(2,1)S(1)}, bf16[2,3,1,64,1024]{4,3,1,2,0:T(8,128)(2,1)}, u32[]{:S(2)}, u32[]{:S(2)}) collective-permute-start(bf16[2,3,1,64,1024]{4,3,1,2,0:T(8,128)(2,1)S(1)} %pad_maximum_fusion.7), channel_id=1, source_target_pairs={{0,16},{4,20},{8,24},{12,28},{16,0},{20,4},{24,8},{28,12},{1,17},{... | collective-permute-start | bytes 2359304 | tf_op jit(solution)/shard_map/ppermute | solution.py:25
  156.1 26.3 %collective-permute-start.29 = (bf16[2,3,1,64,1024]{4,3,2,1,0:T(8,128)(2,1)S(1)}, bf16[2,3,1,64,1024]{4,3,2,1,0:T(8,128)(2,1)}, u32[]{:S(2)}, u32[]{:S(2)}) collective-permute-start(bf16[2,3,1,64,1024]{4,3,2,1,0:T(8,128)(2,1)S(1)} %pad_maximum_fusion.8.refs_7_.refs_28_), channel_id=1, source_target_pairs={{0,8},{4,12},{8,0},{12,4},{16,24},{20,28},{24,16},{28,20},{1,9},{5... | collective-permute-start | bytes 2359304 | tf_op jit(solution)/shard_map/ppermute | solution.py:25
  228.6 27.6 %collective-permute-start.35 = (bf16[2,128,2048]{2,1,0:T(8,128)(2,1)}, bf16[2,128,2048]{2,1,0:T(8,128)(2,1)}, u32[]{:S(2)}, u32[]{:S(2)}) collective-permute-start(bf16[2,128,2048]{2,1,0:T(8,128)(2,1)} %get-tuple-element.398), channel_id=1, source_target_pairs={{0,8},{4,12},{8,0},{12,4},{16,24},{20,28},{24,16},{28,20},{1,9},{5... | collective-permute-start | bytes 3145736 | tf_op jit(solution)/shard_map/ppermute | solution.py:25
  229.2 27.1 %collective-permute-start.36 = (bf16[2,128,2048]{2,1,0:T(8,128)(2,1)}, bf16[2,128,2048]{2,1,0:T(8,128)(2,1)}, u32[]{:S(2)}, u32[]{:S(2)}) collective-permute-start(bf16[2,128,2048]{2,1,0:T(8,128)(2,1)} %get-tuple-element.399), channel_id=1, source_target_pairs={{0,16},{4,20},{8,24},{12,28},{16,0},{20,4},{24,8},{28,12},{1,17},{... | collective-permute-start | bytes 3145736 | tf_op jit(solution)/shard_map/ppermute | solution.py:25
  278.1 43.4 %collective-permute-start.40 = (bf16[2,128,2048]{2,1,0:T(8,128)(2,1)S(1)}, bf16[2,128,2048]{2,1,0:T(8,128)(2,1)S(1)}, u32[]{:S(2)}, u32[]{:S(2)}) collective-permute-start(bf16[2,128,2048]{2,1,0:T(8,128)(2,1)S(1)} %get-tuple-element.433), channel_id=1, source_target_pairs={{0,8},{4,12},{8,0},{12,4},{16,24},{20,28},{24,16},{28,20},{1,9},{5... | collective-permute-start | bytes 3145736 | tf_op jit(solution)/shard_map/ppermute | solution.py:25
  279.7 41.9 %collective-permute-start.41 = (bf16[2,128,2048]{2,1,0:T(8,128)(2,1)S(1)}, bf16[2,128,2048]{2,1,0:T(8,128)(2,1)S(1)}, u32[]{:S(2)}, u32[]{:S(2)}) collective-permute-start(bf16[2,128,2048]{2,1,0:T(8,128)(2,1)S(1)} %get-tuple-element.434), channel_id=1, source_target_pairs={{0,16},{4,20},{8,24},{12,28},{16,0},{20,4},{24,8},{28,12},{1,17},{... | collective-permute-start | bytes 3145736 | tf_op jit(solution)/shard_map/ppermute | solution.py:25
  280.2 35.6 %collective-permute-start.38 = (bf16[128,2048]{1,0:T(8,128)(2,1)S(1)}, bf16[128,2048]{1,0:T(8,128)(2,1)S(1)}, u32[]{:S(2)}, u32[]{:S(2)}) collective-permute-start(bf16[128,2048]{1,0:T(8,128)(2,1)S(1)} %get-tuple-element.423), channel_id=1, source_target_pairs={{0,16},{4,20},{8,24},{12,28},{16,0},{20,4},{24,8},{28,12},{1,17},{... | collective-permute-start | bytes 1572872 | tf_op jit(solution)/shard_map/ppermute | solution.py:25
  281.7 34.1 %collective-permute-start.39 = (bf16[128,2048]{1,0:T(8,128)(2,1)}, bf16[128,2048]{1,0:T(8,128)(2,1)S(1)}, u32[]{:S(2)}, u32[]{:S(2)}) collective-permute-start(bf16[128,2048]{1,0:T(8,128)(2,1)} %get-tuple-element.424), channel_id=1, source_target_pairs={{0,8},{4,12},{8,0},{12,4},{16,24},{20,28},{24,16},{28,20},{1,9},{5... | collective-permute-start | bytes 1572872 | tf_op jit(solution)/shard_map/ppermute | solution.py:25
  323.3 20.8 %collective-permute-start.43 = (bf16[128,2048]{1,0:T(8,128)(2,1)}, bf16[128,2048]{1,0:T(8,128)(2,1)S(1)}, u32[]{:S(2)}, u32[]{:S(2)}) collective-permute-start(bf16[128,2048]{1,0:T(8,128)(2,1)} %get-tuple-element.462), channel_id=1, source_target_pairs={{0,16},{4,20},{8,24},{12,28},{16,0},{20,4},{24,8},{28,12},{1,17},{... | collective-permute-start | bytes 1572872 | tf_op jit(solution)/shard_map/ppermute | solution.py:25
  323.9 20.2 %collective-permute-start.44 = (bf16[128,2048]{1,0:T(8,128)(2,1)S(1)}, bf16[128,2048]{1,0:T(8,128)(2,1)S(1)}, u32[]{:S(2)}, u32[]{:S(2)}) collective-permute-start(bf16[128,2048]{1,0:T(8,128)(2,1)S(1)} %get-tuple-element.463), channel_id=1, source_target_pairs={{0,8},{4,12},{8,0},{12,4},{16,24},{20,28},{24,16},{28,20},{1,9},{5... | collective-permute-start | bytes 1572872 | tf_op jit(solution)/shard_map/ppermute | solution.py:25
  324.4 23.0 %collective-permute-start.45 = (bf16[128,1024]{1,0:T(8,128)(2,1)}, bf16[128,1024]{1,0:T(8,128)(2,1)}, u32[]{:S(2)}, u32[]{:S(2)}) collective-permute-start(bf16[128,1024]{1,0:T(8,128)(2,1)} %add_convert_fusion.25), channel_id=1, source_target_pairs={{0,1},{1,0},{2,3},{3,2},{4,5},{5,4},{6,7},{7,6},{8,9},{9,8},{10,11... | collective-permute-start | bytes 786440 | tf_op jit(solution)/shard_map/ppermute | solution.py:25
  325.8 22.2 %collective-permute-start.46 = (bf16[128,1024]{1,0:T(8,128)(2,1)}, bf16[128,1024]{1,0:T(8,128)(2,1)S(1)}, u32[]{:S(2)}, u32[]{:S(2)}) collective-permute-start(bf16[128,1024]{1,0:T(8,128)(2,1)} %get-tuple-element.476), channel_id=1, source_target_pairs={{0,2},{1,3},{2,0},{3,1},{4,6},{5,7},{6,4},{7,5},{8,10},{9,11},{10,... | collective-permute-start | bytes 786440 | tf_op jit(solution)/shard_map/ppermute | solution.py:25
  334.7 14.7 %collective-permute-start.47 = (bf16[128,1024]{1,0:T(8,128)(2,1)S(1)}, bf16[128,1024]{1,0:T(8,128)(2,1)S(1)}, u32[]{:S(2)}, u32[]{:S(2)}) collective-permute-start(bf16[128,1024]{1,0:T(8,128)(2,1)S(1)} %copy-done.91), channel_id=1, source_target_pairs={{0,3},{1,2},{2,1},{3,0},{4,7},{5,6},{6,5},{7,4},{8,11},{9,10},{10,... | collective-permute-start | bytes 786440 | tf_op jit(solution)/shard_map/ppermute | solution.py:25
  344.1 31.1 %collective-permute-start.51 = (bf16[2,128,1024]{2,1,0:T(8,128)(2,1)S(1)}, bf16[2,128,1024]{2,1,0:T(8,128)(2,1)S(1)}, u32[]{:S(2)}, u32[]{:S(2)}) collective-permute-start(bf16[2,128,1024]{2,1,0:T(8,128)(2,1)S(1)} %get-tuple-element.481), channel_id=1, source_target_pairs={{0,8},{4,12},{8,0},{12,4},{16,24},{20,28},{24,16},{28,20},{1,9},{5... | collective-permute-start | bytes 1572872 | tf_op jit(solution)/shard_map/ppermute | solution.py:25
  345.7 29.6 %collective-permute-start.52 = (bf16[2,128,1024]{2,1,0:T(8,128)(2,1)S(1)}, bf16[2,128,1024]{2,1,0:T(8,128)(2,1)S(1)}, u32[]{:S(2)}, u32[]{:S(2)}) collective-permute-start(bf16[2,128,1024]{2,1,0:T(8,128)(2,1)S(1)} %get-tuple-element.482), channel_id=1, source_target_pairs={{0,16},{4,20},{8,24},{12,28},{16,0},{20,4},{24,8},{28,12},{1,17},{... | collective-permute-start | bytes 1572872 | tf_op jit(solution)/shard_map/ppermute | solution.py:25
  347.5 27.7 %collective-permute-start.48 = (bf16[128,1024]{1,0:T(8,128)(2,1)S(1)}, bf16[128,1024]{1,0:T(8,128)(2,1)S(1)}, u32[]{:S(2)}, u32[]{:S(2)}) collective-permute-start(bf16[128,1024]{1,0:T(8,128)(2,1)S(1)} %add_convert_fusion.22), channel_id=1, source_target_pairs={{0,1},{1,0},{2,3},{3,2},{4,5},{5,4},{6,7},{7,6},{8,9},{9,8},{10,11... | collective-permute-start | bytes 786440 | tf_op jit(solution)/shard_map/ppermute | solution.py:25
  348.1 27.1 %collective-permute-start.49 = (bf16[128,1024]{1,0:T(8,128)(2,1)S(1)}, bf16[128,1024]{1,0:T(8,128)(2,1)S(1)}, u32[]{:S(2)}, u32[]{:S(2)}) collective-permute-start(bf16[128,1024]{1,0:T(8,128)(2,1)S(1)} %get-tuple-element.479), channel_id=1, source_target_pairs={{0,2},{1,3},{2,0},{3,1},{4,6},{5,7},{6,4},{7,5},{8,10},{9,11},{10,... | collective-permute-start | bytes 786440 | tf_op jit(solution)/shard_map/ppermute | solution.py:25
  349.4 25.8 %collective-permute-start.50 = (bf16[128,1024]{1,0:T(8,128)(2,1)S(1)}, bf16[128,1024]{1,0:T(8,128)(2,1)S(1)}, u32[]{:S(2)}, u32[]{:S(2)}) collective-permute-start(bf16[128,1024]{1,0:T(8,128)(2,1)S(1)} %get-tuple-element.480), channel_id=1, source_target_pairs={{0,3},{1,2},{2,1},{3,0},{4,7},{5,6},{6,5},{7,4},{8,11},{9,10},{10,... | collective-permute-start | bytes 786440 | tf_op jit(solution)/shard_map/ppermute | solution.py:25
  378.8 136.3 %all-gather.5.cloned.1.call-start = ((), (), s32[]{:S(2)}) async-start(), calls=%async_computation | async-start | bytes 2359296 | tf_op jit(solution)/shard_map/all_gather | solution.py:1415
  394.4 29.6 %collective-permute-start.53 = (bf16[512,2048]{1,0:T(8,128)(2,1)}, bf16[512,2048]{1,0:T(8,128)(2,1)}, u32[]{:S(2)}, u32[]{:S(2)}) collective-permute-start(bf16[512,2048]{1,0:T(8,128)(2,1)} %attention_other.3), channel_id=1, source_target_pairs={{0,4},{4,0},{8,12},{12,8},{16,20},{20,16},{24,28},{28,24},{1,5},{5... | collective-permute-start | bytes 6291464 | tf_op jit(solution)/shard_map/ppermute | solution.py:25
  413.0 28.0 %collective-permute-start.54 = (bf16[544,1024]{1,0:T(8,128)(2,1)}, bf16[544,1024]{1,0:T(8,128)(2,1)}, u32[]{:S(2)}, u32[]{:S(2)}) collective-permute-start(bf16[544,1024]{1,0:T(8,128)(2,1)} %add_convert_fusion), channel_id=1, source_target_pairs={{0,1},{1,0},{2,3},{3,2},{4,5},{5,4},{6,7},{7,6},{8,9},{9,8},{10,11... | collective-permute-start | bytes 3342344 | tf_op jit(solution)/shard_map/ppermute | solution.py:25
  415.7 14.7 %collective-permute-start.55 = (bf16[128,1024]{1,0:T(8,128)(2,1)}, bf16[128,1024]{1,0:T(8,128)(2,1)}, u32[]{:S(2)}, u32[]{:S(2)}) collective-permute-start(bf16[128,1024]{1,0:T(8,128)(2,1)} %fusion.17), channel_id=1, source_target_pairs={{0,16},{4,20},{8,24},{12,28},{16,0},{20,4},{24,8},{28,12},{1,17},{... | collective-permute-start | bytes 786440 | tf_op jit(solution)/shard_map/ppermute | solution.py:25
  443.2 16.4 %collective-permute-start.61 = (bf16[2,128,1024]{2,1,0:T(8,128)(2,1)S(1)}, bf16[2,128,1024]{2,1,0:T(8,128)(2,1)S(1)}, u32[]{:S(2)}, u32[]{:S(2)}) collective-permute-start(bf16[2,128,1024]{2,1,0:T(8,128)(2,1)S(1)} %get-tuple-element.519), channel_id=1, source_target_pairs={{0,16},{4,20},{8,24},{12,28},{16,0},{20,4},{24,8},{28,12},{1,17},{... | collective-permute-start | bytes 1572872 | tf_op jit(solution)/shard_map/ppermute | solution.py:25
  449.1 18.3 %collective-permute-start.59 = (bf16[2,128,1024]{2,1,0:T(8,128)(2,1)}, bf16[2,128,1024]{2,1,0:T(8,128)(2,1)S(1)}, u32[]{:S(2)}, u32[]{:S(2)}) collective-permute-start(bf16[2,128,1024]{2,1,0:T(8,128)(2,1)} %get-tuple-element.517), channel_id=1, source_target_pairs={{0,8},{4,12},{8,0},{12,4},{16,24},{20,28},{24,16},{28,20},{1,9},{5... | collective-permute-start | bytes 1572872 | tf_op jit(solution)/shard_map/ppermute | solution.py:25
  463.5 21.4 %collective-permute-start.57 = (bf16[128,1024]{1,0:T(8,128)(2,1)S(1)}, bf16[128,1024]{1,0:T(8,128)(2,1)S(1)}, u32[]{:S(2)}, u32[]{:S(2)}) collective-permute-start(bf16[128,1024]{1,0:T(8,128)(2,1)S(1)} %fusion.14), channel_id=1, source_target_pairs={{0,2},{1,3},{2,0},{3,1},{4,6},{5,7},{6,4},{7,5},{8,10},{9,11},{10,... | collective-permute-start | bytes 786440 | tf_op jit(solution)/shard_map/ppermute | solution.py:25
  465.9 18.9 %collective-permute-start.58 = (bf16[128,1024]{1,0:T(8,128)(2,1)S(1)}, bf16[128,1024]{1,0:T(8,128)(2,1)S(1)}, u32[]{:S(2)}, u32[]{:S(2)}) collective-permute-start(bf16[128,1024]{1,0:T(8,128)(2,1)S(1)} %fusion.13), channel_id=1, source_target_pairs={{0,3},{1,2},{2,1},{3,0},{4,7},{5,6},{6,5},{7,4},{8,11},{9,10},{10,... | collective-permute-start | bytes 786440 | tf_op jit(solution)/shard_map/ppermute | solution.py:25
  467.4 17.4 %collective-permute-start.60 = (bf16[128,1024]{1,0:T(8,128)(2,1)S(1)}, bf16[128,1024]{1,0:T(8,128)(2,1)S(1)}, u32[]{:S(2)}, u32[]{:S(2)}) collective-permute-start(bf16[128,1024]{1,0:T(8,128)(2,1)S(1)} %fusion.22), channel_id=1, source_target_pairs={{0,16},{4,20},{8,24},{12,28},{16,0},{20,4},{24,8},{28,12},{1,17},{... | collective-permute-start | bytes 786440 | tf_op jit(solution)/shard_map/ppermute | solution.py:25
  470.7 17.8 %collective-permute-start.63 = (bf16[128,1024]{1,0:T(8,128)(2,1)S(1)}, bf16[128,1024]{1,0:T(8,128)(2,1)S(1)}, u32[]{:S(2)}, u32[]{:S(2)}) collective-permute-start(bf16[128,1024]{1,0:T(8,128)(2,1)S(1)} %fusion.9), channel_id=1, source_target_pairs={{0,1},{1,0},{2,3},{3,2},{4,5},{5,4},{6,7},{7,6},{8,9},{9,8},{10,11... | collective-permute-start | bytes 786440 | tf_op jit(solution)/shard_map/ppermute | solution.py:25
  477.7 13.1 %collective-permute-start.74 = (f32[34,1024]{1,0:T(8,128)S(1)}, f32[34,1024]{1,0:T(8,128)S(1)}, u32[]{:S(2)}, u32[]{:S(2)}) collective-permute-start(f32[34,1024]{1,0:T(8,128)S(1)} %add.367), channel_id=1, source_target_pairs={{0,16},{4,20},{8,24},{12,28},{16,0},{20,4},{24,8},{28,12},{1,17},{... | collective-permute-start | bytes 417800 | tf_op jit(solution)/shard_map/ppermute | solution.py:25
  493.8 13.4 %collective-permute-start.65 = (bf16[2,128,512]{2,1,0:T(8,128)(2,1)S(1)}, bf16[2,128,512]{2,1,0:T(8,128)(2,1)S(1)}, u32[]{:S(2)}, u32[]{:S(2)}) collective-permute-start(bf16[2,128,512]{2,1,0:T(8,128)(2,1)S(1)} %pad_maximum_fusion.10.refs_0_), channel_id=1, source_target_pairs={{0,16},{4,20},{8,24},{12,28},{16,0},{20,4},{24,8},{28,12},{1,17},{... | collective-permute-start | bytes 786440 | tf_op jit(solution)/shard_map/ppermute | solution.py:25
  506.7 12.3 %collective-permute-start.68 = (bf16[2,128,512]{2,1,0:T(8,128)(2,1)S(1)}, bf16[2,128,512]{2,1,0:T(8,128)(2,1)S(1)}, u32[]{:S(2)}, u32[]{:S(2)}) collective-permute-start(bf16[2,128,512]{2,1,0:T(8,128)(2,1)S(1)} %pad_maximum_fusion.10.refs_0_), channel_id=1, source_target_pairs={{0,4},{4,0},{8,12},{12,8},{16,20},{20,16},{24,28},{28,24},{1,5},{5... | collective-permute-start | bytes 786440 | tf_op jit(solution)/shard_map/ppermute | solution.py:25
  506.8 12.3 %collective-permute-start.70 = (bf16[2,128,512]{2,1,0:T(8,128)(2,1)S(1)}, bf16[2,128,512]{2,1,0:T(8,128)(2,1)S(1)}, u32[]{:S(2)}, u32[]{:S(2)}) collective-permute-start(bf16[2,128,512]{2,1,0:T(8,128)(2,1)S(1)} %pad_maximum_fusion.11.refs_2_), channel_id=1, source_target_pairs={{0,4},{4,0},{8,12},{12,8},{16,20},{20,16},{24,28},{28,24},{1,5},{5... | collective-permute-start | bytes 786440 | tf_op jit(solution)/shard_map/ppermute | solution.py:25
  (142 other events, 1796.4 us)
Sparse Core Ops, SparseCore 0:
  379.0 30.7 all-gather.6
  424.0 27.7 all-gather.4

commit v3 on v2

--- a/solution.py
+++ b/solution.py
@@ -64,60 +64,61 @@
     return rows // 2 if (rows // 2) % 16 == 0 else rows
 
 
+def padded(rows):
+    return -(-rows // LANES) * LANES
+
+
+def three_parts(value):
+    high = value.astype(BF16)
+    rest = value - high.astype(F32)
+    mid = rest.astype(BF16)
+    return high, mid, (rest - mid.astype(F32)).astype(BF16)
+
+
 def attend_kernel(blocks, rows, q_ref, k_ref, v_ref, kc_ref, out_ref, aug_ref):
     tile = query_tile(rows)
+    far = (blocks - 1) * rows
     lane = lax.broadcasted_iota(jnp.int32, (1, LANES), 1)
     first = lane < HEAD_DIM
-    k_pair, v_pair, k_const = k_ref[...], v_ref[...], kc_ref[...]
-    q_pair = q_ref[...]
-    outs = []
-    augs = []
-    for head in range(2):
-        mine = first if head == 0 else jnp.logical_not(first)
-        special = lane == (HEAD_DIM if head == 0 else 0)
-        keys = jnp.where(mine, k_pair, k_const)
-        queries = jnp.where(mine, q_pair, jnp.where(special, 1.0, 0.0).astype(BF16))
-        head_out = []
-        head_aug = []
-        for start in range(0, rows, tile):
-            reach = start + tile
-            q_tile = queries[start:reach]
-            own = dot_nt(q_tile, keys[:reach])
-            row_ids = start + lax.broadcasted_iota(jnp.int32, (tile, reach), 0)
-            columns = lax.broadcasted_iota(jnp.int32, (tile, reach), 1)
-            pieces = [jnp.where(columns <= row_ids, own, MASKED_SCORE)]
-            for block in range(1, blocks):
-                pieces.append(dot_nt(q_tile, keys[block * rows : (block + 1) * rows]))
-            top = functools.reduce(
-                jnp.maximum, [jnp.max(piece, axis=-1, keepdims=True) for piece in pieces]
-            )
-            total = jnp.zeros((tile, 1), F32)
-            gathered = jnp.zeros((tile, LANES), F32)
-            for block, piece in enumerate(pieces):
-                exponent = jnp.exp(piece - top)
-                total = total + jnp.sum(exponent, axis=-1, keepdims=True)
-                span = v_pair[:reach] if block == 0 else v_pair[block * rows : (block + 1) * rows]
-                gathered = gathered + dot_nn(exponent.astype(BF16), span)
-            head_out.append(gathered / total)
-            log_sum = -(top + jnp.log(total))
-            high = log_sum.astype(BF16)
-            rest = log_sum - high.astype(F32)
-            mid = rest.astype(BF16)
-            low = (rest - mid.astype(F32)).astype(BF16)
-            zero = jnp.zeros((tile, LANES), BF16)
-            spot = lane % HEAD_DIM
-            aug = jnp.where(spot == 0, jnp.ones_like(zero), zero)
-            aug = jnp.where(spot == 1, high, aug)
-            aug = jnp.where(spot == 2, mid, aug)
-            aug = jnp.where(spot == 3, low, aug)
-            head_aug.append(aug)
-        outs.append(head_out)
-        augs.append(head_aug)
-    for index, start in enumerate(range(0, rows, tile)):
+    mine = [first, jnp.logical_not(first)]
+    keys = jnp.concatenate([k_ref[...], kc_ref[...]], axis=1)
+    special = jnp.where(lane == 0, 1.0, 0.0).astype(BF16)
+    special = jnp.broadcast_to(special, (tile, LANES))
+    starts = list(range(0, rows, tile))
+
+    def scores_of(start):
+        q = q_ref[start : start + tile, :]
+        zero = jnp.zeros_like(q)
+        both = jnp.concatenate(
+            [jnp.concatenate([jnp.where(m, q, zero), special], axis=1) for m in mine], axis=0
+        )
+        return dot_nt(both, keys[: far + start + tile])
+
+    scores = [scores_of(start) for start in starts]
+    for start, score in zip(starts, scores):
+        limit = far + start + tile
+        cut = (far + start) // LANES * LANES
+        row_ids = lax.broadcasted_iota(jnp.int32, (2 * tile, limit - cut), 0)
+        row_ids = start + far - cut + jnp.where(row_ids >= tile, row_ids - tile, row_ids)
+        columns = lax.broadcasted_iota(jnp.int32, (2 * tile, limit - cut), 1)
+        last = jnp.where(columns <= row_ids, score[:, cut:], MASKED_SCORE)
+        score = jnp.concatenate([score[:, :cut], last], axis=1) if cut else last
+        top = jnp.max(score, axis=-1, keepdims=True)
+        exponent = jnp.exp(score - top)
+        total = jnp.sum(exponent, axis=-1, keepdims=True)
+        gathered = dot_nn(exponent.astype(BF16), v_ref[0:limit, :]) / total
         out_ref[start : start + tile, :] = jnp.where(
-            first, outs[0][index], outs[1][index]
+            first, gathered[:tile], gathered[tile:]
         ).astype(BF16)
-        aug_ref[start : start + tile, :] = jnp.where(first, augs[1][index], augs[0][index])
+        parts = three_parts(-(top + jnp.log(total)))
+        spot = lane % HEAD_DIM
+        augs = []
+        for head in range(2):
+            aug = jnp.where(spot == 0, 1.0, jnp.zeros((tile, LANES), F32)).astype(BF16)
+            for index, value in enumerate(parts):
+                aug = jnp.where(spot == index + 1, value[head * tile : (head + 1) * tile], aug)
+            augs.append(aug)
+        aug_ref[start : start + tile, :] = jnp.where(first, augs[0], augs[1])
 
 
 def attend(queries, keys, values, key_const, begin, count):
@@ -141,97 +142,112 @@
             jax.ShapeDtypeStruct((rows, count), BF16),
         ],
         name="attend",
-        compiler_params=pltpu.CompilerParams(vmem_limit_bytes=40 << 20),
+        compiler_params=pltpu.CompilerParams(vmem_limit_bytes=48 << 20),
         cost_estimate=LIGHT,
     )(queries, keys, values, key_const)
 
 
 def attend_back_kernel(
-    blocks, rows, q_ref, k_ref, v_ref, kc_ref, aug_ref, go_ref, out_ref, dq_ref, dk_ref, dv_ref
+    causal, q_ref, k_ref, v_ref, kc_ref, aug_ref, go_ref, out_ref, *refs
 ):
+    before, refs = (refs[0], refs[1:]) if causal else (None, refs)
+    dq_ref, dk_ref, dv_ref, q_both, g_both, ds_ref = refs
+    rows = q_ref.shape[0]
+    span = k_ref.shape[0]
     key_tile = query_tile(rows)
+    wide = padded(rows)
     lane = lax.broadcasted_iota(jnp.int32, (1, LANES), 1)
     first = lane < HEAD_DIM
-    spot = lane % HEAD_DIM
-    k_pair, v_pair, k_const = k_ref[...], v_ref[...], kc_ref[...]
-    q_pair, aug, go_pair = q_ref[...], aug_ref[...], go_ref[...]
-    weighed = go_pair.astype(F32) * out_ref[...].astype(F32)
-    v_const = jnp.where((spot >= 1) & (spot <= 3), 1.0, 0.0).astype(BF16)
-    grads_q = []
-    grads_k = []
-    grads_v = []
+    mine = [first, jnp.logical_not(first)]
+    q_pair, aug, go = q_ref[...], aug_ref[...], go_ref[...]
+    zero = jnp.zeros_like(q_pair)
+    weighed = go.astype(F32) * out_ref[...].astype(F32)
+    pad = jnp.zeros((wide - rows, 2 * LANES), BF16)
     for head in range(2):
-        mine = first if head == 0 else jnp.logical_not(first)
-        keys = jnp.where(mine, k_pair, k_const)
-        queries = jnp.where(mine, q_pair, aug)
-        values = jnp.where(mine, v_pair, v_const)
-        delta = -jnp.sum(jnp.where(mine, weighed, 0.0), axis=-1, keepdims=True)
-        high = delta.astype(BF16)
-        rest = delta - high.astype(F32)
-        mid = rest.astype(BF16)
-        low = (rest - mid.astype(F32)).astype(BF16)
-        go_aug = jnp.where(spot == 1, high, jnp.zeros((rows, LANES), BF16))
-        go_aug = jnp.where(spot == 2, mid, go_aug)
-        go_aug = jnp.where(spot == 3, low, go_aug)
-        grads = jnp.where(mine, go_pair, go_aug)
-        grad_q = jnp.zeros((rows, LANES), F32)
-        head_k = []
-        head_v = []
-        for start in range(0, blocks * rows, key_tile):
-            stop = start + key_tile
-            scores = dot_nt(keys[start:stop], queries)
-            exact = jnp.exp(scores)
-            if start < rows:
-                key_ids = start + lax.broadcasted_iota(jnp.int32, (key_tile, rows), 0)
-                query_ids = lax.broadcasted_iota(jnp.int32, (key_tile, rows), 1)
-                exact = jnp.where(key_ids <= query_ids, exact, 0.0)
-            centred = dot_nt(values[start:stop], grads)
-            grad_scores = (exact * centred).astype(BF16)
-            head_v.append(dot_nn(exact.astype(BF16), go_pair))
-            head_k.append(dot_nn(grad_scores, q_pair))
-            grad_q = grad_q + dot_tn(grad_scores, k_pair[start:stop])
-        grads_q.append(grad_q)
-        grads_k.append(head_k)
-        grads_v.append(head_v)
-    dq_ref[...] = (jnp.where(first, grads_q[0], grads_q[1]) * 0.125).astype(BF16)
-    for index, start in enumerate(range(0, blocks * rows, key_tile)):
-        dk_ref[start : start + key_tile, :] = jnp.where(
-            first, grads_k[0][index], grads_k[1][index]
-        ).astype(BF16)
-        dv_ref[start : start + key_tile, :] = jnp.where(
-            first, grads_v[0][index], grads_v[1][index]
-        ).astype(BF16)
-
-
-def attend_back(queries, keys, values, key_const, aug, grad_out, out, begin):
+        m = mine[head]
+        place = head * wide
+        q_both[place : place + rows, 0:LANES] = jnp.where(m, q_pair, zero)
+        q_both[place : place + rows, LANES:] = jnp.where(m, aug, zero)
+        parts = three_parts(-jnp.sum(jnp.where(m, weighed, 0.0), axis=-1, keepdims=True))
+        g_aug = zero
+        for index, value in enumerate(parts):
+            g_aug = jnp.where(lane == index + 1, value, g_aug)
+        g_both[place : place + rows, 0:LANES] = jnp.where(m, go, zero)
+        g_both[place : place + rows, LANES:] = g_aug
+        if wide > rows:
+            q_both[place + rows : place + wide, :] = pad
+            g_both[place + rows : place + wide, :] = pad
+    keys = jnp.concatenate([k_ref[...], kc_ref[...]], axis=1)
+    v_const = jnp.where((lane >= 1) & (lane <= 3), 1.0, 0.0).astype(BF16)
+    values = jnp.concatenate([v_ref[...], jnp.broadcast_to(v_const, k_ref.shape)], axis=1)
+
+    def dots_of(start):
+        stop = start + key_tile
+        return dot_nt(keys[start:stop], q_both[...]), dot_nt(values[start:stop], g_both[...])
+
+    starts = list(range(0, span, key_tile))
+    ahead = dots_of(starts[0])
+    for index, start in enumerate(starts):
+        stop = start + key_tile
+        scores, centred = ahead
+        if index + 1 < len(starts):
+            ahead = dots_of(starts[index + 1])
+        exact = jnp.exp(scores)
+        if causal:
+            key_ids = start + lax.broadcasted_iota(jnp.int32, (key_tile, 2 * wide), 0)
+            query_ids = lax.broadcasted_iota(jnp.int32, (key_tile, 2 * wide), 1)
+            query_ids = jnp.where(query_ids >= wide, query_ids - wide, query_ids)
+            exact = jnp.where(key_ids <= query_ids, exact, 0.0)
+        grad_scores = (exact * centred).astype(BF16)
+        ds_ref[start:stop, :] = grad_scores
+        dv_ref[start:stop, :] = dot_nn(exact.astype(BF16), g_both[:, 0:LANES]).astype(BF16)
+        dk_ref[start:stop, :] = dot_nn(grad_scores, q_both[:, 0:LANES]).astype(BF16)
+    grad_q = dot_tn(k_ref[...], ds_ref[...]).T
+    grad_q = jnp.where(first, grad_q[0:rows], grad_q[wide : wide + rows])
+    if causal:
+        dq_ref[...] = ((grad_q + before[...]) * 0.125).astype(BF16)
+    else:
+        dq_ref[...] = grad_q
+
+
+def attend_back(queries, keys, values, key_const, aug, grad_out, out, begin, count, before=None):
     rows = queries.shape[0]
-    count = aug.shape[1]
-    span = keys.shape[0]
+    far = keys.shape[0] - rows
+    causal = before is not None
+    span, block = (rows, far // rows) if causal else (far, 0)
     first = begin // LANES
-    pair = lambda height: pl.BlockSpec((height, LANES), lambda i: (0, first + i))
+    wide = padded(rows)
+    pair = pl.BlockSpec((rows, LANES), lambda i: (0, first + i))
+    keys_of = pl.BlockSpec((span, LANES), lambda i: (block, first + i))
     made = lambda height: pl.BlockSpec((height, LANES), lambda i: (0, i))
     return pl.pallas_call(
-        functools.partial(attend_back_kernel, span // rows, rows),
+        functools.partial(attend_back_kernel, causal),
         grid=(count // LANES,),
         in_specs=[
-            pair(rows),
-            pair(span),
-            pair(span),
-            pl.BlockSpec((span, LANES), lambda i: (0, 0)),
-            made(rows),
-            pair(rows),
-            made(rows),
-        ],
+            pair,
+            keys_of,
+            keys_of,
+            pl.BlockSpec((span, LANES), lambda i: (block, 0)),
+            pair,
+            pair,
+            pair,
+        ]
+        + [pair] * causal,
         out_specs=[made(rows), made(span), made(span)],
         out_shape=[
-            jax.ShapeDtypeStruct((rows, count), BF16),
+            jax.ShapeDtypeStruct((rows, count), BF16 if causal else F32),
             jax.ShapeDtypeStruct((span, count), BF16),
             jax.ShapeDtypeStruct((span, count), BF16),
         ],
+        scratch_shapes=[
+            pltpu.VMEM((2 * wide, 2 * LANES), BF16),
+            pltpu.VMEM((2 * wide, 2 * LANES), BF16),
+            pltpu.VMEM((span, 2 * wide), BF16),
+        ],
         name="attend_back",
-        compiler_params=pltpu.CompilerParams(vmem_limit_bytes=48 << 20),
+        compiler_params=pltpu.CompilerParams(vmem_limit_bytes=52 << 20),
         cost_estimate=LIGHT,
-    )(queries, keys, values, key_const, aug, grad_out, out)
+    )(queries, keys, values, key_const, aug, grad_out, out, *([before] if causal else []))
 
 
 def chip_masks(dp):
@@ -352,14 +368,14 @@
         return [pl.BlockSpec(memory_space=pl.ANY)] * len(self.inputs)
 
     def scratch(self, mp, which):
-        count = self.full // self.width + (mp - 1) * sum(len(m) for _, m, _ in self.arrays)
+        count = self.full // self.width + sum(len(m) for _, m, _ in self.arrays)
         return [
             pltpu.VMEM((mp, len(which), self.full, self.width), BF16),
             pltpu.SemaphoreType.DMA((count + 4,)),
         ]
 
     def copies(self, refs, held, sems, device, mp, dp, which):
-        made = [[] for _ in range(mp)]
+        made = [[], []]
         spot = 0
 
         def add(r, source, target):
@@ -376,15 +392,14 @@
             elif not by_rows and first == index:
                 add(0, ref, held.at[0, 0 : ref.shape[0]])
         half = self.full // dp // 2
-        for r in range(1, mp):
-            for ref, (side, masks, _) in zip(refs[self.n_own :], self.arrays):
-                for index, mask in enumerate(masks):
-                    start = pl.multiple_of((position(device, mask, dp) * 2 + side) * half, half)
-                    add(
-                        r,
-                        ref.at[index, r - 1, first:last],
-                        held.at[r, :, pl.ds(start, half), :],
-                    )
+        for ref, (side, masks, _) in zip(refs[self.n_own :], self.arrays):
+            for index, mask in enumerate(masks):
+                start = pl.multiple_of((position(device, mask, dp) * 2 + side) * half, half)
+                add(
+                    1,
+                    ref.at[index, :, first:last],
+                    held.at[1:, :, pl.ds(start, half), :],
+                )
         return made
 
 
@@ -449,7 +464,7 @@
     size = column_tile(group.width)
     for begin in range(0, group.width, size):
         columns = slice(begin, begin + size)
-        q = dot_nn(x_refs[0][...], held[r, 0, :, columns]) + bias_ref[0:1, columns].astype(F32)
+        q = dot_nn(x_refs[-1][...], held[r, 0, :, columns]) + bias_ref[0:1, columns].astype(F32)
         q_ref[:, columns] = ((q * scale).astype(BF16) * RELAX_ALPHA).astype(BF16)
         for block in range(blocks):
             x = x_refs[block][...]
@@ -799,20 +814,24 @@
     )
 
 
-def unproject_kernel(group, begin, steps, scal, *refs):
-    (dq_ref, dk_ref, dv_ref), refs = refs[:3], refs[3:]
+def unproject_kernel(group, which, begin, steps, added, scal, *refs):
+    grads, refs = refs[: len(which)], refs[len(which) :]
+    before, refs = (refs[0], refs[1:]) if added else (None, refs)
     w_refs, refs = refs[: len(group.inputs)], refs[len(group.inputs) :]
-    near_ref, far_ref, held, sems, total = refs
+    out_ref, held, sems, total = refs
     step = pl.program_id(0)
     mp, dp = lax.axis_size("mp"), lax.axis_size("dp")
     copies = group.copies(w_refs, held, sems, scal[0], mp, dp, [0, 1, 2])
-    copies = copies[begin : begin + steps]
-    rows, full = near_ref.shape
+    if begin:
+        copies = copies[1:]
+    elif steps == 1:
+        copies = copies[:1]
+    full = out_ref.shape[1]
 
     @pl.when(step == 0)
     def _():
         start_all(sum(copies, []))
-        total[...] = jnp.zeros_like(total)
+        total[...] = before[...] if added else jnp.zeros_like(total)
 
     wait_step(step, copies)
     r = begin + step
@@ -820,44 +839,40 @@
 
     def add(start):
         columns = pl.ds(start, size)
-        grad = dot_nt(dk_ref[...], held[r, 1, columns, :]) + dot_nt(
-            dv_ref[...], held[r, 2, columns, :]
+        total[:, columns] += functools.reduce(
+            jnp.add,
+            [dot_nt(g[...], held[r, index, columns, :]) for index, g in zip(which, grads)],
         )
-        total[:, columns] += grad
-        total[0:rows, columns] += dot_nt(dq_ref[...], held[r, 0, columns, :])
 
     tiles(full, size, add)
 
     @pl.when(step == pl.num_programs(0) - 1)
     def _():
-        near_ref[...] = total[0:rows, :]
-        far_ref[...] = total[rows:, :].astype(BF16)
-
-
-def unproject(grads, group, begin, device):
-    grad_q, grad_k, grad_v = grads
+        out_ref[...] = total[...].astype(out_ref.dtype)
+
+
+def unproject(grads, which, group, begin, before, dtype, device):
     mp = lax.axis_size("mp")
-    rows, count = grad_q.shape
-    span = grad_k.shape[0]
+    rows, count = grads[0].shape
     full, width = group.full, group.width
-    made = lambda height: pl.BlockSpec((height, width), lambda i, *_: (0, i))
     return pl.pallas_call(
-        functools.partial(unproject_kernel, group, begin, count // width),
+        functools.partial(
+            unproject_kernel, group, which, begin, count // width, before is not None
+        ),
         grid_spec=pltpu.PrefetchScalarGridSpec(
             num_scalar_prefetch=1,
             grid=(count // width,),
-            in_specs=[made(rows), made(span), made(span)] + group.specs(),
-            out_specs=[whole((rows, full)), whole((span - rows, full))],
-            scratch_shapes=group.scratch(mp, [0, 1, 2]) + [pltpu.VMEM((span, full), F32)],
+            in_specs=[pl.BlockSpec((rows, width), lambda i, *_: (0, i))] * len(grads)
+            + ([] if before is None else [whole((rows, full))])
+            + group.specs(),
+            out_specs=whole((rows, full)),
+            scratch_shapes=group.scratch(mp, [0, 1, 2]) + [pltpu.VMEM((rows, full), F32)],
         ),
-        out_shape=[
-            jax.ShapeDtypeStruct((rows, full), F32),
-            jax.ShapeDtypeStruct((span - rows, full), BF16),
-        ],
+        out_shape=jax.ShapeDtypeStruct((rows, full), dtype),
         name="unproject",
         compiler_params=pltpu.CompilerParams(vmem_limit_bytes=48 << 20),
         cost_estimate=LIGHT,
-    )(device.reshape(1), grad_q, grad_k, grad_v, *group.inputs)
+    )(device.reshape(1), *grads, *([] if before is None else [before]), *group.inputs)
 
 
 def other_half_kernel(scal, left_ref, right_ref, out_ref):
@@ -949,16 +964,14 @@
 
 
 def attention_dots(width, lefts, branch, grads, attended, layer, put):
-    grad_q, grad_k, grad_v = grads
+    grad_q, near_k, near_v, far_k, far_v = grads
     rows = grad_q.shape[0]
     columns = slice(layer * width, (layer + 1) * width)
-    put(0, dot_tn(lefts[0][...], grad_q[:, columns]))
-    for index, grad in ((1, grad_k), (2, grad_v)):
-        total = dot_tn(lefts[0][...], grad[0:rows, columns])
-        for block in range(1, len(lefts)):
-            total = total + dot_tn(
-                lefts[block][...], grad[block * rows : (block + 1) * rows, columns]
-            )
+    put(0, dot_tn(lefts[-1][...], grad_q[:, columns]))
+    for index, near, far in ((1, near_k, far_k), (2, near_v, far_v)):
+        total = dot_tn(lefts[-1][...], near[:, columns])
+        for block in range(len(lefts) - 1):
+            total = total + dot_tn(lefts[block][...], far[block * rows : (block + 1) * rows, columns])
         put(index, total)
     put(3, dot_tn(branch[...], attended[:, columns]))
 
@@ -975,8 +988,8 @@
 
 
 def attention_this_kernel(width, blocks, bits_at, scal, *refs):
-    lefts, (branch, *grads, attended, got_ref) = refs[:blocks], refs[blocks : blocks + 6]
-    outs, total = refs[blocks + 6 : -1], refs[-1]
+    lefts, (branch, *grads, attended, got_ref) = refs[:blocks], refs[blocks : blocks + 8]
+    outs, total = refs[blocks + 8 : -1], refs[-1]
     layers = attended.shape[1] // width
     for side in range(2):
         for local in range(layers // 2):
@@ -998,21 +1011,28 @@
             )
 
 
-def attention_specs(normed, branch, grads, attended, core_of):
+def attention_specs(normed, branch, grads, part, core_of):
     rows, full = branch.shape
     left = pl.BlockSpec((rows, full // 2), lambda i, scal: (0, core_of(scal)))
-    return [left] * (len(normed) + 1) + [whole(g.shape) for g in grads] + [whole(attended.shape)]
-
-
-def attention_other(normed, branch, grads, attended, width, device):
+    wide = grads[0].shape[1]
+    some = lambda height: pl.BlockSpec((height, wide), lambda i, scal: (0, part))
+    return (
+        [left] * (len(normed) + 1)
+        + [whole(g.shape) for g in grads[:3]]
+        + [some(g.shape[0]) for g in grads[3:]]
+        + [some(rows)]
+    )
+
+
+def attention_other(normed, branch, grads, attended, part, width, device):
     full = branch.shape[1]
-    out = (full // 2, 4 * attended.shape[1])
+    out = (full // 2, 4 * grads[0].shape[1])
     return pl.pallas_call(
         functools.partial(attention_other_kernel, width, len(normed)),
         grid_spec=pltpu.PrefetchScalarGridSpec(
             num_scalar_prefetch=1,
             grid=(1,),
-            in_specs=attention_specs(normed, branch, grads, attended, lambda s: 1 - s[0] % 2),
+            in_specs=attention_specs(normed, branch, grads, part, lambda s: 1 - s[0] % 2),
             out_specs=whole(out),
         ),
         out_shape=jax.ShapeDtypeStruct(out, BF16),
@@ -1022,16 +1042,16 @@
     )(device.reshape(1), *normed, branch, *grads, attended)
 
 
-def attention_this(normed, branch, grads, attended, got, width, device):
+def attention_this(normed, branch, grads, attended, got, part, width, device):
     full = branch.shape[1]
     quarters = lax.axis_size("dp") // 2
-    shape = (quarters // 2, full // 2 // quarters, 2 * attended.shape[1])
+    shape = (quarters // 2, full // 2 // quarters, 2 * grads[0].shape[1])
     return pl.pallas_call(
         functools.partial(attention_this_kernel, width, len(normed), first_bits()),
         grid_spec=pltpu.PrefetchScalarGridSpec(
             num_scalar_prefetch=1,
             grid=(1,),
-            in_specs=attention_specs(normed, branch, grads, attended, lambda s: s[0] % 2)
+            in_specs=attention_specs(normed, branch, grads, part, lambda s: s[0] % 2)
             + [whole(got.shape)],
             out_specs=[whole(shape)] * 4,
             scratch_shapes=[pltpu.VMEM((full // 2, 4 * width), F32)],
@@ -1041,6 +1061,74 @@
         compiler_params=pltpu.CompilerParams(vmem_limit_bytes=48 << 20),
         cost_estimate=LIGHT,
     )(device.reshape(1), *normed, branch, *grads, attended, got)
+
+
+def next_stage_kernel(scal, *refs):
+    ins, outs = refs[:8], refs[8:]
+    for index, out in enumerate(outs):
+        one, two = ins[2 * index], ins[2 * index + 1]
+        out[...] = (one[0].astype(F32) + two[0].astype(F32)).astype(BF16)
+
+
+def next_stage(keeps, gots, bits, device):
+    _, rows, columns = keeps[0].shape
+    specs, inputs = [], []
+    for side in range(2):
+        for flip in (1, 0):
+            where = lambda i, scal, side=side, flip=flip: (
+                ((scal[0] >> (bits[side] + 1)) & 1) ^ flip,
+                0,
+                0,
+            )
+            specs += [pl.BlockSpec((1, rows, columns), where)] * 2
+            inputs += [keeps[side], gots[side]]
+    return pl.pallas_call(
+        next_stage_kernel,
+        grid_spec=pltpu.PrefetchScalarGridSpec(
+            num_scalar_prefetch=1,
+            grid=(1,),
+            in_specs=specs,
+            out_specs=[whole((rows, columns))] * 4,
+        ),
+        out_shape=[jax.ShapeDtypeStruct((rows, columns), BF16)] * 4,
+        name="next_stage",
+        compiler_params=pltpu.CompilerParams(vmem_limit_bytes=32 << 20),
+        cost_estimate=LIGHT,
+    )(device.reshape(1), *inputs)
+
+
+def by_layer_kernel(places, keep_a, got_a, keep_b, got_b, send_ref, rest_ref):
+    width = send_ref.shape[2]
+    each = len(places) // 2
+    for index, (sent, spot) in enumerate(places):
+        keep, got = ((keep_a, got_a), (keep_b, got_b))[index // each]
+        columns = slice(index % each * width, (index % each + 1) * width)
+        value = keep[:, columns].astype(F32) + got[:, columns].astype(F32)
+        if sent:
+            send_ref[spot] = value.astype(BF16)
+        else:
+            rest_ref[spot] = value
+
+
+def by_layer_pieces(keeps, gots, layers):
+    rows = keeps[0].shape[0]
+    width = keeps[0].shape[1] * 2 // len(layers)
+    odd = [r for r in layers if r & 1]
+    even = [r for r in layers if not r & 1]
+    places = [(r & 1, (odd if r & 1 else even).index(r)) for r in layers]
+    send, rest = pl.pallas_call(
+        functools.partial(by_layer_kernel, places),
+        out_shape=[
+            jax.ShapeDtypeStruct((len(odd), rows, width), BF16),
+            jax.ShapeDtypeStruct((len(even), rows, width), F32),
+        ],
+        in_specs=[pl.BlockSpec(memory_space=pltpu.VMEM)] * 4,
+        out_specs=[pl.BlockSpec(memory_space=pltpu.VMEM)] * 2,
+        name="by_layer_pieces",
+        compiler_params=pltpu.CompilerParams(vmem_limit_bytes=32 << 20),
+        cost_estimate=LIGHT,
+    )(keeps[0], gots[0], keeps[1], gots[1])
+    return send, rest, odd, even
 
 
 def reduce_flow(send, add, layers, device):
@@ -1063,9 +1151,13 @@
         gots = [got.reshape(keep.shape) for got, keep in zip(gots, keeps)]
         if step + 1 == bits:
             break
+        picks = [order[step + 1].bit_length() - 2 for order in orders]
+        if keeps[0].ndim == 3:
+            send_a, keep_a, send_b, keep_b = next_stage(keeps, gots, picks, device)
+            sends, keeps = [send_a, send_b], [keep_a, keep_b]
+            continue
         sends, next_keeps = [], []
-        for side, order in enumerate(orders):
-            which = order[step + 1].bit_length() - 2
+        for side, which in enumerate(picks):
             axis = lefts[side].index(which)
             lefts[side].remove(which)
             bit = (device >> (which + 1)) & 1
@@ -1080,21 +1172,26 @@
             sends.append(part(1 - bit))
             next_keeps.append(part(bit))
         keeps = next_keeps
-    each = len(layers) // 2
-    size = keeps[0].shape[-1] // each
-    pieces = []
-    for side in range(2):
-        for local in range(each):
-            columns = slice(local * size, (local + 1) * size)
-            pieces.append(
-                keeps[side][..., columns].astype(F32) + gots[side][..., columns].astype(F32)
-            )
-    away = [(r, piece.astype(BF16)) for r, piece in zip(layers, pieces) if r]
-    sent = yield tuple(piece for _, piece in away)
-    found = yield tuple(swap(piece, "mp", r) for (r, _), piece in zip(away, sent))
-    return [piece for r, piece in zip(layers, pieces) if r == 0] + [
-        piece.astype(F32) for piece in found
-    ]
+    send, rest, odd, even = by_layer_pieces(keeps, gots, layers)
+    (send,) = yield (send,)
+    (got,) = yield (swap(send, "mp", 1),)
+    held = {r: rest[i] for i, r in enumerate(even)}
+    for i, r in enumerate(odd):
+        value = got[i].astype(F32)
+        held[r ^ 1] = held[r ^ 1] + value if r ^ 1 in held else value
+    for bit in range(1, lax.axis_size("mp").bit_length() - 1):
+        mask = 1 << bit
+        away = [r for r in sorted(held) if r & mask]
+        if away:
+            send = held[away[0]] if len(away) == 1 else jnp.stack([held[r] for r in away])
+            (send,) = yield (send.astype(BF16),)
+            (got,) = yield (swap(send, "mp", mask),)
+            got = [got] if len(away) == 1 else list(got)
+            for r, value in zip(away, got):
+                del held[r]
+                value = value.astype(F32)
+                held[r ^ mask] = held[r ^ mask] + value if r ^ mask in held else value
+    return held[0]
 
 
 def fill_kernel(plan, rows, dp, scal, *refs):
@@ -1252,7 +1349,8 @@
         return (yield tuple(swap(value, "mp", m) for m in range(1, blocks)))
 
     key_ids = lax.broadcasted_iota(jnp.int32, (blocks, rows, 1), 1)
-    block_ids = place_in_seq ^ lax.broadcasted_iota(jnp.int32, (blocks, rows, 1), 0)
+    block_ids = lax.broadcasted_iota(jnp.int32, (blocks, rows, 1), 0)
+    block_ids = place_in_seq ^ ((block_ids + 1) % blocks)
     shown = (block_ids <= place_in_seq) & (block_ids * rows + key_ids < length)
     spot = lax.broadcasted_iota(jnp.int32, (blocks, rows, LANES), 2) % HEAD_DIM
     key_const = jnp.where(
@@ -1265,19 +1363,18 @@
     slice_u = own_slice(up_weight[None], False, device, hidden)
     slice_d = own_slice(down_weight, True, device, hidden)
     flow_r = Flow(rows_flow(normed_low))
-    slice_u, slice_d = begin([flow_r], slice_u, slice_d)
     normed_low, slice_u, slice_d = meet([flow_a], normed_low, slice_u, slice_d)
     flow_u, flow_d = Flow(gather_flow(slice_u)), Flow(gather_flow(slice_d))
     layer_stages = mp.bit_length() - 1
     for _ in range(layer_stages - 1):
         normed_low = meet([flow_a], normed_low)
-    normed_low = begin([flow_u], normed_low)
+    normed_low = begin([flow_r, flow_u], normed_low)
     for _ in range(stages - 1):
         normed_low = meet([flow_a], normed_low)
-    normed_low = meet([flow_a, flow_r, flow_u], normed_low)
-    normed_low = meet([flow_a], normed_low)
-    for _ in range(layer_stages - 1):
+    normed_low = meet([flow_a, flow_u, flow_r], normed_low)
+    for _ in range(layer_stages - 2):
         normed_low = meet([flow_u], normed_low)
+    normed_low = meet([flow_a, flow_u], normed_low)
     normed_low = begin([flow_d], normed_low)
     arrays_a, small_all = flow_a.result
     group_a = Weights(shard_a, arrays_a)
@@ -1286,17 +1383,17 @@
     u_rows = small_all[:, 2 * width :].reshape(1, -1)
     qv_rows = jnp.pad(qv_rows, ((0, 6), (0, 0)))
     u_rows = jnp.pad(u_rows, ((0, 7), (0, 0)))
-    seq_normed = (normed_low,) + tuple(flow_r.result)
+    seq_normed = tuple(flow_r.result) + (normed_low,)
     queries, keys, values = project(seq_normed, qv_rows, group_a, device)
-    for _ in range(stages - 1):
-        queries, keys, values = meet([flow_u, flow_d], queries, keys, values)
+    queries, keys, values = meet([flow_d, flow_u], queries, keys, values)
     attended_a, aug_a = attend(queries, keys, values, key_const, 0, part)
-    attended_a, queries = meet([flow_d], attended_a, queries)
-    for _ in range(layer_stages - 2):
+    for _ in range(layer_stages - 1):
         attended_a, queries = meet([flow_d], attended_a, queries)
     attended_b, aug_b = attend(queries, keys, values, key_const, part, part)
-    attended_b = meet([flow_u], attended_b)
-    for _ in range(stages - 1):
+    attended = jnp.concatenate([attended_a, attended_b], axis=1)
+    aug = jnp.concatenate([aug_a, aug_b], axis=1)
+    attended_b = meet([flow_u, flow_d], attended_b)
+    for _ in range(stages - 2):
         attended_b = meet([flow_d], attended_b)
     (attended_b,) = finish([flow_u], attended_b)
     group_u = Weights(shard_u, flow_u.result[0])
@@ -1346,14 +1443,14 @@
     grad_pre, grad_branch, grad_attended = meet([flow_d], grad_pre, grad_branch, grad_attended)
     flow_u = weight_flow(mid_low, grad_pre)
     grad_branch, grad_attended = begin([flow_u], grad_branch, grad_attended)
-    grad_branch, grad_attended = meet([flow_u], grad_branch, grad_attended)
-
-    def attention_flow(grads, attended, layers):
+
+    def attention_flow(grads, layers):
+        index = layers[0] * width // part
         return Flow(
             reduce_flow(
-                attention_other(seq_normed, grad_branch, grads, attended, width, device),
+                attention_other(seq_normed, grad_branch, grads, attended, index, width, device),
                 lambda got: attention_this(
-                    seq_normed, grad_branch, grads, attended, got, width, device
+                    seq_normed, grad_branch, grads, attended, got, index, width, device
                 ),
                 layers,
                 device,
@@ -1361,24 +1458,34 @@
         )
 
     layers_b, layers_a = everyone[: mp // 2], everyone[mp // 2 :]
-    grads_a = attend_back(queries, keys, values, key_const, aug_b, grad_attended, attended_b, part)
-    grads_a = meet([flow_d], *grads_a)
-    flow_qa = attention_flow(grads_a, attended_b, layers_a)
-    grads_a = meet([flow_u], *grads_a)
-    queries, *grads_a = begin([flow_qa], queries, *grads_a)
-    near_a, far_a = unproject(grads_a, group_a, mp // 2, device)
-    queries, near_a, far_a = meet([flow_qa], queries, near_a, far_a)
-    queries, near_a, far_a = meet([flow_u], queries, near_a, far_a)
-    grads_b = attend_back(queries, keys, values, key_const, aug_a, grad_attended, attended_a, 0)
-    grads_b = meet([flow_d, flow_u, flow_qa], *grads_b)
-    flow_qb = attention_flow(grads_b, attended_a, layers_b)
+    back = functools.partial(
+        attend_back, queries, keys, values, key_const, aug, grad_attended, attended
+    )
+    far_q, far_k, far_v = back(0, full)
+    far_grad = unproject((far_k, far_v), (1, 2), group_a, 0, None, BF16, device)
+    far_grad, far_q, far_k, far_v = ordered([flow_d, flow_u], (far_grad, far_q, far_k, far_v))
+    flow_f = Flow(rows_back(far_grad, rows, blocks))
+    far_q, far_k, far_v = begin([flow_f, flow_u], far_q, far_k, far_v)
+    grads_a = back(part, part, far_q)
+    flow_qa = attention_flow((*grads_a, far_k, far_v), layers_a)
+    far_q, *grads_a = meet([flow_u, flow_f], far_q, *grads_a)
+    far_q, *grads_a = begin([flow_qa], far_q, *grads_a)
+    near_a = unproject(grads_a, (0, 1, 2), group_a, mp // 2, None, F32, device)
+    far_q, near_a = meet([flow_qa], far_q, near_a)
+    far_q, near_a = begin([flow_d], far_q, near_a)
+    grads_b = back(0, part, far_q)
+    grads_b = ordered([flow_u, flow_qa, flow_d], grads_b)
+    flow_qb = attention_flow((*grads_b, far_k, far_v), layers_b)
     grads_b = begin([flow_qb], *grads_b)
-    near_b, far_b = unproject(grads_b, group_a, 0, device)
-    flow_f = Flow(rows_back(far_a, far_b, rows, blocks))
-    near_b = begin([flow_f], near_b)
-    near_b = meet([flow_qb], near_b)
-    near_b = meet([flow_f, flow_qa], near_b)
-    grad_normed = near_a + near_b
+    grads_b = begin([flow_u, flow_qa, flow_d], *grads_b)
+    near_b = unproject(grads_b, (0, 1, 2), group_a, 0, near_a, F32, device)
+    near_b, *grads_a, sums_ffn, sums_back, sums_up = meet(
+        [flow_qb, flow_qa, flow_u, flow_d], near_b, *grads_a, sums_ffn, sums_back, sums_up
+    )
+    drain(flow_d)
+    down_mine = flow_d.result.astype(BF16)
+    down_all = lax.all_gather(down_mine, "dp", axis=0)
+    grad_normed = near_b
     for value in flow_f.result:
         grad_normed = grad_normed + value.astype(F32)
     back_one, gain_one, shift_one = norm_backward(grad_normed, norm_one, inv_one, gains[0])
@@ -1388,6 +1495,7 @@
     )
     grad_q_sum = jnp.concatenate([jnp.sum(g[0].astype(F32), axis=0) for g in (grads_b, grads_a)])
     grad_v_sum = jnp.concatenate([jnp.sum(g[2].astype(F32), axis=0) for g in (grads_b, grads_a)])
+    grad_v_sum = grad_v_sum + jnp.sum(far_v.astype(F32), axis=0)
     ffn_sums = jnp.sum(sums_ffn.reshape(3, 8, full), axis=1)
     back_sums = jnp.sum(sums_back.reshape(5, 8, full), axis=1)
     up_bias_part = jnp.sum(sums_up, axis=0)
@@ -1398,6 +1506,12 @@
     by_layer = jnp.take(by_layer, order_of, axis=0)
     wide = by_layer.shape[1]
     by_layer = jnp.pad(by_layer, ((0, 0), (0, -wide % full))).reshape(-1, full)
+    input_grad, table_part, gain_one, shift_one = meet(
+        [flow_qb, flow_qa, flow_u], input_grad, table_part, gain_one, shift_one
+    )
+    drain(flow_u)
+    up_mine = flow_u.result.astype(BF16)
+    up_all = lax.all_gather(up_mine, "dp", axis=0)
     parts = jnp.concatenate(
         [
             jnp.stack([gain_one, back_sums[2], back_sums[0], ffn_sums[0]]),
@@ -1408,14 +1522,15 @@
         ]
     )
     flow_s = Flow(small_flow(parts))
-    drain(flow_s, flow_u, flow_d, flow_qa, flow_qb)
-    down_mine = sum(flow_d.result).astype(BF16)
-    down_grad = fill_ffn(lax.all_gather(down_mine, "dp", axis=0), True)
-    up_mine = sum(flow_u.result).astype(BF16)
-    up_grad = fill_ffn(lax.all_gather(up_mine, "dp", axis=0), False)
-    mine = sum(flow_qa.result + flow_qb.result).astype(BF16)
+    drain(flow_qa, flow_qb)
+    mine = (flow_qa.result + flow_qb.result).astype(BF16)
     flow_o = Flow(spread_flow((mine[:, : 2 * width], mine[:, 2 * width :])))
-    drain(flow_o)
+    for _ in range(2 * stages):
+        flow_o.move(flow_o.held)
+    down_grad = fill_ffn(down_all, True)
+    up_grad = fill_ffn(up_all, False)
+    down_grad, up_grad = begin([flow_o], down_grad, up_grad)
+    drain(flow_o, flow_s)
     qkv_grad, out_grad = fill_attention(flow_o.result, full, width, device)
 
     parts = flow_s.result
@@ -1444,8 +1559,7 @@
     )
 
 
-def rows_back(far_a, far_b, rows, blocks):
-    value = (far_a.astype(F32) + far_b.astype(F32)).astype(BF16)
+def rows_back(value, rows, blocks):
     (value,) = yield (value,)
     return (
         yield tuple(swap(value[(m - 1) * rows : m * rows], "mp", m) for m in range(1, blocks))

time: 534 us -> 477 us (0.89)
  other arithmetic: 40.1 us -> 17.3 us
  starting transfers between devices: 90.5 us -> 68.5 us
  waiting for transfers between devices: 123 us -> 106 us
    ppermute x77 -> x75, starting transfers between devices: 90.4 us -> 68.2 us  [swap(): return lax.ppermute(value, axis, [(i, i ^ mask) for i in range(count)])]
    convert_element_type x19 -> x6, other arithmetic: 22.8 us -> 4 us  [the longest x1 1.75 us: on_device(): down_mine = flow_d.result.astype(BF16)]
    ppermute x77 -> x75, waiting for transfers between devices: 123 us -> 106 us  [swap(): return lax.ppermute(value, axis, [(i, i ^ mask) for i in range(count)])]
    pallas_call x4 -> x14, Pallas kernels: 58.6 us -> 70.6 us  [the longest x3 41.1 us: attend_back(): pl.pallas_call(functools.partial(attend_back_kernel, causal), grid=(count...]
    pallas_call x2, Pallas kernels: 24.5 us -> 18.6 us  [attend(): pl.pallas_call(functools.partial(attend_kernel, span // rows, rows), grid...]
    unnamed x226 -> x282, local copies, waits for them, and re-layouts: 25.8 us -> 28.7 us
  transfers between devices with their start and end apart: 79 -> 77, of which waited for: 27 -> 31; matrix products, arithmetic and copies ran while one was open for 9% -> 6% of each run, Pallas kernels for 32% -> 35%
where the time goes in v3:
time: 477 us; the launch traced here: 472 us
  Pallas kernels  215 us (45%)
  waiting for transfers between devices  106 us (22%)
  starting transfers between devices  68.5 us (14%)
  local copies, waits for them, and re-layouts  44.9 us (9%)
  other arithmetic  17.3 us (4%)
  between operations  16.3 us (3%)
    ppermute x75, waiting for transfers between devices, swap(): return lax.ppermute(value, axis, [(i, i ^ mask) for i in range(count)])  106 us
    ppermute x75, starting transfers between devices, swap(): return lax.ppermute(value, axis, [(i, i ^ mask) for i in range(count)])  68.2 us
    pallas_call x3, Pallas kernels, attend_back(): pl.pallas_call(functools.partial(attend_back_kernel, causal), grid=(count...  41.1 us
    unnamed x282, local copies, waits for them, and re-layouts  28.7 us
    pallas_call x1, Pallas kernels, feed_back(): pl.pallas_call(functools.partial(back_kernel, group_a, group_u, group_d),...  26 us
    pallas_call x3, Pallas kernels, unproject(): pl.pallas_call(functools.partial(unproject_kernel, group, which, begin, c...  21 us
    pallas_call x1, Pallas kernels, feed_up(): pl.pallas_call(functools.partial(up_kernel, group_a, group_u), grid_spec=...  20.8 us
    pallas_call x2, Pallas kernels, attend(): pl.pallas_call(functools.partial(attend_kernel, span // rows, rows), grid...  18.6 us
  transfers between devices with their start and end apart: 77, of which 31 were waited for; matrix products, arithmetic and copies ran while one was open for 6% of the time, Pallas kernels for 35%

profile of v3, /device:TPU:0, one launch (start us, length us, event | category | flops | bytes accessed | tf_op | source)
XLA Modules:
  0.0 471.6 jit_solution(719051880648352054)
XLA Ops:
  11.3 3.0 collective-permute-start
  14.3 2.6 collective-permute-start.1
  19.3 2.2 dynamic-slice_bitcast_fusion
  21.9 4.9 %collective-permute-done = bf16[528,256]{1,0:T(8,128)(2,1)} collective-permute-done((bf16[528,256]{1,0:T(8,128)(2,1)}, bf16[528,256]{1,0:T(8,128)(2,1)}, u32[]{:S(2)}, u32[]{:S(2)}) %collective-permute-start) | collective-permute-done | bytes 270368 | tf_op jit(solution)/shard_map/ppermute | solution.py:25
  26.8 2.6 collective-permute-done.1
  31.8 4.3 collective-permute-done.2
  41.3 3.6 collective-permute-done.3
  44.9 2.7 collective-permute-done.4
  50.9 3.3 collective-permute-start.8
  54.3 20.5 %collective-permute-done.7 = bf16[128,1024]{1,0:T(8,128)(2,1)} collective-permute-done((bf16[128,1024]{1,0:T(8,128)(2,1)}, bf16[128,1024]{1,0:T(8,128)(2,1)}, u32[]{:S(2)}, u32[]{:S(2)}) %collective-permute-start.7) | collective-permute-done | bytes 262176 | tf_op jit(solution)/shard_map/ppermute | solution.py:25
  79.6 6.9 %collective-permute-done.14 = bf16[128,1024]{1,0:T(8,128)(2,1)} collective-permute-done((bf16[128,1024]{1,0:T(8,128)(2,1)}, bf16[128,1024]{1,0:T(8,128)(2,1)}, u32[]{:S(2)}, u32[]{:S(2)}) %collective-permute-start.14) | collective-permute-done | bytes 262176 | tf_op jit(solution)/shard_map/ppermute | solution.py:25
  93.6 11.1 %project.1 = (bf16[544,1024]{1,0:T(8,128)(2,1)}, bf16[1088,1024]{1,0:T(8,128)(2,1)}, bf16[1088,1024]{1,0:T(8,128)(2,1)}) custom-call(s32[1]{0:T(128)} %bitcast.scal, bf16[544,1024]{1,0:T(8,128)(2,1)} %collective-permute-done.9.refs_0_, bf16[544,1024]{1,0:T(8,128)(2,1)} %copy-done.9, f32[8,1024]{1,0:T(8,128)S(1)} %pad.28.refs_2_, ...), custom_call_target="tpu_custom_call" | custom-call | flops 1000 | bytes 1000 | tf_op jit(solution)/shard_map/project/pallas_call | solution.py:483
  110.9 9.3 %attend.2 = (bf16[544,512]{1,0:T(8,128)(2,1)S(1)}, bf16[544,512]{1,0:T(8,128)(2,1)S(1)}) custom-call(bf16[544,1024]{1,0:T(8,128)(2,1)S(1)} %copy-done.19, bf16[1088,1024]{1,0:T(8,128)(2,1)S(1)} %copy-done.5, bf16[1088,1024]{1,0:T(8,128)(2,1)} %get-tuple-element.364.v_ref, bf16[1088,128]{1,0:T(8,128)(2,1)S(1)} %select_convert_fusion.kc_ref), custom_call_target="tpu_custom_call" | custom-call | flops 1000 | bytes 1000 | tf_op jit(solution)/shard_map/attend/pallas_call | solution.py:130
  121.5 9.3 %attend.3 = (bf16[544,512]{1,0:T(8,128)(2,1)S(1)}, bf16[544,512]{1,0:T(8,128)(2,1)S(1)}) custom-call(bf16[544,1024]{1,0:T(8,128)(2,1)S(1)} %copy-done.19, bf16[1088,1024]{1,0:T(8,128)(2,1)S(1)} %copy-done.5, bf16[1088,1024]{1,0:T(8,128)(2,1)} %get-tuple-element.364.v_ref, bf16[1088,128]{1,0:T(8,128)(2,1)S(1)} %select_convert_fusion.kc_ref), custom_call_target="tpu_custom_call" | custom-call | flops 1000 | bytes 1000 | tf_op jit(solution)/shard_map/attend/pallas_call | solution.py:130
  130.9 3.9 collective-permute-done.22
  141.1 20.8 %feed_up.1 = (f32[544,1024]{1,0:T(8,128)}, f32[544,1024]{1,0:T(8,128)}, bf16[544,1024]{1,0:T(8,128)(2,1)}, bf16[544,4096]{1,0:T(8,128)(2,1)}, bf16[544,4096]{1,0:T(8,128)(2,1)}) custom-call(s32[1]{0:T(128)} %bitcast.scal, bf16[544,512]{1,0:T(8,128)(2,1)} %copy-done.60, bf16[544,512]{1,0:T(8,128)(2,1)} %copy-done.62, f32[544,1024]{1,0:T(8,128)} %copy-done.110, ...), custom_call_target="tpu_custom_call" | custom-call | flops 1000 | bytes 1000 | tf_op jit(solution)/shard_map/feed_up/pallas_call | solution.py:567
  168.6 13.4 %feed_down.1 = (bf16[544,1024]{1,0:T(8,128)(2,1)}, bf16[544,1024]{1,0:T(8,128)(2,1)}, f32[24,1024]{1,0:T(8,128)S(1)}) custom-call(s32[1]{0:T(128)} %bitcast.scal, bf16[544,4096]{1,0:T(8,128)(2,1)} %get-tuple-element.404.refs_0_.right_ref, f32[544,1024]{1,0:T(8,128)} %get-tuple-element.405.refs_1_.refs_3_, bf16[544,1024]{1,0:T(8,128)(2,1)} %refs_4_.7, ...), custom_call_target="tpu_custom_call" | custom-call | flops 1000 | bytes 1000 | tf_op jit(solution)/shard_map/feed_down/pallas_call | solution.py:657
  183.3 4.7 other_half.2
  188.2 7.0 %collective-permute-done.34.got_ref = bf16[512,4096]{1,0:T(8,128)(2,1)S(1)} collective-permute-done((bf16[512,4096]{1,0:T(8,128)(2,1)S(1)}, bf16[512,4096]{1,0:T(8,128)(2,1)S(1)}, u32[]{:S(2)}, u32[]{:S(2)}) %collective-permute-start.34) | collective-permute-done | bytes 4194336 | tf_op jit(solution)/shard_map/ppermute | solution.py:25
  195.2 6.2 %this_half.2 = (bf16[2,128,2048]{2,1,0:T(8,128)(2,1)}, bf16[2,128,2048]{2,1,0:T(8,128)(2,1)S(1)}, bf16[2,128,2048]{2,1,0:T(8,128)(2,1)S(1)}, bf16[2,128,2048]{2,1,0:T(8,128)(2,1)S(1)}) custom-call(s32[1]{0:T(128)} %bitcast.scal, bf16[544,1024]{1,0:T(8,128)(2,1)S(1)} %copy-done.28, bf16[544,4096]{1,0:T(8,128)(2,1)S(1)} %copy-done.6, ...), custom_call_target="tpu_custom_call" | custom-call | flops 1000 | bytes 1000 | tf_op jit(solution)/shard_map/this_half/pallas_call | solution.py:946
  203.3 26.0 %feed_back.1 = (bf16[544,4096]{1,0:T(8,128)(2,1)}, f32[544,1024]{1,0:T(8,128)}, bf16[544,1024]{1,0:T(8,128)(2,1)}, bf16[544,1024]{1,0:T(8,128)(2,1)}, f32[40,1024]{1,0:T(8,128)}, /*index=5*/f32[8,4096]{1,0:T(8,128)}) custom-call(s32[1]{0:T(128)} %bitcast.scal, bf16[544,1024]{1,0:T(8,128)(2,1)} %get-tuple-element.418.left_ref.refs_0_, ...), custom_call_target="tpu_custom_call" | custom-call | flops 1000 | bytes 1000 | tf_op jit(solution)/shard_map/feed_back/pallas_call | solution.py:773
  232.5 5.4 %other_half.3 = bf16[512,4096]{1,0:T(8,128)(2,1)} custom-call(s32[1]{0:T(128)} %bitcast.scal, bf16[544,1024]{1,0:T(8,128)(2,1)S(1)} %copy-done.50, bf16[544,4096]{1,0:T(8,128)(2,1)S(1)} %bitcast.119), custom_call_target="tpu_custom_call" | custom-call | flops 1000 | bytes 1000 | tf_op jit(solution)/shard_map/other_half/pallas_call | solution.py:917
  242.3 20.3 %attend_back.3 = (f32[544,1024]{1,0:T(8,128)}, bf16[544,1024]{1,0:T(8,128)(2,1)S(1)}, bf16[544,1024]{1,0:T(8,128)(2,1)}) custom-call(bf16[544,1024]{1,0:T(8,128)(2,1)} %get-tuple-element.372.q_ref, bf16[1088,1024]{1,0:T(8,128)(2,1)} %get-tuple-element.363.k_ref, bf16[1088,1024]{1,0:T(8,128)(2,1)} %get-tuple-element.364.v_ref, ...), custom_call_target="tpu_custom_call" | custom-call | flops 1000 | bytes 1000 | tf_op jit(solution)/shard_map/attend_back/pallas_call | solution.py:223
  263.7 7.9 %unproject.3 = bf16[544,1024]{1,0:T(8,128)(2,1)} custom-call(s32[1]{0:T(128)} %bitcast.scal, bf16[544,1024]{1,0:T(8,128)(2,1)} %copy-done.20, bf16[544,1024]{1,0:T(8,128)(2,1)} %get-tuple-element.479.refs_1_.refs_7_, bf16[3,1024,256]{2,1,0:T(8,128)(2,1)} %refs_4_.9, bf16[256,1024]{1,0:T(8,128)(2,1)S(1)} %copy-done.24, ...), custom_call_target="tpu_custom_call" | custom-call | flops 1000 | bytes 1000 | tf_op jit(solution)/shard_map/unproject/pallas_call | solution.py:858
  271.7 7.4 %this_half.3 = (bf16[2,128,2048]{2,1,0:T(8,128)(2,1)}, bf16[2,128,2048]{2,1,0:T(8,128)(2,1)S(1)}, bf16[2,128,2048]{2,1,0:T(8,128)(2,1)}, bf16[2,128,2048]{2,1,0:T(8,128)(2,1)S(1)}) custom-call(s32[1]{0:T(128)} %bitcast.scal, bf16[544,1024]{1,0:T(8,128)(2,1)S(1)} %copy-done.50, bf16[544,4096]{1,0:T(8,128)(2,1)S(1)} %bitcast.121, ...), custom_call_target="tpu_custom_call" | custom-call | flops 1000 | bytes 1000 | tf_op jit(solution)/shard_map/this_half/pallas_call | solution.py:946
  284.6 10.4 %attend_back.4 = (bf16[544,512]{1,0:T(8,128)(2,1)S(1)}, bf16[544,512]{1,0:T(8,128)(2,1)S(1)}, bf16[544,512]{1,0:T(8,128)(2,1)S(1)}) custom-call(bf16[544,1024]{1,0:T(8,128)(2,1)} %get-tuple-element.372.q_ref, bf16[1088,1024]{1,0:T(8,128)(2,1)} %get-tuple-element.363.k_ref, bf16[1088,1024]{1,0:T(8,128)(2,1)} %get-tuple-element.364.v_ref, ...), custom_call_target="tpu_custom_call" | custom-call | flops 1000 | bytes 1000 | tf_op jit(solution)/shard_map/attend_back/pallas_call | solution.py:223
  295.1 5.7 %attention_other.2 = bf16[512,2048]{1,0:T(8,128)(2,1)} custom-call(s32[1]{0:T(128)} %bitcast.scal, bf16[544,1024]{1,0:T(8,128)(2,1)} %collective-permute-done.9.refs_0_, bf16[544,1024]{1,0:T(8,128)(2,1)S(1)} %copy-done.10, bf16[544,1024]{1,0:T(8,128)(2,1)S(1)} %copy-done.25, bf16[544,512]{1,0:T(8,128)(2,1)S(1)} %get-tuple-element.591.refs_3_.refs_0_, ...), custom_call_target="tpu_custom_call" | custom-call | flops 1000 | bytes 1000 | tf_op jit(solution)/shard_map/attention_other/pallas_call | solution.py:1030
  300.8 5.9 %collective-permute-done.40.refs_1_.refs_3_ = bf16[2,128,2048]{2,1,0:T(8,128)(2,1)} collective-permute-done((bf16[2,128,2048]{2,1,0:T(8,128)(2,1)}, bf16[2,128,2048]{2,1,0:T(8,128)(2,1)}, u32[]{:S(2)}, u32[]{:S(2)}) %collective-permute-start.40) | collective-permute-done | bytes 1048608 | tf_op jit(solution)/shard_map/ppermute | solution.py:25
  307.9 2.8 next_stage.5
  314.3 6.0 %unproject.4.refs_3_ = f32[544,1024]{1,0:T(8,128)} custom-call(s32[1]{0:T(128)} %bitcast.scal, bf16[544,512]{1,0:T(8,128)(2,1)S(1)} %get-tuple-element.591.refs_3_.refs_0_, bf16[544,512]{1,0:T(8,128)(2,1)S(1)} %get-tuple-element.482.refs_4_.refs_1_, bf16[544,512]{1,0:T(8,128)(2,1)S(1)} %copy-done.36, bf16[3,1024,256]{2,1,0:T(8,128)(2,1)} %refs_4_.9, ...), custom_call_target="tpu_custom_call" | custom-call | flops 1000 | bytes 1000 | tf_op jit(solution)/shard_map/unproject/pallas_call | solution.py:858
  322.8 6.9 %attention_this.2 = (bf16[2,128,1024]{2,1,0:T(8,128)(2,1)}, bf16[2,128,1024]{2,1,0:T(8,128)(2,1)S(1)}, bf16[2,128,1024]{2,1,0:T(8,128)(2,1)}, bf16[2,128,1024]{2,1,0:T(8,128)(2,1)S(1)}) custom-call(s32[1]{0:T(128)} %bitcast.scal, bf16[544,1024]{1,0:T(8,128)(2,1)} %collective-permute-done.9.refs_0_, bf16[544,1024]{1,0:T(8,128)(2,1)S(1)} %copy-done.10, ...), custom_call_target="tpu_custom_call" | custom-call | flops 1000 | bytes 1000 | tf_op jit(solution)/shard_map/attention_this/pallas_call | solution.py:1049
  335.0 10.4 %attend_back.5 = (bf16[544,512]{1,0:T(8,128)(2,1)S(1)}, bf16[544,512]{1,0:T(8,128)(2,1)S(1)}, bf16[544,512]{1,0:T(8,128)(2,1)S(1)}) custom-call(bf16[544,1024]{1,0:T(8,128)(2,1)} %get-tuple-element.372.q_ref, bf16[1088,1024]{1,0:T(8,128)(2,1)} %get-tuple-element.363.k_ref, bf16[1088,1024]{1,0:T(8,128)(2,1)} %get-tuple-element.364.v_ref, ...), custom_call_target="tpu_custom_call" | custom-call | flops 1000 | bytes 1000 | tf_op jit(solution)/shard_map/attend_back/pallas_call | solution.py:223
  347.0 5.2 %attention_other.3 = bf16[512,2048]{1,0:T(8,128)(2,1)} custom-call(s32[1]{0:T(128)} %bitcast.scal, bf16[544,1024]{1,0:T(8,128)(2,1)} %collective-permute-done.9.refs_0_, bf16[544,1024]{1,0:T(8,128)(2,1)S(1)} %copy-done.10, bf16[544,1024]{1,0:T(8,128)(2,1)S(1)} %copy-done.26, bf16[544,512]{1,0:T(8,128)(2,1)S(1)} %get-tuple-element.525.refs_3_.refs_0_, ...), custom_call_target="tpu_custom_call" | custom-call | flops 1000 | bytes 1000 | tf_op jit(solution)/shard_map/attention_other/pallas_call | solution.py:1030
  362.0 7.1 %unproject.5 = f32[544,1024]{1,0:T(8,128)} custom-call(s32[1]{0:T(128)} %bitcast.scal, bf16[544,512]{1,0:T(8,128)(2,1)S(1)} %get-tuple-element.525.refs_3_.refs_0_, bf16[544,512]{1,0:T(8,128)(2,1)S(1)} %get-tuple-element.526.refs_4_.refs_1_, bf16[544,512]{1,0:T(8,128)(2,1)S(1)} %get-tuple-element.527.refs_5_.refs_2_, f32[544,1024]{1,0:T(8,128)} %unproject.4.refs_3_, ...), custom_call_target="tpu_custom_call" | custom-call | flops 1000 | bytes 1000 | tf_op jit(solution)/shard_map/unproject/pallas_call | solution.py:858
  370.6 5.0 %collective-permute-done.53 = bf16[128,1024]{1,0:T(8,128)(2,1)S(1)} collective-permute-done((bf16[128,1024]{1,0:T(8,128)(2,1)S(1)}, bf16[128,1024]{1,0:T(8,128)(2,1)S(1)}, u32[]{:S(2)}, u32[]{:S(2)}) %collective-permute-start.53) | collective-permute-done | bytes 262176 | tf_op jit(solution)/shard_map/ppermute | solution.py:25
  381.4 6.3 %attention_this.3 = (bf16[2,128,1024]{2,1,0:T(8,128)(2,1)S(1)}, bf16[2,128,1024]{2,1,0:T(8,128)(2,1)S(1)}, bf16[2,128,1024]{2,1,0:T(8,128)(2,1)S(1)}, bf16[2,128,1024]{2,1,0:T(8,128)(2,1)S(1)}) custom-call(s32[1]{0:T(128)} %bitcast.scal, bf16[544,1024]{1,0:T(8,128)(2,1)} %collective-permute-done.9.refs_0_, bf16[544,1024]{1,0:T(8,128)(2,1)S(1)} %copy-done.10, ...), custom_call_target="tpu_custom_call" | custom-call | flops 1000 | bytes 1000 | tf_op jit(solution)/shard_map/attention_this/pallas_call | solution.py:1049
  392.8 2.4 multiply_reduce_fusion
  395.3 2.1 multiply_add_fusion
  399.7 3.2 collective-permute-done.56
  402.9 2.5 collective-permute-done.57
  416.2 2.5 collective-permute-done.59.got_a
  421.7 5.5 %collective-permute-done.71 = f32[34,1024]{1,0:T(8,128)S(1)} collective-permute-done((f32[34,1024]{1,0:T(8,128)S(1)}, f32[34,1024]{1,0:T(8,128)S(1)}, u32[]{:S(2)}, u32[]{:S(2)}) %collective-permute-start.71) | collective-permute-done | bytes 139296 | tf_op jit(solution)/shard_map/ppermute | solution.py:25
  434.7 4.1 collective-permute-done.64
  439.7 2.3 collective-permute-done.62
  443.0 6.7 %collective-permute-done.74 = f32[34,1024]{1,0:T(8,128)S(1)} collective-permute-done((f32[34,1024]{1,0:T(8,128)S(1)}, f32[34,1024]{1,0:T(8,128)S(1)}, u32[]{:S(2)}, u32[]{:S(2)}) %collective-permute-start.74) | collective-permute-done | bytes 139296 | tf_op jit(solution)/shard_map/ppermute | solution.py:25
  451.3 2.6 fill_ffn.2
  455.4 2.3 fill_ffn.3
  462.0 2.5 fill_attention.1
  (529 shorter events, 136.1 us)
Async XLA Ops:
  7.2 442.5 %all-gather.5.cloned.1.call-start = ((), (), s32[]{:S(2)}) async-start(), calls=%async_computation | async-start | bytes 2359296 | tf_op jit(solution)/shard_map/all_gather | solution.py:1487
  11.3 15.5 %collective-permute-start = (bf16[528,256]{1,0:T(8,128)(2,1)}, bf16[528,256]{1,0:T(8,128)(2,1)}, u32[]{:S(2)}, u32[]{:S(2)}) collective-permute-start(bf16[528,256]{1,0:T(8,128)(2,1)} %fusion.5), channel_id=1, source_target_pairs={{0,1},{1,0},{2,3},{3,2},{4,5},{5,4},{6,7},{7,6},{8,9},{9,8},{10,11... | collective-permute-start | bytes 811016 | tf_op jit(solution)/shard_map/ppermute | solution.py:25
  14.3 15.0 %collective-permute-start.1 = (bf16[528,256]{1,0:T(8,128)(2,1)}, bf16[528,256]{1,0:T(8,128)(2,1)}, u32[]{:S(2)}, u32[]{:S(2)}) collective-permute-start(bf16[528,256]{1,0:T(8,128)(2,1)} %fusion.5), channel_id=1, source_target_pairs={{0,2},{1,3},{2,0},{3,1},{4,6},{5,7},{6,4},{7,5},{8,10},{9,11},{10,... | collective-permute-start | bytes 811016 | tf_op jit(solution)/shard_map/ppermute | solution.py:25
  40.0 34.8 %collective-permute-start.9 = (bf16[544,1024]{1,0:T(8,128)(2,1)S(1)}, bf16[544,1024]{1,0:T(8,128)(2,1)}, u32[]{:S(2)}, u32[]{:S(2)}) collective-permute-start(bf16[544,1024]{1,0:T(8,128)(2,1)S(1)} %add_convert_fusion.refs_1_), channel_id=1, source_target_pairs={{0,1},{1,0},{2,3},{3,2},{4,5},{5,4},{6,7},{7,6},{8,9},{9,8},{10,11... | collective-permute-start | bytes 3342344 | tf_op jit(solution)/shard_map/ppermute | solution.py:25
  47.8 27.0 %collective-permute-start.5 = (bf16[2,3,4,64,256]{4,3,2,1,0:T(8,128)(2,1)S(1)}, bf16[2,3,4,64,256]{4,3,2,1,0:T(8,128)(2,1)S(1)}, u32[]{:S(2)}, u32[]{:S(2)}) collective-permute-start(bf16[2,3,4,64,256]{4,3,2,1,0:T(8,128)(2,1)S(1)} %pad_maximum_fusion.1.refs_5_.refs_7_.refs_8_.refs_4_.refs_6_), channel_id=1, source_target_pairs={{0,16},{4,20},{8,24},{12,28},{16,0},{20,4},{24,8},{28,12},{1,17},{... | collective-permute-start | bytes 2359304 | tf_op jit(solution)/shard_map/ppermute | solution.py:25
  49.4 25.4 %collective-permute-start.6 = (bf16[2,3,4,64,256]{4,3,2,1,0:T(8,128)(2,1)S(1)}, bf16[2,3,4,64,256]{4,3,2,1,0:T(8,128)(2,1)}, u32[]{:S(2)}, u32[]{:S(2)}) collective-permute-start(bf16[2,3,4,64,256]{4,3,2,1,0:T(8,128)(2,1)S(1)} %pad_maximum_fusion.2.refs_7_.refs_9_.refs_10_.refs_6_.refs_8_), channel_id=1, source_target_pairs={{0,8},{4,12},{8,0},{12,4},{16,24},{20,28},{24,16},{28,20},{1,9},{5... | collective-permute-start | bytes 2359304 | tf_op jit(solution)/shard_map/ppermute | solution.py:25
  49.9 24.9 %collective-permute-start.7 = (bf16[128,1024]{1,0:T(8,128)(2,1)}, bf16[128,1024]{1,0:T(8,128)(2,1)}, u32[]{:S(2)}, u32[]{:S(2)}) collective-permute-start(bf16[128,1024]{1,0:T(8,128)(2,1)} %bitcast.12), channel_id=1, source_target_pairs={{0,1},{1,0},{2,3},{3,2},{4,5},{5,4},{6,7},{7,6},{8,9},{9,8},{10,11... | collective-permute-start | bytes 786440 | tf_op jit(solution)/shard_map/ppermute | solution.py:25
  50.9 23.8 %collective-permute-start.8 = (bf16[128,1024]{1,0:T(8,128)(2,1)}, bf16[128,1024]{1,0:T(8,128)(2,1)}, u32[]{:S(2)}, u32[]{:S(2)}) collective-permute-start(bf16[128,1024]{1,0:T(8,128)(2,1)} %bitcast.12), channel_id=1, source_target_pairs={{0,2},{1,3},{2,0},{3,1},{4,6},{5,7},{6,4},{7,5},{8,10},{9,11},{10,... | collective-permute-start | bytes 786440 | tf_op jit(solution)/shard_map/ppermute | solution.py:25
  74.8 11.7 %collective-permute-start.10 = (bf16[2,3,4,64,256]{4,3,2,1,0:T(8,128)(2,1)S(1)}, bf16[2,3,4,64,256]{4,3,2,1,0:T(8,128)(2,1)S(1)}, u32[]{:S(2)}, u32[]{:S(2)}) collective-permute-start(bf16[2,3,4,64,256]{4,3,2,1,0:T(8,128)(2,1)S(1)} %pad_maximum_fusion.1.refs_5_.refs_7_.refs_8_.refs_4_.refs_6_), channel_id=1, source_target_pairs={{0,4},{4,0},{8,12},{12,8},{16,20},{20,16},{24,28},{28,24},{1,5},{5... | collective-permute-start | bytes 2359304 | tf_op jit(solution)/shard_map/ppermute | solution.py:25
  74.9 11.6 %collective-permute-start.11 = (bf16[2,3,4,64,256]{4,3,2,1,0:T(8,128)(2,1)S(1)}, bf16[2,3,4,64,256]{4,3,2,1,0:T(8,128)(2,1)}, u32[]{:S(2)}, u32[]{:S(2)}) collective-permute-start(bf16[2,3,4,64,256]{4,3,2,1,0:T(8,128)(2,1)S(1)} %collective-permute-done.5.refs_6_.refs_8_.refs_9_.refs_5_.refs_7_), channel_id=1, source_target_pairs={{0,4},{4,0},{8,12},{12,8},{16,20},{20,16},{24,28},{28,24},{1,5},{5... | collective-permute-start | bytes 2359304 | tf_op jit(solution)/shard_map/ppermute | solution.py:25
  75.4 11.1 %collective-permute-start.12 = (bf16[2,3,4,64,256]{4,3,2,1,0:T(8,128)(2,1)S(1)}, bf16[2,3,4,64,256]{4,3,2,1,0:T(8,128)(2,1)}, u32[]{:S(2)}, u32[]{:S(2)}) collective-permute-start(bf16[2,3,4,64,256]{4,3,2,1,0:T(8,128)(2,1)S(1)} %pad_maximum_fusion.2.refs_7_.refs_9_.refs_10_.refs_6_.refs_8_), channel_id=1, source_target_pairs={{0,4},{4,0},{8,12},{12,8},{16,20},{20,16},{24,28},{28,24},{1,5},{5... | collective-permute-start | bytes 2359304 | tf_op jit(solution)/shard_map/ppermute | solution.py:25
  75.5 11.1 %collective-permute-start.13 = (bf16[2,3,4,64,256]{4,3,2,1,0:T(8,128)(2,1)}, bf16[2,3,4,64,256]{4,3,2,1,0:T(8,128)(2,1)}, u32[]{:S(2)}, u32[]{:S(2)}) collective-permute-start(bf16[2,3,4,64,256]{4,3,2,1,0:T(8,128)(2,1)} %collective-permute-done.6.refs_8_.refs_10_.refs_11_.refs_7_.refs_9_), channel_id=1, source_target_pairs={{0,4},{4,0},{8,12},{12,8},{16,20},{20,16},{24,28},{28,24},{1,5},{5... | collective-permute-start | bytes 2359304 | tf_op jit(solution)/shard_map/ppermute | solution.py:25
  88.1 16.7 %collective-permute-start.17 = (bf16[1,3,1,64,1024]{4,3,1,2,0:T(8,128)(2,1)S(1)}, bf16[1,3,1,64,1024]{4,3,1,2,0:T(8,128)(2,1)S(1)}, u32[]{:S(2)}, u32[]{:S(2)}) collective-permute-start(bf16[1,3,1,64,1024]{4,3,1,2,0:T(8,128)(2,1)S(1)} %get-tuple-element.354), channel_id=1, source_target_pairs={{0,8},{4,12},{8,0},{12,4},{16,24},{20,28},{24,16},{28,20},{1,9},{5... | collective-permute-start | bytes 1179656 | tf_op jit(solution)/shard_map/ppermute | solution.py:25
  88.7 16.1 %collective-permute-start.18 = (bf16[1,3,1,64,1024]{4,3,2,1,0:T(8,128)(2,1)S(1)}, bf16[1,3,1,64,1024]{4,3,2,1,0:T(8,128)(2,1)S(1)}, u32[]{:S(2)}, u32[]{:S(2)}) collective-permute-start(bf16[1,3,1,64,1024]{4,3,2,1,0:T(8,128)(2,1)S(1)} %get-tuple-element.355), channel_id=1, source_target_pairs={{0,16},{4,20},{8,24},{12,28},{16,0},{20,4},{24,8},{28,12},{1,17},{... | collective-permute-start | bytes 1179656 | tf_op jit(solution)/shard_map/ppermute | solution.py:25
  89.9 14.8 %collective-permute-start.15 = (bf16[128,1024]{1,0:T(8,128)(2,1)S(1)}, bf16[128,1024]{1,0:T(8,128)(2,1)S(1)}, u32[]{:S(2)}, u32[]{:S(2)}) collective-permute-start(bf16[128,1024]{1,0:T(8,128)(2,1)S(1)} %bitcast.142), channel_id=1, source_target_pairs={{0,1},{1,0},{2,3},{3,2},{4,5},{5,4},{6,7},{7,6},{8,9},{9,8},{10,11... | collective-permute-start | bytes 786440 | tf_op jit(solution)/shard_map/ppermute | solution.py:25
  90.8 14.0 %collective-permute-start.16 = (bf16[128,1024]{1,0:T(8,128)(2,1)S(1)}, bf16[128,1024]{1,0:T(8,128)(2,1)S(1)}, u32[]{:S(2)}, u32[]{:S(2)}) collective-permute-start(bf16[128,1024]{1,0:T(8,128)(2,1)S(1)} %bitcast.143), channel_id=1, source_target_pairs={{0,2},{1,3},{2,0},{3,1},{4,6},{5,7},{6,4},{7,5},{8,10},{9,11},{10,... | collective-permute-start | bytes 786440 | tf_op jit(solution)/shard_map/ppermute | solution.py:25
  105.8 14.4 %collective-permute-start.19 = (bf16[128,1024]{1,0:T(8,128)(2,1)S(1)}, bf16[128,1024]{1,0:T(8,128)(2,1)S(1)}, u32[]{:S(2)}, u32[]{:S(2)}) collective-permute-start(bf16[128,1024]{1,0:T(8,128)(2,1)S(1)} %collective-permute-done.16), channel_id=1, source_target_pairs={{0,1},{1,0},{2,3},{3,2},{4,5},{5,4},{6,7},{7,6},{8,9},{9,8},{10,11... | collective-permute-start | bytes 786440 | tf_op jit(solution)/shard_map/ppermute | solution.py:25
  107.6 27.2 %collective-permute-start.20 = (bf16[2,3,1,64,1024]{4,3,1,2,0:T(8,128)(2,1)S(1)}, bf16[2,3,1,64,1024]{4,3,1,2,0:T(8,128)(2,1)}, u32[]{:S(2)}, u32[]{:S(2)}) collective-permute-start(bf16[2,3,1,64,1024]{4,3,1,2,0:T(8,128)(2,1)S(1)} %pad_maximum_fusion.4), channel_id=1, source_target_pairs={{0,16},{4,20},{8,24},{12,28},{16,0},{20,4},{24,8},{28,12},{1,17},{... | collective-permute-start | bytes 2359304 | tf_op jit(solution)/shard_map/ppermute | solution.py:25
  109.2 25.7 %collective-permute-start.21 = (bf16[2,3,1,64,1024]{4,3,2,1,0:T(8,128)(2,1)}, bf16[2,3,1,64,1024]{4,3,2,1,0:T(8,128)(2,1)}, u32[]{:S(2)}, u32[]{:S(2)}) collective-permute-start(bf16[2,3,1,64,1024]{4,3,2,1,0:T(8,128)(2,1)} %pad_maximum_fusion.5.refs_18_.refs_19_), channel_id=1, source_target_pairs={{0,8},{4,12},{8,0},{12,4},{16,24},{20,28},{24,16},{28,20},{1,9},{5... | collective-permute-start | bytes 2359304 | tf_op jit(solution)/shard_map/ppermute | solution.py:25
  120.4 14.4 %collective-permute-start.22 = (bf16[1,3,1,64,1024]{4,3,1,2,0:T(8,128)(2,1)S(1)}, bf16[1,3,1,64,1024]{4,3,1,2,0:T(8,128)(2,1)S(1)}, u32[]{:S(2)}, u32[]{:S(2)}) collective-permute-start(bf16[1,3,1,64,1024]{4,3,1,2,0:T(8,128)(2,1)S(1)} %get-tuple-element.376), channel_id=1, source_target_pairs={{0,8},{4,12},{8,0},{12,4},{16,24},{20,28},{24,16},{28,20},{1,9},{5... | collective-permute-start | bytes 1179656 | tf_op jit(solution)/shard_map/ppermute | solution.py:25
  121.0 13.8 %collective-permute-start.23 = (bf16[1,3,1,64,1024]{4,3,2,1,0:T(8,128)(2,1)S(1)}, bf16[1,3,1,64,1024]{4,3,2,1,0:T(8,128)(2,1)S(1)}, u32[]{:S(2)}, u32[]{:S(2)}) collective-permute-start(bf16[1,3,1,64,1024]{4,3,2,1,0:T(8,128)(2,1)S(1)} %get-tuple-element.377), channel_id=1, source_target_pairs={{0,16},{4,20},{8,24},{12,28},{16,0},{20,4},{24,8},{28,12},{1,17},{... | collective-permute-start | bytes 1179656 | tf_op jit(solution)/shard_map/ppermute | solution.py:25
  136.1 25.8 %collective-permute-start.28 = (bf16[2,3,1,64,1024]{4,3,1,2,0:T(8,128)(2,1)S(1)}, bf16[2,3,1,64,1024]{4,3,1,2,0:T(8,128)(2,1)S(1)}, u32[]{:S(2)}, u32[]{:S(2)}) collective-permute-start(bf16[2,3,1,64,1024]{4,3,1,2,0:T(8,128)(2,1)S(1)} %pad_maximum_fusion.7), channel_id=1, source_target_pairs={{0,16},{4,20},{8,24},{12,28},{16,0},{20,4},{24,8},{28,12},{1,17},{... | collective-permute-start | bytes 2359304 | tf_op jit(solution)/shard_map/ppermute | solution.py:25
  137.7 24.2 %collective-permute-start.29 = (bf16[2,3,1,64,1024]{4,3,2,1,0:T(8,128)(2,1)S(1)}, bf16[2,3,1,64,1024]{4,3,2,1,0:T(8,128)(2,1)S(1)}, u32[]{:S(2)}, u32[]{:S(2)}) collective-permute-start(bf16[2,3,1,64,1024]{4,3,2,1,0:T(8,128)(2,1)S(1)} %pad_maximum_fusion.8.refs_7_.refs_28_), channel_id=1, source_target_pairs={{0,8},{4,12},{8,0},{12,4},{16,24},{20,28},{24,16},{28,20},{1,9},{5... | collective-permute-start | bytes 2359304 | tf_op jit(solution)/shard_map/ppermute | solution.py:25
  201.3 28.0 %collective-permute-start.35 = (bf16[2,128,2048]{2,1,0:T(8,128)(2,1)}, bf16[2,128,2048]{2,1,0:T(8,128)(2,1)S(1)}, u32[]{:S(2)}, u32[]{:S(2)}) collective-permute-start(bf16[2,128,2048]{2,1,0:T(8,128)(2,1)} %get-tuple-element.427), channel_id=1, source_target_pairs={{0,8},{4,12},{8,0},{12,4},{16,24},{20,28},{24,16},{28,20},{1,9},{5... | collective-permute-start | bytes 3145736 | tf_op jit(solution)/shard_map/ppermute | solution.py:25
  202.8 26.5 %collective-permute-start.36 = (bf16[2,128,2048]{2,1,0:T(8,128)(2,1)S(1)}, bf16[2,128,2048]{2,1,0:T(8,128)(2,1)S(1)}, u32[]{:S(2)}, u32[]{:S(2)}) collective-permute-start(bf16[2,128,2048]{2,1,0:T(8,128)(2,1)S(1)} %get-tuple-element.428), channel_id=1, source_target_pairs={{0,16},{4,20},{8,24},{12,28},{16,0},{20,4},{24,8},{28,12},{1,17},{... | collective-permute-start | bytes 3145736 | tf_op jit(solution)/shard_map/ppermute | solution.py:25
  237.9 33.7 %collective-permute-start.39 = (bf16[512,4096]{1,0:T(8,128)(2,1)}, bf16[512,4096]{1,0:T(8,128)(2,1)}, u32[]{:S(2)}, u32[]{:S(2)}) collective-permute-start(bf16[512,4096]{1,0:T(8,128)(2,1)} %other_half.3), channel_id=1, source_target_pairs={{0,4},{4,0},{8,12},{12,8},{16,20},{20,16},{24,28},{28,24},{1,5},{5... | collective-permute-start | bytes 12582920 | tf_op jit(solution)/shard_map/ppermute | solution.py:25
  237.9 33.7 %collective-permute-start.37 = (bf16[128,2048]{1,0:T(8,128)(2,1)}, bf16[128,2048]{1,0:T(8,128)(2,1)S(1)}, u32[]{:S(2)}, u32[]{:S(2)}) collective-permute-start(bf16[128,2048]{1,0:T(8,128)(2,1)} %get-tuple-element.446), channel_id=1, source_target_pairs={{0,16},{4,20},{8,24},{12,28},{16,0},{20,4},{24,8},{28,12},{1,17},{... | collective-permute-start | bytes 1572872 | tf_op jit(solution)/shard_map/ppermute | solution.py:25
  239.5 32.1 %collective-permute-start.38 = (bf16[128,2048]{1,0:T(8,128)(2,1)}, bf16[128,2048]{1,0:T(8,128)(2,1)S(1)}, u32[]{:S(2)}, u32[]{:S(2)}) collective-permute-start(bf16[128,2048]{1,0:T(8,128)(2,1)} %get-tuple-element.447), channel_id=1, source_target_pairs={{0,8},{4,12},{8,0},{12,4},{16,24},{20,28},{24,16},{28,20},{1,9},{5... | collective-permute-start | bytes 1572872 | tf_op jit(solution)/shard_map/ppermute | solution.py:25
  281.0 26.9 %collective-permute-start.42 = (bf16[544,1024]{1,0:T(8,128)(2,1)}, bf16[544,1024]{1,0:T(8,128)(2,1)}, u32[]{:S(2)}, u32[]{:S(2)}) collective-permute-start(bf16[544,1024]{1,0:T(8,128)(2,1)} %unproject.3), channel_id=1, source_target_pairs={{0,1},{1,0},{2,3},{3,2},{4,5},{5,4},{6,7},{7,6},{8,9},{9,8},{10,11... | collective-permute-start | bytes 3342344 | tf_op jit(solution)/shard_map/ppermute | solution.py:25
  281.7 25.0 %collective-permute-start.40 = (bf16[2,128,2048]{2,1,0:T(8,128)(2,1)}, bf16[2,128,2048]{2,1,0:T(8,128)(2,1)}, u32[]{:S(2)}, u32[]{:S(2)}) collective-permute-start(bf16[2,128,2048]{2,1,0:T(8,128)(2,1)} %get-tuple-element.460), channel_id=1, source_target_pairs={{0,8},{4,12},{8,0},{12,4},{16,24},{20,28},{24,16},{28,20},{1,9},{5... | collective-permute-start | bytes 3145736 | tf_op jit(solution)/shard_map/ppermute | solution.py:25
  283.1 24.7 %collective-permute-start.41 = (bf16[2,128,2048]{2,1,0:T(8,128)(2,1)}, bf16[2,128,2048]{2,1,0:T(8,128)(2,1)}, u32[]{:S(2)}, u32[]{:S(2)}) collective-permute-start(bf16[2,128,2048]{2,1,0:T(8,128)(2,1)} %get-tuple-element.461), channel_id=1, source_target_pairs={{0,16},{4,20},{8,24},{12,28},{16,0},{20,4},{24,8},{28,12},{1,17},{... | collective-permute-start | bytes 3145736 | tf_op jit(solution)/shard_map/ppermute | solution.py:25
  312.5 33.0 %collective-permute-start.44 = (bf16[128,2048]{1,0:T(8,128)(2,1)}, bf16[128,2048]{1,0:T(8,128)(2,1)}, u32[]{:S(2)}, u32[]{:S(2)}) collective-permute-start(bf16[128,2048]{1,0:T(8,128)(2,1)} %get-tuple-element.501), channel_id=1, source_target_pairs={{0,16},{4,20},{8,24},{12,28},{16,0},{20,4},{24,8},{28,12},{1,17},{... | collective-permute-start | bytes 1572872 | tf_op jit(solution)/shard_map/ppermute | solution.py:25
  313.0 32.5 %collective-permute-start.45 = (bf16[128,2048]{1,0:T(8,128)(2,1)}, bf16[128,2048]{1,0:T(8,128)(2,1)}, u32[]{:S(2)}, u32[]{:S(2)}) collective-permute-start(bf16[128,2048]{1,0:T(8,128)(2,1)} %get-tuple-element.502), channel_id=1, source_target_pairs={{0,8},{4,12},{8,0},{12,4},{16,24},{20,28},{24,16},{28,20},{1,9},{5... | collective-permute-start | bytes 1572872 | tf_op jit(solution)/shard_map/ppermute | solution.py:25
  331.3 14.2 %collective-permute-start.48 = (bf16[2,128,1024]{2,1,0:T(8,128)(2,1)}, bf16[2,128,1024]{2,1,0:T(8,128)(2,1)}, u32[]{:S(2)}, u32[]{:S(2)}) collective-permute-start(bf16[2,128,1024]{2,1,0:T(8,128)(2,1)} %get-tuple-element.505), channel_id=1, source_target_pairs={{0,1},{1,0},{2,3},{3,2},{4,5},{5,4},{6,7},{7,6},{8,9},{9,8},{10,11... | collective-permute-start | bytes 1572872 | tf_op jit(solution)/shard_map/ppermute | solution.py:25
  332.0 13.7 %collective-permute-start.46 = (bf16[2,128,1024]{2,1,0:T(8,128)(2,1)}, bf16[2,128,1024]{2,1,0:T(8,128)(2,1)S(1)}, u32[]{:S(2)}, u32[]{:S(2)}) collective-permute-start(bf16[2,128,1024]{2,1,0:T(8,128)(2,1)} %get-tuple-element.503), channel_id=1, source_target_pairs={{0,8},{4,12},{8,0},{12,4},{16,24},{20,28},{24,16},{28,20},{1,9},{5... | collective-permute-start | bytes 1572872 | tf_op jit(solution)/shard_map/ppermute | solution.py:25
  333.5 13.5 %collective-permute-start.47 = (bf16[2,128,1024]{2,1,0:T(8,128)(2,1)}, bf16[2,128,1024]{2,1,0:T(8,128)(2,1)}, u32[]{:S(2)}, u32[]{:S(2)}) collective-permute-start(bf16[2,128,1024]{2,1,0:T(8,128)(2,1)} %get-tuple-element.504), channel_id=1, source_target_pairs={{0,16},{4,20},{8,24},{12,28},{16,0},{20,4},{24,8},{28,12},{1,17},{... | collective-permute-start | bytes 1572872 | tf_op jit(solution)/shard_map/ppermute | solution.py:25
  352.2 25.7 %collective-permute-start.49 = (bf16[512,2048]{1,0:T(8,128)(2,1)}, bf16[512,2048]{1,0:T(8,128)(2,1)}, u32[]{:S(2)}, u32[]{:S(2)}) collective-permute-start(bf16[512,2048]{1,0:T(8,128)(2,1)} %attention_other.3), channel_id=1, source_target_pairs={{0,4},{4,0},{8,12},{12,8},{16,20},{20,16},{24,28},{28,24},{1,5},{5... | collective-permute-start | bytes 6291464 | tf_op jit(solution)/shard_map/ppermute | solution.py:25
  357.2 20.0 %collective-permute-start.52 = (bf16[2,128,1024]{2,1,0:T(8,128)(2,1)S(1)}, bf16[2,128,1024]{2,1,0:T(8,128)(2,1)S(1)}, u32[]{:S(2)}, u32[]{:S(2)}) collective-permute-start(bf16[2,128,1024]{2,1,0:T(8,128)(2,1)S(1)} %get-tuple-element.535), channel_id=1, source_target_pairs={{0,1},{1,0},{2,3},{3,2},{4,5},{5,4},{6,7},{7,6},{8,9},{9,8},{10,11... | collective-permute-start | bytes 1572872 | tf_op jit(solution)/shard_map/ppermute | solution.py:25
  360.7 14.8 %collective-permute-start.53 = (bf16[128,1024]{1,0:T(8,128)(2,1)S(1)}, bf16[128,1024]{1,0:T(8,128)(2,1)S(1)}, u32[]{:S(2)}, u32[]{:S(2)}) collective-permute-start(bf16[128,1024]{1,0:T(8,128)(2,1)S(1)} %fusion.6), channel_id=1, source_target_pairs={{0,2},{1,3},{2,0},{3,1},{4,6},{5,7},{6,4},{7,5},{8,10},{9,11},{10,... | collective-permute-start | bytes 786440 | tf_op jit(solution)/shard_map/ppermute | solution.py:25
  379.7 74.1 %all-gather.7.cloned.1.call-start = ((), (), s32[]{:S(2)}) async-start(), calls=%async_computation.1 | async-start | bytes 2359296 | tf_op jit(solution)/shard_map/all_gather | solution.py:1514
  388.0 17.4 %collective-permute-start.54 = (bf16[2,128,1024]{2,1,0:T(8,128)(2,1)S(1)}, bf16[2,128,1024]{2,1,0:T(8,128)(2,1)S(1)}, u32[]{:S(2)}, u32[]{:S(2)}) collective-permute-start(bf16[2,128,1024]{2,1,0:T(8,128)(2,1)S(1)} %get-tuple-element.555), channel_id=1, source_target_pairs={{0,8},{4,12},{8,0},{12,4},{16,24},{20,28},{24,16},{28,20},{1,9},{5... | collective-permute-start | bytes 1572872 | tf_op jit(solution)/shard_map/ppermute | solution.py:25
  389.0 17.2 %collective-permute-start.55 = (bf16[2,128,1024]{2,1,0:T(8,128)(2,1)S(1)}, bf16[2,128,1024]{2,1,0:T(8,128)(2,1)S(1)}, u32[]{:S(2)}, u32[]{:S(2)}) collective-permute-start(bf16[2,128,1024]{2,1,0:T(8,128)(2,1)S(1)} %get-tuple-element.556), channel_id=1, source_target_pairs={{0,16},{4,20},{8,24},{12,28},{16,0},{20,4},{24,8},{28,12},{1,17},{... | collective-permute-start | bytes 1572872 | tf_op jit(solution)/shard_map/ppermute | solution.py:25
  390.5 12.4 %collective-permute-start.56 = (bf16[1,128,1024]{2,1,0:T(8,128)(2,1)S(1)}, bf16[1,128,1024]{2,1,0:T(8,128)(2,1)S(1)}, u32[]{:S(2)}, u32[]{:S(2)}) collective-permute-start(bf16[1,128,1024]{2,1,0:T(8,128)(2,1)S(1)} %get-tuple-element.557), channel_id=1, source_target_pairs={{0,1},{1,0},{2,3},{3,2},{4,5},{5,4},{6,7},{7,6},{8,9},{9,8},{10,11... | collective-permute-start | bytes 786440 | tf_op jit(solution)/shard_map/ppermute | solution.py:25
  391.8 13.6 %collective-permute-start.57 = (bf16[128,1024]{1,0:T(8,128)(2,1)S(1)}, bf16[128,1024]{1,0:T(8,128)(2,1)S(1)}, u32[]{:S(2)}, u32[]{:S(2)}) collective-permute-start(bf16[128,1024]{1,0:T(8,128)(2,1)S(1)} %fusion.7), channel_id=1, source_target_pairs={{0,2},{1,3},{2,0},{3,1},{4,6},{5,7},{6,4},{7,5},{8,10},{9,11},{10,... | collective-permute-start | bytes 786440 | tf_op jit(solution)/shard_map/ppermute | solution.py:25
  414.5 15.3 %collective-permute-start.58 = (bf16[128,1024]{1,0:T(8,128)(2,1)S(1)}, bf16[128,1024]{1,0:T(8,128)(2,1)S(1)}, u32[]{:S(2)}, u32[]{:S(2)}) collective-permute-start(bf16[128,1024]{1,0:T(8,128)(2,1)S(1)} %fusion.8), channel_id=1, source_target_pairs={{0,2},{1,3},{2,0},{3,1},{4,6},{5,7},{6,4},{7,5},{8,10},{9,11},{10,... | collective-permute-start | bytes 786440 | tf_op jit(solution)/shard_map/ppermute | solution.py:25
  419.5 11.8 %collective-permute-start.61 = (bf16[1,128,1024]{2,1,0:T(8,128)(2,1)S(1)}, bf16[1,128,1024]{2,1,0:T(8,128)(2,1)S(1)}, u32[]{:S(2)}, u32[]{:S(2)}) collective-permute-start(bf16[1,128,1024]{2,1,0:T(8,128)(2,1)S(1)} %get-tuple-element.580), channel_id=1, source_target_pairs={{0,1},{1,0},{2,3},{3,2},{4,5},{5,4},{6,7},{7,6},{8,9},{9,8},{10,11... | collective-permute-start | bytes 786440 | tf_op jit(solution)/shard_map/ppermute | solution.py:25
  438.8 18.9 %collective-permute-start.65 = (bf16[2,128,512]{2,1,0:T(8,128)(2,1)S(1)}, bf16[2,128,512]{2,1,0:T(8,128)(2,1)S(1)}, u32[]{:S(2)}, u32[]{:S(2)}) collective-permute-start(bf16[2,128,512]{2,1,0:T(8,128)(2,1)S(1)} %pad_maximum_fusion.11.refs_2_), channel_id=1, source_target_pairs={{0,8},{4,12},{8,0},{12,4},{16,24},{20,28},{24,16},{28,20},{1,9},{5... | collective-permute-start | bytes 786440 | tf_op jit(solution)/shard_map/ppermute | solution.py:25
  442.0 15.7 %collective-permute-start.63 = (bf16[2,128,512]{2,1,0:T(8,128)(2,1)S(1)}, bf16[2,128,512]{2,1,0:T(8,128)(2,1)S(1)}, u32[]{:S(2)}, u32[]{:S(2)}) collective-permute-start(bf16[2,128,512]{2,1,0:T(8,128)(2,1)S(1)} %pad_maximum_fusion.10.refs_0_), channel_id=1, source_target_pairs={{0,16},{4,20},{8,24},{12,28},{16,0},{20,4},{24,8},{28,12},{1,17},{... | collective-permute-start | bytes 786440 | tf_op jit(solution)/shard_map/ppermute | solution.py:25
  (167 other events, 1447.1 us)
Sparse Core Ops, SparseCore 0:
  379.8 30.4 all-gather.4
  412.3 33.6 all-gather.6

commit v4 on v3

--- a/solution.py
+++ b/solution.py
@@ -142,7 +142,7 @@
             jax.ShapeDtypeStruct((rows, count), BF16),
         ],
         name="attend",
-        compiler_params=pltpu.CompilerParams(vmem_limit_bytes=48 << 20),
+        compiler_params=pltpu.CompilerParams(vmem_limit_bytes=24 << 20),
         cost_estimate=LIGHT,
     )(queries, keys, values, key_const)
 
@@ -245,7 +245,7 @@
             pltpu.VMEM((span, 2 * wide), BF16),
         ],
         name="attend_back",
-        compiler_params=pltpu.CompilerParams(vmem_limit_bytes=52 << 20),
+        compiler_params=pltpu.CompilerParams(vmem_limit_bytes=24 << 20),
         cost_estimate=LIGHT,
     )(queries, keys, values, key_const, aug, grad_out, out, *([before] if causal else []))
 
@@ -497,7 +497,7 @@
             jax.ShapeDtypeStruct((blocks * rows, full), BF16),
         ],
         name="project",
-        compiler_params=pltpu.CompilerParams(vmem_limit_bytes=48 << 20),
+        compiler_params=pltpu.CompilerParams(vmem_limit_bytes=28 << 20),
         cost_estimate=LIGHT,
     )(device.reshape(1), *normed, biases, *group.inputs)
 
@@ -584,7 +584,7 @@
             jax.ShapeDtypeStruct((rows, mp * hidden), BF16),
         ],
         name="feed_up",
-        compiler_params=pltpu.CompilerParams(vmem_limit_bytes=56 << 20),
+        compiler_params=pltpu.CompilerParams(vmem_limit_bytes=44 << 20),
         cost_estimate=LIGHT,
     )(
         device.reshape(1), att_a, att_b, residual, vectors, u_bias, *group_a.inputs, *group_u.inputs
@@ -671,7 +671,7 @@
             jax.ShapeDtypeStruct((24, full), F32),
         ],
         name="feed_down",
-        compiler_params=pltpu.CompilerParams(vmem_limit_bytes=48 << 20),
+        compiler_params=pltpu.CompilerParams(vmem_limit_bytes=30 << 20),
         cost_estimate=LIGHT,
     )(device.reshape(1), act, middle, cotangent, vectors, *group_d.inputs)
 
@@ -798,7 +798,7 @@
             jax.ShapeDtypeStruct((8, mp * hidden), F32),
         ],
         name="feed_back",
-        compiler_params=pltpu.CompilerParams(vmem_limit_bytes=58 << 20),
+        compiler_params=pltpu.CompilerParams(vmem_limit_bytes=52 << 20),
         cost_estimate=LIGHT,
     )(
         device.reshape(1),
@@ -870,7 +870,7 @@
         ),
         out_shape=jax.ShapeDtypeStruct((rows, full), dtype),
         name="unproject",
-        compiler_params=pltpu.CompilerParams(vmem_limit_bytes=48 << 20),
+        compiler_params=pltpu.CompilerParams(vmem_limit_bytes=22 << 20),
         cost_estimate=LIGHT,
     )(device.reshape(1), *grads, *([] if before is None else [before]), *group.inputs)
 
@@ -927,7 +927,7 @@
         ),
         out_shape=jax.ShapeDtypeStruct((full // 2, right.shape[1]), BF16),
         name="other_half",
-        compiler_params=pltpu.CompilerParams(vmem_limit_bytes=32 << 20),
+        compiler_params=pltpu.CompilerParams(vmem_limit_bytes=16 << 20),
         cost_estimate=LIGHT,
     )(device.reshape(1), left, right)
 
@@ -958,7 +958,7 @@
         ),
         out_shape=[jax.ShapeDtypeStruct(shape, BF16)] * 4,
         name="this_half",
-        compiler_params=pltpu.CompilerParams(vmem_limit_bytes=40 << 20),
+        compiler_params=pltpu.CompilerParams(vmem_limit_bytes=24 << 20),
         cost_estimate=LIGHT,
     )(device.reshape(1), left, right, got)
 
@@ -1037,7 +1037,7 @@
         ),
         out_shape=jax.ShapeDtypeStruct(out, BF16),
         name="attention_other",
-        compiler_params=pltpu.CompilerParams(vmem_limit_bytes=40 << 20),
+        compiler_params=pltpu.CompilerParams(vmem_limit_bytes=16 << 20),
         cost_estimate=LIGHT,
     )(device.reshape(1), *normed, branch, *grads, attended)
 
@@ -1058,7 +1058,7 @@
         ),
         out_shape=[jax.ShapeDtypeStruct(shape, BF16)] * 4,
         name="attention_this",
-        compiler_params=pltpu.CompilerParams(vmem_limit_bytes=48 << 20),
+        compiler_params=pltpu.CompilerParams(vmem_limit_bytes=24 << 20),
         cost_estimate=LIGHT,
     )(device.reshape(1), *normed, branch, *grads, attended, got)
 
@@ -1092,7 +1092,7 @@
         ),
         out_shape=[jax.ShapeDtypeStruct((rows, columns), BF16)] * 4,
         name="next_stage",
-        compiler_params=pltpu.CompilerParams(vmem_limit_bytes=32 << 20),
+        compiler_params=pltpu.CompilerParams(vmem_limit_bytes=16 << 20),
         cost_estimate=LIGHT,
     )(device.reshape(1), *inputs)
 
@@ -1125,7 +1125,7 @@
         in_specs=[pl.BlockSpec(memory_space=pltpu.VMEM)] * 4,
         out_specs=[pl.BlockSpec(memory_space=pltpu.VMEM)] * 2,
         name="by_layer_pieces",
-        compiler_params=pltpu.CompilerParams(vmem_limit_bytes=32 << 20),
+        compiler_params=pltpu.CompilerParams(vmem_limit_bytes=12 << 20),
         cost_estimate=LIGHT,
     )(keeps[0], gots[0], keeps[1], gots[1])
     return send, rest, odd, even

time: 477 us -> 464 us (0.973)
  Pallas kernels: 215 us -> 184 us
  starting transfers between devices: 68.5 us -> 79 us
  waiting for transfers between devices: 106 us -> 113 us
    ppermute x75, starting transfers between devices: 68.2 us -> 78.7 us  [swap(): return lax.ppermute(value, axis, [(i, i ^ mask) for i in range(count)])]
    ppermute x75, waiting for transfers between devices: 106 us -> 113 us  [swap(): return lax.ppermute(value, axis, [(i, i ^ mask) for i in range(count)])]
    pallas_call x3, Pallas kernels: 21 us -> 15.5 us  [unproject(): pl.pallas_call(functools.partial(unproject_kernel, group, which, begin, c...]
    unnamed x282 -> x236, local copies, waits for them, and re-layouts: 28.7 us -> 34.2 us
  transfers between devices with their start and end apart: 77 -> 77, of which waited for: 31 -> 29; matrix products, arithmetic and copies ran while one was open for 6% -> 5% of each run, Pallas kernels for 35% -> 32%
where the time goes in v4:
time: 464 us; the launch traced here: 459 us
  Pallas kernels  184 us (40%)
  waiting for transfers between devices  113 us (24%)
  starting transfers between devices  79 us (17%)
  local copies, waits for them, and re-layouts  49.1 us (11%)
  between operations  16.4 us (4%)
  other arithmetic  14.6 us (3%)
    ppermute x75, waiting for transfers between devices, swap(): return lax.ppermute(value, axis, [(i, i ^ mask) for i in range(count)])  113 us
    ppermute x75, starting transfers between devices, swap(): return lax.ppermute(value, axis, [(i, i ^ mask) for i in range(count)])  78.7 us
    pallas_call x3, Pallas kernels, attend_back(): pl.pallas_call(functools.partial(attend_back_kernel, causal), grid=(count...  40.5 us
    unnamed x236, local copies, waits for them, and re-layouts  34.2 us
    pallas_call x1, Pallas kernels, feed_back(): pl.pallas_call(functools.partial(back_kernel, group_a, group_u, group_d),...  24.7 us
    pallas_call x1, Pallas kernels, feed_up(): pl.pallas_call(functools.partial(up_kernel, group_a, group_u), grid_spec=...  18.1 us
    pallas_call x2, Pallas kernels, attend(): pl.pallas_call(functools.partial(attend_kernel, span // rows, rows), grid...  17.6 us
    pallas_call x3, Pallas kernels, unproject(): pl.pallas_call(functools.partial(unproject_kernel, group, which, begin, c...  15.5 us
  transfers between devices with their start and end apart: 77, of which 29 were waited for; matrix products, arithmetic and copies ran while one was open for 5% of the time, Pallas kernels for 32%

profile of v4, /device:TPU:0, one launch (start us, length us, event | category | flops | bytes accessed | tf_op | source)
XLA Modules:
  0.0 458.8 jit_solution(5581462862950001566)
XLA Ops:
  11.3 3.0 collective-permute-start
  14.3 2.6 collective-permute-start.1
  21.9 4.9 %collective-permute-done = bf16[528,256]{1,0:T(8,128)(2,1)} collective-permute-done((bf16[528,256]{1,0:T(8,128)(2,1)}, bf16[528,256]{1,0:T(8,128)(2,1)}, u32[]{:S(2)}, u32[]{:S(2)}) %collective-permute-start) | collective-permute-done | bytes 270368 | tf_op jit(solution)/shard_map/ppermute | solution.py:25
  26.8 2.6 collective-permute-done.1
  31.8 4.3 collective-permute-done.2
  41.3 3.6 collective-permute-done.3
  51.6 2.5 collective-permute-start.8
  54.0 20.7 %collective-permute-done.7 = bf16[128,1024]{1,0:T(8,128)(2,1)} collective-permute-done((bf16[128,1024]{1,0:T(8,128)(2,1)}, bf16[128,1024]{1,0:T(8,128)(2,1)}, u32[]{:S(2)}, u32[]{:S(2)}) %collective-permute-start.7) | collective-permute-done | bytes 262176 | tf_op jit(solution)/shard_map/ppermute | solution.py:25
  79.6 6.9 %collective-permute-done.14 = bf16[128,1024]{1,0:T(8,128)(2,1)} collective-permute-done((bf16[128,1024]{1,0:T(8,128)(2,1)}, bf16[128,1024]{1,0:T(8,128)(2,1)}, u32[]{:S(2)}, u32[]{:S(2)}) %collective-permute-start.14) | collective-permute-done | bytes 262176 | tf_op jit(solution)/shard_map/ppermute | solution.py:25
  93.3 9.5 %project.1 = (bf16[544,1024]{1,0:T(8,128)(2,1)S(1)}, bf16[1088,1024]{1,0:T(8,128)(2,1)S(1)}, bf16[1088,1024]{1,0:T(8,128)(2,1)S(1)}) custom-call(s32[1]{0:T(128)} %bitcast.scal, bf16[544,1024]{1,0:T(8,128)(2,1)} %collective-permute-done.9.refs_0_, bf16[544,1024]{1,0:T(8,128)(2,1)S(1)} %add_convert_fusion.refs_1_, f32[8,1024]{1,0:T(8,128)S(1)} %pad.28.refs_2_, ...), custom_call_target="tpu_custom_call" | custom-call | flops 1000 | bytes 1000 | tf_op jit(solution)/shard_map/project/pallas_call | solution.py:483
  109.3 8.8 %attend.2 = (bf16[544,512]{1,0:T(8,128)(2,1)S(1)}, bf16[544,512]{1,0:T(8,128)(2,1)S(1)}) custom-call(bf16[544,1024]{1,0:T(8,128)(2,1)S(1)} %get-tuple-element.372.q_ref, bf16[1088,1024]{1,0:T(8,128)(2,1)S(1)} %get-tuple-element.363.k_ref, bf16[1088,1024]{1,0:T(8,128)(2,1)S(1)} %get-tuple-element.364.v_ref, bf16[1088,128]{1,0:T(8,128)(2,1)S(1)} %select_convert_fusion.kc_ref), custom_call_target="tpu_custom_call" | custom-call | flops 1000 | bytes 1000 | tf_op jit(solution)/shard_map/attend/pallas_call | solution.py:130
  119.5 8.8 %attend.3 = (bf16[544,512]{1,0:T(8,128)(2,1)S(1)}, bf16[544,512]{1,0:T(8,128)(2,1)S(1)}) custom-call(bf16[544,1024]{1,0:T(8,128)(2,1)S(1)} %get-tuple-element.372.q_ref, bf16[1088,1024]{1,0:T(8,128)(2,1)S(1)} %get-tuple-element.363.k_ref, bf16[1088,1024]{1,0:T(8,128)(2,1)S(1)} %get-tuple-element.364.v_ref, bf16[1088,128]{1,0:T(8,128)(2,1)S(1)} %select_convert_fusion.kc_ref), custom_call_target="tpu_custom_call" | custom-call | flops 1000 | bytes 1000 | tf_op jit(solution)/shard_map/attend/pallas_call | solution.py:130
  128.4 4.6 %collective-permute-done.22 = bf16[1,3,1,64,1024]{4,3,1,2,0:T(8,128)(2,1)S(1)} collective-permute-done((bf16[1,3,1,64,1024]{4,3,1,2,0:T(8,128)(2,1)S(1)}, bf16[1,3,1,64,1024]{4,3,1,2,0:T(8,128)(2,1)S(1)}, u32[]{:S(2)}, u32[]{:S(2)}) %collective-permute-start.22) | collective-permute-done | bytes 393248 | tf_op jit(solution)/shard_map/ppermute | solution.py:25
  142.3 18.1 %feed_up.1 = (f32[544,1024]{1,0:T(8,128)}, f32[544,1024]{1,0:T(8,128)}, bf16[544,1024]{1,0:T(8,128)(2,1)}, bf16[544,4096]{1,0:T(8,128)(2,1)}, bf16[544,4096]{1,0:T(8,128)(2,1)}) custom-call(s32[1]{0:T(128)} %bitcast.scal, bf16[544,512]{1,0:T(8,128)(2,1)S(1)} %copy-done.51, bf16[544,512]{1,0:T(8,128)(2,1)S(1)} %copy-done.54, f32[544,1024]{1,0:T(8,128)} %copy-done.92, ...), custom_call_target="tpu_custom_call" | custom-call | flops 1000 | bytes 1000 | tf_op jit(solution)/shard_map/feed_up/pallas_call | solution.py:567
  166.4 2.5 copy-done.8
  170.6 10.2 %feed_down.1 = (bf16[544,1024]{1,0:T(8,128)(2,1)}, bf16[544,1024]{1,0:T(8,128)(2,1)S(1)}, f32[24,1024]{1,0:T(8,128)S(1)}) custom-call(s32[1]{0:T(128)} %bitcast.scal, bf16[544,4096]{1,0:T(8,128)(2,1)S(1)} %copy-done.8, f32[544,1024]{1,0:T(8,128)S(1)} %copy-done.29, bf16[544,1024]{1,0:T(8,128)(2,1)S(1)} %copy-done.44, ...), custom_call_target="tpu_custom_call" | custom-call | flops 1000 | bytes 1000 | tf_op jit(solution)/shard_map/feed_down/pallas_call | solution.py:657
  180.8 4.7 %other_half.2 = bf16[512,4096]{1,0:T(8,128)(2,1)S(1)} custom-call(s32[1]{0:T(128)} %bitcast.scal, bf16[544,1024]{1,0:T(8,128)(2,1)S(1)} %get-tuple-element.418.left_ref.refs_0_, bf16[544,4096]{1,0:T(8,128)(2,1)S(1)} %copy-done.8), custom_call_target="tpu_custom_call" | custom-call | flops 1000 | bytes 1000 | tf_op jit(solution)/shard_map/other_half/pallas_call | solution.py:917
  185.7 7.0 %collective-permute-done.34.got_ref = bf16[512,4096]{1,0:T(8,128)(2,1)S(1)} collective-permute-done((bf16[512,4096]{1,0:T(8,128)(2,1)S(1)}, bf16[512,4096]{1,0:T(8,128)(2,1)S(1)}, u32[]{:S(2)}, u32[]{:S(2)}) %collective-permute-start.34) | collective-permute-done | bytes 4194336 | tf_op jit(solution)/shard_map/ppermute | solution.py:25
  192.8 5.6 %this_half.2 = (bf16[2,128,2048]{2,1,0:T(8,128)(2,1)S(1)}, bf16[2,128,2048]{2,1,0:T(8,128)(2,1)S(1)}, bf16[2,128,2048]{2,1,0:T(8,128)(2,1)S(1)}, bf16[2,128,2048]{2,1,0:T(8,128)(2,1)S(1)}) custom-call(s32[1]{0:T(128)} %bitcast.scal, bf16[544,1024]{1,0:T(8,128)(2,1)S(1)} %get-tuple-element.418.left_ref.refs_0_, bf16[544,4096]{1,0:T(8,128)(2,1)S(1)} %bitcast.119, ...), custom_call_target="tpu_custom_call" | custom-call | flops 1000 | bytes 1000 | tf_op jit(solution)/shard_map/this_half/pallas_call | solution.py:946
  200.5 24.7 %feed_back.1 = (bf16[544,4096]{1,0:T(8,128)(2,1)}, f32[544,1024]{1,0:T(8,128)}, bf16[544,1024]{1,0:T(8,128)(2,1)}, bf16[544,1024]{1,0:T(8,128)(2,1)}, f32[40,1024]{1,0:T(8,128)S(1)}, /*index=5*/f32[8,4096]{1,0:T(8,128)S(1)}) custom-call(s32[1]{0:T(128)} %bitcast.scal, bf16[544,1024]{1,0:T(8,128)(2,1)} %copy-done.24, ...), custom_call_target="tpu_custom_call" | custom-call | flops 1000 | bytes 1000 | tf_op jit(solution)/shard_map/feed_back/pallas_call | solution.py:773
  228.1 4.7 %other_half.3 = bf16[512,4096]{1,0:T(8,128)(2,1)S(1)} custom-call(s32[1]{0:T(128)} %bitcast.scal, bf16[544,1024]{1,0:T(8,128)(2,1)S(1)} %copy-done.45, bf16[544,4096]{1,0:T(8,128)(2,1)S(1)} %bitcast.121), custom_call_target="tpu_custom_call" | custom-call | flops 1000 | bytes 1000 | tf_op jit(solution)/shard_map/other_half/pallas_call | solution.py:917
  237.3 20.2 %attend_back.3 = (f32[544,1024]{1,0:T(8,128)S(1)}, bf16[544,1024]{1,0:T(8,128)(2,1)S(1)}, bf16[544,1024]{1,0:T(8,128)(2,1)S(1)}) custom-call(bf16[544,1024]{1,0:T(8,128)(2,1)S(1)} %copy-done.14, bf16[1088,1024]{1,0:T(8,128)(2,1)S(1)} %copy-done.5, bf16[1088,1024]{1,0:T(8,128)(2,1)S(1)} %copy-done.7, bf16[1088,128]{1,0:T(8,128)(2,1)S(1)} %select_convert_fusion.kc_ref, ...), custom_call_target="tpu_custom_call" | custom-call | flops 1000 | bytes 1000 | tf_op jit(solution)/shard_map/attend_back/pallas_call | solution.py:223
  257.6 6.5 %unproject.3 = bf16[544,1024]{1,0:T(8,128)(2,1)} custom-call(s32[1]{0:T(128)} %bitcast.scal, bf16[544,1024]{1,0:T(8,128)(2,1)S(1)} %get-tuple-element.478.refs_0_.refs_6_, bf16[544,1024]{1,0:T(8,128)(2,1)S(1)} %get-tuple-element.479.refs_1_.refs_7_, bf16[3,1024,256]{2,1,0:T(8,128)(2,1)S(1)} %copy-done.3, bf16[256,1024]{1,0:T(8,128)(2,1)S(1)} %copy-done.21, ...), custom_call_target="tpu_custom_call" | custom-call | flops 1000 | bytes 1000 | tf_op jit(solution)/shard_map/unproject/pallas_call | solution.py:858
  265.0 5.6 %this_half.3 = (bf16[2,128,2048]{2,1,0:T(8,128)(2,1)S(1)}, bf16[2,128,2048]{2,1,0:T(8,128)(2,1)S(1)}, bf16[2,128,2048]{2,1,0:T(8,128)(2,1)S(1)}, bf16[2,128,2048]{2,1,0:T(8,128)(2,1)S(1)}) custom-call(s32[1]{0:T(128)} %bitcast.scal, bf16[544,1024]{1,0:T(8,128)(2,1)S(1)} %copy-done.45, bf16[544,4096]{1,0:T(8,128)(2,1)S(1)} %bitcast.121, ...), custom_call_target="tpu_custom_call" | custom-call | flops 1000 | bytes 1000 | tf_op jit(solution)/shard_map/this_half/pallas_call | solution.py:946
  273.2 10.1 %attend_back.4 = (bf16[544,512]{1,0:T(8,128)(2,1)S(1)}, bf16[544,512]{1,0:T(8,128)(2,1)S(1)}, bf16[544,512]{1,0:T(8,128)(2,1)S(1)}) custom-call(bf16[544,1024]{1,0:T(8,128)(2,1)S(1)} %copy-done.14, bf16[1088,1024]{1,0:T(8,128)(2,1)S(1)} %copy-done.5, bf16[1088,1024]{1,0:T(8,128)(2,1)S(1)} %copy-done.7, bf16[1088,128]{1,0:T(8,128)(2,1)S(1)} %copy-done.26, ...), custom_call_target="tpu_custom_call" | custom-call | flops 1000 | bytes 1000 | tf_op jit(solution)/shard_map/attend_back/pallas_call | solution.py:223
  283.4 4.1 attention_other.2
  287.6 8.4 %collective-permute-done.40.refs_1_.refs_3_ = bf16[2,128,2048]{2,1,0:T(8,128)(2,1)S(1)} collective-permute-done((bf16[2,128,2048]{2,1,0:T(8,128)(2,1)S(1)}, bf16[2,128,2048]{2,1,0:T(8,128)(2,1)S(1)}, u32[]{:S(2)}, u32[]{:S(2)}) %collective-permute-start.40) | collective-permute-done | bytes 1048608 | tf_op jit(solution)/shard_map/ppermute | solution.py:25
  301.2 5.1 %unproject.4.refs_3_ = f32[544,1024]{1,0:T(8,128)S(1)} custom-call(s32[1]{0:T(128)} %bitcast.scal, bf16[544,512]{1,0:T(8,128)(2,1)S(1)} %get-tuple-element.591.refs_3_.refs_0_, bf16[544,512]{1,0:T(8,128)(2,1)S(1)} %get-tuple-element.482.refs_4_.refs_1_, bf16[544,512]{1,0:T(8,128)(2,1)S(1)} %get-tuple-element.592.refs_5_.refs_2_, ...), custom_call_target="tpu_custom_call" | custom-call | flops 1000 | bytes 1000 | tf_op jit(solution)/shard_map/unproject/pallas_call | solution.py:858
  306.3 4.8 %attention_this.2 = (bf16[2,128,1024]{2,1,0:T(8,128)(2,1)S(1)}, bf16[2,128,1024]{2,1,0:T(8,128)(2,1)S(1)}, bf16[2,128,1024]{2,1,0:T(8,128)(2,1)S(1)}, bf16[2,128,1024]{2,1,0:T(8,128)(2,1)S(1)}) custom-call(s32[1]{0:T(128)} %bitcast.scal, bf16[544,1024]{1,0:T(8,128)(2,1)} %collective-permute-done.9.refs_0_, bf16[544,1024]{1,0:T(8,128)(2,1)S(1)} %copy-done.10, ...), custom_call_target="tpu_custom_call" | custom-call | flops 1000 | bytes 1000 | tf_op jit(solution)/shard_map/attention_this/pallas_call | solution.py:1049
  314.6 10.1 %attend_back.5 = (bf16[544,512]{1,0:T(8,128)(2,1)S(1)}, bf16[544,512]{1,0:T(8,128)(2,1)S(1)}, bf16[544,512]{1,0:T(8,128)(2,1)S(1)}) custom-call(bf16[544,1024]{1,0:T(8,128)(2,1)S(1)} %copy-done.14, bf16[1088,1024]{1,0:T(8,128)(2,1)S(1)} %copy-done.5, bf16[1088,1024]{1,0:T(8,128)(2,1)S(1)} %copy-done.7, bf16[1088,128]{1,0:T(8,128)(2,1)S(1)} %copy-done.26, ...), custom_call_target="tpu_custom_call" | custom-call | flops 1000 | bytes 1000 | tf_op jit(solution)/shard_map/attend_back/pallas_call | solution.py:223
  325.6 3.8 attention_other.3
  333.8 2.8 collective-permute-start.53
  336.6 3.9 unproject.5
  343.2 4.9 %collective-permute-done.53 = bf16[128,1024]{1,0:T(8,128)(2,1)S(1)} collective-permute-done((bf16[128,1024]{1,0:T(8,128)(2,1)S(1)}, bf16[128,1024]{1,0:T(8,128)(2,1)S(1)}, u32[]{:S(2)}, u32[]{:S(2)}) %collective-permute-start.53) | collective-permute-done | bytes 262176 | tf_op jit(solution)/shard_map/ppermute | solution.py:25
  360.9 5.0 %attention_this.3 = (bf16[2,128,1024]{2,1,0:T(8,128)(2,1)S(1)}, bf16[2,128,1024]{2,1,0:T(8,128)(2,1)S(1)}, bf16[2,128,1024]{2,1,0:T(8,128)(2,1)S(1)}, bf16[2,128,1024]{2,1,0:T(8,128)(2,1)S(1)}) custom-call(s32[1]{0:T(128)} %bitcast.scal, bf16[544,1024]{1,0:T(8,128)(2,1)} %collective-permute-done.9.refs_0_, bf16[544,1024]{1,0:T(8,128)(2,1)S(1)} %copy-done.10, ...), custom_call_target="tpu_custom_call" | custom-call | flops 1000 | bytes 1000 | tf_op jit(solution)/shard_map/attention_this/pallas_call | solution.py:1049
  369.0 2.7 collective-permute-start.56
  376.3 5.3 %collective-permute-done.56 = bf16[1,128,1024]{2,1,0:T(8,128)(2,1)S(1)} collective-permute-done((bf16[1,128,1024]{2,1,0:T(8,128)(2,1)S(1)}, bf16[1,128,1024]{2,1,0:T(8,128)(2,1)S(1)}, u32[]{:S(2)}, u32[]{:S(2)}) %collective-permute-start.56) | collective-permute-done | bytes 262176 | tf_op jit(solution)/shard_map/ppermute | solution.py:25
  381.6 3.7 collective-permute-done.57
  398.9 3.2 collective-permute-done.59.got_a
  402.1 2.4 collective-permute-done.60.got_b
  404.5 3.3 collective-permute-start.61
  408.6 7.5 %collective-permute-done.71 = f32[34,1024]{1,0:T(8,128)S(1)} collective-permute-done((f32[34,1024]{1,0:T(8,128)S(1)}, f32[34,1024]{1,0:T(8,128)S(1)}, u32[]{:S(2)}, u32[]{:S(2)}) %collective-permute-start.71) | collective-permute-done | bytes 139296 | tf_op jit(solution)/shard_map/ppermute | solution.py:25
  419.7 2.6 collective-permute-done.72
  425.9 2.4 collective-permute-done.73
  428.4 3.2 collective-permute-start.74
  431.6 5.1 %collective-permute-done.74 = f32[34,1024]{1,0:T(8,128)S(1)} collective-permute-done((f32[34,1024]{1,0:T(8,128)S(1)}, f32[34,1024]{1,0:T(8,128)S(1)}, u32[]{:S(2)}, u32[]{:S(2)}) %collective-permute-start.74) | collective-permute-done | bytes 139296 | tf_op jit(solution)/shard_map/ppermute | solution.py:25
  438.3 2.6 fill_ffn.2
  449.0 2.5 fill_attention.1
  (483 shorter events, 140.6 us)
Async XLA Ops:
  7.2 429.5 %all-gather.5.cloned.1.call-start = ((), (), s32[]{:S(2)}) async-start(), calls=%async_computation | async-start | bytes 2359296 | tf_op jit(solution)/shard_map/all_gather | solution.py:1487
  11.3 15.5 %collective-permute-start = (bf16[528,256]{1,0:T(8,128)(2,1)}, bf16[528,256]{1,0:T(8,128)(2,1)}, u32[]{:S(2)}, u32[]{:S(2)}) collective-permute-start(bf16[528,256]{1,0:T(8,128)(2,1)} %fusion.5), channel_id=1, source_target_pairs={{0,1},{1,0},{2,3},{3,2},{4,5},{5,4},{6,7},{7,6},{8,9},{9,8},{10,11... | collective-permute-start | bytes 811016 | tf_op jit(solution)/shard_map/ppermute | solution.py:25
  14.3 15.0 %collective-permute-start.1 = (bf16[528,256]{1,0:T(8,128)(2,1)}, bf16[528,256]{1,0:T(8,128)(2,1)}, u32[]{:S(2)}, u32[]{:S(2)}) collective-permute-start(bf16[528,256]{1,0:T(8,128)(2,1)} %fusion.5), channel_id=1, source_target_pairs={{0,2},{1,3},{2,0},{3,1},{4,6},{5,7},{6,4},{7,5},{8,10},{9,11},{10,... | collective-permute-start | bytes 811016 | tf_op jit(solution)/shard_map/ppermute | solution.py:25
  40.0 34.8 %collective-permute-start.9 = (bf16[544,1024]{1,0:T(8,128)(2,1)S(1)}, bf16[544,1024]{1,0:T(8,128)(2,1)}, u32[]{:S(2)}, u32[]{:S(2)}) collective-permute-start(bf16[544,1024]{1,0:T(8,128)(2,1)S(1)} %add_convert_fusion.refs_1_), channel_id=1, source_target_pairs={{0,1},{1,0},{2,3},{3,2},{4,5},{5,4},{6,7},{7,6},{8,9},{9,8},{10,11... | collective-permute-start | bytes 3342344 | tf_op jit(solution)/shard_map/ppermute | solution.py:25
  47.6 27.1 %collective-permute-start.5 = (bf16[2,3,4,64,256]{4,3,2,1,0:T(8,128)(2,1)}, bf16[2,3,4,64,256]{4,3,2,1,0:T(8,128)(2,1)}, u32[]{:S(2)}, u32[]{:S(2)}) collective-permute-start(bf16[2,3,4,64,256]{4,3,2,1,0:T(8,128)(2,1)} %pad_maximum_fusion.1.refs_5_.refs_7_.refs_8_.refs_4_.refs_6_), channel_id=1, source_target_pairs={{0,16},{4,20},{8,24},{12,28},{16,0},{20,4},{24,8},{28,12},{1,17},{... | collective-permute-start | bytes 2359304 | tf_op jit(solution)/shard_map/ppermute | solution.py:25
  49.2 25.6 %collective-permute-start.6 = (bf16[2,3,4,64,256]{4,3,2,1,0:T(8,128)(2,1)S(1)}, bf16[2,3,4,64,256]{4,3,2,1,0:T(8,128)(2,1)}, u32[]{:S(2)}, u32[]{:S(2)}) collective-permute-start(bf16[2,3,4,64,256]{4,3,2,1,0:T(8,128)(2,1)S(1)} %pad_maximum_fusion.2.refs_7_.refs_9_.refs_10_.refs_6_.refs_8_), channel_id=1, source_target_pairs={{0,8},{4,12},{8,0},{12,4},{16,24},{20,28},{24,16},{28,20},{1,9},{5... | collective-permute-start | bytes 2359304 | tf_op jit(solution)/shard_map/ppermute | solution.py:25
  49.7 25.1 %collective-permute-start.7 = (bf16[128,1024]{1,0:T(8,128)(2,1)}, bf16[128,1024]{1,0:T(8,128)(2,1)}, u32[]{:S(2)}, u32[]{:S(2)}) collective-permute-start(bf16[128,1024]{1,0:T(8,128)(2,1)} %bitcast.12), channel_id=1, source_target_pairs={{0,1},{1,0},{2,3},{3,2},{4,5},{5,4},{6,7},{7,6},{8,9},{9,8},{10,11... | collective-permute-start | bytes 786440 | tf_op jit(solution)/shard_map/ppermute | solution.py:25
  51.6 23.2 %collective-permute-start.8 = (bf16[128,1024]{1,0:T(8,128)(2,1)}, bf16[128,1024]{1,0:T(8,128)(2,1)}, u32[]{:S(2)}, u32[]{:S(2)}) collective-permute-start(bf16[128,1024]{1,0:T(8,128)(2,1)} %bitcast.12), channel_id=1, source_target_pairs={{0,2},{1,3},{2,0},{3,1},{4,6},{5,7},{6,4},{7,5},{8,10},{9,11},{10,... | collective-permute-start | bytes 786440 | tf_op jit(solution)/shard_map/ppermute | solution.py:25
  74.8 11.7 %collective-permute-start.10 = (bf16[2,3,4,64,256]{4,3,2,1,0:T(8,128)(2,1)}, bf16[2,3,4,64,256]{4,3,2,1,0:T(8,128)(2,1)}, u32[]{:S(2)}, u32[]{:S(2)}) collective-permute-start(bf16[2,3,4,64,256]{4,3,2,1,0:T(8,128)(2,1)} %pad_maximum_fusion.1.refs_5_.refs_7_.refs_8_.refs_4_.refs_6_), channel_id=1, source_target_pairs={{0,4},{4,0},{8,12},{12,8},{16,20},{20,16},{24,28},{28,24},{1,5},{5... | collective-permute-start | bytes 2359304 | tf_op jit(solution)/shard_map/ppermute | solution.py:25
  74.8 11.6 %collective-permute-start.11 = (bf16[2,3,4,64,256]{4,3,2,1,0:T(8,128)(2,1)}, bf16[2,3,4,64,256]{4,3,2,1,0:T(8,128)(2,1)}, u32[]{:S(2)}, u32[]{:S(2)}) collective-permute-start(bf16[2,3,4,64,256]{4,3,2,1,0:T(8,128)(2,1)} %collective-permute-done.5.refs_6_.refs_8_.refs_9_.refs_5_.refs_7_), channel_id=1, source_target_pairs={{0,4},{4,0},{8,12},{12,8},{16,20},{20,16},{24,28},{28,24},{1,5},{5... | collective-permute-start | bytes 2359304 | tf_op jit(solution)/shard_map/ppermute | solution.py:25
  75.3 11.1 %collective-permute-start.12 = (bf16[2,3,4,64,256]{4,3,2,1,0:T(8,128)(2,1)S(1)}, bf16[2,3,4,64,256]{4,3,2,1,0:T(8,128)(2,1)}, u32[]{:S(2)}, u32[]{:S(2)}) collective-permute-start(bf16[2,3,4,64,256]{4,3,2,1,0:T(8,128)(2,1)S(1)} %pad_maximum_fusion.2.refs_7_.refs_9_.refs_10_.refs_6_.refs_8_), channel_id=1, source_target_pairs={{0,4},{4,0},{8,12},{12,8},{16,20},{20,16},{24,28},{28,24},{1,5},{5... | collective-permute-start | bytes 2359304 | tf_op jit(solution)/shard_map/ppermute | solution.py:25
  87.8 15.1 %collective-permute-start.17 = (bf16[1,3,1,64,1024]{4,3,1,2,0:T(8,128)(2,1)S(1)}, bf16[1,3,1,64,1024]{4,3,1,2,0:T(8,128)(2,1)S(1)}, u32[]{:S(2)}, u32[]{:S(2)}) collective-permute-start(bf16[1,3,1,64,1024]{4,3,1,2,0:T(8,128)(2,1)S(1)} %get-tuple-element.354), channel_id=1, source_target_pairs={{0,8},{4,12},{8,0},{12,4},{16,24},{20,28},{24,16},{28,20},{1,9},{5... | collective-permute-start | bytes 1179656 | tf_op jit(solution)/shard_map/ppermute | solution.py:25
  88.4 14.5 %collective-permute-start.18 = (bf16[1,3,1,64,1024]{4,3,2,1,0:T(8,128)(2,1)S(1)}, bf16[1,3,1,64,1024]{4,3,2,1,0:T(8,128)(2,1)S(1)}, u32[]{:S(2)}, u32[]{:S(2)}) collective-permute-start(bf16[1,3,1,64,1024]{4,3,2,1,0:T(8,128)(2,1)S(1)} %get-tuple-element.355), channel_id=1, source_target_pairs={{0,16},{4,20},{8,24},{12,28},{16,0},{20,4},{24,8},{28,12},{1,17},{... | collective-permute-start | bytes 1179656 | tf_op jit(solution)/shard_map/ppermute | solution.py:25
  89.6 13.2 %collective-permute-start.15 = (bf16[128,1024]{1,0:T(8,128)(2,1)S(1)}, bf16[128,1024]{1,0:T(8,128)(2,1)S(1)}, u32[]{:S(2)}, u32[]{:S(2)}) collective-permute-start(bf16[128,1024]{1,0:T(8,128)(2,1)S(1)} %bitcast.138), channel_id=1, source_target_pairs={{0,1},{1,0},{2,3},{3,2},{4,5},{5,4},{6,7},{7,6},{8,9},{9,8},{10,11... | collective-permute-start | bytes 786440 | tf_op jit(solution)/shard_map/ppermute | solution.py:25
  90.5 12.4 %collective-permute-start.16 = (bf16[128,1024]{1,0:T(8,128)(2,1)S(1)}, bf16[128,1024]{1,0:T(8,128)(2,1)S(1)}, u32[]{:S(2)}, u32[]{:S(2)}) collective-permute-start(bf16[128,1024]{1,0:T(8,128)(2,1)S(1)} %bitcast.139), channel_id=1, source_target_pairs={{0,2},{1,3},{2,0},{3,1},{4,6},{5,7},{6,4},{7,5},{8,10},{9,11},{10,... | collective-permute-start | bytes 786440 | tf_op jit(solution)/shard_map/ppermute | solution.py:25
  104.0 14.2 %collective-permute-start.19 = (bf16[128,1024]{1,0:T(8,128)(2,1)S(1)}, bf16[128,1024]{1,0:T(8,128)(2,1)S(1)}, u32[]{:S(2)}, u32[]{:S(2)}) collective-permute-start(bf16[128,1024]{1,0:T(8,128)(2,1)S(1)} %collective-permute-done.16), channel_id=1, source_target_pairs={{0,1},{1,0},{2,3},{3,2},{4,5},{5,4},{6,7},{7,6},{8,9},{9,8},{10,11... | collective-permute-start | bytes 786440 | tf_op jit(solution)/shard_map/ppermute | solution.py:25
  106.1 26.9 %collective-permute-start.20 = (bf16[2,3,1,64,1024]{4,3,1,2,0:T(8,128)(2,1)S(1)}, bf16[2,3,1,64,1024]{4,3,1,2,0:T(8,128)(2,1)}, u32[]{:S(2)}, u32[]{:S(2)}) collective-permute-start(bf16[2,3,1,64,1024]{4,3,1,2,0:T(8,128)(2,1)S(1)} %pad_maximum_fusion.4), channel_id=1, source_target_pairs={{0,16},{4,20},{8,24},{12,28},{16,0},{20,4},{24,8},{28,12},{1,17},{... | collective-permute-start | bytes 2359304 | tf_op jit(solution)/shard_map/ppermute | solution.py:25
  107.6 25.4 %collective-permute-start.21 = (bf16[2,3,1,64,1024]{4,3,2,1,0:T(8,128)(2,1)}, bf16[2,3,1,64,1024]{4,3,2,1,0:T(8,128)(2,1)}, u32[]{:S(2)}, u32[]{:S(2)}) collective-permute-start(bf16[2,3,1,64,1024]{4,3,2,1,0:T(8,128)(2,1)} %pad_maximum_fusion.5.refs_18_.refs_19_), channel_id=1, source_target_pairs={{0,8},{4,12},{8,0},{12,4},{16,24},{20,28},{24,16},{28,20},{1,9},{5... | collective-permute-start | bytes 2359304 | tf_op jit(solution)/shard_map/ppermute | solution.py:25
  118.3 14.6 %collective-permute-start.22 = (bf16[1,3,1,64,1024]{4,3,1,2,0:T(8,128)(2,1)S(1)}, bf16[1,3,1,64,1024]{4,3,1,2,0:T(8,128)(2,1)S(1)}, u32[]{:S(2)}, u32[]{:S(2)}) collective-permute-start(bf16[1,3,1,64,1024]{4,3,1,2,0:T(8,128)(2,1)S(1)} %get-tuple-element.376), channel_id=1, source_target_pairs={{0,8},{4,12},{8,0},{12,4},{16,24},{20,28},{24,16},{28,20},{1,9},{5... | collective-permute-start | bytes 1179656 | tf_op jit(solution)/shard_map/ppermute | solution.py:25
  119.0 14.0 %collective-permute-start.23 = (bf16[1,3,1,64,1024]{4,3,2,1,0:T(8,128)(2,1)S(1)}, bf16[1,3,1,64,1024]{4,3,2,1,0:T(8,128)(2,1)S(1)}, u32[]{:S(2)}, u32[]{:S(2)}) collective-permute-start(bf16[1,3,1,64,1024]{4,3,2,1,0:T(8,128)(2,1)S(1)} %get-tuple-element.377), channel_id=1, source_target_pairs={{0,16},{4,20},{8,24},{12,28},{16,0},{20,4},{24,8},{28,12},{1,17},{... | collective-permute-start | bytes 1179656 | tf_op jit(solution)/shard_map/ppermute | solution.py:25
  135.2 25.3 %collective-permute-start.28 = (bf16[2,3,1,64,1024]{4,3,1,2,0:T(8,128)(2,1)}, bf16[2,3,1,64,1024]{4,3,1,2,0:T(8,128)(2,1)}, u32[]{:S(2)}, u32[]{:S(2)}) collective-permute-start(bf16[2,3,1,64,1024]{4,3,1,2,0:T(8,128)(2,1)} %pad_maximum_fusion.7), channel_id=1, source_target_pairs={{0,16},{4,20},{8,24},{12,28},{16,0},{20,4},{24,8},{28,12},{1,17},{... | collective-permute-start | bytes 2359304 | tf_op jit(solution)/shard_map/ppermute | solution.py:25
  138.4 22.0 %collective-permute-start.29 = (bf16[2,3,1,64,1024]{4,3,2,1,0:T(8,128)(2,1)S(1)}, bf16[2,3,1,64,1024]{4,3,2,1,0:T(8,128)(2,1)}, u32[]{:S(2)}, u32[]{:S(2)}) collective-permute-start(bf16[2,3,1,64,1024]{4,3,2,1,0:T(8,128)(2,1)S(1)} %pad_maximum_fusion.8.refs_7_.refs_28_), channel_id=1, source_target_pairs={{0,8},{4,12},{8,0},{12,4},{16,24},{20,28},{24,16},{28,20},{1,9},{5... | collective-permute-start | bytes 2359304 | tf_op jit(solution)/shard_map/ppermute | solution.py:25
  198.4 26.8 %collective-permute-start.35 = (bf16[2,128,2048]{2,1,0:T(8,128)(2,1)S(1)}, bf16[2,128,2048]{2,1,0:T(8,128)(2,1)S(1)}, u32[]{:S(2)}, u32[]{:S(2)}) collective-permute-start(bf16[2,128,2048]{2,1,0:T(8,128)(2,1)S(1)} %get-tuple-element.427), channel_id=1, source_target_pairs={{0,8},{4,12},{8,0},{12,4},{16,24},{20,28},{24,16},{28,20},{1,9},{5... | collective-permute-start | bytes 3145736 | tf_op jit(solution)/shard_map/ppermute | solution.py:25
  200.0 25.3 %collective-permute-start.36 = (bf16[2,128,2048]{2,1,0:T(8,128)(2,1)S(1)}, bf16[2,128,2048]{2,1,0:T(8,128)(2,1)S(1)}, u32[]{:S(2)}, u32[]{:S(2)}) collective-permute-start(bf16[2,128,2048]{2,1,0:T(8,128)(2,1)S(1)} %get-tuple-element.428), channel_id=1, source_target_pairs={{0,16},{4,20},{8,24},{12,28},{16,0},{20,4},{24,8},{28,12},{1,17},{... | collective-permute-start | bytes 3145736 | tf_op jit(solution)/shard_map/ppermute | solution.py:25
  232.8 32.2 %collective-permute-start.39 = (bf16[512,4096]{1,0:T(8,128)(2,1)S(1)}, bf16[512,4096]{1,0:T(8,128)(2,1)S(1)}, u32[]{:S(2)}, u32[]{:S(2)}) collective-permute-start(bf16[512,4096]{1,0:T(8,128)(2,1)S(1)} %other_half.3), channel_id=1, source_target_pairs={{0,4},{4,0},{8,12},{12,8},{16,20},{20,16},{24,28},{28,24},{1,5},{5... | collective-permute-start | bytes 12582920 | tf_op jit(solution)/shard_map/ppermute | solution.py:25
  232.9 31.2 %collective-permute-start.37 = (bf16[128,2048]{1,0:T(8,128)(2,1)S(1)}, bf16[128,2048]{1,0:T(8,128)(2,1)S(1)}, u32[]{:S(2)}, u32[]{:S(2)}) collective-permute-start(bf16[128,2048]{1,0:T(8,128)(2,1)S(1)} %get-tuple-element.446), channel_id=1, source_target_pairs={{0,16},{4,20},{8,24},{12,28},{16,0},{20,4},{24,8},{28,12},{1,17},{... | collective-permute-start | bytes 1572872 | tf_op jit(solution)/shard_map/ppermute | solution.py:25
  234.5 29.6 %collective-permute-start.38 = (bf16[128,2048]{1,0:T(8,128)(2,1)S(1)}, bf16[128,2048]{1,0:T(8,128)(2,1)S(1)}, u32[]{:S(2)}, u32[]{:S(2)}) collective-permute-start(bf16[128,2048]{1,0:T(8,128)(2,1)S(1)} %get-tuple-element.447), channel_id=1, source_target_pairs={{0,8},{4,12},{8,0},{12,4},{16,24},{20,28},{24,16},{28,20},{1,9},{5... | collective-permute-start | bytes 1572872 | tf_op jit(solution)/shard_map/ppermute | solution.py:25
  270.6 26.6 %collective-permute-start.42 = (bf16[544,1024]{1,0:T(8,128)(2,1)}, bf16[544,1024]{1,0:T(8,128)(2,1)S(1)}, u32[]{:S(2)}, u32[]{:S(2)}) collective-permute-start(bf16[544,1024]{1,0:T(8,128)(2,1)} %unproject.3), channel_id=1, source_target_pairs={{0,1},{1,0},{2,3},{3,2},{4,5},{5,4},{6,7},{7,6},{8,9},{9,8},{10,11... | collective-permute-start | bytes 3342344 | tf_op jit(solution)/shard_map/ppermute | solution.py:25
  271.2 24.7 %collective-permute-start.40 = (bf16[2,128,2048]{2,1,0:T(8,128)(2,1)S(1)}, bf16[2,128,2048]{2,1,0:T(8,128)(2,1)S(1)}, u32[]{:S(2)}, u32[]{:S(2)}) collective-permute-start(bf16[2,128,2048]{2,1,0:T(8,128)(2,1)S(1)} %get-tuple-element.460), channel_id=1, source_target_pairs={{0,8},{4,12},{8,0},{12,4},{16,24},{20,28},{24,16},{28,20},{1,9},{5... | collective-permute-start | bytes 3145736 | tf_op jit(solution)/shard_map/ppermute | solution.py:25
  272.7 24.4 %collective-permute-start.41 = (bf16[2,128,2048]{2,1,0:T(8,128)(2,1)S(1)}, bf16[2,128,2048]{2,1,0:T(8,128)(2,1)S(1)}, u32[]{:S(2)}, u32[]{:S(2)}) collective-permute-start(bf16[2,128,2048]{2,1,0:T(8,128)(2,1)S(1)} %get-tuple-element.461), channel_id=1, source_target_pairs={{0,16},{4,20},{8,24},{12,28},{16,0},{20,4},{24,8},{28,12},{1,17},{... | collective-permute-start | bytes 3145736 | tf_op jit(solution)/shard_map/ppermute | solution.py:25
  299.2 25.6 %collective-permute-start.44 = (bf16[128,2048]{1,0:T(8,128)(2,1)S(1)}, bf16[128,2048]{1,0:T(8,128)(2,1)S(1)}, u32[]{:S(2)}, u32[]{:S(2)}) collective-permute-start(bf16[128,2048]{1,0:T(8,128)(2,1)S(1)} %get-tuple-element.501), channel_id=1, source_target_pairs={{0,16},{4,20},{8,24},{12,28},{16,0},{20,4},{24,8},{28,12},{1,17},{... | collective-permute-start | bytes 1572872 | tf_op jit(solution)/shard_map/ppermute | solution.py:25
  299.7 25.0 %collective-permute-start.45 = (bf16[128,2048]{1,0:T(8,128)(2,1)S(1)}, bf16[128,2048]{1,0:T(8,128)(2,1)S(1)}, u32[]{:S(2)}, u32[]{:S(2)}) collective-permute-start(bf16[128,2048]{1,0:T(8,128)(2,1)S(1)} %get-tuple-element.502), channel_id=1, source_target_pairs={{0,8},{4,12},{8,0},{12,4},{16,24},{20,28},{24,16},{28,20},{1,9},{5... | collective-permute-start | bytes 1572872 | tf_op jit(solution)/shard_map/ppermute | solution.py:25
  311.1 13.6 %collective-permute-start.48 = (bf16[2,128,1024]{2,1,0:T(8,128)(2,1)S(1)}, bf16[2,128,1024]{2,1,0:T(8,128)(2,1)S(1)}, u32[]{:S(2)}, u32[]{:S(2)}) collective-permute-start(bf16[2,128,1024]{2,1,0:T(8,128)(2,1)S(1)} %get-tuple-element.505), channel_id=1, source_target_pairs={{0,1},{1,0},{2,3},{3,2},{4,5},{5,4},{6,7},{7,6},{8,9},{9,8},{10,11... | collective-permute-start | bytes 1572872 | tf_op jit(solution)/shard_map/ppermute | solution.py:25
  311.8 13.0 %collective-permute-start.46 = (bf16[2,128,1024]{2,1,0:T(8,128)(2,1)S(1)}, bf16[2,128,1024]{2,1,0:T(8,128)(2,1)S(1)}, u32[]{:S(2)}, u32[]{:S(2)}) collective-permute-start(bf16[2,128,1024]{2,1,0:T(8,128)(2,1)S(1)} %get-tuple-element.503), channel_id=1, source_target_pairs={{0,8},{4,12},{8,0},{12,4},{16,24},{20,28},{24,16},{28,20},{1,9},{5... | collective-permute-start | bytes 1572872 | tf_op jit(solution)/shard_map/ppermute | solution.py:25
  313.1 12.5 %collective-permute-start.47 = (bf16[2,128,1024]{2,1,0:T(8,128)(2,1)S(1)}, bf16[2,128,1024]{2,1,0:T(8,128)(2,1)S(1)}, u32[]{:S(2)}, u32[]{:S(2)}) collective-permute-start(bf16[2,128,1024]{2,1,0:T(8,128)(2,1)S(1)} %get-tuple-element.504), channel_id=1, source_target_pairs={{0,16},{4,20},{8,24},{12,28},{16,0},{20,4},{24,8},{28,12},{1,17},{... | collective-permute-start | bytes 1572872 | tf_op jit(solution)/shard_map/ppermute | solution.py:25
  329.3 20.7 %collective-permute-start.49 = (bf16[512,2048]{1,0:T(8,128)(2,1)S(1)}, bf16[512,2048]{1,0:T(8,128)(2,1)S(1)}, u32[]{:S(2)}, u32[]{:S(2)}) collective-permute-start(bf16[512,2048]{1,0:T(8,128)(2,1)S(1)} %attention_other.3), channel_id=1, source_target_pairs={{0,4},{4,0},{8,12},{12,8},{16,20},{20,16},{24,28},{28,24},{1,5},{5... | collective-permute-start | bytes 6291464 | tf_op jit(solution)/shard_map/ppermute | solution.py:25
  330.0 20.0 %collective-permute-start.52 = (bf16[2,128,1024]{2,1,0:T(8,128)(2,1)S(1)}, bf16[2,128,1024]{2,1,0:T(8,128)(2,1)S(1)}, u32[]{:S(2)}, u32[]{:S(2)}) collective-permute-start(bf16[2,128,1024]{2,1,0:T(8,128)(2,1)S(1)} %get-tuple-element.535), channel_id=1, source_target_pairs={{0,1},{1,0},{2,3},{3,2},{4,5},{5,4},{6,7},{7,6},{8,9},{9,8},{10,11... | collective-permute-start | bytes 1572872 | tf_op jit(solution)/shard_map/ppermute | solution.py:25
  333.8 14.4 %collective-permute-start.53 = (bf16[128,1024]{1,0:T(8,128)(2,1)S(1)}, bf16[128,1024]{1,0:T(8,128)(2,1)S(1)}, u32[]{:S(2)}, u32[]{:S(2)}) collective-permute-start(bf16[128,1024]{1,0:T(8,128)(2,1)S(1)} %fusion.6), channel_id=1, source_target_pairs={{0,2},{1,3},{2,0},{3,1},{4,6},{5,7},{6,4},{7,5},{8,10},{9,11},{10,... | collective-permute-start | bytes 786440 | tf_op jit(solution)/shard_map/ppermute | solution.py:25
  352.9 87.9 %all-gather.7.cloned.1.call-start = ((), (), s32[]{:S(2)}) async-start(), calls=%async_computation.1 | async-start | bytes 2359296 | tf_op jit(solution)/shard_map/all_gather | solution.py:1514
  366.8 19.1 %collective-permute-start.54 = (bf16[2,128,1024]{2,1,0:T(8,128)(2,1)S(1)}, bf16[2,128,1024]{2,1,0:T(8,128)(2,1)S(1)}, u32[]{:S(2)}, u32[]{:S(2)}) collective-permute-start(bf16[2,128,1024]{2,1,0:T(8,128)(2,1)S(1)} %get-tuple-element.555), channel_id=1, source_target_pairs={{0,8},{4,12},{8,0},{12,4},{16,24},{20,28},{24,16},{28,20},{1,9},{5... | collective-permute-start | bytes 1572872 | tf_op jit(solution)/shard_map/ppermute | solution.py:25
  367.5 19.2 %collective-permute-start.55 = (bf16[2,128,1024]{2,1,0:T(8,128)(2,1)S(1)}, bf16[2,128,1024]{2,1,0:T(8,128)(2,1)S(1)}, u32[]{:S(2)}, u32[]{:S(2)}) collective-permute-start(bf16[2,128,1024]{2,1,0:T(8,128)(2,1)S(1)} %get-tuple-element.556), channel_id=1, source_target_pairs={{0,16},{4,20},{8,24},{12,28},{16,0},{20,4},{24,8},{28,12},{1,17},{... | collective-permute-start | bytes 1572872 | tf_op jit(solution)/shard_map/ppermute | solution.py:25
  369.0 12.6 %collective-permute-start.56 = (bf16[1,128,1024]{2,1,0:T(8,128)(2,1)S(1)}, bf16[1,128,1024]{2,1,0:T(8,128)(2,1)S(1)}, u32[]{:S(2)}, u32[]{:S(2)}) collective-permute-start(bf16[1,128,1024]{2,1,0:T(8,128)(2,1)S(1)} %get-tuple-element.557), channel_id=1, source_target_pairs={{0,1},{1,0},{2,3},{3,2},{4,5},{5,4},{6,7},{7,6},{8,9},{9,8},{10,11... | collective-permute-start | bytes 786440 | tf_op jit(solution)/shard_map/ppermute | solution.py:25
  371.7 13.6 %collective-permute-start.57 = (bf16[128,1024]{1,0:T(8,128)(2,1)S(1)}, bf16[128,1024]{1,0:T(8,128)(2,1)S(1)}, u32[]{:S(2)}, u32[]{:S(2)}) collective-permute-start(bf16[128,1024]{1,0:T(8,128)(2,1)S(1)} %fusion.7), channel_id=1, source_target_pairs={{0,2},{1,3},{2,0},{3,1},{4,6},{5,7},{6,4},{7,5},{8,10},{9,11},{10,... | collective-permute-start | bytes 786440 | tf_op jit(solution)/shard_map/ppermute | solution.py:25
  396.6 11.2 %collective-permute-start.70 = (f32[34,1024]{1,0:T(8,128)S(1)}, f32[34,1024]{1,0:T(8,128)S(1)}, u32[]{:S(2)}, u32[]{:S(2)}) collective-permute-start(f32[34,1024]{1,0:T(8,128)S(1)} %concatenate.81), channel_id=1, source_target_pairs={{0,4},{4,0},{8,12},{12,8},{16,20},{20,16},{24,28},{28,24},{1,5},{5... | collective-permute-start | bytes 417800 | tf_op jit(solution)/shard_map/ppermute | solution.py:25
  396.7 19.4 %collective-permute-start.58 = (bf16[128,1024]{1,0:T(8,128)(2,1)S(1)}, bf16[128,1024]{1,0:T(8,128)(2,1)S(1)}, u32[]{:S(2)}, u32[]{:S(2)}) collective-permute-start(bf16[128,1024]{1,0:T(8,128)(2,1)S(1)} %fusion.8), channel_id=1, source_target_pairs={{0,2},{1,3},{2,0},{3,1},{4,6},{5,7},{6,4},{7,5},{8,10},{9,11},{10,... | collective-permute-start | bytes 786440 | tf_op jit(solution)/shard_map/ppermute | solution.py:25
  404.5 11.6 %collective-permute-start.61 = (bf16[1,128,1024]{2,1,0:T(8,128)(2,1)S(1)}, bf16[1,128,1024]{2,1,0:T(8,128)(2,1)S(1)}, u32[]{:S(2)}, u32[]{:S(2)}) collective-permute-start(bf16[1,128,1024]{2,1,0:T(8,128)(2,1)S(1)} %get-tuple-element.580), channel_id=1, source_target_pairs={{0,1},{1,0},{2,3},{3,2},{4,5},{5,4},{6,7},{7,6},{8,9},{9,8},{10,11... | collective-permute-start | bytes 786440 | tf_op jit(solution)/shard_map/ppermute | solution.py:25
  423.8 21.0 %collective-permute-start.65 = (bf16[2,128,512]{2,1,0:T(8,128)(2,1)S(1)}, bf16[2,128,512]{2,1,0:T(8,128)(2,1)S(1)}, u32[]{:S(2)}, u32[]{:S(2)}) collective-permute-start(bf16[2,128,512]{2,1,0:T(8,128)(2,1)S(1)} %pad_maximum_fusion.11.refs_2_), channel_id=1, source_target_pairs={{0,8},{4,12},{8,0},{12,4},{16,24},{20,28},{24,16},{28,20},{1,9},{5... | collective-permute-start | bytes 786440 | tf_op jit(solution)/shard_map/ppermute | solution.py:25
  425.3 19.4 %collective-permute-start.63 = (bf16[2,128,512]{2,1,0:T(8,128)(2,1)S(1)}, bf16[2,128,512]{2,1,0:T(8,128)(2,1)S(1)}, u32[]{:S(2)}, u32[]{:S(2)}) collective-permute-start(bf16[2,128,512]{2,1,0:T(8,128)(2,1)S(1)} %pad_maximum_fusion.10.refs_0_), channel_id=1, source_target_pairs={{0,16},{4,20},{8,24},{12,28},{16,0},{20,4},{24,8},{28,12},{1,17},{... | collective-permute-start | bytes 786440 | tf_op jit(solution)/shard_map/ppermute | solution.py:25
  (144 other events, 1532.1 us)
Sparse Core Ops, SparseCore 0:
  353.1 33.7 all-gather.4
  388.7 32.4 all-gather.6

commit v5 on v4

--- a/solution.py
+++ b/solution.py
@@ -142,7 +142,7 @@
             jax.ShapeDtypeStruct((rows, count), BF16),
         ],
         name="attend",
-        compiler_params=pltpu.CompilerParams(vmem_limit_bytes=24 << 20),
+        compiler_params=pltpu.CompilerParams(vmem_limit_bytes=16 << 20),
         cost_estimate=LIGHT,
     )(queries, keys, values, key_const)
 
@@ -245,7 +245,7 @@
             pltpu.VMEM((span, 2 * wide), BF16),
         ],
         name="attend_back",
-        compiler_params=pltpu.CompilerParams(vmem_limit_bytes=24 << 20),
+        compiler_params=pltpu.CompilerParams(vmem_limit_bytes=16 << 20),
         cost_estimate=LIGHT,
     )(queries, keys, values, key_const, aug, grad_out, out, *([before] if causal else []))
 
@@ -497,7 +497,7 @@
             jax.ShapeDtypeStruct((blocks * rows, full), BF16),
         ],
         name="project",
-        compiler_params=pltpu.CompilerParams(vmem_limit_bytes=28 << 20),
+        compiler_params=pltpu.CompilerParams(vmem_limit_bytes=22 << 20),
         cost_estimate=LIGHT,
     )(device.reshape(1), *normed, biases, *group.inputs)
 
@@ -584,7 +584,7 @@
             jax.ShapeDtypeStruct((rows, mp * hidden), BF16),
         ],
         name="feed_up",
-        compiler_params=pltpu.CompilerParams(vmem_limit_bytes=44 << 20),
+        compiler_params=pltpu.CompilerParams(vmem_limit_bytes=38 << 20),
         cost_estimate=LIGHT,
     )(
         device.reshape(1), att_a, att_b, residual, vectors, u_bias, *group_a.inputs, *group_u.inputs
@@ -671,7 +671,7 @@
             jax.ShapeDtypeStruct((24, full), F32),
         ],
         name="feed_down",
-        compiler_params=pltpu.CompilerParams(vmem_limit_bytes=30 << 20),
+        compiler_params=pltpu.CompilerParams(vmem_limit_bytes=26 << 20),
         cost_estimate=LIGHT,
     )(device.reshape(1), act, middle, cotangent, vectors, *group_d.inputs)
 
@@ -798,7 +798,7 @@
             jax.ShapeDtypeStruct((8, mp * hidden), F32),
         ],
         name="feed_back",
-        compiler_params=pltpu.CompilerParams(vmem_limit_bytes=52 << 20),
+        compiler_params=pltpu.CompilerParams(vmem_limit_bytes=46 << 20),
         cost_estimate=LIGHT,
     )(
         device.reshape(1),
@@ -870,7 +870,7 @@
         ),
         out_shape=jax.ShapeDtypeStruct((rows, full), dtype),
         name="unproject",
-        compiler_params=pltpu.CompilerParams(vmem_limit_bytes=22 << 20),
+        compiler_params=pltpu.CompilerParams(vmem_limit_bytes=18 << 20),
         cost_estimate=LIGHT,
     )(device.reshape(1), *grads, *([] if before is None else [before]), *group.inputs)
 
@@ -927,7 +927,7 @@
         ),
         out_shape=jax.ShapeDtypeStruct((full // 2, right.shape[1]), BF16),
         name="other_half",
-        compiler_params=pltpu.CompilerParams(vmem_limit_bytes=16 << 20),
+        compiler_params=pltpu.CompilerParams(vmem_limit_bytes=12 << 20),
         cost_estimate=LIGHT,
     )(device.reshape(1), left, right)
 
@@ -958,7 +958,7 @@
         ),
         out_shape=[jax.ShapeDtypeStruct(shape, BF16)] * 4,
         name="this_half",
-        compiler_params=pltpu.CompilerParams(vmem_limit_bytes=24 << 20),
+        compiler_params=pltpu.CompilerParams(vmem_limit_bytes=18 << 20),
         cost_estimate=LIGHT,
     )(device.reshape(1), left, right, got)
 
@@ -1037,7 +1037,7 @@
         ),
         out_shape=jax.ShapeDtypeStruct(out, BF16),
         name="attention_other",
-        compiler_params=pltpu.CompilerParams(vmem_limit_bytes=16 << 20),
+        compiler_params=pltpu.CompilerParams(vmem_limit_bytes=12 << 20),
         cost_estimate=LIGHT,
     )(device.reshape(1), *normed, branch, *grads, attended)
 
@@ -1058,7 +1058,7 @@
         ),
         out_shape=[jax.ShapeDtypeStruct(shape, BF16)] * 4,
         name="attention_this",
-        compiler_params=pltpu.CompilerParams(vmem_limit_bytes=24 << 20),
+        compiler_params=pltpu.CompilerParams(vmem_limit_bytes=16 << 20),
         cost_estimate=LIGHT,
     )(device.reshape(1), *normed, branch, *grads, attended, got)
 
@@ -1092,7 +1092,7 @@
         ),
         out_shape=[jax.ShapeDtypeStruct((rows, columns), BF16)] * 4,
         name="next_stage",
-        compiler_params=pltpu.CompilerParams(vmem_limit_bytes=16 << 20),
+        compiler_params=pltpu.CompilerParams(vmem_limit_bytes=10 << 20),
         cost_estimate=LIGHT,
     )(device.reshape(1), *inputs)
 
@@ -1125,7 +1125,7 @@
         in_specs=[pl.BlockSpec(memory_space=pltpu.VMEM)] * 4,
         out_specs=[pl.BlockSpec(memory_space=pltpu.VMEM)] * 2,
         name="by_layer_pieces",
-        compiler_params=pltpu.CompilerParams(vmem_limit_bytes=12 << 20),
+        compiler_params=pltpu.CompilerParams(vmem_limit_bytes=8 << 20),
         cost_estimate=LIGHT,
     )(keeps[0], gots[0], keeps[1], gots[1])
     return send, rest, odd, even
@@ -1480,8 +1480,9 @@
     grads_b = begin([flow_u, flow_qa, flow_d], *grads_b)
     near_b = unproject(grads_b, (0, 1, 2), group_a, 0, near_a, F32, device)
     near_b, *grads_a, sums_ffn, sums_back, sums_up = meet(
-        [flow_qb, flow_qa, flow_u, flow_d], near_b, *grads_a, sums_ffn, sums_back, sums_up
-    )
+        [flow_qb, flow_qa], near_b, *grads_a, sums_ffn, sums_back, sums_up
+    )
+    near_b = meet([flow_u, flow_d], near_b)
     drain(flow_d)
     down_mine = flow_d.result.astype(BF16)
     down_all = lax.all_gather(down_mine, "dp", axis=0)
@@ -1525,11 +1526,11 @@
     drain(flow_qa, flow_qb)
     mine = (flow_qa.result + flow_qb.result).astype(BF16)
     flow_o = Flow(spread_flow((mine[:, : 2 * width], mine[:, 2 * width :])))
-    for _ in range(2 * stages):
-        flow_o.move(flow_o.held)
+    for _ in range(2 * (dp.bit_length() + mp.bit_length() - 3)):
+        flow_s.move(flow_s.held)
     down_grad = fill_ffn(down_all, True)
     up_grad = fill_ffn(up_all, False)
-    down_grad, up_grad = begin([flow_o], down_grad, up_grad)
+    down_grad, up_grad = begin([flow_s], down_grad, up_grad)
     drain(flow_o, flow_s)
     qkv_grad, out_grad = fill_attention(flow_o.result, full, width, device)
 

time: 464 us -> 461 us (level)
  local copies, waits for them, and re-layouts: 49.1 us -> 38.9 us
  other arithmetic: 14.6 us -> 19.8 us
    unnamed x236 -> x194, local copies, waits for them, and re-layouts: 34.2 us -> 26.1 us
  transfers between devices with their start and end apart: 77 -> 77, of which waited for: 29 -> 32; matrix products, arithmetic and copies ran while one was open for 5% -> 5% of each run, Pallas kernels for 32% -> 33%
where the time goes in v5:
time: 461 us; the launch traced here: 456 us
  Pallas kernels  185 us (40%)
  waiting for transfers between devices  113 us (25%)
  starting transfers between devices  81.2 us (18%)
  local copies, waits for them, and re-layouts  38.9 us (8%)
  other arithmetic  19.8 us (4%)
  between operations  16.1 us (3%)
    ppermute x75, waiting for transfers between devices, swap(): return lax.ppermute(value, axis, [(i, i ^ mask) for i in range(count)])  113 us
    ppermute x75, starting transfers between devices, swap(): return lax.ppermute(value, axis, [(i, i ^ mask) for i in range(count)])  81.2 us
    pallas_call x3, Pallas kernels, attend_back(): pl.pallas_call(functools.partial(attend_back_kernel, causal), grid=(count...  40.4 us
    unnamed x194, local copies, waits for them, and re-layouts  26.1 us
    pallas_call x1, Pallas kernels, feed_back(): pl.pallas_call(functools.partial(back_kernel, group_a, group_u, group_d),...  25.7 us
    pallas_call x1, Pallas kernels, feed_up(): pl.pallas_call(functools.partial(up_kernel, group_a, group_u), grid_spec=...  18.2 us
    pallas_call x2, Pallas kernels, attend(): pl.pallas_call(functools.partial(attend_kernel, span // rows, rows), grid...  17.6 us
    pallas_call x3, Pallas kernels, unproject(): pl.pallas_call(functools.partial(unproject_kernel, group, which, begin, c...  14.7 us
  transfers between devices with their start and end apart: 77, of which 32 were waited for; matrix products, arithmetic and copies ran while one was open for 5% of the time, Pallas kernels for 33%

profile of v5, /device:TPU:0, one launch (start us, length us, event | category | flops | bytes accessed | tf_op | source)
XLA Modules:
  0.0 456.5 jit_solution(2845826871347097919)
XLA Ops:
  10.7 3.1 collective-permute-start
  13.8 2.6 collective-permute-start.1
  23.4 2.5 collective-permute-done
  25.9 2.5 collective-permute-done.1
  28.9 6.0 %collective-permute-done.2 = bf16[528,256]{1,0:T(8,128)(2,1)S(1)} collective-permute-done((bf16[528,256]{1,0:T(8,128)(2,1)S(1)}, bf16[528,256]{1,0:T(8,128)(2,1)S(1)}, u32[]{:S(2)}, u32[]{:S(2)}) %collective-permute-start.2) | collective-permute-done | bytes 270368 | tf_op jit(solution)/shard_map/ppermute | solution.py:25
  40.2 3.5 collective-permute-done.3
  52.7 21.0 %collective-permute-done.7 = bf16[128,1024]{1,0:T(8,128)(2,1)} collective-permute-done((bf16[128,1024]{1,0:T(8,128)(2,1)}, bf16[128,1024]{1,0:T(8,128)(2,1)}, u32[]{:S(2)}, u32[]{:S(2)}) %collective-permute-start.7) | collective-permute-done | bytes 262176 | tf_op jit(solution)/shard_map/ppermute | solution.py:25
  78.5 6.9 %collective-permute-done.14 = bf16[128,1024]{1,0:T(8,128)(2,1)} collective-permute-done((bf16[128,1024]{1,0:T(8,128)(2,1)}, bf16[128,1024]{1,0:T(8,128)(2,1)}, u32[]{:S(2)}, u32[]{:S(2)}) %collective-permute-start.14) | collective-permute-done | bytes 262176 | tf_op jit(solution)/shard_map/ppermute | solution.py:25
  92.2 9.5 %project.1 = (bf16[544,1024]{1,0:T(8,128)(2,1)S(1)}, bf16[1088,1024]{1,0:T(8,128)(2,1)S(1)}, bf16[1088,1024]{1,0:T(8,128)(2,1)S(1)}) custom-call(s32[1]{0:T(128)} %bitcast.scal, bf16[544,1024]{1,0:T(8,128)(2,1)} %collective-permute-done.9.refs_0_, bf16[544,1024]{1,0:T(8,128)(2,1)S(1)} %add_convert_fusion.refs_1_, f32[8,1024]{1,0:T(8,128)S(1)} %pad.28.refs_2_, ...), custom_call_target="tpu_custom_call" | custom-call | flops 1000 | bytes 1000 | tf_op jit(solution)/shard_map/project/pallas_call | solution.py:483
  108.2 8.8 %attend.2 = (bf16[544,512]{1,0:T(8,128)(2,1)S(1)}, bf16[544,512]{1,0:T(8,128)(2,1)S(1)}) custom-call(bf16[544,1024]{1,0:T(8,128)(2,1)S(1)} %get-tuple-element.371.q_ref, bf16[1088,1024]{1,0:T(8,128)(2,1)S(1)} %get-tuple-element.362.k_ref, bf16[1088,1024]{1,0:T(8,128)(2,1)S(1)} %get-tuple-element.363.v_ref, bf16[1088,128]{1,0:T(8,128)(2,1)S(1)} %select_convert_fusion.kc_ref), custom_call_target="tpu_custom_call" | custom-call | flops 1000 | bytes 1000 | tf_op jit(solution)/shard_map/attend/pallas_call | solution.py:130
  118.4 8.8 %attend.3 = (bf16[544,512]{1,0:T(8,128)(2,1)S(1)}, bf16[544,512]{1,0:T(8,128)(2,1)S(1)}) custom-call(bf16[544,1024]{1,0:T(8,128)(2,1)S(1)} %get-tuple-element.371.q_ref, bf16[1088,1024]{1,0:T(8,128)(2,1)S(1)} %get-tuple-element.362.k_ref, bf16[1088,1024]{1,0:T(8,128)(2,1)S(1)} %get-tuple-element.363.v_ref, bf16[1088,128]{1,0:T(8,128)(2,1)S(1)} %select_convert_fusion.kc_ref), custom_call_target="tpu_custom_call" | custom-call | flops 1000 | bytes 1000 | tf_op jit(solution)/shard_map/attend/pallas_call | solution.py:130
  127.2 4.7 %collective-permute-done.22 = bf16[1,3,1,64,1024]{4,3,1,2,0:T(8,128)(2,1)S(1)} collective-permute-done((bf16[1,3,1,64,1024]{4,3,1,2,0:T(8,128)(2,1)S(1)}, bf16[1,3,1,64,1024]{4,3,1,2,0:T(8,128)(2,1)S(1)}, u32[]{:S(2)}, u32[]{:S(2)}) %collective-permute-start.22) | collective-permute-done | bytes 393248 | tf_op jit(solution)/shard_map/ppermute | solution.py:25
  143.2 18.2 %feed_up.1 = (f32[544,1024]{1,0:T(8,128)}, f32[544,1024]{1,0:T(8,128)}, bf16[544,1024]{1,0:T(8,128)(2,1)S(1)}, bf16[544,4096]{1,0:T(8,128)(2,1)}, bf16[544,4096]{1,0:T(8,128)(2,1)}) custom-call(s32[1]{0:T(128)} %bitcast.scal, bf16[544,512]{1,0:T(8,128)(2,1)S(1)} %get-tuple-element.370.refs_0_, bf16[544,512]{1,0:T(8,128)(2,1)S(1)} %copy-done.40, ...), custom_call_target="tpu_custom_call" | custom-call | flops 1000 | bytes 1000 | tf_op jit(solution)/shard_map/feed_up/pallas_call | solution.py:567
  167.4 2.5 copy-done.8
  171.5 10.1 %feed_down.1 = (bf16[544,1024]{1,0:T(8,128)(2,1)}, bf16[544,1024]{1,0:T(8,128)(2,1)S(1)}, f32[24,1024]{1,0:T(8,128)S(1)}) custom-call(s32[1]{0:T(128)} %bitcast.scal, bf16[544,4096]{1,0:T(8,128)(2,1)S(1)} %copy-done.8, f32[544,1024]{1,0:T(8,128)S(1)} %copy-done.20, bf16[544,1024]{1,0:T(8,128)(2,1)S(1)} %copy-done.32, ...), custom_call_target="tpu_custom_call" | custom-call | flops 1000 | bytes 1000 | tf_op jit(solution)/shard_map/feed_down/pallas_call | solution.py:657
  181.7 4.7 %other_half.2 = bf16[512,4096]{1,0:T(8,128)(2,1)S(1)} custom-call(s32[1]{0:T(128)} %bitcast.scal, bf16[544,1024]{1,0:T(8,128)(2,1)S(1)} %get-tuple-element.417.left_ref.refs_0_, bf16[544,4096]{1,0:T(8,128)(2,1)S(1)} %copy-done.8), custom_call_target="tpu_custom_call" | custom-call | flops 1000 | bytes 1000 | tf_op jit(solution)/shard_map/other_half/pallas_call | solution.py:917
  186.6 7.0 %collective-permute-done.34.got_ref = bf16[512,4096]{1,0:T(8,128)(2,1)S(1)} collective-permute-done((bf16[512,4096]{1,0:T(8,128)(2,1)S(1)}, bf16[512,4096]{1,0:T(8,128)(2,1)S(1)}, u32[]{:S(2)}, u32[]{:S(2)}) %collective-permute-start.34) | collective-permute-done | bytes 4194336 | tf_op jit(solution)/shard_map/ppermute | solution.py:25
  193.7 6.2 %this_half.2 = (bf16[2,128,2048]{2,1,0:T(8,128)(2,1)}, bf16[2,128,2048]{2,1,0:T(8,128)(2,1)S(1)}, bf16[2,128,2048]{2,1,0:T(8,128)(2,1)S(1)}, bf16[2,128,2048]{2,1,0:T(8,128)(2,1)S(1)}) custom-call(s32[1]{0:T(128)} %bitcast.scal, bf16[544,1024]{1,0:T(8,128)(2,1)S(1)} %get-tuple-element.417.left_ref.refs_0_, bf16[544,4096]{1,0:T(8,128)(2,1)S(1)} %bitcast.119, ...), custom_call_target="tpu_custom_call" | custom-call | flops 1000 | bytes 1000 | tf_op jit(solution)/shard_map/this_half/pallas_call | solution.py:946
  201.9 25.7 %feed_back.1 = (bf16[544,4096]{1,0:T(8,128)(2,1)}, f32[544,1024]{1,0:T(8,128)}, bf16[544,1024]{1,0:T(8,128)(2,1)}, bf16[544,1024]{1,0:T(8,128)(2,1)}, f32[40,1024]{1,0:T(8,128)S(1)}, /*index=5*/f32[8,4096]{1,0:T(8,128)S(1)}) custom-call(s32[1]{0:T(128)} %bitcast.scal, bf16[544,1024]{1,0:T(8,128)(2,1)} %copy-done.17, ...), custom_call_target="tpu_custom_call" | custom-call | flops 1000 | bytes 1000 | tf_op jit(solution)/shard_map/feed_back/pallas_call | solution.py:773
  229.9 5.4 %other_half.3 = bf16[512,4096]{1,0:T(8,128)(2,1)} custom-call(s32[1]{0:T(128)} %bitcast.scal, bf16[544,1024]{1,0:T(8,128)(2,1)S(1)} %get-tuple-element.439.left_ref, bf16[544,4096]{1,0:T(8,128)(2,1)S(1)} %bitcast.121), custom_call_target="tpu_custom_call" | custom-call | flops 1000 | bytes 1000 | tf_op jit(solution)/shard_map/other_half/pallas_call | solution.py:917
  239.7 20.2 %attend_back.3 = (f32[544,1024]{1,0:T(8,128)S(1)}, bf16[544,1024]{1,0:T(8,128)(2,1)S(1)}, bf16[544,1024]{1,0:T(8,128)(2,1)S(1)}) custom-call(bf16[544,1024]{1,0:T(8,128)(2,1)S(1)} %copy-done.10, bf16[1088,1024]{1,0:T(8,128)(2,1)S(1)} %copy-done.5, bf16[1088,1024]{1,0:T(8,128)(2,1)S(1)} %copy-done.7, bf16[1088,128]{1,0:T(8,128)(2,1)S(1)} %select_convert_fusion.kc_ref, ...), custom_call_target="tpu_custom_call" | custom-call | flops 1000 | bytes 1000 | tf_op jit(solution)/shard_map/attend_back/pallas_call | solution.py:223
  259.9 5.5 %unproject.3 = bf16[544,1024]{1,0:T(8,128)(2,1)S(1)} custom-call(s32[1]{0:T(128)} %bitcast.scal, bf16[544,1024]{1,0:T(8,128)(2,1)S(1)} %get-tuple-element.477.refs_0_.refs_6_, bf16[544,1024]{1,0:T(8,128)(2,1)S(1)} %get-tuple-element.478.refs_1_.refs_7_, bf16[3,1024,256]{2,1,0:T(8,128)(2,1)S(1)} %copy-done.3, bf16[256,1024]{1,0:T(8,128)(2,1)S(1)} %copy-done.15, ...), custom_call_target="tpu_custom_call" | custom-call | flops 1000 | bytes 1000 | tf_op jit(solution)/shard_map/unproject/pallas_call | solution.py:858
  265.5 5.6 %this_half.3 = (bf16[2,128,2048]{2,1,0:T(8,128)(2,1)S(1)}, bf16[2,128,2048]{2,1,0:T(8,128)(2,1)S(1)}, bf16[2,128,2048]{2,1,0:T(8,128)(2,1)S(1)}, bf16[2,128,2048]{2,1,0:T(8,128)(2,1)S(1)}) custom-call(s32[1]{0:T(128)} %bitcast.scal, bf16[544,1024]{1,0:T(8,128)(2,1)S(1)} %get-tuple-element.439.left_ref, bf16[544,4096]{1,0:T(8,128)(2,1)S(1)} %bitcast.121, ...), custom_call_target="tpu_custom_call" | custom-call | flops 1000 | bytes 1000 | tf_op jit(solution)/shard_map/this_half/pallas_call | solution.py:946
  273.8 10.1 %attend_back.4 = (bf16[544,512]{1,0:T(8,128)(2,1)S(1)}, bf16[544,512]{1,0:T(8,128)(2,1)S(1)}, bf16[544,512]{1,0:T(8,128)(2,1)S(1)}) custom-call(bf16[544,1024]{1,0:T(8,128)(2,1)S(1)} %copy-done.10, bf16[1088,1024]{1,0:T(8,128)(2,1)S(1)} %copy-done.5, bf16[1088,1024]{1,0:T(8,128)(2,1)S(1)} %copy-done.7, bf16[1088,128]{1,0:T(8,128)(2,1)S(1)} %select_convert_fusion.kc_ref, ...), custom_call_target="tpu_custom_call" | custom-call | flops 1000 | bytes 1000 | tf_op jit(solution)/shard_map/attend_back/pallas_call | solution.py:223
  283.9 4.2 attention_other.2
  288.0 8.5 %collective-permute-done.40.refs_1_.refs_3_ = bf16[2,128,2048]{2,1,0:T(8,128)(2,1)S(1)} collective-permute-done((bf16[2,128,2048]{2,1,0:T(8,128)(2,1)S(1)}, bf16[2,128,2048]{2,1,0:T(8,128)(2,1)S(1)}, u32[]{:S(2)}, u32[]{:S(2)}) %collective-permute-start.40) | collective-permute-done | bytes 1048608 | tf_op jit(solution)/shard_map/ppermute | solution.py:25
  301.5 5.1 %unproject.4.refs_3_ = f32[544,1024]{1,0:T(8,128)S(1)} custom-call(s32[1]{0:T(128)} %bitcast.scal, bf16[544,512]{1,0:T(8,128)(2,1)S(1)} %get-tuple-element.588.refs_3_.refs_0_, bf16[544,512]{1,0:T(8,128)(2,1)S(1)} %get-tuple-element.481.refs_4_.refs_1_, bf16[544,512]{1,0:T(8,128)(2,1)S(1)} %get-tuple-element.589.refs_5_.refs_2_, ...), custom_call_target="tpu_custom_call" | custom-call | flops 1000 | bytes 1000 | tf_op jit(solution)/shard_map/unproject/pallas_call | solution.py:858
  306.6 4.8 %attention_this.2 = (bf16[2,128,1024]{2,1,0:T(8,128)(2,1)S(1)}, bf16[2,128,1024]{2,1,0:T(8,128)(2,1)S(1)}, bf16[2,128,1024]{2,1,0:T(8,128)(2,1)S(1)}, bf16[2,128,1024]{2,1,0:T(8,128)(2,1)S(1)}) custom-call(s32[1]{0:T(128)} %bitcast.scal, bf16[544,1024]{1,0:T(8,128)(2,1)} %collective-permute-done.9.refs_0_, bf16[544,1024]{1,0:T(8,128)(2,1)S(1)} %add_convert_fusion.refs_1_, ...), custom_call_target="tpu_custom_call" | custom-call | flops 1000 | bytes 1000 | tf_op jit(solution)/shard_map/attention_this/pallas_call | solution.py:1049
  315.0 10.1 %attend_back.5 = (bf16[544,512]{1,0:T(8,128)(2,1)S(1)}, bf16[544,512]{1,0:T(8,128)(2,1)S(1)}, bf16[544,512]{1,0:T(8,128)(2,1)S(1)}) custom-call(bf16[544,1024]{1,0:T(8,128)(2,1)S(1)} %copy-done.10, bf16[1088,1024]{1,0:T(8,128)(2,1)S(1)} %copy-done.5, bf16[1088,1024]{1,0:T(8,128)(2,1)S(1)} %copy-done.7, bf16[1088,128]{1,0:T(8,128)(2,1)S(1)} %select_convert_fusion.kc_ref, ...), custom_call_target="tpu_custom_call" | custom-call | flops 1000 | bytes 1000 | tf_op jit(solution)/shard_map/attend_back/pallas_call | solution.py:223
  326.7 3.8 attention_other.3
  334.7 2.8 collective-permute-start.53
  337.5 4.1 unproject.5
  341.7 5.2 %attention_this.3 = (bf16[2,128,1024]{2,1,0:T(8,128)(2,1)S(1)}, bf16[2,128,1024]{2,1,0:T(8,128)(2,1)S(1)}, bf16[2,128,1024]{2,1,0:T(8,128)(2,1)S(1)}, bf16[2,128,1024]{2,1,0:T(8,128)(2,1)S(1)}) custom-call(s32[1]{0:T(128)} %bitcast.scal, bf16[544,1024]{1,0:T(8,128)(2,1)} %collective-permute-done.9.refs_0_, bf16[544,1024]{1,0:T(8,128)(2,1)S(1)} %add_convert_fusion.refs_1_, ...), custom_call_target="tpu_custom_call" | custom-call | flops 1000 | bytes 1000 | tf_op jit(solution)/shard_map/attention_this/pallas_call | solution.py:1049
  360.9 3.0 multiply_reduce_fusion
  365.9 3.3 collective-permute-done.57
  369.7 2.7 collective-permute-done.54.refs_1_.refs_3_
  384.2 3.9 collective-permute-done.59.got_a
  391.0 5.0 %collective-permute-done.58 = bf16[128,1024]{1,0:T(8,128)(2,1)S(1)} collective-permute-done((bf16[128,1024]{1,0:T(8,128)(2,1)S(1)}, bf16[128,1024]{1,0:T(8,128)(2,1)S(1)}, u32[]{:S(2)}, u32[]{:S(2)}) %collective-permute-start.58) | collective-permute-done | bytes 262176 | tf_op jit(solution)/shard_map/ppermute | solution.py:25
  396.0 3.0 collective-permute-done.61
  409.5 2.7 collective-permute-start.72
  412.2 8.6 %collective-permute-done.72 = f32[34,1024]{1,0:T(8,128)S(1)} collective-permute-done((f32[34,1024]{1,0:T(8,128)S(1)}, f32[34,1024]{1,0:T(8,128)S(1)}, u32[]{:S(2)}, u32[]{:S(2)}) %collective-permute-start.72) | collective-permute-done | bytes 139296 | tf_op jit(solution)/shard_map/ppermute | solution.py:25
  420.9 2.4 collective-permute-start.73
  424.3 2.3 collective-permute-done.73
  428.2 2.6 fill_ffn.2
  432.3 2.3 fill_ffn.3
  434.6 4.7 %collective-permute-start.74 = (f32[34,1024]{1,0:T(8,128)S(1)}, f32[34,1024]{1,0:T(8,128)S(1)}, u32[]{:S(2)}, u32[]{:S(2)}) collective-permute-start(f32[34,1024]{1,0:T(8,128)S(1)} %add.235), channel_id=1, source_target_pairs={{0,2},{1,3},{2,0},{3,1},{4,6},{5,7},{6,4},{7,5},{8,10},{9,11},{10,... | collective-permute-start | bytes 417800 | tf_op jit(solution)/shard_map/ppermute | solution.py:25
  439.3 2.5 fill_attention.1
  441.8 4.1 collective-permute-done.74
  (441 shorter events, 137.9 us)
Async XLA Ops:
  7.2 419.4 %all-gather.5.cloned.1.call-start = ((), (), s32[]{:S(2)}) async-start(), calls=%async_computation | async-start | bytes 2359296 | tf_op jit(solution)/shard_map/all_gather | solution.py:1488
  10.7 15.2 %collective-permute-start = (bf16[528,256]{1,0:T(8,128)(2,1)S(1)}, bf16[528,256]{1,0:T(8,128)(2,1)S(1)}, u32[]{:S(2)}, u32[]{:S(2)}) collective-permute-start(bf16[528,256]{1,0:T(8,128)(2,1)S(1)} %fusion.5), channel_id=1, source_target_pairs={{0,1},{1,0},{2,3},{3,2},{4,5},{5,4},{6,7},{7,6},{8,9},{9,8},{10,11... | collective-permute-start | bytes 811016 | tf_op jit(solution)/shard_map/ppermute | solution.py:25
  13.8 14.7 %collective-permute-start.1 = (bf16[528,256]{1,0:T(8,128)(2,1)S(1)}, bf16[528,256]{1,0:T(8,128)(2,1)S(1)}, u32[]{:S(2)}, u32[]{:S(2)}) collective-permute-start(bf16[528,256]{1,0:T(8,128)(2,1)S(1)} %fusion.5), channel_id=1, source_target_pairs={{0,2},{1,3},{2,0},{3,1},{4,6},{5,7},{6,4},{7,5},{8,10},{9,11},{10,... | collective-permute-start | bytes 811016 | tf_op jit(solution)/shard_map/ppermute | solution.py:25
  38.9 34.8 %collective-permute-start.9 = (bf16[544,1024]{1,0:T(8,128)(2,1)S(1)}, bf16[544,1024]{1,0:T(8,128)(2,1)}, u32[]{:S(2)}, u32[]{:S(2)}) collective-permute-start(bf16[544,1024]{1,0:T(8,128)(2,1)S(1)} %add_convert_fusion.refs_1_), channel_id=1, source_target_pairs={{0,1},{1,0},{2,3},{3,2},{4,5},{5,4},{6,7},{7,6},{8,9},{9,8},{10,11... | collective-permute-start | bytes 3342344 | tf_op jit(solution)/shard_map/ppermute | solution.py:25
  46.6 27.1 %collective-permute-start.5 = (bf16[2,3,4,64,256]{4,3,2,1,0:T(8,128)(2,1)}, bf16[2,3,4,64,256]{4,3,2,1,0:T(8,128)(2,1)}, u32[]{:S(2)}, u32[]{:S(2)}) collective-permute-start(bf16[2,3,4,64,256]{4,3,2,1,0:T(8,128)(2,1)} %pad_maximum_fusion.1.refs_5_.refs_7_.refs_8_.refs_4_.refs_6_), channel_id=1, source_target_pairs={{0,16},{4,20},{8,24},{12,28},{16,0},{20,4},{24,8},{28,12},{1,17},{... | collective-permute-start | bytes 2359304 | tf_op jit(solution)/shard_map/ppermute | solution.py:25
  48.1 25.5 %collective-permute-start.6 = (bf16[2,3,4,64,256]{4,3,2,1,0:T(8,128)(2,1)S(1)}, bf16[2,3,4,64,256]{4,3,2,1,0:T(8,128)(2,1)}, u32[]{:S(2)}, u32[]{:S(2)}) collective-permute-start(bf16[2,3,4,64,256]{4,3,2,1,0:T(8,128)(2,1)S(1)} %pad_maximum_fusion.2.refs_7_.refs_9_.refs_10_.refs_6_.refs_8_), channel_id=1, source_target_pairs={{0,8},{4,12},{8,0},{12,4},{16,24},{20,28},{24,16},{28,20},{1,9},{5... | collective-permute-start | bytes 2359304 | tf_op jit(solution)/shard_map/ppermute | solution.py:25
  48.7 25.0 %collective-permute-start.7 = (bf16[128,1024]{1,0:T(8,128)(2,1)}, bf16[128,1024]{1,0:T(8,128)(2,1)}, u32[]{:S(2)}, u32[]{:S(2)}) collective-permute-start(bf16[128,1024]{1,0:T(8,128)(2,1)} %bitcast.12), channel_id=1, source_target_pairs={{0,1},{1,0},{2,3},{3,2},{4,5},{5,4},{6,7},{7,6},{8,9},{9,8},{10,11... | collective-permute-start | bytes 786440 | tf_op jit(solution)/shard_map/ppermute | solution.py:25
  50.5 23.2 %collective-permute-start.8 = (bf16[128,1024]{1,0:T(8,128)(2,1)}, bf16[128,1024]{1,0:T(8,128)(2,1)}, u32[]{:S(2)}, u32[]{:S(2)}) collective-permute-start(bf16[128,1024]{1,0:T(8,128)(2,1)} %bitcast.12), channel_id=1, source_target_pairs={{0,2},{1,3},{2,0},{3,1},{4,6},{5,7},{6,4},{7,5},{8,10},{9,11},{10,... | collective-permute-start | bytes 786440 | tf_op jit(solution)/shard_map/ppermute | solution.py:25
  73.7 11.7 %collective-permute-start.10 = (bf16[2,3,4,64,256]{4,3,2,1,0:T(8,128)(2,1)}, bf16[2,3,4,64,256]{4,3,2,1,0:T(8,128)(2,1)}, u32[]{:S(2)}, u32[]{:S(2)}) collective-permute-start(bf16[2,3,4,64,256]{4,3,2,1,0:T(8,128)(2,1)} %pad_maximum_fusion.1.refs_5_.refs_7_.refs_8_.refs_4_.refs_6_), channel_id=1, source_target_pairs={{0,4},{4,0},{8,12},{12,8},{16,20},{20,16},{24,28},{28,24},{1,5},{5... | collective-permute-start | bytes 2359304 | tf_op jit(solution)/shard_map/ppermute | solution.py:25
  73.8 11.6 %collective-permute-start.11 = (bf16[2,3,4,64,256]{4,3,2,1,0:T(8,128)(2,1)}, bf16[2,3,4,64,256]{4,3,2,1,0:T(8,128)(2,1)}, u32[]{:S(2)}, u32[]{:S(2)}) collective-permute-start(bf16[2,3,4,64,256]{4,3,2,1,0:T(8,128)(2,1)} %collective-permute-done.5.refs_6_.refs_8_.refs_9_.refs_5_.refs_7_), channel_id=1, source_target_pairs={{0,4},{4,0},{8,12},{12,8},{16,20},{20,16},{24,28},{28,24},{1,5},{5... | collective-permute-start | bytes 2359304 | tf_op jit(solution)/shard_map/ppermute | solution.py:25
  86.7 15.1 %collective-permute-start.17 = (bf16[1,3,1,64,1024]{4,3,1,2,0:T(8,128)(2,1)S(1)}, bf16[1,3,1,64,1024]{4,3,1,2,0:T(8,128)(2,1)S(1)}, u32[]{:S(2)}, u32[]{:S(2)}) collective-permute-start(bf16[1,3,1,64,1024]{4,3,1,2,0:T(8,128)(2,1)S(1)} %get-tuple-element.353), channel_id=1, source_target_pairs={{0,8},{4,12},{8,0},{12,4},{16,24},{20,28},{24,16},{28,20},{1,9},{5... | collective-permute-start | bytes 1179656 | tf_op jit(solution)/shard_map/ppermute | solution.py:25
  87.3 14.5 %collective-permute-start.18 = (bf16[1,3,1,64,1024]{4,3,2,1,0:T(8,128)(2,1)S(1)}, bf16[1,3,1,64,1024]{4,3,2,1,0:T(8,128)(2,1)S(1)}, u32[]{:S(2)}, u32[]{:S(2)}) collective-permute-start(bf16[1,3,1,64,1024]{4,3,2,1,0:T(8,128)(2,1)S(1)} %get-tuple-element.354), channel_id=1, source_target_pairs={{0,16},{4,20},{8,24},{12,28},{16,0},{20,4},{24,8},{28,12},{1,17},{... | collective-permute-start | bytes 1179656 | tf_op jit(solution)/shard_map/ppermute | solution.py:25
  88.5 13.2 %collective-permute-start.15 = (bf16[128,1024]{1,0:T(8,128)(2,1)S(1)}, bf16[128,1024]{1,0:T(8,128)(2,1)S(1)}, u32[]{:S(2)}, u32[]{:S(2)}) collective-permute-start(bf16[128,1024]{1,0:T(8,128)(2,1)S(1)} %bitcast.138), channel_id=1, source_target_pairs={{0,1},{1,0},{2,3},{3,2},{4,5},{5,4},{6,7},{7,6},{8,9},{9,8},{10,11... | collective-permute-start | bytes 786440 | tf_op jit(solution)/shard_map/ppermute | solution.py:25
  89.4 12.4 %collective-permute-start.16 = (bf16[128,1024]{1,0:T(8,128)(2,1)S(1)}, bf16[128,1024]{1,0:T(8,128)(2,1)S(1)}, u32[]{:S(2)}, u32[]{:S(2)}) collective-permute-start(bf16[128,1024]{1,0:T(8,128)(2,1)S(1)} %bitcast.139), channel_id=1, source_target_pairs={{0,2},{1,3},{2,0},{3,1},{4,6},{5,7},{6,4},{7,5},{8,10},{9,11},{10,... | collective-permute-start | bytes 786440 | tf_op jit(solution)/shard_map/ppermute | solution.py:25
  102.9 14.1 %collective-permute-start.19 = (bf16[128,1024]{1,0:T(8,128)(2,1)S(1)}, bf16[128,1024]{1,0:T(8,128)(2,1)S(1)}, u32[]{:S(2)}, u32[]{:S(2)}) collective-permute-start(bf16[128,1024]{1,0:T(8,128)(2,1)S(1)} %collective-permute-done.16), channel_id=1, source_target_pairs={{0,1},{1,0},{2,3},{3,2},{4,5},{5,4},{6,7},{7,6},{8,9},{9,8},{10,11... | collective-permute-start | bytes 786440 | tf_op jit(solution)/shard_map/ppermute | solution.py:25
  105.0 26.9 %collective-permute-start.20 = (bf16[2,3,1,64,1024]{4,3,1,2,0:T(8,128)(2,1)S(1)}, bf16[2,3,1,64,1024]{4,3,1,2,0:T(8,128)(2,1)}, u32[]{:S(2)}, u32[]{:S(2)}) collective-permute-start(bf16[2,3,1,64,1024]{4,3,1,2,0:T(8,128)(2,1)S(1)} %pad_maximum_fusion.4), channel_id=1, source_target_pairs={{0,16},{4,20},{8,24},{12,28},{16,0},{20,4},{24,8},{28,12},{1,17},{... | collective-permute-start | bytes 2359304 | tf_op jit(solution)/shard_map/ppermute | solution.py:25
  106.5 25.4 %collective-permute-start.21 = (bf16[2,3,1,64,1024]{4,3,2,1,0:T(8,128)(2,1)}, bf16[2,3,1,64,1024]{4,3,2,1,0:T(8,128)(2,1)}, u32[]{:S(2)}, u32[]{:S(2)}) collective-permute-start(bf16[2,3,1,64,1024]{4,3,2,1,0:T(8,128)(2,1)} %pad_maximum_fusion.5.refs_18_.refs_19_), channel_id=1, source_target_pairs={{0,8},{4,12},{8,0},{12,4},{16,24},{20,28},{24,16},{28,20},{1,9},{5... | collective-permute-start | bytes 2359304 | tf_op jit(solution)/shard_map/ppermute | solution.py:25
  117.2 14.7 %collective-permute-start.22 = (bf16[1,3,1,64,1024]{4,3,1,2,0:T(8,128)(2,1)S(1)}, bf16[1,3,1,64,1024]{4,3,1,2,0:T(8,128)(2,1)S(1)}, u32[]{:S(2)}, u32[]{:S(2)}) collective-permute-start(bf16[1,3,1,64,1024]{4,3,1,2,0:T(8,128)(2,1)S(1)} %get-tuple-element.375), channel_id=1, source_target_pairs={{0,8},{4,12},{8,0},{12,4},{16,24},{20,28},{24,16},{28,20},{1,9},{5... | collective-permute-start | bytes 1179656 | tf_op jit(solution)/shard_map/ppermute | solution.py:25
  117.8 14.0 %collective-permute-start.23 = (bf16[1,3,1,64,1024]{4,3,2,1,0:T(8,128)(2,1)S(1)}, bf16[1,3,1,64,1024]{4,3,2,1,0:T(8,128)(2,1)S(1)}, u32[]{:S(2)}, u32[]{:S(2)}) collective-permute-start(bf16[1,3,1,64,1024]{4,3,2,1,0:T(8,128)(2,1)S(1)} %get-tuple-element.376), channel_id=1, source_target_pairs={{0,16},{4,20},{8,24},{12,28},{16,0},{20,4},{24,8},{28,12},{1,17},{... | collective-permute-start | bytes 1179656 | tf_op jit(solution)/shard_map/ppermute | solution.py:25
  134.9 26.5 %collective-permute-start.28 = (bf16[2,3,1,64,1024]{4,3,1,2,0:T(8,128)(2,1)}, bf16[2,3,1,64,1024]{4,3,1,2,0:T(8,128)(2,1)}, u32[]{:S(2)}, u32[]{:S(2)}) collective-permute-start(bf16[2,3,1,64,1024]{4,3,1,2,0:T(8,128)(2,1)} %pad_maximum_fusion.7), channel_id=1, source_target_pairs={{0,16},{4,20},{8,24},{12,28},{16,0},{20,4},{24,8},{28,12},{1,17},{... | collective-permute-start | bytes 2359304 | tf_op jit(solution)/shard_map/ppermute | solution.py:25
  138.2 23.2 %collective-permute-start.29 = (bf16[2,3,1,64,1024]{4,3,2,1,0:T(8,128)(2,1)}, bf16[2,3,1,64,1024]{4,3,2,1,0:T(8,128)(2,1)}, u32[]{:S(2)}, u32[]{:S(2)}) collective-permute-start(bf16[2,3,1,64,1024]{4,3,2,1,0:T(8,128)(2,1)} %pad_maximum_fusion.8.refs_7_.refs_28_), channel_id=1, source_target_pairs={{0,8},{4,12},{8,0},{12,4},{16,24},{20,28},{24,16},{28,20},{1,9},{5... | collective-permute-start | bytes 2359304 | tf_op jit(solution)/shard_map/ppermute | solution.py:25
  199.9 27.7 %collective-permute-start.35 = (bf16[2,128,2048]{2,1,0:T(8,128)(2,1)}, bf16[2,128,2048]{2,1,0:T(8,128)(2,1)S(1)}, u32[]{:S(2)}, u32[]{:S(2)}) collective-permute-start(bf16[2,128,2048]{2,1,0:T(8,128)(2,1)} %get-tuple-element.426), channel_id=1, source_target_pairs={{0,8},{4,12},{8,0},{12,4},{16,24},{20,28},{24,16},{28,20},{1,9},{5... | collective-permute-start | bytes 3145736 | tf_op jit(solution)/shard_map/ppermute | solution.py:25
  201.4 26.2 %collective-permute-start.36 = (bf16[2,128,2048]{2,1,0:T(8,128)(2,1)S(1)}, bf16[2,128,2048]{2,1,0:T(8,128)(2,1)S(1)}, u32[]{:S(2)}, u32[]{:S(2)}) collective-permute-start(bf16[2,128,2048]{2,1,0:T(8,128)(2,1)S(1)} %get-tuple-element.427), channel_id=1, source_target_pairs={{0,16},{4,20},{8,24},{12,28},{16,0},{20,4},{24,8},{28,12},{1,17},{... | collective-permute-start | bytes 3145736 | tf_op jit(solution)/shard_map/ppermute | solution.py:25
  235.3 30.2 %collective-permute-start.39 = (bf16[512,4096]{1,0:T(8,128)(2,1)}, bf16[512,4096]{1,0:T(8,128)(2,1)S(1)}, u32[]{:S(2)}, u32[]{:S(2)}) collective-permute-start(bf16[512,4096]{1,0:T(8,128)(2,1)} %other_half.3), channel_id=1, source_target_pairs={{0,4},{4,0},{8,12},{12,8},{16,20},{20,16},{24,28},{28,24},{1,5},{5... | collective-permute-start | bytes 12582920 | tf_op jit(solution)/shard_map/ppermute | solution.py:25
  235.3 30.1 %collective-permute-start.37 = (bf16[128,2048]{1,0:T(8,128)(2,1)S(1)}, bf16[128,2048]{1,0:T(8,128)(2,1)S(1)}, u32[]{:S(2)}, u32[]{:S(2)}) collective-permute-start(bf16[128,2048]{1,0:T(8,128)(2,1)S(1)} %get-tuple-element.445), channel_id=1, source_target_pairs={{0,16},{4,20},{8,24},{12,28},{16,0},{20,4},{24,8},{28,12},{1,17},{... | collective-permute-start | bytes 1572872 | tf_op jit(solution)/shard_map/ppermute | solution.py:25
  236.9 28.6 %collective-permute-start.38 = (bf16[128,2048]{1,0:T(8,128)(2,1)S(1)}, bf16[128,2048]{1,0:T(8,128)(2,1)S(1)}, u32[]{:S(2)}, u32[]{:S(2)}) collective-permute-start(bf16[128,2048]{1,0:T(8,128)(2,1)S(1)} %get-tuple-element.446), channel_id=1, source_target_pairs={{0,8},{4,12},{8,0},{12,4},{16,24},{20,28},{24,16},{28,20},{1,9},{5... | collective-permute-start | bytes 1572872 | tf_op jit(solution)/shard_map/ppermute | solution.py:25
  271.1 26.6 %collective-permute-start.42 = (bf16[544,1024]{1,0:T(8,128)(2,1)S(1)}, bf16[544,1024]{1,0:T(8,128)(2,1)S(1)}, u32[]{:S(2)}, u32[]{:S(2)}) collective-permute-start(bf16[544,1024]{1,0:T(8,128)(2,1)S(1)} %unproject.3), channel_id=1, source_target_pairs={{0,1},{1,0},{2,3},{3,2},{4,5},{5,4},{6,7},{7,6},{8,9},{9,8},{10,11... | collective-permute-start | bytes 3342344 | tf_op jit(solution)/shard_map/ppermute | solution.py:25
  271.8 24.7 %collective-permute-start.40 = (bf16[2,128,2048]{2,1,0:T(8,128)(2,1)S(1)}, bf16[2,128,2048]{2,1,0:T(8,128)(2,1)S(1)}, u32[]{:S(2)}, u32[]{:S(2)}) collective-permute-start(bf16[2,128,2048]{2,1,0:T(8,128)(2,1)S(1)} %get-tuple-element.459), channel_id=1, source_target_pairs={{0,8},{4,12},{8,0},{12,4},{16,24},{20,28},{24,16},{28,20},{1,9},{5... | collective-permute-start | bytes 3145736 | tf_op jit(solution)/shard_map/ppermute | solution.py:25
  273.3 24.4 %collective-permute-start.41 = (bf16[2,128,2048]{2,1,0:T(8,128)(2,1)S(1)}, bf16[2,128,2048]{2,1,0:T(8,128)(2,1)S(1)}, u32[]{:S(2)}, u32[]{:S(2)}) collective-permute-start(bf16[2,128,2048]{2,1,0:T(8,128)(2,1)S(1)} %get-tuple-element.460), channel_id=1, source_target_pairs={{0,16},{4,20},{8,24},{12,28},{16,0},{20,4},{24,8},{28,12},{1,17},{... | collective-permute-start | bytes 3145736 | tf_op jit(solution)/shard_map/ppermute | solution.py:25
  299.5 25.6 %collective-permute-start.44 = (bf16[128,2048]{1,0:T(8,128)(2,1)S(1)}, bf16[128,2048]{1,0:T(8,128)(2,1)S(1)}, u32[]{:S(2)}, u32[]{:S(2)}) collective-permute-start(bf16[128,2048]{1,0:T(8,128)(2,1)S(1)} %get-tuple-element.500), channel_id=1, source_target_pairs={{0,16},{4,20},{8,24},{12,28},{16,0},{20,4},{24,8},{28,12},{1,17},{... | collective-permute-start | bytes 1572872 | tf_op jit(solution)/shard_map/ppermute | solution.py:25
  300.1 25.1 %collective-permute-start.45 = (bf16[128,2048]{1,0:T(8,128)(2,1)S(1)}, bf16[128,2048]{1,0:T(8,128)(2,1)S(1)}, u32[]{:S(2)}, u32[]{:S(2)}) collective-permute-start(bf16[128,2048]{1,0:T(8,128)(2,1)S(1)} %get-tuple-element.501), channel_id=1, source_target_pairs={{0,8},{4,12},{8,0},{12,4},{16,24},{20,28},{24,16},{28,20},{1,9},{5... | collective-permute-start | bytes 1572872 | tf_op jit(solution)/shard_map/ppermute | solution.py:25
  311.4 13.8 %collective-permute-start.48 = (bf16[2,128,1024]{2,1,0:T(8,128)(2,1)S(1)}, bf16[2,128,1024]{2,1,0:T(8,128)(2,1)S(1)}, u32[]{:S(2)}, u32[]{:S(2)}) collective-permute-start(bf16[2,128,1024]{2,1,0:T(8,128)(2,1)S(1)} %get-tuple-element.504), channel_id=1, source_target_pairs={{0,1},{1,0},{2,3},{3,2},{4,5},{5,4},{6,7},{7,6},{8,9},{9,8},{10,11... | collective-permute-start | bytes 1572872 | tf_op jit(solution)/shard_map/ppermute | solution.py:25
  312.0 13.5 %collective-permute-start.46 = (bf16[2,128,1024]{2,1,0:T(8,128)(2,1)S(1)}, bf16[2,128,1024]{2,1,0:T(8,128)(2,1)S(1)}, u32[]{:S(2)}, u32[]{:S(2)}) collective-permute-start(bf16[2,128,1024]{2,1,0:T(8,128)(2,1)S(1)} %get-tuple-element.502), channel_id=1, source_target_pairs={{0,8},{4,12},{8,0},{12,4},{16,24},{20,28},{24,16},{28,20},{1,9},{5... | collective-permute-start | bytes 1572872 | tf_op jit(solution)/shard_map/ppermute | solution.py:25
  313.5 13.2 %collective-permute-start.47 = (bf16[2,128,1024]{2,1,0:T(8,128)(2,1)S(1)}, bf16[2,128,1024]{2,1,0:T(8,128)(2,1)S(1)}, u32[]{:S(2)}, u32[]{:S(2)}) collective-permute-start(bf16[2,128,1024]{2,1,0:T(8,128)(2,1)S(1)} %get-tuple-element.503), channel_id=1, source_target_pairs={{0,16},{4,20},{8,24},{12,28},{16,0},{20,4},{24,8},{28,12},{1,17},{... | collective-permute-start | bytes 1572872 | tf_op jit(solution)/shard_map/ppermute | solution.py:25
  331.1 20.0 %collective-permute-start.52 = (bf16[2,128,1024]{2,1,0:T(8,128)(2,1)S(1)}, bf16[2,128,1024]{2,1,0:T(8,128)(2,1)S(1)}, u32[]{:S(2)}, u32[]{:S(2)}) collective-permute-start(bf16[2,128,1024]{2,1,0:T(8,128)(2,1)S(1)} %get-tuple-element.549), channel_id=1, source_target_pairs={{0,1},{1,0},{2,3},{3,2},{4,5},{5,4},{6,7},{7,6},{8,9},{9,8},{10,11... | collective-permute-start | bytes 1572872 | tf_op jit(solution)/shard_map/ppermute | solution.py:25
  334.7 15.4 %collective-permute-start.53 = (bf16[128,1024]{1,0:T(8,128)(2,1)S(1)}, bf16[128,1024]{1,0:T(8,128)(2,1)S(1)}, u32[]{:S(2)}, u32[]{:S(2)}) collective-permute-start(bf16[128,1024]{1,0:T(8,128)(2,1)S(1)} %fusion.6), channel_id=1, source_target_pairs={{0,2},{1,3},{2,0},{3,1},{4,6},{5,7},{6,4},{7,5},{8,10},{9,11},{10,... | collective-permute-start | bytes 786440 | tf_op jit(solution)/shard_map/ppermute | solution.py:25
  352.8 78.0 %all-gather.7.cloned.1.call-start = ((), (), s32[]{:S(2)}) async-start(), calls=%async_computation.1 | async-start | bytes 2359296 | tf_op jit(solution)/shard_map/all_gather | solution.py:1515
  354.6 14.6 %collective-permute-start.57 = (bf16[128,1024]{1,0:T(8,128)(2,1)S(1)}, bf16[128,1024]{1,0:T(8,128)(2,1)S(1)}, u32[]{:S(2)}, u32[]{:S(2)}) collective-permute-start(bf16[128,1024]{1,0:T(8,128)(2,1)S(1)} %fusion.7), channel_id=1, source_target_pairs={{0,2},{1,3},{2,0},{3,1},{4,6},{5,7},{6,4},{7,5},{8,10},{9,11},{10,... | collective-permute-start | bytes 786440 | tf_op jit(solution)/shard_map/ppermute | solution.py:25
  356.3 16.1 %collective-permute-start.54 = (bf16[2,128,1024]{2,1,0:T(8,128)(2,1)}, bf16[2,128,1024]{2,1,0:T(8,128)(2,1)S(1)}, u32[]{:S(2)}, u32[]{:S(2)}) collective-permute-start(bf16[2,128,1024]{2,1,0:T(8,128)(2,1)} %copy-done.67), channel_id=1, source_target_pairs={{0,8},{4,12},{8,0},{12,4},{16,24},{20,28},{24,16},{28,20},{1,9},{5... | collective-permute-start | bytes 1572872 | tf_op jit(solution)/shard_map/ppermute | solution.py:25
  357.8 15.7 %collective-permute-start.55 = (bf16[2,128,1024]{2,1,0:T(8,128)(2,1)}, bf16[2,128,1024]{2,1,0:T(8,128)(2,1)S(1)}, u32[]{:S(2)}, u32[]{:S(2)}) collective-permute-start(bf16[2,128,1024]{2,1,0:T(8,128)(2,1)} %copy-done.66), channel_id=1, source_target_pairs={{0,16},{4,20},{8,24},{12,28},{16,0},{20,4},{24,8},{28,12},{1,17},{... | collective-permute-start | bytes 1572872 | tf_op jit(solution)/shard_map/ppermute | solution.py:25
  383.2 12.9 %collective-permute-start.58 = (bf16[128,1024]{1,0:T(8,128)(2,1)S(1)}, bf16[128,1024]{1,0:T(8,128)(2,1)S(1)}, u32[]{:S(2)}, u32[]{:S(2)}) collective-permute-start(bf16[128,1024]{1,0:T(8,128)(2,1)S(1)} %fusion.8), channel_id=1, source_target_pairs={{0,2},{1,3},{2,0},{3,1},{4,6},{5,7},{6,4},{7,5},{8,10},{9,11},{10,... | collective-permute-start | bytes 786440 | tf_op jit(solution)/shard_map/ppermute | solution.py:25
  404.3 19.5 %collective-permute-start.65 = (bf16[2,128,512]{2,1,0:T(8,128)(2,1)S(1)}, bf16[2,128,512]{2,1,0:T(8,128)(2,1)S(1)}, u32[]{:S(2)}, u32[]{:S(2)}) collective-permute-start(bf16[2,128,512]{2,1,0:T(8,128)(2,1)S(1)} %pad_maximum_fusion.11.refs_2_), channel_id=1, source_target_pairs={{0,8},{4,12},{8,0},{12,4},{16,24},{20,28},{24,16},{28,20},{1,9},{5... | collective-permute-start | bytes 786440 | tf_op jit(solution)/shard_map/ppermute | solution.py:25
  405.9 17.9 %collective-permute-start.63 = (bf16[2,128,512]{2,1,0:T(8,128)(2,1)S(1)}, bf16[2,128,512]{2,1,0:T(8,128)(2,1)S(1)}, u32[]{:S(2)}, u32[]{:S(2)}) collective-permute-start(bf16[2,128,512]{2,1,0:T(8,128)(2,1)S(1)} %pad_maximum_fusion.10.refs_0_), channel_id=1, source_target_pairs={{0,16},{4,20},{8,24},{12,28},{16,0},{20,4},{24,8},{28,12},{1,17},{... | collective-permute-start | bytes 786440 | tf_op jit(solution)/shard_map/ppermute | solution.py:25
  423.3 16.1 %collective-permute-start.68 = (bf16[2,128,512]{2,1,0:T(8,128)(2,1)S(1)}, bf16[2,128,512]{2,1,0:T(8,128)(2,1)S(1)}, u32[]{:S(2)}, u32[]{:S(2)}) collective-permute-start(bf16[2,128,512]{2,1,0:T(8,128)(2,1)S(1)} %pad_maximum_fusion.11.refs_2_), channel_id=1, source_target_pairs={{0,4},{4,0},{8,12},{12,8},{16,20},{20,16},{24,28},{28,24},{1,5},{5... | collective-permute-start | bytes 786440 | tf_op jit(solution)/shard_map/ppermute | solution.py:25
  423.3 16.1 %collective-permute-start.66 = (bf16[2,128,512]{2,1,0:T(8,128)(2,1)S(1)}, bf16[2,128,512]{2,1,0:T(8,128)(2,1)S(1)}, u32[]{:S(2)}, u32[]{:S(2)}) collective-permute-start(bf16[2,128,512]{2,1,0:T(8,128)(2,1)S(1)} %pad_maximum_fusion.10.refs_0_), channel_id=1, source_target_pairs={{0,4},{4,0},{8,12},{12,8},{16,20},{20,16},{24,28},{28,24},{1,5},{5... | collective-permute-start | bytes 786440 | tf_op jit(solution)/shard_map/ppermute | solution.py:25
  423.8 15.6 %collective-permute-start.69 = (bf16[2,128,512]{2,1,0:T(8,128)(2,1)S(1)}, bf16[2,128,512]{2,1,0:T(8,128)(2,1)S(1)}, u32[]{:S(2)}, u32[]{:S(2)}) collective-permute-start(bf16[2,128,512]{2,1,0:T(8,128)(2,1)S(1)} %collective-permute-done.65.refs_3_), channel_id=1, source_target_pairs={{0,4},{4,0},{8,12},{12,8},{16,20},{20,16},{24,28},{28,24},{1,5},{5... | collective-permute-start | bytes 786440 | tf_op jit(solution)/shard_map/ppermute | solution.py:25
  423.8 15.5 %collective-permute-start.67 = (bf16[2,128,512]{2,1,0:T(8,128)(2,1)S(1)}, bf16[2,128,512]{2,1,0:T(8,128)(2,1)S(1)}, u32[]{:S(2)}, u32[]{:S(2)}) collective-permute-start(bf16[2,128,512]{2,1,0:T(8,128)(2,1)S(1)} %collective-permute-done.63.refs_1_), channel_id=1, source_target_pairs={{0,4},{4,0},{8,12},{12,8},{16,20},{20,16},{24,28},{28,24},{1,5},{5... | collective-permute-start | bytes 786440 | tf_op jit(solution)/shard_map/ppermute | solution.py:25
  434.6 11.3 %collective-permute-start.74 = (f32[34,1024]{1,0:T(8,128)S(1)}, f32[34,1024]{1,0:T(8,128)S(1)}, u32[]{:S(2)}, u32[]{:S(2)}) collective-permute-start(f32[34,1024]{1,0:T(8,128)S(1)} %add.235), channel_id=1, source_target_pairs={{0,2},{1,3},{2,0},{3,1},{4,6},{5,7},{6,4},{7,5},{8,10},{9,11},{10,... | collective-permute-start | bytes 417800 | tf_op jit(solution)/shard_map/ppermute | solution.py:25
  (123 other events, 1064.1 us)
Sparse Core Ops, SparseCore 0:
  352.9 31.9 all-gather.4
  387.3 33.2 all-gather.6

commit v6 on v5

--- a/solution.py
+++ b/solution.py
@@ -142,7 +142,7 @@
             jax.ShapeDtypeStruct((rows, count), BF16),
         ],
         name="attend",
-        compiler_params=pltpu.CompilerParams(vmem_limit_bytes=16 << 20),
+        compiler_params=pltpu.CompilerParams(vmem_limit_bytes=14 << 20),
         cost_estimate=LIGHT,
     )(queries, keys, values, key_const)
 
@@ -245,7 +245,7 @@
             pltpu.VMEM((span, 2 * wide), BF16),
         ],
         name="attend_back",
-        compiler_params=pltpu.CompilerParams(vmem_limit_bytes=16 << 20),
+        compiler_params=pltpu.CompilerParams(vmem_limit_bytes=14 << 20),
         cost_estimate=LIGHT,
     )(queries, keys, values, key_const, aug, grad_out, out, *([before] if causal else []))
 
@@ -870,7 +870,7 @@
         ),
         out_shape=jax.ShapeDtypeStruct((rows, full), dtype),
         name="unproject",
-        compiler_params=pltpu.CompilerParams(vmem_limit_bytes=18 << 20),
+        compiler_params=pltpu.CompilerParams(vmem_limit_bytes=16 << 20),
         cost_estimate=LIGHT,
     )(device.reshape(1), *grads, *([] if before is None else [before]), *group.inputs)
 
@@ -1058,7 +1058,7 @@
         ),
         out_shape=[jax.ShapeDtypeStruct(shape, BF16)] * 4,
         name="attention_this",
-        compiler_params=pltpu.CompilerParams(vmem_limit_bytes=16 << 20),
+        compiler_params=pltpu.CompilerParams(vmem_limit_bytes=14 << 20),
         cost_estimate=LIGHT,
     )(device.reshape(1), *normed, branch, *grads, attended, got)
 

time: 461 us -> 460 us (level)
  no operation moved by 1% of the time
where the time goes in v6:
time: 460 us; the launch traced here: 455 us
  Pallas kernels  185 us (40%)
  waiting for transfers between devices  113 us (25%)
  starting transfers between devices  81.4 us (18%)
  local copies, waits for them, and re-layouts  38.4 us (8%)
  other arithmetic  19.8 us (4%)
  between operations  16.2 us (4%)
    ppermute x75, waiting for transfers between devices, swap(): return lax.ppermute(value, axis, [(i, i ^ mask) for i in range(count)])  113 us
    ppermute x75, starting transfers between devices, swap(): return lax.ppermute(value, axis, [(i, i ^ mask) for i in range(count)])  81.3 us
    pallas_call x3, Pallas kernels, attend_back(): pl.pallas_call(functools.partial(attend_back_kernel, causal), grid=(count...  40.4 us
    pallas_call x1, Pallas kernels, feed_back(): pl.pallas_call(functools.partial(back_kernel, group_a, group_u, group_d),...  25.7 us
    unnamed x194, local copies, waits for them, and re-layouts  25.7 us
    pallas_call x1, Pallas kernels, feed_up(): pl.pallas_call(functools.partial(up_kernel, group_a, group_u), grid_spec=...  18.2 us
    pallas_call x2, Pallas kernels, attend(): pl.pallas_call(functools.partial(attend_kernel, span // rows, rows), grid...  17.6 us
    pallas_call x3, Pallas kernels, unproject(): pl.pallas_call(functools.partial(unproject_kernel, group, which, begin, c...  14.7 us
  transfers between devices with their start and end apart: 77, of which 32 were waited for; matrix products, arithmetic and copies ran while one was open for 5% of the time, Pallas kernels for 33%

profile of v6, /device:TPU:0, one launch (start us, length us, event | category | flops | bytes accessed | tf_op | source)
XLA Modules:
  0.0 455.3 jit_solution(10342256675596344384)
XLA Ops:
  10.7 3.1 collective-permute-start
  13.8 2.6 collective-permute-start.1
  23.4 2.5 collective-permute-done
  25.9 2.5 collective-permute-done.1
  28.9 6.0 %collective-permute-done.2 = bf16[528,256]{1,0:T(8,128)(2,1)S(1)} collective-permute-done((bf16[528,256]{1,0:T(8,128)(2,1)S(1)}, bf16[528,256]{1,0:T(8,128)(2,1)S(1)}, u32[]{:S(2)}, u32[]{:S(2)}) %collective-permute-start.2) | collective-permute-done | bytes 270368 | tf_op jit(solution)/shard_map/ppermute | solution.py:25
  40.2 3.5 collective-permute-done.3
  52.7 21.0 %collective-permute-done.7 = bf16[128,1024]{1,0:T(8,128)(2,1)} collective-permute-done((bf16[128,1024]{1,0:T(8,128)(2,1)}, bf16[128,1024]{1,0:T(8,128)(2,1)}, u32[]{:S(2)}, u32[]{:S(2)}) %collective-permute-start.7) | collective-permute-done | bytes 262176 | tf_op jit(solution)/shard_map/ppermute | solution.py:25
  78.5 6.9 %collective-permute-done.14 = bf16[128,1024]{1,0:T(8,128)(2,1)} collective-permute-done((bf16[128,1024]{1,0:T(8,128)(2,1)}, bf16[128,1024]{1,0:T(8,128)(2,1)}, u32[]{:S(2)}, u32[]{:S(2)}) %collective-permute-start.14) | collective-permute-done | bytes 262176 | tf_op jit(solution)/shard_map/ppermute | solution.py:25
  92.2 9.5 %project.1 = (bf16[544,1024]{1,0:T(8,128)(2,1)S(1)}, bf16[1088,1024]{1,0:T(8,128)(2,1)S(1)}, bf16[1088,1024]{1,0:T(8,128)(2,1)S(1)}) custom-call(s32[1]{0:T(128)} %bitcast.scal, bf16[544,1024]{1,0:T(8,128)(2,1)} %collective-permute-done.9.refs_0_, bf16[544,1024]{1,0:T(8,128)(2,1)S(1)} %add_convert_fusion.refs_1_, f32[8,1024]{1,0:T(8,128)S(1)} %pad.28.refs_2_, ...), custom_call_target="tpu_custom_call" | custom-call | flops 1000 | bytes 1000 | tf_op jit(solution)/shard_map/project/pallas_call | solution.py:483
  108.2 8.8 %attend.2 = (bf16[544,512]{1,0:T(8,128)(2,1)S(1)}, bf16[544,512]{1,0:T(8,128)(2,1)S(1)}) custom-call(bf16[544,1024]{1,0:T(8,128)(2,1)S(1)} %get-tuple-element.371.q_ref, bf16[1088,1024]{1,0:T(8,128)(2,1)S(1)} %get-tuple-element.362.k_ref, bf16[1088,1024]{1,0:T(8,128)(2,1)S(1)} %get-tuple-element.363.v_ref, bf16[1088,128]{1,0:T(8,128)(2,1)S(1)} %select_convert_fusion.kc_ref), custom_call_target="tpu_custom_call" | custom-call | flops 1000 | bytes 1000 | tf_op jit(solution)/shard_map/attend/pallas_call | solution.py:130
  118.3 8.8 %attend.3 = (bf16[544,512]{1,0:T(8,128)(2,1)S(1)}, bf16[544,512]{1,0:T(8,128)(2,1)S(1)}) custom-call(bf16[544,1024]{1,0:T(8,128)(2,1)S(1)} %get-tuple-element.371.q_ref, bf16[1088,1024]{1,0:T(8,128)(2,1)S(1)} %get-tuple-element.362.k_ref, bf16[1088,1024]{1,0:T(8,128)(2,1)S(1)} %get-tuple-element.363.v_ref, bf16[1088,128]{1,0:T(8,128)(2,1)S(1)} %select_convert_fusion.kc_ref), custom_call_target="tpu_custom_call" | custom-call | flops 1000 | bytes 1000 | tf_op jit(solution)/shard_map/attend/pallas_call | solution.py:130
  127.2 4.7 %collective-permute-done.22 = bf16[1,3,1,64,1024]{4,3,1,2,0:T(8,128)(2,1)S(1)} collective-permute-done((bf16[1,3,1,64,1024]{4,3,1,2,0:T(8,128)(2,1)S(1)}, bf16[1,3,1,64,1024]{4,3,1,2,0:T(8,128)(2,1)S(1)}, u32[]{:S(2)}, u32[]{:S(2)}) %collective-permute-start.22) | collective-permute-done | bytes 393248 | tf_op jit(solution)/shard_map/ppermute | solution.py:25
  143.2 18.2 %feed_up.1 = (f32[544,1024]{1,0:T(8,128)}, f32[544,1024]{1,0:T(8,128)}, bf16[544,1024]{1,0:T(8,128)(2,1)S(1)}, bf16[544,4096]{1,0:T(8,128)(2,1)}, bf16[544,4096]{1,0:T(8,128)(2,1)}) custom-call(s32[1]{0:T(128)} %bitcast.scal, bf16[544,512]{1,0:T(8,128)(2,1)S(1)} %get-tuple-element.370.refs_0_, bf16[544,512]{1,0:T(8,128)(2,1)S(1)} %copy-done.40, ...), custom_call_target="tpu_custom_call" | custom-call | flops 1000 | bytes 1000 | tf_op jit(solution)/shard_map/feed_up/pallas_call | solution.py:567
  167.4 2.5 copy-done.8
  171.5 10.1 %feed_down.1 = (bf16[544,1024]{1,0:T(8,128)(2,1)}, bf16[544,1024]{1,0:T(8,128)(2,1)S(1)}, f32[24,1024]{1,0:T(8,128)S(1)}) custom-call(s32[1]{0:T(128)} %bitcast.scal, bf16[544,4096]{1,0:T(8,128)(2,1)S(1)} %copy-done.8, f32[544,1024]{1,0:T(8,128)S(1)} %copy-done.20, bf16[544,1024]{1,0:T(8,128)(2,1)S(1)} %copy-done.32, ...), custom_call_target="tpu_custom_call" | custom-call | flops 1000 | bytes 1000 | tf_op jit(solution)/shard_map/feed_down/pallas_call | solution.py:657
  181.7 4.7 %other_half.2 = bf16[512,4096]{1,0:T(8,128)(2,1)S(1)} custom-call(s32[1]{0:T(128)} %bitcast.scal, bf16[544,1024]{1,0:T(8,128)(2,1)S(1)} %get-tuple-element.417.left_ref.refs_0_, bf16[544,4096]{1,0:T(8,128)(2,1)S(1)} %copy-done.8), custom_call_target="tpu_custom_call" | custom-call | flops 1000 | bytes 1000 | tf_op jit(solution)/shard_map/other_half/pallas_call | solution.py:917
  186.6 7.0 %collective-permute-done.34.got_ref = bf16[512,4096]{1,0:T(8,128)(2,1)S(1)} collective-permute-done((bf16[512,4096]{1,0:T(8,128)(2,1)S(1)}, bf16[512,4096]{1,0:T(8,128)(2,1)S(1)}, u32[]{:S(2)}, u32[]{:S(2)}) %collective-permute-start.34) | collective-permute-done | bytes 4194336 | tf_op jit(solution)/shard_map/ppermute | solution.py:25
  193.7 6.2 %this_half.2 = (bf16[2,128,2048]{2,1,0:T(8,128)(2,1)}, bf16[2,128,2048]{2,1,0:T(8,128)(2,1)S(1)}, bf16[2,128,2048]{2,1,0:T(8,128)(2,1)S(1)}, bf16[2,128,2048]{2,1,0:T(8,128)(2,1)S(1)}) custom-call(s32[1]{0:T(128)} %bitcast.scal, bf16[544,1024]{1,0:T(8,128)(2,1)S(1)} %get-tuple-element.417.left_ref.refs_0_, bf16[544,4096]{1,0:T(8,128)(2,1)S(1)} %bitcast.119, ...), custom_call_target="tpu_custom_call" | custom-call | flops 1000 | bytes 1000 | tf_op jit(solution)/shard_map/this_half/pallas_call | solution.py:946
  201.9 25.7 %feed_back.1 = (bf16[544,4096]{1,0:T(8,128)(2,1)}, f32[544,1024]{1,0:T(8,128)}, bf16[544,1024]{1,0:T(8,128)(2,1)}, bf16[544,1024]{1,0:T(8,128)(2,1)}, f32[40,1024]{1,0:T(8,128)S(1)}, /*index=5*/f32[8,4096]{1,0:T(8,128)S(1)}) custom-call(s32[1]{0:T(128)} %bitcast.scal, bf16[544,1024]{1,0:T(8,128)(2,1)} %copy-done.17, ...), custom_call_target="tpu_custom_call" | custom-call | flops 1000 | bytes 1000 | tf_op jit(solution)/shard_map/feed_back/pallas_call | solution.py:773
  229.9 4.7 %other_half.3 = bf16[512,4096]{1,0:T(8,128)(2,1)S(1)} custom-call(s32[1]{0:T(128)} %bitcast.scal, bf16[544,1024]{1,0:T(8,128)(2,1)S(1)} %get-tuple-element.439.left_ref, bf16[544,4096]{1,0:T(8,128)(2,1)S(1)} %bitcast.121), custom_call_target="tpu_custom_call" | custom-call | flops 1000 | bytes 1000 | tf_op jit(solution)/shard_map/other_half/pallas_call | solution.py:917
  239.1 20.2 %attend_back.3 = (f32[544,1024]{1,0:T(8,128)S(1)}, bf16[544,1024]{1,0:T(8,128)(2,1)S(1)}, bf16[544,1024]{1,0:T(8,128)(2,1)S(1)}) custom-call(bf16[544,1024]{1,0:T(8,128)(2,1)S(1)} %copy-done.10, bf16[1088,1024]{1,0:T(8,128)(2,1)S(1)} %copy-done.5, bf16[1088,1024]{1,0:T(8,128)(2,1)S(1)} %copy-done.7, bf16[1088,128]{1,0:T(8,128)(2,1)S(1)} %select_convert_fusion.kc_ref, ...), custom_call_target="tpu_custom_call" | custom-call | flops 1000 | bytes 1000 | tf_op jit(solution)/shard_map/attend_back/pallas_call | solution.py:223
  259.3 5.5 %unproject.3 = bf16[544,1024]{1,0:T(8,128)(2,1)S(1)} custom-call(s32[1]{0:T(128)} %bitcast.scal, bf16[544,1024]{1,0:T(8,128)(2,1)S(1)} %get-tuple-element.477.refs_0_.refs_6_, bf16[544,1024]{1,0:T(8,128)(2,1)S(1)} %get-tuple-element.478.refs_1_.refs_7_, bf16[3,1024,256]{2,1,0:T(8,128)(2,1)S(1)} %copy-done.3, bf16[256,1024]{1,0:T(8,128)(2,1)S(1)} %copy-done.15, ...), custom_call_target="tpu_custom_call" | custom-call | flops 1000 | bytes 1000 | tf_op jit(solution)/shard_map/unproject/pallas_call | solution.py:858
  264.9 5.6 %this_half.3 = (bf16[2,128,2048]{2,1,0:T(8,128)(2,1)S(1)}, bf16[2,128,2048]{2,1,0:T(8,128)(2,1)S(1)}, bf16[2,128,2048]{2,1,0:T(8,128)(2,1)S(1)}, bf16[2,128,2048]{2,1,0:T(8,128)(2,1)S(1)}) custom-call(s32[1]{0:T(128)} %bitcast.scal, bf16[544,1024]{1,0:T(8,128)(2,1)S(1)} %get-tuple-element.439.left_ref, bf16[544,4096]{1,0:T(8,128)(2,1)S(1)} %bitcast.121, ...), custom_call_target="tpu_custom_call" | custom-call | flops 1000 | bytes 1000 | tf_op jit(solution)/shard_map/this_half/pallas_call | solution.py:946
  273.2 10.1 %attend_back.4 = (bf16[544,512]{1,0:T(8,128)(2,1)S(1)}, bf16[544,512]{1,0:T(8,128)(2,1)S(1)}, bf16[544,512]{1,0:T(8,128)(2,1)S(1)}) custom-call(bf16[544,1024]{1,0:T(8,128)(2,1)S(1)} %copy-done.10, bf16[1088,1024]{1,0:T(8,128)(2,1)S(1)} %copy-done.5, bf16[1088,1024]{1,0:T(8,128)(2,1)S(1)} %copy-done.7, bf16[1088,128]{1,0:T(8,128)(2,1)S(1)} %select_convert_fusion.kc_ref, ...), custom_call_target="tpu_custom_call" | custom-call | flops 1000 | bytes 1000 | tf_op jit(solution)/shard_map/attend_back/pallas_call | solution.py:223
  283.3 4.2 attention_other.2
  287.4 8.4 %collective-permute-done.40.refs_1_.refs_3_ = bf16[2,128,2048]{2,1,0:T(8,128)(2,1)S(1)} collective-permute-done((bf16[2,128,2048]{2,1,0:T(8,128)(2,1)S(1)}, bf16[2,128,2048]{2,1,0:T(8,128)(2,1)S(1)}, u32[]{:S(2)}, u32[]{:S(2)}) %collective-permute-start.40) | collective-permute-done | bytes 1048608 | tf_op jit(solution)/shard_map/ppermute | solution.py:25
  300.2 5.1 %unproject.4.refs_3_ = f32[544,1024]{1,0:T(8,128)S(1)} custom-call(s32[1]{0:T(128)} %bitcast.scal, bf16[544,512]{1,0:T(8,128)(2,1)S(1)} %get-tuple-element.588.refs_3_.refs_0_, bf16[544,512]{1,0:T(8,128)(2,1)S(1)} %get-tuple-element.481.refs_4_.refs_1_, bf16[544,512]{1,0:T(8,128)(2,1)S(1)} %get-tuple-element.589.refs_5_.refs_2_, ...), custom_call_target="tpu_custom_call" | custom-call | flops 1000 | bytes 1000 | tf_op jit(solution)/shard_map/unproject/pallas_call | solution.py:858
  305.3 4.8 %attention_this.2 = (bf16[2,128,1024]{2,1,0:T(8,128)(2,1)S(1)}, bf16[2,128,1024]{2,1,0:T(8,128)(2,1)S(1)}, bf16[2,128,1024]{2,1,0:T(8,128)(2,1)S(1)}, bf16[2,128,1024]{2,1,0:T(8,128)(2,1)S(1)}) custom-call(s32[1]{0:T(128)} %bitcast.scal, bf16[544,1024]{1,0:T(8,128)(2,1)} %collective-permute-done.9.refs_0_, bf16[544,1024]{1,0:T(8,128)(2,1)S(1)} %add_convert_fusion.refs_1_, ...), custom_call_target="tpu_custom_call" | custom-call | flops 1000 | bytes 1000 | tf_op jit(solution)/shard_map/attention_this/pallas_call | solution.py:1049
  313.8 10.1 %attend_back.5 = (bf16[544,512]{1,0:T(8,128)(2,1)S(1)}, bf16[544,512]{1,0:T(8,128)(2,1)S(1)}, bf16[544,512]{1,0:T(8,128)(2,1)S(1)}) custom-call(bf16[544,1024]{1,0:T(8,128)(2,1)S(1)} %copy-done.10, bf16[1088,1024]{1,0:T(8,128)(2,1)S(1)} %copy-done.5, bf16[1088,1024]{1,0:T(8,128)(2,1)S(1)} %copy-done.7, bf16[1088,128]{1,0:T(8,128)(2,1)S(1)} %select_convert_fusion.kc_ref, ...), custom_call_target="tpu_custom_call" | custom-call | flops 1000 | bytes 1000 | tf_op jit(solution)/shard_map/attend_back/pallas_call | solution.py:223
  325.5 3.8 attention_other.3
  333.5 2.8 collective-permute-start.53
  336.2 4.1 unproject.5
  340.4 5.2 %attention_this.3 = (bf16[2,128,1024]{2,1,0:T(8,128)(2,1)S(1)}, bf16[2,128,1024]{2,1,0:T(8,128)(2,1)S(1)}, bf16[2,128,1024]{2,1,0:T(8,128)(2,1)S(1)}, bf16[2,128,1024]{2,1,0:T(8,128)(2,1)S(1)}) custom-call(s32[1]{0:T(128)} %bitcast.scal, bf16[544,1024]{1,0:T(8,128)(2,1)} %collective-permute-done.9.refs_0_, bf16[544,1024]{1,0:T(8,128)(2,1)S(1)} %add_convert_fusion.refs_1_, ...), custom_call_target="tpu_custom_call" | custom-call | flops 1000 | bytes 1000 | tf_op jit(solution)/shard_map/attention_this/pallas_call | solution.py:1049
  359.7 3.0 multiply_reduce_fusion
  364.6 3.3 collective-permute-done.57
  368.5 2.7 collective-permute-done.54.refs_1_.refs_3_
  383.0 3.8 collective-permute-done.59.got_a
  389.8 5.0 %collective-permute-done.58 = bf16[128,1024]{1,0:T(8,128)(2,1)S(1)} collective-permute-done((bf16[128,1024]{1,0:T(8,128)(2,1)S(1)}, bf16[128,1024]{1,0:T(8,128)(2,1)S(1)}, u32[]{:S(2)}, u32[]{:S(2)}) %collective-permute-start.58) | collective-permute-done | bytes 262176 | tf_op jit(solution)/shard_map/ppermute | solution.py:25
  394.8 3.0 collective-permute-done.61
  408.3 2.7 collective-permute-start.72
  411.0 8.6 %collective-permute-done.72 = f32[34,1024]{1,0:T(8,128)S(1)} collective-permute-done((f32[34,1024]{1,0:T(8,128)S(1)}, f32[34,1024]{1,0:T(8,128)S(1)}, u32[]{:S(2)}, u32[]{:S(2)}) %collective-permute-start.72) | collective-permute-done | bytes 139296 | tf_op jit(solution)/shard_map/ppermute | solution.py:25
  419.6 2.4 collective-permute-start.73
  423.1 2.3 collective-permute-done.73
  427.0 2.6 fill_ffn.2
  431.1 2.3 fill_ffn.3
  433.4 4.7 %collective-permute-start.74 = (f32[34,1024]{1,0:T(8,128)S(1)}, f32[34,1024]{1,0:T(8,128)S(1)}, u32[]{:S(2)}, u32[]{:S(2)}) collective-permute-start(f32[34,1024]{1,0:T(8,128)S(1)} %add.235), channel_id=1, source_target_pairs={{0,2},{1,3},{2,0},{3,1},{4,6},{5,7},{6,4},{7,5},{8,10},{9,11},{10,... | collective-permute-start | bytes 417800 | tf_op jit(solution)/shard_map/ppermute | solution.py:25
  438.1 2.5 fill_attention.1
  440.7 4.2 collective-permute-done.74
  (441 shorter events, 137.6 us)
Async XLA Ops:
  7.2 418.2 %all-gather.5.cloned.1.call-start = ((), (), s32[]{:S(2)}) async-start(), calls=%async_computation | async-start | bytes 2359296 | tf_op jit(solution)/shard_map/all_gather | solution.py:1488
  10.7 15.2 %collective-permute-start = (bf16[528,256]{1,0:T(8,128)(2,1)S(1)}, bf16[528,256]{1,0:T(8,128)(2,1)S(1)}, u32[]{:S(2)}, u32[]{:S(2)}) collective-permute-start(bf16[528,256]{1,0:T(8,128)(2,1)S(1)} %fusion.5), channel_id=1, source_target_pairs={{0,1},{1,0},{2,3},{3,2},{4,5},{5,4},{6,7},{7,6},{8,9},{9,8},{10,11... | collective-permute-start | bytes 811016 | tf_op jit(solution)/shard_map/ppermute | solution.py:25
  13.8 14.7 %collective-permute-start.1 = (bf16[528,256]{1,0:T(8,128)(2,1)S(1)}, bf16[528,256]{1,0:T(8,128)(2,1)S(1)}, u32[]{:S(2)}, u32[]{:S(2)}) collective-permute-start(bf16[528,256]{1,0:T(8,128)(2,1)S(1)} %fusion.5), channel_id=1, source_target_pairs={{0,2},{1,3},{2,0},{3,1},{4,6},{5,7},{6,4},{7,5},{8,10},{9,11},{10,... | collective-permute-start | bytes 811016 | tf_op jit(solution)/shard_map/ppermute | solution.py:25
  38.9 34.8 %collective-permute-start.9 = (bf16[544,1024]{1,0:T(8,128)(2,1)S(1)}, bf16[544,1024]{1,0:T(8,128)(2,1)}, u32[]{:S(2)}, u32[]{:S(2)}) collective-permute-start(bf16[544,1024]{1,0:T(8,128)(2,1)S(1)} %add_convert_fusion.refs_1_), channel_id=1, source_target_pairs={{0,1},{1,0},{2,3},{3,2},{4,5},{5,4},{6,7},{7,6},{8,9},{9,8},{10,11... | collective-permute-start | bytes 3342344 | tf_op jit(solution)/shard_map/ppermute | solution.py:25
  46.6 27.1 %collective-permute-start.5 = (bf16[2,3,4,64,256]{4,3,2,1,0:T(8,128)(2,1)}, bf16[2,3,4,64,256]{4,3,2,1,0:T(8,128)(2,1)}, u32[]{:S(2)}, u32[]{:S(2)}) collective-permute-start(bf16[2,3,4,64,256]{4,3,2,1,0:T(8,128)(2,1)} %pad_maximum_fusion.1.refs_5_.refs_7_.refs_8_.refs_4_.refs_6_), channel_id=1, source_target_pairs={{0,16},{4,20},{8,24},{12,28},{16,0},{20,4},{24,8},{28,12},{1,17},{... | collective-permute-start | bytes 2359304 | tf_op jit(solution)/shard_map/ppermute | solution.py:25
  48.1 25.5 %collective-permute-start.6 = (bf16[2,3,4,64,256]{4,3,2,1,0:T(8,128)(2,1)S(1)}, bf16[2,3,4,64,256]{4,3,2,1,0:T(8,128)(2,1)}, u32[]{:S(2)}, u32[]{:S(2)}) collective-permute-start(bf16[2,3,4,64,256]{4,3,2,1,0:T(8,128)(2,1)S(1)} %pad_maximum_fusion.2.refs_7_.refs_9_.refs_10_.refs_6_.refs_8_), channel_id=1, source_target_pairs={{0,8},{4,12},{8,0},{12,4},{16,24},{20,28},{24,16},{28,20},{1,9},{5... | collective-permute-start | bytes 2359304 | tf_op jit(solution)/shard_map/ppermute | solution.py:25
  48.7 25.0 %collective-permute-start.7 = (bf16[128,1024]{1,0:T(8,128)(2,1)}, bf16[128,1024]{1,0:T(8,128)(2,1)}, u32[]{:S(2)}, u32[]{:S(2)}) collective-permute-start(bf16[128,1024]{1,0:T(8,128)(2,1)} %bitcast.12), channel_id=1, source_target_pairs={{0,1},{1,0},{2,3},{3,2},{4,5},{5,4},{6,7},{7,6},{8,9},{9,8},{10,11... | collective-permute-start | bytes 786440 | tf_op jit(solution)/shard_map/ppermute | solution.py:25
  50.5 23.2 %collective-permute-start.8 = (bf16[128,1024]{1,0:T(8,128)(2,1)}, bf16[128,1024]{1,0:T(8,128)(2,1)}, u32[]{:S(2)}, u32[]{:S(2)}) collective-permute-start(bf16[128,1024]{1,0:T(8,128)(2,1)} %bitcast.12), channel_id=1, source_target_pairs={{0,2},{1,3},{2,0},{3,1},{4,6},{5,7},{6,4},{7,5},{8,10},{9,11},{10,... | collective-permute-start | bytes 786440 | tf_op jit(solution)/shard_map/ppermute | solution.py:25
  73.7 11.7 %collective-permute-start.10 = (bf16[2,3,4,64,256]{4,3,2,1,0:T(8,128)(2,1)}, bf16[2,3,4,64,256]{4,3,2,1,0:T(8,128)(2,1)}, u32[]{:S(2)}, u32[]{:S(2)}) collective-permute-start(bf16[2,3,4,64,256]{4,3,2,1,0:T(8,128)(2,1)} %pad_maximum_fusion.1.refs_5_.refs_7_.refs_8_.refs_4_.refs_6_), channel_id=1, source_target_pairs={{0,4},{4,0},{8,12},{12,8},{16,20},{20,16},{24,28},{28,24},{1,5},{5... | collective-permute-start | bytes 2359304 | tf_op jit(solution)/shard_map/ppermute | solution.py:25
  73.8 11.6 %collective-permute-start.11 = (bf16[2,3,4,64,256]{4,3,2,1,0:T(8,128)(2,1)}, bf16[2,3,4,64,256]{4,3,2,1,0:T(8,128)(2,1)}, u32[]{:S(2)}, u32[]{:S(2)}) collective-permute-start(bf16[2,3,4,64,256]{4,3,2,1,0:T(8,128)(2,1)} %collective-permute-done.5.refs_6_.refs_8_.refs_9_.refs_5_.refs_7_), channel_id=1, source_target_pairs={{0,4},{4,0},{8,12},{12,8},{16,20},{20,16},{24,28},{28,24},{1,5},{5... | collective-permute-start | bytes 2359304 | tf_op jit(solution)/shard_map/ppermute | solution.py:25
  86.7 15.1 %collective-permute-start.17 = (bf16[1,3,1,64,1024]{4,3,1,2,0:T(8,128)(2,1)S(1)}, bf16[1,3,1,64,1024]{4,3,1,2,0:T(8,128)(2,1)S(1)}, u32[]{:S(2)}, u32[]{:S(2)}) collective-permute-start(bf16[1,3,1,64,1024]{4,3,1,2,0:T(8,128)(2,1)S(1)} %get-tuple-element.353), channel_id=1, source_target_pairs={{0,8},{4,12},{8,0},{12,4},{16,24},{20,28},{24,16},{28,20},{1,9},{5... | collective-permute-start | bytes 1179656 | tf_op jit(solution)/shard_map/ppermute | solution.py:25
  87.3 14.5 %collective-permute-start.18 = (bf16[1,3,1,64,1024]{4,3,2,1,0:T(8,128)(2,1)S(1)}, bf16[1,3,1,64,1024]{4,3,2,1,0:T(8,128)(2,1)S(1)}, u32[]{:S(2)}, u32[]{:S(2)}) collective-permute-start(bf16[1,3,1,64,1024]{4,3,2,1,0:T(8,128)(2,1)S(1)} %get-tuple-element.354), channel_id=1, source_target_pairs={{0,16},{4,20},{8,24},{12,28},{16,0},{20,4},{24,8},{28,12},{1,17},{... | collective-permute-start | bytes 1179656 | tf_op jit(solution)/shard_map/ppermute | solution.py:25
  88.5 13.2 %collective-permute-start.15 = (bf16[128,1024]{1,0:T(8,128)(2,1)S(1)}, bf16[128,1024]{1,0:T(8,128)(2,1)S(1)}, u32[]{:S(2)}, u32[]{:S(2)}) collective-permute-start(bf16[128,1024]{1,0:T(8,128)(2,1)S(1)} %bitcast.138), channel_id=1, source_target_pairs={{0,1},{1,0},{2,3},{3,2},{4,5},{5,4},{6,7},{7,6},{8,9},{9,8},{10,11... | collective-permute-start | bytes 786440 | tf_op jit(solution)/shard_map/ppermute | solution.py:25
  89.4 12.4 %collective-permute-start.16 = (bf16[128,1024]{1,0:T(8,128)(2,1)S(1)}, bf16[128,1024]{1,0:T(8,128)(2,1)S(1)}, u32[]{:S(2)}, u32[]{:S(2)}) collective-permute-start(bf16[128,1024]{1,0:T(8,128)(2,1)S(1)} %bitcast.139), channel_id=1, source_target_pairs={{0,2},{1,3},{2,0},{3,1},{4,6},{5,7},{6,4},{7,5},{8,10},{9,11},{10,... | collective-permute-start | bytes 786440 | tf_op jit(solution)/shard_map/ppermute | solution.py:25
  102.9 14.1 %collective-permute-start.19 = (bf16[128,1024]{1,0:T(8,128)(2,1)S(1)}, bf16[128,1024]{1,0:T(8,128)(2,1)S(1)}, u32[]{:S(2)}, u32[]{:S(2)}) collective-permute-start(bf16[128,1024]{1,0:T(8,128)(2,1)S(1)} %collective-permute-done.16), channel_id=1, source_target_pairs={{0,1},{1,0},{2,3},{3,2},{4,5},{5,4},{6,7},{7,6},{8,9},{9,8},{10,11... | collective-permute-start | bytes 786440 | tf_op jit(solution)/shard_map/ppermute | solution.py:25
  105.0 26.9 %collective-permute-start.20 = (bf16[2,3,1,64,1024]{4,3,1,2,0:T(8,128)(2,1)S(1)}, bf16[2,3,1,64,1024]{4,3,1,2,0:T(8,128)(2,1)}, u32[]{:S(2)}, u32[]{:S(2)}) collective-permute-start(bf16[2,3,1,64,1024]{4,3,1,2,0:T(8,128)(2,1)S(1)} %pad_maximum_fusion.4), channel_id=1, source_target_pairs={{0,16},{4,20},{8,24},{12,28},{16,0},{20,4},{24,8},{28,12},{1,17},{... | collective-permute-start | bytes 2359304 | tf_op jit(solution)/shard_map/ppermute | solution.py:25
  106.5 25.4 %collective-permute-start.21 = (bf16[2,3,1,64,1024]{4,3,2,1,0:T(8,128)(2,1)}, bf16[2,3,1,64,1024]{4,3,2,1,0:T(8,128)(2,1)}, u32[]{:S(2)}, u32[]{:S(2)}) collective-permute-start(bf16[2,3,1,64,1024]{4,3,2,1,0:T(8,128)(2,1)} %pad_maximum_fusion.5.refs_18_.refs_19_), channel_id=1, source_target_pairs={{0,8},{4,12},{8,0},{12,4},{16,24},{20,28},{24,16},{28,20},{1,9},{5... | collective-permute-start | bytes 2359304 | tf_op jit(solution)/shard_map/ppermute | solution.py:25
  117.2 14.7 %collective-permute-start.22 = (bf16[1,3,1,64,1024]{4,3,1,2,0:T(8,128)(2,1)S(1)}, bf16[1,3,1,64,1024]{4,3,1,2,0:T(8,128)(2,1)S(1)}, u32[]{:S(2)}, u32[]{:S(2)}) collective-permute-start(bf16[1,3,1,64,1024]{4,3,1,2,0:T(8,128)(2,1)S(1)} %get-tuple-element.375), channel_id=1, source_target_pairs={{0,8},{4,12},{8,0},{12,4},{16,24},{20,28},{24,16},{28,20},{1,9},{5... | collective-permute-start | bytes 1179656 | tf_op jit(solution)/shard_map/ppermute | solution.py:25
  117.8 14.1 %collective-permute-start.23 = (bf16[1,3,1,64,1024]{4,3,2,1,0:T(8,128)(2,1)S(1)}, bf16[1,3,1,64,1024]{4,3,2,1,0:T(8,128)(2,1)S(1)}, u32[]{:S(2)}, u32[]{:S(2)}) collective-permute-start(bf16[1,3,1,64,1024]{4,3,2,1,0:T(8,128)(2,1)S(1)} %get-tuple-element.376), channel_id=1, source_target_pairs={{0,16},{4,20},{8,24},{12,28},{16,0},{20,4},{24,8},{28,12},{1,17},{... | collective-permute-start | bytes 1179656 | tf_op jit(solution)/shard_map/ppermute | solution.py:25
  134.9 26.5 %collective-permute-start.28 = (bf16[2,3,1,64,1024]{4,3,1,2,0:T(8,128)(2,1)}, bf16[2,3,1,64,1024]{4,3,1,2,0:T(8,128)(2,1)}, u32[]{:S(2)}, u32[]{:S(2)}) collective-permute-start(bf16[2,3,1,64,1024]{4,3,1,2,0:T(8,128)(2,1)} %pad_maximum_fusion.7), channel_id=1, source_target_pairs={{0,16},{4,20},{8,24},{12,28},{16,0},{20,4},{24,8},{28,12},{1,17},{... | collective-permute-start | bytes 2359304 | tf_op jit(solution)/shard_map/ppermute | solution.py:25
  138.2 23.2 %collective-permute-start.29 = (bf16[2,3,1,64,1024]{4,3,2,1,0:T(8,128)(2,1)}, bf16[2,3,1,64,1024]{4,3,2,1,0:T(8,128)(2,1)}, u32[]{:S(2)}, u32[]{:S(2)}) collective-permute-start(bf16[2,3,1,64,1024]{4,3,2,1,0:T(8,128)(2,1)} %pad_maximum_fusion.8.refs_7_.refs_28_), channel_id=1, source_target_pairs={{0,8},{4,12},{8,0},{12,4},{16,24},{20,28},{24,16},{28,20},{1,9},{5... | collective-permute-start | bytes 2359304 | tf_op jit(solution)/shard_map/ppermute | solution.py:25
  199.9 27.7 %collective-permute-start.35 = (bf16[2,128,2048]{2,1,0:T(8,128)(2,1)}, bf16[2,128,2048]{2,1,0:T(8,128)(2,1)S(1)}, u32[]{:S(2)}, u32[]{:S(2)}) collective-permute-start(bf16[2,128,2048]{2,1,0:T(8,128)(2,1)} %get-tuple-element.426), channel_id=1, source_target_pairs={{0,8},{4,12},{8,0},{12,4},{16,24},{20,28},{24,16},{28,20},{1,9},{5... | collective-permute-start | bytes 3145736 | tf_op jit(solution)/shard_map/ppermute | solution.py:25
  201.4 26.2 %collective-permute-start.36 = (bf16[2,128,2048]{2,1,0:T(8,128)(2,1)S(1)}, bf16[2,128,2048]{2,1,0:T(8,128)(2,1)S(1)}, u32[]{:S(2)}, u32[]{:S(2)}) collective-permute-start(bf16[2,128,2048]{2,1,0:T(8,128)(2,1)S(1)} %get-tuple-element.427), channel_id=1, source_target_pairs={{0,16},{4,20},{8,24},{12,28},{16,0},{20,4},{24,8},{28,12},{1,17},{... | collective-permute-start | bytes 3145736 | tf_op jit(solution)/shard_map/ppermute | solution.py:25
  234.6 30.3 %collective-permute-start.39 = (bf16[512,4096]{1,0:T(8,128)(2,1)S(1)}, bf16[512,4096]{1,0:T(8,128)(2,1)S(1)}, u32[]{:S(2)}, u32[]{:S(2)}) collective-permute-start(bf16[512,4096]{1,0:T(8,128)(2,1)S(1)} %other_half.3), channel_id=1, source_target_pairs={{0,4},{4,0},{8,12},{12,8},{16,20},{20,16},{24,28},{28,24},{1,5},{5... | collective-permute-start | bytes 12582920 | tf_op jit(solution)/shard_map/ppermute | solution.py:25
  234.7 30.2 %collective-permute-start.37 = (bf16[128,2048]{1,0:T(8,128)(2,1)S(1)}, bf16[128,2048]{1,0:T(8,128)(2,1)S(1)}, u32[]{:S(2)}, u32[]{:S(2)}) collective-permute-start(bf16[128,2048]{1,0:T(8,128)(2,1)S(1)} %get-tuple-element.445), channel_id=1, source_target_pairs={{0,16},{4,20},{8,24},{12,28},{16,0},{20,4},{24,8},{28,12},{1,17},{... | collective-permute-start | bytes 1572872 | tf_op jit(solution)/shard_map/ppermute | solution.py:25
  236.3 28.6 %collective-permute-start.38 = (bf16[128,2048]{1,0:T(8,128)(2,1)S(1)}, bf16[128,2048]{1,0:T(8,128)(2,1)S(1)}, u32[]{:S(2)}, u32[]{:S(2)}) collective-permute-start(bf16[128,2048]{1,0:T(8,128)(2,1)S(1)} %get-tuple-element.446), channel_id=1, source_target_pairs={{0,8},{4,12},{8,0},{12,4},{16,24},{20,28},{24,16},{28,20},{1,9},{5... | collective-permute-start | bytes 1572872 | tf_op jit(solution)/shard_map/ppermute | solution.py:25
  270.5 26.6 %collective-permute-start.42 = (bf16[544,1024]{1,0:T(8,128)(2,1)S(1)}, bf16[544,1024]{1,0:T(8,128)(2,1)S(1)}, u32[]{:S(2)}, u32[]{:S(2)}) collective-permute-start(bf16[544,1024]{1,0:T(8,128)(2,1)S(1)} %unproject.3), channel_id=1, source_target_pairs={{0,1},{1,0},{2,3},{3,2},{4,5},{5,4},{6,7},{7,6},{8,9},{9,8},{10,11... | collective-permute-start | bytes 3342344 | tf_op jit(solution)/shard_map/ppermute | solution.py:25
  271.2 24.7 %collective-permute-start.40 = (bf16[2,128,2048]{2,1,0:T(8,128)(2,1)S(1)}, bf16[2,128,2048]{2,1,0:T(8,128)(2,1)S(1)}, u32[]{:S(2)}, u32[]{:S(2)}) collective-permute-start(bf16[2,128,2048]{2,1,0:T(8,128)(2,1)S(1)} %get-tuple-element.459), channel_id=1, source_target_pairs={{0,8},{4,12},{8,0},{12,4},{16,24},{20,28},{24,16},{28,20},{1,9},{5... | collective-permute-start | bytes 3145736 | tf_op jit(solution)/shard_map/ppermute | solution.py:25
  272.7 24.4 %collective-permute-start.41 = (bf16[2,128,2048]{2,1,0:T(8,128)(2,1)S(1)}, bf16[2,128,2048]{2,1,0:T(8,128)(2,1)S(1)}, u32[]{:S(2)}, u32[]{:S(2)}) collective-permute-start(bf16[2,128,2048]{2,1,0:T(8,128)(2,1)S(1)} %get-tuple-element.460), channel_id=1, source_target_pairs={{0,16},{4,20},{8,24},{12,28},{16,0},{20,4},{24,8},{28,12},{1,17},{... | collective-permute-start | bytes 3145736 | tf_op jit(solution)/shard_map/ppermute | solution.py:25
  298.3 25.6 %collective-permute-start.44 = (bf16[128,2048]{1,0:T(8,128)(2,1)S(1)}, bf16[128,2048]{1,0:T(8,128)(2,1)S(1)}, u32[]{:S(2)}, u32[]{:S(2)}) collective-permute-start(bf16[128,2048]{1,0:T(8,128)(2,1)S(1)} %get-tuple-element.500), channel_id=1, source_target_pairs={{0,16},{4,20},{8,24},{12,28},{16,0},{20,4},{24,8},{28,12},{1,17},{... | collective-permute-start | bytes 1572872 | tf_op jit(solution)/shard_map/ppermute | solution.py:25
  298.8 25.1 %collective-permute-start.45 = (bf16[128,2048]{1,0:T(8,128)(2,1)S(1)}, bf16[128,2048]{1,0:T(8,128)(2,1)S(1)}, u32[]{:S(2)}, u32[]{:S(2)}) collective-permute-start(bf16[128,2048]{1,0:T(8,128)(2,1)S(1)} %get-tuple-element.501), channel_id=1, source_target_pairs={{0,8},{4,12},{8,0},{12,4},{16,24},{20,28},{24,16},{28,20},{1,9},{5... | collective-permute-start | bytes 1572872 | tf_op jit(solution)/shard_map/ppermute | solution.py:25
  310.1 13.8 %collective-permute-start.48 = (bf16[2,128,1024]{2,1,0:T(8,128)(2,1)S(1)}, bf16[2,128,1024]{2,1,0:T(8,128)(2,1)S(1)}, u32[]{:S(2)}, u32[]{:S(2)}) collective-permute-start(bf16[2,128,1024]{2,1,0:T(8,128)(2,1)S(1)} %get-tuple-element.504), channel_id=1, source_target_pairs={{0,1},{1,0},{2,3},{3,2},{4,5},{5,4},{6,7},{7,6},{8,9},{9,8},{10,11... | collective-permute-start | bytes 1572872 | tf_op jit(solution)/shard_map/ppermute | solution.py:25
  310.8 13.5 %collective-permute-start.46 = (bf16[2,128,1024]{2,1,0:T(8,128)(2,1)S(1)}, bf16[2,128,1024]{2,1,0:T(8,128)(2,1)S(1)}, u32[]{:S(2)}, u32[]{:S(2)}) collective-permute-start(bf16[2,128,1024]{2,1,0:T(8,128)(2,1)S(1)} %get-tuple-element.502), channel_id=1, source_target_pairs={{0,8},{4,12},{8,0},{12,4},{16,24},{20,28},{24,16},{28,20},{1,9},{5... | collective-permute-start | bytes 1572872 | tf_op jit(solution)/shard_map/ppermute | solution.py:25
  312.2 13.2 %collective-permute-start.47 = (bf16[2,128,1024]{2,1,0:T(8,128)(2,1)S(1)}, bf16[2,128,1024]{2,1,0:T(8,128)(2,1)S(1)}, u32[]{:S(2)}, u32[]{:S(2)}) collective-permute-start(bf16[2,128,1024]{2,1,0:T(8,128)(2,1)S(1)} %get-tuple-element.503), channel_id=1, source_target_pairs={{0,16},{4,20},{8,24},{12,28},{16,0},{20,4},{24,8},{28,12},{1,17},{... | collective-permute-start | bytes 1572872 | tf_op jit(solution)/shard_map/ppermute | solution.py:25
  329.9 20.0 %collective-permute-start.52 = (bf16[2,128,1024]{2,1,0:T(8,128)(2,1)S(1)}, bf16[2,128,1024]{2,1,0:T(8,128)(2,1)S(1)}, u32[]{:S(2)}, u32[]{:S(2)}) collective-permute-start(bf16[2,128,1024]{2,1,0:T(8,128)(2,1)S(1)} %get-tuple-element.549), channel_id=1, source_target_pairs={{0,1},{1,0},{2,3},{3,2},{4,5},{5,4},{6,7},{7,6},{8,9},{9,8},{10,11... | collective-permute-start | bytes 1572872 | tf_op jit(solution)/shard_map/ppermute | solution.py:25
  333.5 15.4 %collective-permute-start.53 = (bf16[128,1024]{1,0:T(8,128)(2,1)S(1)}, bf16[128,1024]{1,0:T(8,128)(2,1)S(1)}, u32[]{:S(2)}, u32[]{:S(2)}) collective-permute-start(bf16[128,1024]{1,0:T(8,128)(2,1)S(1)} %fusion.6), channel_id=1, source_target_pairs={{0,2},{1,3},{2,0},{3,1},{4,6},{5,7},{6,4},{7,5},{8,10},{9,11},{10,... | collective-permute-start | bytes 786440 | tf_op jit(solution)/shard_map/ppermute | solution.py:25
  351.5 78.0 %all-gather.7.cloned.1.call-start = ((), (), s32[]{:S(2)}) async-start(), calls=%async_computation.1 | async-start | bytes 2359296 | tf_op jit(solution)/shard_map/all_gather | solution.py:1515
  353.3 14.6 %collective-permute-start.57 = (bf16[128,1024]{1,0:T(8,128)(2,1)S(1)}, bf16[128,1024]{1,0:T(8,128)(2,1)S(1)}, u32[]{:S(2)}, u32[]{:S(2)}) collective-permute-start(bf16[128,1024]{1,0:T(8,128)(2,1)S(1)} %fusion.7), channel_id=1, source_target_pairs={{0,2},{1,3},{2,0},{3,1},{4,6},{5,7},{6,4},{7,5},{8,10},{9,11},{10,... | collective-permute-start | bytes 786440 | tf_op jit(solution)/shard_map/ppermute | solution.py:25
  355.0 16.1 %collective-permute-start.54 = (bf16[2,128,1024]{2,1,0:T(8,128)(2,1)}, bf16[2,128,1024]{2,1,0:T(8,128)(2,1)S(1)}, u32[]{:S(2)}, u32[]{:S(2)}) collective-permute-start(bf16[2,128,1024]{2,1,0:T(8,128)(2,1)} %copy-done.67), channel_id=1, source_target_pairs={{0,8},{4,12},{8,0},{12,4},{16,24},{20,28},{24,16},{28,20},{1,9},{5... | collective-permute-start | bytes 1572872 | tf_op jit(solution)/shard_map/ppermute | solution.py:25
  356.5 15.7 %collective-permute-start.55 = (bf16[2,128,1024]{2,1,0:T(8,128)(2,1)}, bf16[2,128,1024]{2,1,0:T(8,128)(2,1)S(1)}, u32[]{:S(2)}, u32[]{:S(2)}) collective-permute-start(bf16[2,128,1024]{2,1,0:T(8,128)(2,1)} %copy-done.66), channel_id=1, source_target_pairs={{0,16},{4,20},{8,24},{12,28},{16,0},{20,4},{24,8},{28,12},{1,17},{... | collective-permute-start | bytes 1572872 | tf_op jit(solution)/shard_map/ppermute | solution.py:25
  381.9 12.9 %collective-permute-start.58 = (bf16[128,1024]{1,0:T(8,128)(2,1)S(1)}, bf16[128,1024]{1,0:T(8,128)(2,1)S(1)}, u32[]{:S(2)}, u32[]{:S(2)}) collective-permute-start(bf16[128,1024]{1,0:T(8,128)(2,1)S(1)} %fusion.8), channel_id=1, source_target_pairs={{0,2},{1,3},{2,0},{3,1},{4,6},{5,7},{6,4},{7,5},{8,10},{9,11},{10,... | collective-permute-start | bytes 786440 | tf_op jit(solution)/shard_map/ppermute | solution.py:25
  403.0 19.5 %collective-permute-start.65 = (bf16[2,128,512]{2,1,0:T(8,128)(2,1)S(1)}, bf16[2,128,512]{2,1,0:T(8,128)(2,1)S(1)}, u32[]{:S(2)}, u32[]{:S(2)}) collective-permute-start(bf16[2,128,512]{2,1,0:T(8,128)(2,1)S(1)} %pad_maximum_fusion.11.refs_2_), channel_id=1, source_target_pairs={{0,8},{4,12},{8,0},{12,4},{16,24},{20,28},{24,16},{28,20},{1,9},{5... | collective-permute-start | bytes 786440 | tf_op jit(solution)/shard_map/ppermute | solution.py:25
  404.7 17.9 %collective-permute-start.63 = (bf16[2,128,512]{2,1,0:T(8,128)(2,1)S(1)}, bf16[2,128,512]{2,1,0:T(8,128)(2,1)S(1)}, u32[]{:S(2)}, u32[]{:S(2)}) collective-permute-start(bf16[2,128,512]{2,1,0:T(8,128)(2,1)S(1)} %pad_maximum_fusion.10.refs_0_), channel_id=1, source_target_pairs={{0,16},{4,20},{8,24},{12,28},{16,0},{20,4},{24,8},{28,12},{1,17},{... | collective-permute-start | bytes 786440 | tf_op jit(solution)/shard_map/ppermute | solution.py:25
  422.0 16.1 %collective-permute-start.68 = (bf16[2,128,512]{2,1,0:T(8,128)(2,1)S(1)}, bf16[2,128,512]{2,1,0:T(8,128)(2,1)S(1)}, u32[]{:S(2)}, u32[]{:S(2)}) collective-permute-start(bf16[2,128,512]{2,1,0:T(8,128)(2,1)S(1)} %pad_maximum_fusion.11.refs_2_), channel_id=1, source_target_pairs={{0,4},{4,0},{8,12},{12,8},{16,20},{20,16},{24,28},{28,24},{1,5},{5... | collective-permute-start | bytes 786440 | tf_op jit(solution)/shard_map/ppermute | solution.py:25
  422.0 16.1 %collective-permute-start.66 = (bf16[2,128,512]{2,1,0:T(8,128)(2,1)S(1)}, bf16[2,128,512]{2,1,0:T(8,128)(2,1)S(1)}, u32[]{:S(2)}, u32[]{:S(2)}) collective-permute-start(bf16[2,128,512]{2,1,0:T(8,128)(2,1)S(1)} %pad_maximum_fusion.10.refs_0_), channel_id=1, source_target_pairs={{0,4},{4,0},{8,12},{12,8},{16,20},{20,16},{24,28},{28,24},{1,5},{5... | collective-permute-start | bytes 786440 | tf_op jit(solution)/shard_map/ppermute | solution.py:25
  422.6 15.6 %collective-permute-start.69 = (bf16[2,128,512]{2,1,0:T(8,128)(2,1)S(1)}, bf16[2,128,512]{2,1,0:T(8,128)(2,1)S(1)}, u32[]{:S(2)}, u32[]{:S(2)}) collective-permute-start(bf16[2,128,512]{2,1,0:T(8,128)(2,1)S(1)} %collective-permute-done.65.refs_3_), channel_id=1, source_target_pairs={{0,4},{4,0},{8,12},{12,8},{16,20},{20,16},{24,28},{28,24},{1,5},{5... | collective-permute-start | bytes 786440 | tf_op jit(solution)/shard_map/ppermute | solution.py:25
  422.6 15.6 %collective-permute-start.67 = (bf16[2,128,512]{2,1,0:T(8,128)(2,1)S(1)}, bf16[2,128,512]{2,1,0:T(8,128)(2,1)S(1)}, u32[]{:S(2)}, u32[]{:S(2)}) collective-permute-start(bf16[2,128,512]{2,1,0:T(8,128)(2,1)S(1)} %collective-permute-done.63.refs_1_), channel_id=1, source_target_pairs={{0,4},{4,0},{8,12},{12,8},{16,20},{20,16},{24,28},{28,24},{1,5},{5... | collective-permute-start | bytes 786440 | tf_op jit(solution)/shard_map/ppermute | solution.py:25
  433.4 11.4 %collective-permute-start.74 = (f32[34,1024]{1,0:T(8,128)S(1)}, f32[34,1024]{1,0:T(8,128)S(1)}, u32[]{:S(2)}, u32[]{:S(2)}) collective-permute-start(f32[34,1024]{1,0:T(8,128)S(1)} %add.235), channel_id=1, source_target_pairs={{0,2},{1,3},{2,0},{3,1},{4,6},{5,7},{6,4},{7,5},{8,10},{9,11},{10,... | collective-permute-start | bytes 417800 | tf_op jit(solution)/shard_map/ppermute | solution.py:25
  (123 other events, 1066.7 us)
Sparse Core Ops, SparseCore 0:
  351.6 31.9 all-gather.4
  386.1 33.2 all-gather.6
